TPU v7x, 32 devices: a whole 2x2x4 slice. The times are simulated.
32 devices in a mesh: dp: 4 (over z), fsdp: 8 (over y, x, core).
Axes of the slice: x: 2, y: 2, z: 4, core: 2. Of those that a mesh axis runs over, the one named last changes fastest.
Arguments:
- tokens: bfloat16 [4096, 1280], P(('dp', 'fsdp')), may hold values from -6 to 6
- lengths: int32 [32, 2], P(('dp', 'fsdp')), may hold values from 1 to 96, 128 in all within a row
- padding: int32 [4096], P(('dp', 'fsdp')), may hold values 0 or 1
- ln1_gain: bfloat16 [1280], P('fsdp'), may hold values from 0.099609375 to 1.8984375
- ln1_bias: bfloat16 [1280], P('fsdp'), may hold values from -4 to 4
- w_qkv: bfloat16 [1280, 3840], P('fsdp'), may hold values from -0.15625 to 0.15625
- b_query: bfloat16 [1280], P('fsdp'), may hold values from -4 to 4
- b_value: bfloat16 [1280], P('fsdp'), may hold values from -4 to 4
- w_out: bfloat16 [1280, 1280], P('fsdp'), may hold values from -0.625 to 0.625
- b_out: bfloat16 [1280], P('fsdp'), may hold values from -4 to 4
- ln2_gain: bfloat16 [1280], P('fsdp'), may hold values from 0.099609375 to 1.8984375
- ln2_bias: bfloat16 [1280], P('fsdp'), may hold values from -4 to 4
- w_up: bfloat16 [1280, 5120], P('fsdp'), may hold values from -0.15625 to 0.15625
- b_up: bfloat16 [5120], P('fsdp'), may hold values from -6 to 6
- w_down: bfloat16 [5120, 1280], P('fsdp'), may hold values from -0.078125 to 0.078125
- b_down: bfloat16 [1280], P('fsdp'), may hold values from -4 to 4
- cotangent: bfloat16 [4096, 1280], P(('dp', 'fsdp')), may hold values from -6 to 6
Outputs:
- layer_out: bfloat16 [4096, 1280], P(('dp', 'fsdp'))
- grad_tokens: float32 [4096, 1280], P(('dp', 'fsdp'))
- grad_ln1_gain: float32 [1280], P('fsdp')
- grad_ln1_bias: float32 [1280], P('fsdp')
- grad_w_qkv: float32 [1280, 3840], P('fsdp')
- grad_b_query: float32 [1280], P('fsdp')
- grad_b_value: float32 [1280], P('fsdp')
- grad_w_out: float32 [1280, 1280], P('fsdp')
- grad_b_out: float32 [1280], P('fsdp')
- grad_ln2_gain: float32 [1280], P('fsdp')
- grad_ln2_bias: float32 [1280], P('fsdp')
- grad_w_up: float32 [1280, 5120], P('fsdp')
- grad_b_up: float32 [5120], P('fsdp')
- grad_w_down: float32 [5120, 1280], P('fsdp')
- grad_b_down: float32 [1280], P('fsdp')
- cls_mean: float32 [1280], replicated
- cls_var: float32 [1280], replicated
Inputs may be any that keep to these rules, and one draw needn't show every extreme that they name: `lengths`: each row sums to 128; each length lies between 32 and 96. `padding`: A CLS token is a key whatever its mark.
All inputs are finite; a program needn't handle non-finite values. No bound on the sum of `padding` on one device may be relied on, other than what follows from the above.
Results may differ from a plain program's by a relative error of at most 0.015.
Values may be sent and summed in bfloat16 or wider, within the bound.
No kernel may reach another device: no remote copies, remote signals or barrier semaphores. Data moves between devices by JAX's collectives and lax.ppermute only.
A program may use at most 256 MiB of HBM per device.

v0:
```python
from functools import partial

import jax
import jax.numpy as jnp
from jax import lax
from jax.sharding import PartitionSpec as P

D = 1280
HEADS = 20
HEAD_DIM = 64
CELLS_DEV = 2


EPS = 1e-05


def norm_forward(values, norm_gain, norm_bias):
    center = jnp.mean(values, axis=-1, keepdims=True)
    centred = values - center
    spread = jnp.mean(centred * centred, axis=-1, keepdims=True)
    inverse = lax.rsqrt(spread + EPS)
    normed = centred * inverse
    return (normed * norm_gain + norm_bias, normed, inverse)


def norm_backward(grad_out, normed, inverse, norm_gain):
    grad_normed = grad_out * norm_gain
    first_mean = jnp.mean(grad_normed, axis=-1, keepdims=True)
    second_mean = jnp.mean(grad_normed * normed, axis=-1, keepdims=True)
    grad_in = inverse * (grad_normed - first_mean - normed * second_mean)
    return (grad_in, jnp.sum(grad_out * normed, axis=0), jnp.sum(grad_out, axis=0))


def cell_layout(lengths_row, padding_row):
    places = jnp.arange(padding_row.shape[0], dtype=jnp.int32)
    finish = jnp.cumsum(lengths_row)
    starts = finish - lengths_row
    member = jnp.sum((places[:, None] >= finish[None, :]).astype(jnp.int32), axis=1)
    leading = jnp.any(places[:, None] == starts[None, :], axis=1)
    usable = (padding_row > 0) | leading
    allowed = (member[:, None] == member[None, :]) & usable[None, :]
    return (allowed, leading)


def masked_scores(query_low, key_low, allowed, score_scale):
    raw = jnp.einsum("thd,shd->hts", query_low, key_low, preferred_element_type=jnp.float32)
    return jnp.where(allowed[None], raw * score_scale, -1e30)


def reduce_late(values):
    owned = (
        lax.psum_scatter(values[0], "fsdp", scatter_dimension=0, tiled=True),
        lax.psum_scatter(values[1], "fsdp", scatter_dimension=0, tiled=True),
        lax.psum_scatter(values[2], "fsdp", scatter_dimension=0, tiled=True),
        lax.psum_scatter(values[3], "fsdp", scatter_dimension=0, tiled=True),
        lax.psum_scatter(values[4], "fsdp", scatter_dimension=0, tiled=True),
        lax.psum_scatter(values[5], "fsdp", scatter_dimension=0, tiled=True),
        lax.psum_scatter(values[6], "fsdp", scatter_dimension=0, tiled=True),
        lax.psum_scatter(values[7], "fsdp", scatter_dimension=0, tiled=True),
        lax.psum_scatter(values[8], "fsdp", scatter_dimension=0, tiled=True),
        lax.psum_scatter(values[9], "fsdp", scatter_dimension=0, tiled=True),
        lax.psum_scatter(values[10], "fsdp", scatter_dimension=0, tiled=True),
        lax.psum_scatter(values[11], "fsdp", scatter_dimension=0, tiled=True),
        lax.psum_scatter(values[12], "fsdp", scatter_dimension=0, tiled=True),
    )
    shares = (
        lax.psum_scatter(
            owned[0].astype(jnp.bfloat16), "dp", scatter_dimension=0, tiled=True
        ).astype(jnp.float32),
        lax.psum_scatter(
            owned[1].astype(jnp.bfloat16), "dp", scatter_dimension=0, tiled=True
        ).astype(jnp.float32),
        lax.psum_scatter(
            owned[2].astype(jnp.bfloat16), "dp", scatter_dimension=0, tiled=True
        ).astype(jnp.float32),
        lax.psum_scatter(
            owned[3].astype(jnp.bfloat16), "dp", scatter_dimension=0, tiled=True
        ).astype(jnp.float32),
        lax.psum_scatter(
            owned[4].astype(jnp.bfloat16), "dp", scatter_dimension=0, tiled=True
        ).astype(jnp.float32),
        lax.psum_scatter(
            owned[5].astype(jnp.bfloat16), "dp", scatter_dimension=0, tiled=True
        ).astype(jnp.float32),
        lax.psum_scatter(
            owned[6].astype(jnp.bfloat16), "dp", scatter_dimension=0, tiled=True
        ).astype(jnp.float32),
        lax.psum_scatter(
            owned[7].astype(jnp.bfloat16), "dp", scatter_dimension=0, tiled=True
        ).astype(jnp.float32),
        lax.psum_scatter(
            owned[8].astype(jnp.bfloat16), "dp", scatter_dimension=0, tiled=True
        ).astype(jnp.float32),
        lax.psum_scatter(
            owned[9].astype(jnp.bfloat16), "dp", scatter_dimension=0, tiled=True
        ).astype(jnp.float32),
        lax.psum_scatter(
            owned[10].astype(jnp.bfloat16), "dp", scatter_dimension=0, tiled=True
        ).astype(jnp.float32),
        lax.psum_scatter(
            owned[11].astype(jnp.bfloat16), "dp", scatter_dimension=0, tiled=True
        ).astype(jnp.float32),
        lax.psum_scatter(
            owned[12].astype(jnp.bfloat16), "dp", scatter_dimension=0, tiled=True
        ).astype(jnp.float32),
    )
    return (
        lax.all_gather(shares[0].astype(jnp.bfloat16), "dp", axis=0, tiled=True).astype(
            jnp.float32
        ),
        lax.all_gather(shares[1].astype(jnp.bfloat16), "dp", axis=0, tiled=True).astype(
            jnp.float32
        ),
        lax.all_gather(shares[2].astype(jnp.bfloat16), "dp", axis=0, tiled=True).astype(
            jnp.float32
        ),
        lax.all_gather(shares[3].astype(jnp.bfloat16), "dp", axis=0, tiled=True).astype(
            jnp.float32
        ),
        lax.all_gather(shares[4].astype(jnp.bfloat16), "dp", axis=0, tiled=True).astype(
            jnp.float32
        ),
        lax.all_gather(shares[5].astype(jnp.bfloat16), "dp", axis=0, tiled=True).astype(
            jnp.float32
        ),
        lax.all_gather(shares[6].astype(jnp.bfloat16), "dp", axis=0, tiled=True).astype(
            jnp.float32
        ),
        lax.all_gather(shares[7].astype(jnp.bfloat16), "dp", axis=0, tiled=True).astype(
            jnp.float32
        ),
        lax.all_gather(shares[8].astype(jnp.bfloat16), "dp", axis=0, tiled=True).astype(
            jnp.float32
        ),
        lax.all_gather(shares[9].astype(jnp.bfloat16), "dp", axis=0, tiled=True).astype(
            jnp.float32
        ),
        lax.all_gather(shares[10].astype(jnp.bfloat16), "dp", axis=0, tiled=True).astype(
            jnp.float32
        ),
        lax.all_gather(shares[11].astype(jnp.bfloat16), "dp", axis=0, tiled=True).astype(
            jnp.float32
        ),
        lax.all_gather(shares[12].astype(jnp.bfloat16), "dp", axis=0, tiled=True).astype(
            jnp.float32
        ),
    )


def local(
    tokens,
    lengths,
    padding,
    ln1_gain,
    ln1_bias,
    w_qkv,
    b_query,
    b_value,
    w_out,
    b_out,
    ln2_gain,
    ln2_bias,
    w_up,
    b_up,
    w_down,
    b_down,
    cotangent,
):
    fsdp_count = lax.axis_size("fsdp")
    dp_count = lax.axis_size("dp")
    f32 = jnp.float32
    bf16 = jnp.bfloat16
    row_total = tokens.shape[0]
    score_scale = HEAD_DIM ** (-0.5)
    (
        first_gain,
        first_bias,
        whole_qkv,
        query_bias,
        value_bias,
        whole_out,
        out_bias,
        second_gain,
        second_bias,
        whole_up,
        up_bias,
        whole_down,
        down_bias,
    ) = (
        lax.all_gather(ln1_gain, "fsdp", axis=0, tiled=True),
        lax.all_gather(ln1_bias, "fsdp", axis=0, tiled=True),
        lax.all_gather(w_qkv, "fsdp", axis=0, tiled=True),
        lax.all_gather(b_query, "fsdp", axis=0, tiled=True),
        lax.all_gather(b_value, "fsdp", axis=0, tiled=True),
        lax.all_gather(w_out, "fsdp", axis=0, tiled=True),
        lax.all_gather(b_out, "fsdp", axis=0, tiled=True),
        lax.all_gather(ln2_gain, "fsdp", axis=0, tiled=True),
        lax.all_gather(ln2_bias, "fsdp", axis=0, tiled=True),
        lax.all_gather(w_up, "fsdp", axis=0, tiled=True),
        lax.all_gather(b_up, "fsdp", axis=0, tiled=True),
        lax.all_gather(w_down, "fsdp", axis=0, tiled=True),
        lax.all_gather(b_down, "fsdp", axis=0, tiled=True),
    )
    allowed, leading = cell_layout(lengths[0], padding)
    inputs = tokens.astype(f32)
    first_out, first_normed, first_inverse = norm_forward(
        inputs, first_gain.astype(f32), first_bias.astype(f32)
    )
    first_low = first_out.astype(bf16)
    projected = jnp.dot(first_low, whole_qkv, preferred_element_type=f32)
    query_low = (
        (projected[:, :D] + query_bias.astype(f32)).astype(bf16).reshape(row_total, HEADS, HEAD_DIM)
    )
    key_low = projected[:, D : 2 * D].astype(bf16).reshape(row_total, HEADS, HEAD_DIM)
    value_low = (
        (projected[:, 2 * D :] + value_bias.astype(f32))
        .astype(bf16)
        .reshape(row_total, HEADS, HEAD_DIM)
    )
    masked = masked_scores(query_low, key_low, allowed, score_scale)
    top_score = jnp.max(masked, axis=-1, keepdims=True)
    log_total = top_score + jnp.log(jnp.sum(jnp.exp(masked - top_score), axis=-1, keepdims=True))
    probs_low = jnp.exp(masked - log_total).astype(bf16)
    context = jnp.einsum("hts,shd->thd", probs_low, value_low, preferred_element_type=f32)
    context_low = context.reshape(row_total, D).astype(bf16)
    mixed = (
        inputs + jnp.dot(context_low, whole_out, preferred_element_type=f32) + out_bias.astype(f32)
    )
    second_out, second_normed, second_inverse = norm_forward(
        mixed, second_gain.astype(f32), second_bias.astype(f32)
    )
    second_low = second_out.astype(bf16)
    hidden_pre = jnp.dot(second_low, whole_up, preferred_element_type=f32) + up_bias.astype(f32)
    activated, gelu_pull = jax.vjp(partial(jax.nn.gelu, approximate=False), hidden_pre)
    act_low = activated.astype(bf16)
    result = (
        mixed + jnp.dot(act_low, whole_down, preferred_element_type=f32) + down_bias.astype(f32)
    )
    picked = jnp.where(leading[:, None], result, 0.0)
    moment_sum, moment_square = lax.psum(
        (jnp.sum(picked, axis=0), jnp.sum(picked * picked, axis=0)), ("dp", "fsdp")
    )
    cell_total = CELLS_DEV * dp_count * fsdp_count
    cls_mean = moment_sum / cell_total
    cls_var = moment_square / cell_total - cls_mean * cls_mean
    (
        first_gain,
        first_bias,
        whole_qkv,
        query_bias,
        value_bias,
        whole_out,
        out_bias,
        second_gain,
        second_bias,
        whole_up,
        up_bias,
        whole_down,
        down_bias,
    ) = (
        lax.all_gather(ln1_gain, "fsdp", axis=0, tiled=True),
        lax.all_gather(ln1_bias, "fsdp", axis=0, tiled=True),
        lax.all_gather(w_qkv, "fsdp", axis=0, tiled=True),
        lax.all_gather(b_query, "fsdp", axis=0, tiled=True),
        lax.all_gather(b_value, "fsdp", axis=0, tiled=True),
        lax.all_gather(w_out, "fsdp", axis=0, tiled=True),
        lax.all_gather(b_out, "fsdp", axis=0, tiled=True),
        lax.all_gather(ln2_gain, "fsdp", axis=0, tiled=True),
        lax.all_gather(ln2_bias, "fsdp", axis=0, tiled=True),
        lax.all_gather(w_up, "fsdp", axis=0, tiled=True),
        lax.all_gather(b_up, "fsdp", axis=0, tiled=True),
        lax.all_gather(w_down, "fsdp", axis=0, tiled=True),
        lax.all_gather(b_down, "fsdp", axis=0, tiled=True),
    )
    grad_result = cotangent.astype(f32)
    grad_down_bias = jnp.sum(grad_result, axis=0)
    grad_whole_down = jnp.einsum("tf,td->fd", act_low, cotangent, preferred_element_type=f32)
    grad_act = jnp.einsum("td,fd->tf", cotangent, whole_down, preferred_element_type=f32)
    grad_pre = gelu_pull(grad_act)[0].astype(bf16)
    grad_up_bias = jnp.sum(grad_pre.astype(f32), axis=0)
    grad_whole_up = jnp.einsum("td,tf->df", second_low, grad_pre, preferred_element_type=f32)
    grad_second = jnp.einsum("tf,df->td", grad_pre, whole_up, preferred_element_type=f32)
    grad_from_second, grad_second_gain, grad_second_bias = norm_backward(
        grad_second, second_normed, second_inverse, second_gain.astype(f32)
    )
    grad_mixed = grad_result + grad_from_second
    grad_branch = grad_mixed.astype(bf16)
    grad_out_bias = jnp.sum(grad_branch.astype(f32), axis=0)
    grad_whole_out = jnp.einsum("td,te->de", context_low, grad_branch, preferred_element_type=f32)
    grad_context = jnp.einsum("te,de->td", grad_branch, whole_out, preferred_element_type=f32)
    grad_context = grad_context.astype(bf16).reshape(row_total, HEADS, HEAD_DIM)
    masked = masked_scores(query_low, key_low, allowed, score_scale)
    probs = jnp.exp(masked - log_total)
    probs_low = probs.astype(bf16)
    grad_probs = jnp.einsum("thd,shd->hts", grad_context, value_low, preferred_element_type=f32)
    along = jnp.sum(grad_probs * probs, axis=-1, keepdims=True)
    grad_scores = (probs * (grad_probs - along) * score_scale).astype(bf16)
    grad_value = jnp.einsum(
        "hts,thd->shd", probs_low, grad_context, preferred_element_type=f32
    ).astype(bf16)
    grad_query = jnp.einsum(
        "hts,shd->thd", grad_scores, key_low, preferred_element_type=f32
    ).astype(bf16)
    grad_key = jnp.einsum(
        "hts,thd->shd", grad_scores, query_low, preferred_element_type=f32
    ).astype(bf16)
    grad_query = grad_query.reshape(row_total, D)
    grad_key = grad_key.reshape(row_total, D)
    grad_value = grad_value.reshape(row_total, D)
    grad_query_bias = jnp.sum(grad_query.astype(f32), axis=0)
    grad_value_bias = jnp.sum(grad_value.astype(f32), axis=0)
    grad_projected = jnp.concatenate([grad_query, grad_key, grad_value], axis=1)
    grad_whole_qkv = jnp.einsum("td,te->de", first_low, grad_projected, preferred_element_type=f32)
    grad_first = jnp.einsum("te,de->td", grad_projected, whole_qkv, preferred_element_type=f32)
    grad_from_first, grad_first_gain, grad_first_bias = norm_backward(
        grad_first, first_normed, first_inverse, first_gain.astype(f32)
    )
    grad_inputs = grad_mixed + grad_from_first
    totals = reduce_late(
        (
            grad_first_gain,
            grad_first_bias,
            grad_whole_qkv,
            grad_query_bias,
            grad_value_bias,
            grad_whole_out,
            grad_out_bias,
            grad_second_gain,
            grad_second_bias,
            grad_whole_up,
            grad_up_bias,
            grad_whole_down,
            grad_down_bias,
        )
    )
    return (
        result.astype(bf16),
        grad_inputs,
        totals[0],
        totals[1],
        totals[2],
        totals[3],
        totals[4],
        totals[5],
        totals[6],
        totals[7],
        totals[8],
        totals[9],
        totals[10],
        totals[11],
        totals[12],
        cls_mean,
        cls_var,
    )


def solution(mesh):
    in_specs = (
        P(("dp", "fsdp"), None),
        P(("dp", "fsdp"), None),
        P(("dp", "fsdp")),
        P("fsdp"),
        P("fsdp"),
        P("fsdp", None),
        P("fsdp"),
        P("fsdp"),
        P("fsdp", None),
        P("fsdp"),
        P("fsdp"),
        P("fsdp"),
        P("fsdp", None),
        P("fsdp"),
        P("fsdp", None),
        P("fsdp"),
        P(("dp", "fsdp"), None),
    )
    out_specs = (
        P(("dp", "fsdp"), None),
        P(("dp", "fsdp"), None),
        P("fsdp"),
        P("fsdp"),
        P("fsdp", None),
        P("fsdp"),
        P("fsdp"),
        P("fsdp", None),
        P("fsdp"),
        P("fsdp"),
        P("fsdp"),
        P("fsdp", None),
        P("fsdp"),
        P("fsdp", None),
        P("fsdp"),
        P(),
        P(),
    )
    return jax.shard_map(local, mesh=mesh, in_specs=in_specs, out_specs=out_specs, check_vma=False)
```

profile of v0, /device:TPU:0, one launch (start us, length us, event | category | flops | bytes accessed | tf_op | source)
XLA Modules:
  0.0 1096.5 jit_solution(2530237779539740819)
XLA Ops:
  13.5 25.9 %all-reduce.37 = (bf16[1280]{0:T(1024)(128)(2,1)S(1)}, bf16[1280]{0:T(1024)(128)(2,1)S(1)}, bf16[1280]{0:T(1024)(128)(2,1)S(1)}, bf16[1280]{0:T(1024)(128)(2,1)S...) all-reduce(bf16[1280]{0:T(1024)(128)(2,1)S(1)} %dynamic-update-slic, ...), channel_id=1, replica_groups=mesh['dp'=4,'fsdp'=8] {'fsdp'}, use_global_device_ids=true, to_apply=%add.1 | all-reduce | flops 10240 | bytes 40960
  39.5 8.1 all-gather
  48.6 24.9 %all-gather.9.cloned.1.call-done = bf16[1280,3840]{1,0:T(8,128)(2,1)} async-done(((bf16[160,3840]{1,0:T(8,128)(2,1)}), bf16[1280,3840]{1,0:T(8,128)(2,1)}) %all-gather.9.cloned.1.call-update) | async-done | bytes 9830416 | tf_op jit(solution)/shard_map/all_gather | solution.py:192
  73.4 5.3 fusion.66
  81.4 26.8 %all-gather.11.cloned.1.call-done = bf16[1280,1280]{1,0:T(8,128)(2,1)} async-done(((bf16[160,1280]{1,0:T(8,128)(2,1)}), bf16[1280,1280]{1,0:T(8,128)(2,1)}) %all-gather.11.cloned.1.call-update) | async-done | bytes 3276816 | tf_op jit(solution)/shard_map/all_gather | solution.py:195
  111.1 73.4 %all-gather.13.cloned.1.call-done = bf16[1280,5120]{1,0:T(8,128)(2,1)} async-done(((bf16[160,5120]{1,0:T(8,128)(2,1)}), bf16[1280,5120]{1,0:T(8,128)(2,1)}) %all-gather.13.cloned.1.call-update) | async-done | bytes 13107216 | tf_op jit(solution)/shard_map/all_gather | solution.py:199
  184.5 8.2 convolution_add_fusion
  192.7 67.9 %all-gather.15.cloned.1.call-done = bf16[5120,1280]{1,0:T(8,128)(2,1)} async-done(((bf16[640,1280]{1,0:T(8,128)(2,1)}), bf16[5120,1280]{1,0:T(8,128)(2,1)}) %all-gather.15.cloned.1.call-update) | async-done | bytes 13107216 | tf_op jit(solution)/shard_map/all_gather | solution.py:201
  260.6 14.1 %convert_reduce_fusion = (f32[5120]{0:T(1024)S(1)}, bf16[128,5120]{1,0:T(8,128)(2,1)}, f32[128,5120]{1,0:T(8,128)}) fusion(f32[128,5120]{1,0:T(8,128)} %convolution_add_fusion, bf16[128,1280]{1,0:T(8,128)(2,1)} %param.33, bf16[5120,1280]{1,0:T(8,128)(2,1)} %all-gather.15.cloned.1.call-done), kind=kOutput, calls=%fused_computation.4 | convolution fusion | flops 1726213120 | bytes 20008960 | tf_op jit(solution)/shard_map/td,fd->tf/dot_general | solution.py:278
  274.7 6.6 multiply_reduce_fusion.2
  282.9 4.0 convolution_convert_fusion
  299.6 9.3 fusion.50
  310.3 15.4 %fusion.68 = f32[1280,5120]{1,0:T(8,128)} fusion(bf16[128,5120]{1,0:T(8,128)(2,1)S(1)} %copy-done.4, f32[128,1280]{1,0:T(8,128)S(1)} %get-tuple-element.82, f32[1280]{0:T(1024)S(1)} %convert_element_type.233, f32[1280]{0:T(1024)S(1)} %convert_element_type.232, f32[128]{0:T(128)S(1)} %add_rsqrt_fusion, f32[128]{0:T(128)S(1)} %broadcast_multiply_fusion.5), kind=kOutput, calls=%fused_computation.121 | convolution fusion | flops 1678540800 | bytes 28191744 | tf_op jit(solution)/shard_map/td,tf->df/dot_general | solution.py:281
  325.8 4.0 multiply_convert_fusion
  329.9 12.6 %fusion.77 = f32[5120,1280]{1,0:T(8,128)} fusion(bf16[128,5120]{1,0:T(8,128)(2,1)S(1)} %multiply_convert_fusion, bf16[128,1280]{1,0:T(8,128)(2,1)S(1)} %copy-done.8), kind=kOutput, calls=%fused_computation.127 | convolution fusion | flops 1677721600 | bytes 27852800 | tf_op jit(solution)/shard_map/tf,td->fd/dot_general | solution.py:277
  342.6 3.8 fusion.60
  346.5 92.3 %reduce-scatter.9.cloned.1.call-done = f32[160,3840]{1,0:T(8,128)} async-done(((f32[1280,3840]{1,0:T(8,128)}), f32[160,3840]{1,0:T(8,128)}) %reduce-scatter.9.cloned.1.call-update) | async-done | bytes 2457616 | tf_op jit(solution)/shard_map/reduce_scatter | solution.py:54
  441.7 163.0 %reduce-scatter.17.cloned.1.call-done = f32[160,5120]{1,0:T(8,128)} async-done(((f32[1280,5120]{1,0:T(8,128)}), f32[160,5120]{1,0:T(8,128)}) %reduce-scatter.17.cloned.1.call-update) | async-done | bytes 3276816 | tf_op jit(solution)/shard_map/reduce_scatter | solution.py:61
  608.1 162.7 %reduce-scatter.21.cloned.1.call-done = f32[640,1280]{1,0:T(8,128)} async-done(((f32[5120,1280]{1,0:T(8,128)}), f32[640,1280]{1,0:T(8,128)}) %reduce-scatter.21.cloned.1.call-update) | async-done | bytes 3276816 | tf_op jit(solution)/shard_map/reduce_scatter | solution.py:63
  774.1 63.1 %reduce-scatter.13.cloned.1.call-done = f32[160,1280]{1,0:T(8,128)} async-done(((f32[1280,1280]{1,0:T(8,128)}), f32[160,1280]{1,0:T(8,128)}) %reduce-scatter.13.cloned.1.call-update) | async-done | bytes 819216 | tf_op jit(solution)/shard_map/reduce_scatter | solution.py:57
  839.3 31.1 %reduce-scatter.11.cloned.1.call-done = bf16[40,3840]{1,0:T(8,128)(2,1)} async-done(((bf16[160,3840]{1,0:T(8,128)(2,1)}), bf16[40,3840]{1,0:T(8,128)(2,1)}) %reduce-scatter.11.cloned.1.call-update) | async-done | bytes 307216 | tf_op jit(solution)/shard_map/reduce_scatter | solution.py:73
  870.5 37.8 %reduce-scatter.19.cloned.1.call-done = bf16[40,5120]{1,0:T(8,128)(2,1)} async-done(((bf16[160,5120]{1,0:T(8,128)(2,1)}), bf16[40,5120]{1,0:T(8,128)(2,1)}) %reduce-scatter.19.cloned.1.call-update) | async-done | bytes 409616 | tf_op jit(solution)/shard_map/reduce_scatter | solution.py:94
  912.2 34.4 %reduce-scatter.23.cloned.1.call-done = bf16[160,1280]{1,0:T(8,128)(2,1)} async-done(((bf16[640,1280]{1,0:T(8,128)(2,1)}), bf16[160,1280]{1,0:T(8,128)(2,1)}) %reduce-scatter.23.cloned.1.call-update) | async-done | bytes 409616 | tf_op jit(solution)/shard_map/reduce_scatter | solution.py:100
  946.6 8.2 fusion.40
  955.0 25.6 %all-reduce.36 = (bf16[1280]{0:T(1024)(128)(2,1)S(1)}, bf16[1280]{0:T(1024)(128)(2,1)S(1)}, bf16[1280]{0:T(1024)(128)(2,1)S(1)}, bf16[1280]{0:T(1024)(128)(2,1)S...) all-reduce(f32[1280]{0:T(1024)S(1)} %get-tuple-element.19, ...), channel_id=2, replica_groups=mesh['dp'=4,'fsdp'=8] {'fsdp'}, use_global_device_ids=true, to_apply=%region_15.16.clone | all-reduce | flops 15360 | bytes 92160
  981.3 10.3 all-reduce.39
  994.2 9.7 all-reduce.38
  1009.0 7.6 multiply_reduce_fusion.1
  1016.6 40.4 %all-reduce.35 = (f32[1280]{0:T(1024)S(1)}, f32[1280]{0:T(1024)S(1)}) all-reduce(f32[1280]{0:T(1024)S(1)} %get-tuple-element.24, f32[1280]{0:T(1024)S(1)} %get-tuple-element.23), channel_id=1, replica_groups=mesh['dp'=4,'fsdp'=8] {'dp','fsdp'}, use_global_device_ids=true, to_apply=%region_50.51 | all-reduce | flops 2560 | bytes 20480 | tf_op jit(solution)/shard_map/psum | solution.py:240
  1059.8 18.6 %all_gather.102 = bf16[160,1280]{1,0:T(8,128)(2,1)S(1)} all-gather(bf16[40,1280]{1,0:T(8,128)(2,1)} %reduce-scatter.15.cloned.1.call-done), channel_id=1, replica_groups=mesh['dp'=4,'fsdp'=8] {'dp'}, dimensions={0}, use_global_device_ids=true | all-gather | bytes 512000 | tf_op jit(solution)/shard_map/all_gather | solution.py:123
  1082.2 3.5 convert_element_type.272
  1086.2 3.4 convert_element_type.277
  (195 shorter events, 54.9 us)
Async XLA Ops:
  7.2 3.0 copy-start.10
  7.2 3.0 copy-start.11
  7.2 4.3 copy-start.13
  7.2 4.5 copy-start.14
  7.2 4.8 copy-start.15
  7.3 5.0 copy-start.16
  7.3 5.3 copy-start.17
  7.3 5.5 copy-start.18
  7.3 5.8 copy-start.19
  7.3 6.0 copy-start.20
  7.3 40.4 %copy-start.21 = (s32[1,2]{1,0:T(1,128)S(1)}, s32[1,2]{1,0:T(1,128)}, u32[]{:S(2)}) copy-start(s32[1,2]{1,0:T(1,128)} %param.18) | copy-start | bytes 28
  7.3 40.7 %copy-start.3 = (bf16[128,1280]{1,0:T(8,128)(2,1)S(1)}, bf16[128,1280]{1,0:T(8,128)(2,1)}, u32[]{:S(2)}) copy-start(bf16[128,1280]{1,0:T(8,128)(2,1)} %param.17) | copy-start | bytes 983044
  7.3 66.1 %all-gather.9.cloned.1.call-start = ((), (), s32[]{:S(2)}) async-start(), calls=%async_computation.8 | async-start | bytes 11059200 | tf_op jit(solution)/shard_map/all_gather | solution.py:192
  8.1 40.4 %copy-start.22 = (s32[128]{0:T(128)S(1)}, s32[128]{0:T(128)}, u32[]{:S(2)}) copy-start(s32[128]{0:T(128)} %param.19) | copy-start | bytes 1540
  8.1 100.2 %all-gather.11.cloned.1.call-start = ((), (), s32[]{:S(2)}) async-start(), calls=%async_computation.9 | async-start | bytes 3686400 | tf_op jit(solution)/shard_map/all_gather | solution.py:195
  8.8 175.7 %all-gather.13.cloned.1.call-start = ((), (), s32[]{:S(2)}) async-start(), calls=%async_computation.10 | async-start | bytes 14745600 | tf_op jit(solution)/shard_map/all_gather | solution.py:199
  9.6 251.1 %all-gather.15.cloned.1.call-start = ((), (), s32[]{:S(2)}) async-start(), calls=%async_computation.11 | async-start | bytes 14745600 | tf_op jit(solution)/shard_map/all_gather | solution.py:201
  10.1 428.7 %reduce-scatter.9.cloned.1.call-start = ((), (), s32[]{:S(2)}) async-start(), calls=%async_computation.12 | async-start | bytes 22118400 | tf_op jit(solution)/shard_map/reduce_scatter | solution.py:54
  260.6 14.1 %copy-start = (bf16[1280,5120]{1,0:T(8,128)(2,1)S(1)}, bf16[1280,5120]{1,0:T(8,128)(2,1)}, u32[]{:S(2)}) copy-start(bf16[1280,5120]{1,0:T(8,128)(2,1)} %all-gather.13.cloned.1.call-done) | copy-start | bytes 39321604
  282.9 5.8 copy-start.2
  309.0 295.7 %reduce-scatter.17.cloned.1.call-start = ((), (), s32[]{:S(2)}) async-start(), calls=%async_computation.17 | async-start | bytes 29491200 | tf_op jit(solution)/shard_map/reduce_scatter | solution.py:61
  325.7 445.1 %reduce-scatter.21.cloned.1.call-start = ((), (), s32[]{:S(2)}) async-start(), calls=%async_computation.20 | async-start | bytes 29491200 | tf_op jit(solution)/shard_map/reduce_scatter | solution.py:63
  325.8 4.1 copy-start.8
  342.5 494.8 %reduce-scatter.13.cloned.1.call-start = ((), (), s32[]{:S(2)}) async-start(), calls=%async_computation.15 | async-start | bytes 7372800 | tf_op jit(solution)/shard_map/reduce_scatter | solution.py:57
  346.4 524.0 %reduce-scatter.11.cloned.1.call-start = ((), (), s32[]{:S(2)}) async-start(), calls=%async_computation.13 | async-start | bytes 1536000 | tf_op jit(solution)/shard_map/reduce_scatter | solution.py:73
  441.7 466.6 %reduce-scatter.19.cloned.1.call-start = ((), (), s32[]{:S(2)}) async-start(), calls=%async_computation.18 | async-start | bytes 2048000 | tf_op jit(solution)/shard_map/reduce_scatter | solution.py:94
  608.1 338.6 %reduce-scatter.23.cloned.1.call-start = ((), (), s32[]{:S(2)}) async-start(), calls=%async_computation.21 | async-start | bytes 2048000 | tf_op jit(solution)/shard_map/reduce_scatter | solution.py:100
  774.0 172.6 %copy-start.9 = (bf16[20,64,128]{2,1,0:T(8,128)(2,1)S(1)}, bf16[20,64,128]{2,1,0:T(8,128)(2,1)}, u32[]{:S(2)}) copy-start(bf16[20,64,128]{2,1,0:T(8,128)(2,1)} %get-tuple-element.89) | copy-start | bytes 983044
  774.1 285.7 %reduce-scatter.15.cloned.1.call-start = ((), (), s32[]{:S(2)}) async-start(), calls=%async_computation.16 | async-start | bytes 512000 | tf_op jit(solution)/shard_map/reduce_scatter | solution.py:82
  839.2 240.1 %all-gather.17.cloned.1.call-start = ((), (), s32[]{:S(2)}) async-start(), calls=%async_computation.14 | async-start | bytes 1536000 | tf_op jit(solution)/shard_map/all_gather | solution.py:114
  870.4 211.8 %all-gather.19.cloned.1.call-start = ((), (), s32[]{:S(2)}) async-start(), calls=%async_computation.19 | async-start | bytes 2048000 | tf_op jit(solution)/shard_map/all_gather | solution.py:135
  908.3 177.9 %all-gather.21.cloned.1.call-start = ((), (), s32[]{:S(2)}) async-start(), calls=%async_computation.22 | async-start | bytes 2048000 | tf_op jit(solution)/shard_map/all_gather | solution.py:141
  (6 other events, 11.5 us)
Sparse Core Ops, SparseCore 0:
  10.0 63.3 all-gather.8
  75.3 32.8 all-gather.10
  110.1 74.3 all-gather.12
  186.2 74.3 all-gather.14
  309.1 129.6 reduce-scatter.8
  442.3 162.3 reduce-scatter.16
  608.4 162.3 reduce-scatter.20
  774.2 62.9 reduce-scatter.12
  840.3 30.0 reduce-scatter.10
  873.1 35.0 reduce-scatter.18
  911.2 35.3 reduce-scatter.22
  949.3 19.8 reduce-scatter.14
  970.8 30.5 all-gather.16
  1002.9 37.9 all-gather.18
  1042.4 43.7 all-gather.20
where the time goes:
time: 1100 us
  waiting for transfers between devices  781 us (71%)
  blocking collectives  139 us (13%)
  matrix products  109 us (10%)
  other arithmetic  36.9 us (3%)
  between operations  19.5 us (2%)
    reduce_scatter x1, waiting for transfers between devices, reduce_late(): lax.psum_scatter(values[9], 'fsdp', scatter_dimension=0, tiled=True)  163 us
    reduce_scatter x1, waiting for transfers between devices, reduce_late(): lax.psum_scatter(values[11], 'fsdp', scatter_dimension=0, tiled=True)  163 us
    reduce_scatter x1, waiting for transfers between devices, reduce_late(): lax.psum_scatter(values[2], 'fsdp', scatter_dimension=0, tiled=True)  92.3 us
    all_gather x1, waiting for transfers between devices, local(): lax.all_gather(w_up, 'fsdp', axis=0, tiled=True)  73.4 us
    unnamed x4, blocking collectives  71.5 us
    all_gather x1, waiting for transfers between devices, local(): lax.all_gather(w_down, 'fsdp', axis=0, tiled=True)  67.9 us
    reduce_scatter x1, waiting for transfers between devices, reduce_late(): lax.psum_scatter(values[5], 'fsdp', scatter_dimension=0, tiled=True)  63.1 us
    psum x1, blocking collectives, local(): lax.psum((jnp.sum(picked, axis=0), jnp.sum(picked * picked, axis=0)), ('d...  40.4 us
  transfers between devices with their start and end apart: 15, of which 12 were waited for; matrix products, arithmetic and copies ran while one was open for 9% of the time, Pallas kernels for 0%

commit v1 on v0

v1 whole, which is shorter than its diff:
```python
from functools import partial

import jax
import jax.numpy as jnp
from jax import lax
from jax.experimental import pallas as pl
from jax.experimental.pallas import tpu as pltpu
from jax.sharding import PartitionSpec as P

D = 1280
HEADS = 20
HEAD_DIM = 64
FF = 5120
CELLS_DEV = 2
EPS = 1e-05

TEAM = 8
CHIPS = 4
HEADS_CHIP = HEADS // CHIPS
D_CHIP = D // CHIPS
FF_CHIP = FF // CHIPS

f32 = jnp.float32
bf16 = jnp.bfloat16


def dot(a, b, dims):
    return lax.dot_general(a, b, (dims, ((), ())), preferred_element_type=f32)


def mm(a, b):
    return dot(a, b, ((1,), (0,)))


def mm_t(a, b):
    return dot(a, b, ((1,), (1,)))


def t_mm(a, b):
    return dot(a, b, ((0,), (0,)))


def normalize(values):
    center = jnp.mean(values, axis=-1, keepdims=True)
    centred = values - center
    spread = jnp.mean(centred * centred, axis=-1, keepdims=True)
    inverse = lax.rsqrt(spread + EPS)
    return centred * inverse, inverse


def norm_backward(grad_out, normed, inverse, norm_gain):
    grad_normed = grad_out * norm_gain
    first_mean = jnp.mean(grad_normed, axis=-1, keepdims=True)
    second_mean = jnp.mean(grad_normed * normed, axis=-1, keepdims=True)
    grad_in = inverse * (grad_normed - first_mean - normed * second_mean)
    return grad_in, jnp.sum(grad_out * normed, axis=0), jnp.sum(grad_out, axis=0)


def softmax_rows(query, key, keep):
    raw = dot(query, key, ((1,), (1,))) * (HEAD_DIM ** (-0.5))
    masked = jnp.where(keep, raw, -1e30)
    grown = jnp.exp(masked - jnp.max(masked, axis=-1, keepdims=True))
    return grown / jnp.sum(grown, axis=-1, keepdims=True)


def attention_kernel(projected, mask, context):
    keep = mask[...].astype(f32) > 0.5
    for head in range(HEADS_CHIP):
        lo = head * HEAD_DIM
        query = projected[:, lo : lo + HEAD_DIM]
        key = projected[:, D_CHIP + lo : D_CHIP + lo + HEAD_DIM]
        value = projected[:, 2 * D_CHIP + lo : 2 * D_CHIP + lo + HEAD_DIM]
        probs = softmax_rows(query, key, keep).astype(bf16)
        context[:, lo : lo + HEAD_DIM] = mm(probs, value).astype(bf16)


def attention_back_kernel(projected, mask, grad_context, grad_projected):
    keep = mask[...].astype(f32) > 0.5
    for head in range(HEADS_CHIP):
        lo = head * HEAD_DIM
        query = projected[:, lo : lo + HEAD_DIM]
        key = projected[:, D_CHIP + lo : D_CHIP + lo + HEAD_DIM]
        value = projected[:, 2 * D_CHIP + lo : 2 * D_CHIP + lo + HEAD_DIM]
        grad = grad_context[:, lo : lo + HEAD_DIM]
        probs = softmax_rows(query, key, keep)
        grad_probs = mm_t(grad, value)
        along = jnp.sum(grad_probs * probs, axis=-1, keepdims=True)
        grad_scores = (probs * (grad_probs - along) * (HEAD_DIM ** (-0.5))).astype(bf16)
        grad_projected[:, lo : lo + HEAD_DIM] = mm(grad_scores, key).astype(bf16)
        grad_projected[:, D_CHIP + lo : D_CHIP + lo + HEAD_DIM] = t_mm(grad_scores, query).astype(bf16)
        grad_projected[:, 2 * D_CHIP + lo : 2 * D_CHIP + lo + HEAD_DIM] = t_mm(
            probs.astype(bf16), grad
        ).astype(bf16)


def attention(projected, mask):
    rows = mask.shape[1]
    return pl.pallas_call(
        attention_kernel,
        grid=(projected.shape[0] // rows,),
        in_specs=[
            pl.BlockSpec((rows, 3 * D_CHIP), lambda i: (i, 0)),
            pl.BlockSpec((rows, rows), lambda i: (i, 0)),
        ],
        out_specs=pl.BlockSpec((rows, D_CHIP), lambda i: (i, 0)),
        out_shape=jax.ShapeDtypeStruct((projected.shape[0], D_CHIP), bf16),
        cost_estimate=pl.CostEstimate(flops=10**9, bytes_accessed=2 * 10**6, transcendentals=330000),
        name="attention",
    )(projected, mask)


def attention_back(projected, mask, grad_context):
    rows = mask.shape[1]
    return pl.pallas_call(
        attention_back_kernel,
        grid=(projected.shape[0] // rows,),
        in_specs=[
            pl.BlockSpec((rows, 3 * D_CHIP), lambda i: (i, 0)),
            pl.BlockSpec((rows, rows), lambda i: (i, 0)),
            pl.BlockSpec((rows, D_CHIP), lambda i: (i, 0)),
        ],
        out_specs=pl.BlockSpec((rows, 3 * D_CHIP), lambda i: (i, 0)),
        out_shape=jax.ShapeDtypeStruct(projected.shape, bf16),
        cost_estimate=pl.CostEstimate(flops=3 * 10**9, bytes_accessed=4 * 10**6, transcendentals=330000),
        name="attention_back",
    )(projected, mask, grad_context)


def local(
    tokens,
    lengths,
    padding,
    ln1_gain,
    ln1_bias,
    w_qkv,
    b_query,
    b_value,
    w_out,
    b_out,
    ln2_gain,
    ln2_bias,
    w_up,
    b_up,
    w_down,
    b_down,
    cotangent,
):
    fsdp_count = lax.axis_size("fsdp")
    dp_count = lax.axis_size("dp")
    groups = fsdp_count // TEAM
    place = lax.axis_index("fsdp") // groups
    chip = place // 2
    core = place % 2
    depth = lax.axis_index("dp")
    rows = tokens.shape[0]

    def swap(value, mask):
        pairs = [
            (team * groups + group, (team ^ mask) * groups + group)
            for team in range(TEAM)
            for group in range(groups)
        ]
        return lax.ppermute(value, "fsdp", pairs)

    shard_groups = [[team * groups + group for group in range(groups)] for team in range(TEAM)]

    def gather_shards(value):
        if groups == 1:
            return value
        return lax.all_gather(value, "fsdp", axis=0, tiled=True, axis_index_groups=shard_groups)

    def scatter_shards(value):
        if groups == 1:
            return value
        return lax.psum_scatter(
            value, "fsdp", scatter_dimension=0, tiled=True, axis_index_groups=shard_groups
        )

    def by_core(mine, other):
        return jnp.where(core == 0, mine, other), jnp.where(core == 0, other, mine)

    def pick(stack, index):
        return lax.dynamic_index_in_dim(stack, index, 0, keepdims=False)

    def from_chips(send_to):
        return [send_to(0)] + [swap(send_to(i), 2 * i) for i in range(1, CHIPS)]

    def gather_chips(value):
        return jnp.concatenate(from_chips(lambda i: value), axis=0)

    def scatter_chips(partial_sum):
        low = partial_sum.astype(bf16)
        parts = from_chips(
            lambda i: partial_sum[:rows] if i == 0 else low[i * rows : (i + 1) * rows]
        )
        return parts[0] + parts[1].astype(f32) + parts[2].astype(f32) + parts[3].astype(f32)

    def along_z(pairs, value):
        return lax.ppermute(value, "dp", pairs)

    def sum_dp(low):
        if dp_count != 4:
            return lax.psum(low, "dp")
        inward = along_z([(0, 1), (3, 2)], low)
        half = (low.astype(f32) + inward.astype(f32)).astype(bf16)
        across = along_z([(1, 2), (2, 1)], half)
        whole = (half.astype(f32) + across.astype(f32)).astype(bf16)
        outward = along_z([(1, 0), (2, 3)], whole)
        return jnp.where((depth == 1) | (depth == 2), whole, outward)

    def sum_everywhere(value):
        for mask in (1, 2, 4):
            value = value + swap(value, mask)
        if groups > 1:
            value = lax.psum(
                value,
                "fsdp",
                axis_index_groups=shard_groups,
            )
        return sum_dp_wide(value)

    def sum_dp_wide(value):
        if dp_count != 4:
            return lax.psum(value, "dp")
        for mask in (1, 2):
            value = value + along_z([(z, z ^ mask) for z in range(4)], value)
        return value

    w_qkv, w_out, w_up, w_down = (gather_shards(w) for w in (w_qkv, w_out, w_up, w_down))
    share = D // TEAM
    finish = jnp.cumsum(lengths[0])
    places = jnp.arange(rows, dtype=jnp.int32)
    member = jnp.sum((places[:, None] >= finish[None, :]).astype(jnp.int32), axis=1)
    leading = jnp.any(places[:, None] == (finish - lengths[0])[None, :], axis=1)
    usable = (padding > 0) | leading
    code = (2 * member + usable.astype(jnp.int32)).astype(bf16)
    vectors = [
        gather_shards(v)
        for v in (ln1_gain, ln1_bias, b_query, b_value, b_out, ln2_gain, ln2_bias, b_down, b_up)
    ]
    small = jnp.concatenate(vectors + [code]).reshape(1, -1)
    for bit, mask in ((core, 1), (chip % 2, 2), (chip // 2, 4)):
        other = swap(small, mask)
        small = jnp.concatenate(
            [jnp.where(bit == 0, small, other), jnp.where(bit == 0, other, small)], axis=0
        )
    wide = small.astype(f32)
    first_gain, first_bias, query_bias, value_bias, out_bias, second_gain, second_bias, down_bias = (
        wide[:, i * share : (i + 1) * share].reshape(D) for i in range(8)
    )
    up_bias = lax.dynamic_slice(wide, (2 * chip, 8 * share), (2, FF // TEAM)).reshape(FF_CHIP)
    query_bias = lax.dynamic_slice(query_bias, (chip * D_CHIP,), (D_CHIP,))
    value_bias = lax.dynamic_slice(value_bias, (chip * D_CHIP,), (D_CHIP,))
    codes = jnp.stack(
        [pick(wide, 2 * (chip ^ i) + core)[8 * share + FF // TEAM :] for i in range(CHIPS)]
    )
    of_cell = jnp.floor(codes * 0.5)
    open_key = codes - 2.0 * of_cell
    mask = (of_cell[:, :, None] == of_cell[:, None, :]) & (open_key[:, None, :] > 0.5)
    mask = mask.astype(bf16).reshape(CHIPS * rows, rows)

    by_chip = w_qkv.reshape(share, 3, CHIPS, D_CHIP).transpose(2, 0, 1, 3).reshape(CHIPS, share, 3 * D_CHIP)

    def all_rows(parts):
        mine = jnp.stack(parts)
        lower, upper = by_core(mine, swap(mine, 1))
        both = jnp.stack([lower, upper], axis=1)
        ordered = jnp.stack([pick(both, chip ^ i) for i in range(CHIPS)])
        return ordered.reshape(D, -1)

    whole_tokens = gather_chips(tokens)
    qkv_cols = all_rows(from_chips(lambda i: pick(by_chip, chip ^ i)))
    up_cols = all_rows(
        from_chips(lambda i: lax.dynamic_slice(w_up, (0, (chip ^ i) * FF_CHIP), (share, FF_CHIP)))
    )
    out_rows = jnp.concatenate(by_core(w_out, swap(w_out, 1)), axis=0)
    down_rows = jnp.concatenate(by_core(w_down, swap(w_down, 1)), axis=0)
    whole_cotangent = gather_chips(cotangent)

    inputs = tokens.astype(f32)
    normed_all, _ = normalize(whole_tokens.astype(f32))
    first_low = (normed_all * first_gain + first_bias).astype(bf16)
    qkv_bias = jnp.concatenate([query_bias, jnp.zeros((D_CHIP,), f32), value_bias])
    projected = (mm(first_low, qkv_cols) + qkv_bias).astype(bf16)
    context = attention(projected, mask)
    mixed = inputs + scatter_chips(mm(context, out_rows)) + out_bias
    second_normed, second_inverse = normalize(mixed)
    second_low = gather_chips((second_normed * second_gain + second_bias).astype(bf16))
    hidden_pre = mm(second_low, up_cols) + up_bias
    below = 0.5 * (1.0 + lax.erf(hidden_pre * (0.5**0.5)))
    bell = jnp.exp(-0.5 * hidden_pre * hidden_pre) * 0.3989422804014327
    act_low = (hidden_pre * below).astype(bf16)
    result = mixed + scatter_chips(mm(act_low, down_rows)) + down_bias
    picked = jnp.where(leading[:, None], result, 0.0)
    moments = sum_everywhere(jnp.stack([jnp.sum(picked, axis=0), jnp.sum(picked * picked, axis=0)]))
    moments = moments / (CELLS_DEV * dp_count * fsdp_count)
    cls_mean = moments[0]
    cls_var = moments[1] - cls_mean * cls_mean

    grad_result = cotangent.astype(f32)
    grad_down_bias = jnp.sum(grad_result, axis=0)

    def own_core(grad, parts):
        halves = grad.reshape(parts, 2, -1, grad.shape[-1])
        kept = lax.dynamic_index_in_dim(halves, core, 1, keepdims=False)
        sent = lax.dynamic_index_in_dim(halves, 1 - core, 1, keepdims=False)
        return (kept + swap(sent.astype(bf16), 1).astype(f32)).astype(bf16)

    def own_rows(grad):
        kept = own_core(grad, CHIPS)
        return jnp.stack(from_chips(lambda i: pick(kept, chip ^ i)))

    down_sum = sum_dp(own_core(t_mm(act_low, whole_cotangent), 1)[0])
    grad_act = mm_t(whole_cotangent, down_rows)
    grad_pre = (grad_act * (below + hidden_pre * bell)).astype(bf16)
    grad_up_bias = jnp.sum(grad_pre.astype(f32), axis=0)
    up_sum = sum_dp(own_rows(t_mm(second_low, grad_pre)))
    grad_second = scatter_chips(mm_t(grad_pre, up_cols))
    grad_from_second, grad_second_gain, grad_second_bias = norm_backward(
        grad_second, second_normed, second_inverse, second_gain
    )
    grad_mixed = grad_result + grad_from_second
    grad_branch = grad_mixed.astype(bf16)
    grad_out_bias = jnp.sum(grad_branch.astype(f32), axis=0)
    whole_branch = gather_chips(grad_branch)
    out_sum = sum_dp(own_core(t_mm(context, whole_branch), 1)[0])
    grad_context = mm_t(whole_branch, out_rows).astype(bf16)
    grad_projected = attention_back(projected, mask, grad_context)
    grad_qkv_bias = jnp.sum(grad_projected.astype(f32), axis=0)
    qkv_sum = sum_dp(own_rows(t_mm(first_low, grad_projected)))
    grad_first = scatter_chips(mm_t(grad_projected, qkv_cols))
    first_normed, first_inverse = normalize(inputs)
    grad_from_first, grad_first_gain, grad_first_bias = norm_backward(
        grad_first, first_normed, first_inverse, first_gain
    )
    grad_inputs = grad_mixed + grad_from_first

    full = jnp.stack(
        [
            grad_first_gain,
            grad_first_bias,
            grad_out_bias,
            grad_second_gain,
            grad_second_bias,
            grad_down_bias,
        ]
    ).reshape(6, CHIPS, 2, share)
    full = full.transpose(1, 2, 0, 3).reshape(CHIPS, 2, 6 * share)
    parts = from_chips(lambda i: pick(full, chip ^ i))
    of_chip = jnp.concatenate(
        [
            grad_qkv_bias[:D_CHIP].reshape(2, share),
            grad_qkv_bias[2 * D_CHIP :].reshape(2, share),
            grad_up_bias.reshape(2, FF // TEAM),
        ],
        axis=1,
    )
    both = jnp.concatenate([parts[0] + parts[1] + parts[2] + parts[3], of_chip], axis=1)
    vector = pick(both, core) + swap(pick(both, 1 - core), 1)
    vector = sum_dp_wide(vector)
    cuts = [vector[i * share : (i + 1) * share] for i in range(8)] + [vector[8 * share :]]
    (
        first_gain_sum,
        first_bias_sum,
        out_bias_sum,
        second_gain_sum,
        second_bias_sum,
        down_bias_sum,
        query_bias_sum,
        value_bias_sum,
        up_bias_sum,
    ) = (scatter_shards(v) for v in cuts)

    qkv_total = jnp.stack([pick(qkv_sum, chip ^ i) for i in range(CHIPS)])
    qkv_total = (
        qkv_total.reshape(CHIPS, share, 3, D_CHIP).transpose(1, 2, 0, 3).reshape(share, 3 * D)
    ).astype(f32)
    up_total = jnp.concatenate([pick(up_sum, chip ^ i) for i in range(CHIPS)], axis=1).astype(f32)

    return (
        result.astype(bf16),
        grad_inputs,
        first_gain_sum,
        first_bias_sum,
        scatter_shards(qkv_total),
        query_bias_sum,
        value_bias_sum,
        scatter_shards(out_sum.astype(f32)),
        out_bias_sum,
        second_gain_sum,
        second_bias_sum,
        scatter_shards(up_total),
        up_bias_sum,
        scatter_shards(down_sum.astype(f32)),
        down_bias_sum,
        cls_mean,
        cls_var,
    )


def solution(mesh):
    tokens_spec = P(("dp", "fsdp"), None)
    vector = P("fsdp")
    matrix = P("fsdp", None)
    in_specs = (
        tokens_spec,
        P(("dp", "fsdp"), None),
        P(("dp", "fsdp")),
        vector,
        vector,
        matrix,
        vector,
        vector,
        matrix,
        vector,
        vector,
        vector,
        matrix,
        vector,
        matrix,
        vector,
        tokens_spec,
    )
    out_specs = (
        tokens_spec,
        tokens_spec,
        vector,
        vector,
        matrix,
        vector,
        vector,
        matrix,
        vector,
        vector,
        vector,
        matrix,
        vector,
        matrix,
        vector,
        P(),
        P(),
    )
    return jax.shard_map(local, mesh=mesh, in_specs=in_specs, out_specs=out_specs, check_vma=False)
```

time: 1100 us -> 548 us (0.50)
  waiting for transfers between devices: 781 us -> 306 us
  blocking collectives: 139 us -> 0 us
  starting transfers between devices: 0.6 us -> 75.2 us
  matrix products: 109 us -> 37.1 us
  local copies, waits for them, and re-layouts: 10.8 us -> 55.4 us
  Pallas kernels: 0 us -> 21.5 us
  between operations: 19.5 us -> 2.06 us
    reduce_scatter x8 -> x0, waiting for transfers between devices: 584 us -> none  [the longest x1 163 us: reduce_late(): lax.psum_scatter(values[9], 'fsdp', scatter_dimension=0, tiled=True)]
    ppermute x0 -> x70, waiting for transfers between devices: none -> 306 us  [the longest x16 170 us: along_z(): return lax.ppermute(value, 'dp', pairs)]
    all_gather x7 -> x0, waiting for transfers between devices: 193 us -> none  [the longest x1 73.4 us: local(): lax.all_gather(w_up, 'fsdp', axis=0, tiled=True)]
    ppermute x0 -> x70, starting transfers between devices: none -> 75.2 us  [the longest x54 54.9 us: swap(): return lax.ppermute(value, 'fsdp', pairs)]
    dot_general x18 -> x12, matrix products: 109 us -> 37.1 us  [dot(): return lax.dot_general(a, b, (dims, ((), ())), preferred_element_type=f32)]
    unnamed x4 -> x0, blocking collectives: 71.5 us -> none
    psum x1 -> x0, blocking collectives: 40.4 us -> none  [local(): lax.psum((jnp.sum(picked, axis=0), jnp.sum(picked * picked, axis=0)), ('d...]
    all_gather x2 -> x0, blocking collectives: 26.7 us -> none  [the longest x1 18.6 us: reduce_late(): lax.all_gather(shares[5].astype(jnp.bfloat16), 'dp', axis=0, tiled=True)]
  transfers between devices with their start and end apart: 15 -> 70, of which waited for: 12 -> 39; matrix products, arithmetic and copies ran while one was open for 9% -> 22% of each run, Pallas kernels for 0% -> 4%
where the time goes in v1:
time: 548 us; the launch traced here: 539 us
  waiting for transfers between devices  306 us (56%)
  starting transfers between devices  75.2 us (14%)
  local copies, waits for them, and re-layouts  55.4 us (10%)
  other arithmetic  41.5 us (8%)
  matrix products  37.1 us (7%)
  Pallas kernels  21.5 us (4%)
    ppermute x16, waiting for transfers between devices, along_z(): return lax.ppermute(value, 'dp', pairs)  170 us
    ppermute x54, waiting for transfers between devices, swap(): return lax.ppermute(value, 'fsdp', pairs)  136 us
    ppermute x54, starting transfers between devices, swap(): return lax.ppermute(value, 'fsdp', pairs)  54.9 us
    dot_general x12, matrix products, dot(): return lax.dot_general(a, b, (dims, ((), ())), preferred_element_type=f32)  37.1 us
    ppermute x16, starting transfers between devices, along_z(): return lax.ppermute(value, 'dp', pairs)  20.4 us
    pallas_call x1, Pallas kernels, attention_back(): pl.pallas_call(attention_back_kernel, grid=(projected.shape[0] // rows,),...  12.3 us
  transfers between devices with their start and end apart: 70, of which 39 were waited for; matrix products, arithmetic and copies ran while one was open for 22% of the time, Pallas kernels for 4%

profile of v1, /device:TPU:0, one launch (start us, length us, event | category | flops | bytes accessed | tf_op | source)
XLA Modules:
  0.0 539.0 jit_solution(13340525823649981914)
XLA Ops:
  8.0 6.1 %concatenate.54 = bf16[2048]{0:T(1024)(128)(2,1)S(1)} concatenate(bf16[160]{0:T(256)(128)(2,1)} %param.20, bf16[160]{0:T(256)(128)(2,1)} %param.21, bf16[160]{0:T(256)(128)(2,1)} %param.23, bf16[160]{0:T(256)(128)(2,1)} %param.24, bf16[160]{0:T(256)(128)(2,1)} %param.26, bf16[160]{0:T(256)(128)(2,1)} %param.27, bf16[160]{0:T(256)(128)(2,1)} %param.28, bf16[160]{0:T(256)(128)(2,1)} %param.32, ...), dimensions={0} | concatenate | bytes 8192 | tf_op jit(solution)/shard_map/concatenate | solution.py:241
  33.4 5.1 collective-permute-done.5
  59.8 11.2 %collective-permute-done.1 = bf16[128,1280]{1,0:T(8,128)(2,1)S(1)} collective-permute-done((bf16[128,1280]{1,0:T(8,128)(2,1)S(1)}, bf16[128,1280]{1,0:T(8,128)(2,1)S(1)}, u32[]{:S(2)}, u32[]{:S(2)}) %collective-permute-start.1) | collective-permute-done | bytes 327712 | tf_op jit(solution)/shard_map/ppermute | solution.py:163
  72.8 5.3 collective-permute-done.2
  79.3 6.4 %collective-permute-done.17 = bf16[160,1280]{1,0:T(8,128)(2,1)S(1)} collective-permute-done((bf16[160,1280]{1,0:T(8,128)(2,1)S(1)}, bf16[160,1280]{1,0:T(8,128)(2,1)S(1)}, u32[]{:S(2)}, u32[]{:S(2)}) %collective-permute-start.17) | collective-permute-done | bytes 409632 | tf_op jit(solution)/shard_map/ppermute | solution.py:163
  85.7 8.8 %collective-permute-done.19 = bf16[160,1280]{1,0:T(8,128)(2,1)S(1)} collective-permute-done((bf16[160,1280]{1,0:T(8,128)(2,1)S(1)}, bf16[160,1280]{1,0:T(8,128)(2,1)S(1)}, u32[]{:S(2)}, u32[]{:S(2)}) %collective-permute-start.19) | collective-permute-done | bytes 409632 | tf_op jit(solution)/shard_map/ppermute | solution.py:163
  102.6 9.1 %attention.1 = bf16[512,320]{1,0:T(8,128)(2,1)} custom-call(bf16[512,960]{1,0:T(8,128)(2,1)} %add_convert_fusion.6.projected, bf16[512,128]{1,0:T(8,128)(2,1)} %fusion.54.mask), custom_call_target="tpu_custom_call" | custom-call | flops 1000000000 | bytes 2000000 | tf_op jit(solution)/shard_map/attention/pallas_call | solution.py:98
  119.5 4.9 collective-permute-done.11
  124.4 6.5 %collective-permute-done.13 = bf16[128,1280]{1,0:T(8,128)(2,1)S(1)} collective-permute-done((bf16[128,1280]{1,0:T(8,128)(2,1)S(1)}, bf16[128,1280]{1,0:T(8,128)(2,1)S(1)}, u32[]{:S(2)}, u32[]{:S(2)}) %collective-permute-start.13) | collective-permute-done | bytes 327712 | tf_op jit(solution)/shard_map/ppermute | solution.py:163
  139.3 5.5 %collective-permute-done.16 = bf16[128,1280]{1,0:T(8,128)(2,1)S(1)} collective-permute-done((bf16[128,1280]{1,0:T(8,128)(2,1)S(1)}, bf16[128,1280]{1,0:T(8,128)(2,1)S(1)}, u32[]{:S(2)}, u32[]{:S(2)}) %collective-permute-start.16) | collective-permute-done | bytes 327712 | tf_op jit(solution)/shard_map/ppermute | solution.py:163
  144.8 5.0 collective-permute-done.15
  152.1 4.5 convert_reduce_fusion.1
  170.7 6.5 %collective-permute-done.30 = bf16[128,1280]{1,0:T(8,128)(2,1)S(1)} collective-permute-done((bf16[128,1280]{1,0:T(8,128)(2,1)S(1)}, bf16[128,1280]{1,0:T(8,128)(2,1)S(1)}, u32[]{:S(2)}, u32[]{:S(2)}) %collective-permute-start.30) | collective-permute-done | bytes 327712 | tf_op jit(solution)/shard_map/ppermute | solution.py:163
  179.7 3.6 collective-permute-done.22
  183.4 7.0 %collective-permute-done.24 = bf16[128,1280]{1,0:T(8,128)(2,1)S(1)} collective-permute-done((bf16[128,1280]{1,0:T(8,128)(2,1)S(1)}, bf16[128,1280]{1,0:T(8,128)(2,1)S(1)}, u32[]{:S(2)}, u32[]{:S(2)}) %collective-permute-start.24) | collective-permute-done | bytes 327712 | tf_op jit(solution)/shard_map/ppermute | solution.py:163
  195.2 4.6 fusion.99
  206.5 6.3 %fusion.55 = f32[1280,1280]{1,0:T(8,128)} fusion(bf16[512,1280]{1,0:T(8,128)(2,1)} %copy-done.42, bf16[128,1280]{1,0:T(8,128)(2,1)} %copy-done.37, bf16[128,1280]{1,0:T(8,128)(2,1)} %copy-done.38, bf16[128,1280]{1,0:T(8,128)(2,1)} %copy-done.39, bf16[128,1280]{1,0:T(8,128)(2,1)S(1)} %copy-done.25), kind=kOutput, calls=%fused_computation.158 | convolution fusion | flops 1682964480 | bytes 9175040 | tf_op jit(solution)/shard_map/dot_general | solution.py:28
  223.3 7.2 %collective-permute-done.33 = bf16[128,1280]{1,0:T(8,128)(2,1)} collective-permute-done((bf16[128,1280]{1,0:T(8,128)(2,1)}, bf16[128,1280]{1,0:T(8,128)(2,1)}, u32[]{:S(2)}, u32[]{:S(2)}) %collective-permute-start.33) | collective-permute-done | bytes 327712 | tf_op jit(solution)/shard_map/ppermute | solution.py:163
  230.5 6.6 %collective-permute-done.32 = bf16[128,1280]{1,0:T(8,128)(2,1)} collective-permute-done((bf16[128,1280]{1,0:T(8,128)(2,1)}, bf16[128,1280]{1,0:T(8,128)(2,1)}, u32[]{:S(2)}, u32[]{:S(2)}) %collective-permute-start.32) | collective-permute-done | bytes 327712 | tf_op jit(solution)/shard_map/ppermute | solution.py:163
  242.4 12.3 %attention_back.1 = bf16[512,960]{1,0:T(8,128)(2,1)} custom-call(bf16[512,960]{1,0:T(8,128)(2,1)} %add_convert_fusion.6.projected, bf16[512,128]{1,0:T(8,128)(2,1)} %fusion.54.mask, bf16[512,320]{1,0:T(8,128)(2,1)} %copy.68.grad_context), custom_call_target="tpu_custom_call" | custom-call | flops 3000000000 | bytes 4000000 | tf_op jit(solution)/shard_map/attention_back/pallas_call | solution.py:114
  264.5 4.1 fusion.79
  269.6 6.1 %collective-permute-done.36 = bf16[128,1280]{1,0:T(8,128)(2,1)S(1)} collective-permute-done((bf16[128,1280]{1,0:T(8,128)(2,1)S(1)}, bf16[128,1280]{1,0:T(8,128)(2,1)S(1)}, u32[]{:S(2)}, u32[]{:S(2)}) %collective-permute-start.36) | collective-permute-done | bytes 327712 | tf_op jit(solution)/shard_map/ppermute | solution.py:163
  306.6 6.2 %collective-permute-done.57 = bf16[160,1280]{1,0:T(8,128)(2,1)S(1)} collective-permute-done((bf16[160,1280]{1,0:T(8,128)(2,1)S(1)}, bf16[160,1280]{1,0:T(8,128)(2,1)S(1)}, u32[]{:S(2)}, u32[]{:S(2)}) %collective-permute-start.57) | collective-permute-done | bytes 409632 | tf_op jit(solution)/shard_map/ppermute | solution.py:163
  314.4 7.2 %collective-permute-done.56 = bf16[160,1280]{1,0:T(8,128)(2,1)S(1)} collective-permute-done((bf16[160,1280]{1,0:T(8,128)(2,1)S(1)}, bf16[160,1280]{1,0:T(8,128)(2,1)S(1)}, u32[]{:S(2)}, u32[]{:S(2)}) %collective-permute-start.56) | collective-permute-done | bytes 409632 | tf_op jit(solution)/shard_map/ppermute | solution.py:163
  323.6 4.0 collective-permute-done.46
  329.4 3.9 collective-permute-done.45
  343.6 59.2 %collective-permute-done.47 = bf16[4,160,960]{2,1,0:T(8,128)(2,1)S(1)} collective-permute-done((bf16[4,160,960]{2,1,0:T(8,128)(2,1)S(1)}, bf16[4,160,960]{2,1,0:T(8,128)(2,1)S(1)}, u32[]{:S(2)}, u32[]{:S(2)}) %collective-permute-start.47) | collective-permute-done | bytes 1228832 | tf_op jit(solution)/shard_map/ppermute | solution.py:199
  415.6 5.6 %collective-permute-done.53 = bf16[160,1280]{1,0:T(8,128)(2,1)S(1)} collective-permute-done((bf16[160,1280]{1,0:T(8,128)(2,1)S(1)}, bf16[160,1280]{1,0:T(8,128)(2,1)S(1)}, u32[]{:S(2)}, u32[]{:S(2)}) %collective-permute-start.53) | collective-permute-done | bytes 409632 | tf_op jit(solution)/shard_map/ppermute | solution.py:199
  422.2 49.1 %collective-permute-done.49 = bf16[4,160,960]{2,1,0:T(8,128)(2,1)S(1)} collective-permute-done((bf16[4,160,960]{2,1,0:T(8,128)(2,1)S(1)}, bf16[4,160,960]{2,1,0:T(8,128)(2,1)S(1)}, u32[]{:S(2)}, u32[]{:S(2)}) %collective-permute-start.49) | collective-permute-done | bytes 1228832 | tf_op jit(solution)/shard_map/ppermute | solution.py:199
  475.4 4.0 copy.70
  482.2 24.3 %collective-permute-done.64 = bf16[640,1280]{1,0:T(8,128)(2,1)} collective-permute-done((bf16[640,1280]{1,0:T(8,128)(2,1)}, bf16[640,1280]{1,0:T(8,128)(2,1)}, u32[]{:S(2)}, u32[]{:S(2)}) %collective-permute-start.64) | collective-permute-done | bytes 1638432 | tf_op jit(solution)/shard_map/ppermute | solution.py:199
  509.8 25.2 %collective-permute-done.60 = bf16[4,160,1280]{2,1,0:T(8,128)(2,1)} collective-permute-done((bf16[4,160,1280]{2,1,0:T(8,128)(2,1)}, bf16[4,160,1280]{2,1,0:T(8,128)(2,1)}, u32[]{:S(2)}, u32[]{:S(2)}) %collective-permute-start.60) | collective-permute-done | bytes 1638432 | tf_op jit(solution)/shard_map/ppermute | solution.py:199
  (353 shorter events, 205.5 us)
Async XLA Ops:
  0.7 58.0 %collective-permute-start.26 = (bf16[128,1280]{1,0:T(8,128)(2,1)}, bf16[128,1280]{1,0:T(8,128)(2,1)}, u32[]{:S(2)}, u32[]{:S(2)}) collective-permute-start(bf16[128,1280]{1,0:T(8,128)(2,1)} %param.33), channel_id=1, source_target_pairs={{0,4},{1,5},{2,6},{3,7},{4,0},{5,1},{6,2},{7,3},{8,12},{9,13},{10,... | collective-permute-start | bytes 983048 | tf_op jit(solution)/shard_map/ppermute | solution.py:163
  3.7 52.5 %collective-permute-start.25 = (bf16[128,1280]{1,0:T(8,128)(2,1)}, bf16[128,1280]{1,0:T(8,128)(2,1)}, u32[]{:S(2)}, u32[]{:S(2)}) collective-permute-start(bf16[128,1280]{1,0:T(8,128)(2,1)} %param.33), channel_id=1, source_target_pairs={{0,2},{1,3},{2,0},{3,1},{4,6},{5,7},{6,4},{7,5},{8,10},{9,11},{10,... | collective-permute-start | bytes 983048 | tf_op jit(solution)/shard_map/ppermute | solution.py:163
  20.8 31.7 %collective-permute-start.8 = (bf16[160,960]{1,0:T(8,128)(2,1)}, bf16[160,960]{1,0:T(8,128)(2,1)S(1)}, u32[]{:S(2)}, u32[]{:S(2)}) collective-permute-start(bf16[160,960]{1,0:T(8,128)(2,1)} %get-tuple-element.86), channel_id=1, source_target_pairs={{0,6},{1,7},{2,4},{3,5},{4,2},{5,3},{6,0},{7,1},{8,14},{9,15},{10,... | collective-permute-start | bytes 921608 | tf_op jit(solution)/shard_map/ppermute | solution.py:163
  20.9 33.1 %collective-permute-start.7 = (bf16[160,960]{1,0:T(8,128)(2,1)}, bf16[160,960]{1,0:T(8,128)(2,1)S(1)}, u32[]{:S(2)}, u32[]{:S(2)}) collective-permute-start(bf16[160,960]{1,0:T(8,128)(2,1)} %get-tuple-element.87), channel_id=1, source_target_pairs={{0,4},{1,5},{2,6},{3,7},{4,0},{5,1},{6,2},{7,3},{8,12},{9,13},{10,... | collective-permute-start | bytes 921608 | tf_op jit(solution)/shard_map/ppermute | solution.py:163
  52.5 26.7 %collective-permute-start.27 = (bf16[128,1280]{1,0:T(8,128)(2,1)S(1)}, bf16[128,1280]{1,0:T(8,128)(2,1)S(1)}, u32[]{:S(2)}, u32[]{:S(2)}) collective-permute-start(bf16[128,1280]{1,0:T(8,128)(2,1)S(1)} %copy-done.9), channel_id=1, source_target_pairs={{0,6},{1,7},{2,4},{3,5},{4,2},{5,3},{6,0},{7,1},{8,14},{9,15},{10,... | collective-permute-start | bytes 983048 | tf_op jit(solution)/shard_map/ppermute | solution.py:163
  56.2 21.9 %collective-permute-start.2 = (bf16[128,1280]{1,0:T(8,128)(2,1)S(1)}, bf16[128,1280]{1,0:T(8,128)(2,1)S(1)}, u32[]{:S(2)}, u32[]{:S(2)}) collective-permute-start(bf16[128,1280]{1,0:T(8,128)(2,1)S(1)} %copy-done), channel_id=1, source_target_pairs={{0,6},{1,7},{2,4},{3,5},{4,2},{5,3},{6,0},{7,1},{8,14},{9,15},{10,... | collective-permute-start | bytes 983048 | tf_op jit(solution)/shard_map/ppermute | solution.py:163
  58.7 38.6 %collective-permute-start.10 = (bf16[160,1280]{1,0:T(8,128)(2,1)S(1)}, bf16[160,1280]{1,0:T(8,128)(2,1)S(1)}, u32[]{:S(2)}, u32[]{:S(2)}) collective-permute-start(bf16[160,1280]{1,0:T(8,128)(2,1)S(1)} %copy-done.20), channel_id=1, source_target_pairs={{0,1},{1,0},{2,3},{3,2},{4,5},{5,4},{6,7},{7,6},{8,9},{9,8},{10,11... | collective-permute-start | bytes 1228808 | tf_op jit(solution)/shard_map/ppermute | solution.py:163
  71.7 22.9 %collective-permute-start.19 = (bf16[160,1280]{1,0:T(8,128)(2,1)S(1)}, bf16[160,1280]{1,0:T(8,128)(2,1)S(1)}, u32[]{:S(2)}, u32[]{:S(2)}) collective-permute-start(bf16[160,1280]{1,0:T(8,128)(2,1)S(1)} %get-tuple-element.63), channel_id=1, source_target_pairs={{0,6},{1,7},{2,4},{3,5},{4,2},{5,3},{6,0},{7,1},{8,14},{9,15},{10,... | collective-permute-start | bytes 1228808 | tf_op jit(solution)/shard_map/ppermute | solution.py:163
  78.1 17.8 %collective-permute-start.18 = (bf16[160,1280]{1,0:T(8,128)(2,1)S(1)}, bf16[160,1280]{1,0:T(8,128)(2,1)S(1)}, u32[]{:S(2)}, u32[]{:S(2)}) collective-permute-start(bf16[160,1280]{1,0:T(8,128)(2,1)S(1)} %get-tuple-element.64), channel_id=1, source_target_pairs={{0,4},{1,5},{2,6},{3,7},{4,0},{5,1},{6,2},{7,3},{8,12},{9,13},{10,... | collective-permute-start | bytes 1228808 | tf_op jit(solution)/shard_map/ppermute | solution.py:163
  79.2 19.2 %collective-permute-start.9 = (bf16[4,160,960]{2,1,0:T(8,128)(2,1)S(1)}, bf16[4,160,960]{2,1,0:T(8,128)(2,1)S(1)}, u32[]{:S(2)}, u32[]{:S(2)}) collective-permute-start(bf16[4,160,960]{2,1,0:T(8,128)(2,1)S(1)} %pad_maximum_fusion.8), channel_id=1, source_target_pairs={{0,1},{1,0},{2,3},{3,2},{4,5},{5,4},{6,7},{7,6},{8,9},{9,8},{10,11... | collective-permute-start | bytes 3686408 | tf_op jit(solution)/shard_map/ppermute | solution.py:163
  85.7 31.7 %collective-permute-start.21 = (bf16[640,1280]{1,0:T(8,128)(2,1)}, bf16[640,1280]{1,0:T(8,128)(2,1)}, u32[]{:S(2)}, u32[]{:S(2)}) collective-permute-start(bf16[640,1280]{1,0:T(8,128)(2,1)} %param.31), channel_id=1, source_target_pairs={{0,1},{1,0},{2,3},{3,2},{4,5},{5,4},{6,7},{7,6},{8,9},{9,8},{10,11... | collective-permute-start | bytes 4915208 | tf_op jit(solution)/shard_map/ppermute | solution.py:163
  97.3 39.4 %collective-permute-start.20 = (bf16[4,160,1280]{2,1,0:T(8,128)(2,1)}, bf16[4,160,1280]{2,1,0:T(8,128)(2,1)}, u32[]{:S(2)}, u32[]{:S(2)}) collective-permute-start(bf16[4,160,1280]{2,1,0:T(8,128)(2,1)} %pad_maximum_fusion.5), channel_id=1, source_target_pairs={{0,1},{1,0},{2,3},{3,2},{4,5},{5,4},{6,7},{7,6},{8,9},{9,8},{10,11... | collective-permute-start | bytes 4915208 | tf_op jit(solution)/shard_map/ppermute | solution.py:163
  161.6 17.7 %collective-permute-start.29 = (bf16[128,1280]{1,0:T(8,128)(2,1)S(1)}, bf16[128,1280]{1,0:T(8,128)(2,1)S(1)}, u32[]{:S(2)}, u32[]{:S(2)}) collective-permute-start(bf16[128,1280]{1,0:T(8,128)(2,1)S(1)} %get-tuple-element.78), channel_id=1, source_target_pairs={{0,4},{1,5},{2,6},{3,7},{4,0},{5,1},{6,2},{7,3},{8,12},{9,13},{10,... | collective-permute-start | bytes 983048 | tf_op jit(solution)/shard_map/ppermute | solution.py:163
  164.1 19.2 %collective-permute-start.22 = (bf16[128,1280]{1,0:T(8,128)(2,1)S(1)}, bf16[128,1280]{1,0:T(8,128)(2,1)S(1)}, u32[]{:S(2)}, u32[]{:S(2)}) collective-permute-start(bf16[128,1280]{1,0:T(8,128)(2,1)S(1)} %get-tuple-element.79), channel_id=1, source_target_pairs={{0,2},{1,3},{2,0},{3,1},{4,6},{5,7},{6,4},{7,5},{8,10},{9,11},{10,... | collective-permute-start | bytes 983048 | tf_op jit(solution)/shard_map/ppermute | solution.py:163
  165.6 24.8 %collective-permute-start.24 = (bf16[128,1280]{1,0:T(8,128)(2,1)S(1)}, bf16[128,1280]{1,0:T(8,128)(2,1)S(1)}, u32[]{:S(2)}, u32[]{:S(2)}) collective-permute-start(bf16[128,1280]{1,0:T(8,128)(2,1)S(1)} %get-tuple-element.80), channel_id=1, source_target_pairs={{0,6},{1,7},{2,4},{3,5},{4,2},{5,3},{6,0},{7,1},{8,14},{9,15},{10,... | collective-permute-start | bytes 983048 | tf_op jit(solution)/shard_map/ppermute | solution.py:163
  169.3 22.4 %collective-permute-start.23 = (bf16[128,1280]{1,0:T(8,128)(2,1)S(1)}, bf16[128,1280]{1,0:T(8,128)(2,1)S(1)}, u32[]{:S(2)}, u32[]{:S(2)}) collective-permute-start(bf16[128,1280]{1,0:T(8,128)(2,1)S(1)} %get-tuple-element.81), channel_id=1, source_target_pairs={{0,4},{1,5},{2,6},{3,7},{4,0},{5,1},{6,2},{7,3},{8,12},{9,13},{10,... | collective-permute-start | bytes 983048 | tf_op jit(solution)/shard_map/ppermute | solution.py:163
  204.8 86.2 %collective-permute-start.61 = (bf16[1,640,1280]{2,1,0:T(8,128)(2,1)}, bf16[1,640,1280]{2,1,0:T(8,128)(2,1)}, u32[]{:S(2)}, u32[]{:S(2)}) collective-permute-start(bf16[1,640,1280]{2,1,0:T(8,128)(2,1)} %fusion.16), channel_id=1, source_target_pairs={{0,1},{1,0},{2,3},{3,2},{4,5},{5,4},{6,7},{7,6},{8,9},{9,8},{10,11... | collective-permute-start | bytes 4915208 | tf_op jit(solution)/shard_map/ppermute | solution.py:163
  218.7 77.8 %collective-permute-start.54 = (bf16[4,160,1280]{2,1,0:T(8,128)(2,1)}, bf16[4,160,1280]{2,1,0:T(8,128)(2,1)}, u32[]{:S(2)}, u32[]{:S(2)}) collective-permute-start(bf16[4,160,1280]{2,1,0:T(8,128)(2,1)} %fusion.15), channel_id=1, source_target_pairs={{0,1},{1,0},{2,3},{3,2},{4,5},{5,4},{6,7},{7,6},{8,9},{9,8},{10,11... | collective-permute-start | bytes 4915208 | tf_op jit(solution)/shard_map/ppermute | solution.py:163
  283.7 21.3 %collective-permute-start.50 = (bf16[1,160,1280]{2,1,0:T(8,128)(2,1)S(1)}, bf16[1,160,1280]{2,1,0:T(8,128)(2,1)S(1)}, u32[]{:S(2)}, u32[]{:S(2)}) collective-permute-start(bf16[1,160,1280]{2,1,0:T(8,128)(2,1)S(1)} %fusion.51), channel_id=1, source_target_pairs={{0,1},{1,0},{2,3},{3,2},{4,5},{5,4},{6,7},{7,6},{8,9},{9,8},{10,11... | collective-permute-start | bytes 1228808 | tf_op jit(solution)/shard_map/ppermute | solution.py:163
  284.2 18.3 %collective-permute-start.43 = (bf16[4,160,960]{2,1,0:T(8,128)(2,1)S(1)}, bf16[4,160,960]{2,1,0:T(8,128)(2,1)}, u32[]{:S(2)}, u32[]{:S(2)}) collective-permute-start(bf16[4,160,960]{2,1,0:T(8,128)(2,1)S(1)} %fusion.18), channel_id=1, source_target_pairs={{0,1},{1,0},{2,3},{3,2},{4,5},{5,4},{6,7},{7,6},{8,9},{9,8},{10,11... | collective-permute-start | bytes 3686408 | tf_op jit(solution)/shard_map/ppermute | solution.py:163
  293.9 48.5 %collective-permute-start.62 = (bf16[640,1280]{1,0:T(8,128)(2,1)S(1)}, bf16[640,1280]{1,0:T(8,128)(2,1)S(1)}, u32[]{:S(2)}, u32[]{:S(2)}) collective-permute-start(bf16[640,1280]{1,0:T(8,128)(2,1)S(1)} %fusion.17), channel_id=1, source_target_pairs={{0,8},{24,16},{1,9},{25,17},{2,10},{26,18},{3,11},{27,19},{4,12},{... | collective-permute-start | bytes 4915208 | tf_op jit(solution)/shard_map/ppermute | solution.py:199
  301.1 20.6 %collective-permute-start.56 = (bf16[160,1280]{1,0:T(8,128)(2,1)S(1)}, bf16[160,1280]{1,0:T(8,128)(2,1)S(1)}, u32[]{:S(2)}, u32[]{:S(2)}) collective-permute-start(bf16[160,1280]{1,0:T(8,128)(2,1)S(1)} %get-tuple-element.59), channel_id=1, source_target_pairs={{0,4},{1,5},{2,6},{3,7},{4,0},{5,1},{6,2},{7,3},{8,12},{9,13},{10,... | collective-permute-start | bytes 1228808 | tf_op jit(solution)/shard_map/ppermute | solution.py:163
  302.6 20.8 %collective-permute-start.55 = (bf16[160,1280]{1,0:T(8,128)(2,1)S(1)}, bf16[160,1280]{1,0:T(8,128)(2,1)S(1)}, u32[]{:S(2)}, u32[]{:S(2)}) collective-permute-start(bf16[160,1280]{1,0:T(8,128)(2,1)S(1)} %get-tuple-element.60), channel_id=1, source_target_pairs={{0,2},{1,3},{2,0},{3,1},{4,6},{5,7},{6,4},{7,5},{8,10},{9,11},{10,... | collective-permute-start | bytes 1228808 | tf_op jit(solution)/shard_map/ppermute | solution.py:163
  304.9 22.7 %collective-permute-start.46 = (bf16[160,960]{1,0:T(8,128)(2,1)S(1)}, bf16[160,960]{1,0:T(8,128)(2,1)S(1)}, u32[]{:S(2)}, u32[]{:S(2)}) collective-permute-start(bf16[160,960]{1,0:T(8,128)(2,1)S(1)} %get-tuple-element.70), channel_id=1, source_target_pairs={{0,6},{1,7},{2,4},{3,5},{4,2},{5,3},{6,0},{7,1},{8,14},{9,15},{10,... | collective-permute-start | bytes 921608 | tf_op jit(solution)/shard_map/ppermute | solution.py:163
  312.8 20.5 %collective-permute-start.45 = (bf16[160,960]{1,0:T(8,128)(2,1)S(1)}, bf16[160,960]{1,0:T(8,128)(2,1)S(1)}, u32[]{:S(2)}, u32[]{:S(2)}) collective-permute-start(bf16[160,960]{1,0:T(8,128)(2,1)S(1)} %get-tuple-element.71), channel_id=1, source_target_pairs={{0,4},{1,5},{2,6},{3,7},{4,0},{5,1},{6,2},{7,3},{8,12},{9,13},{10,... | collective-permute-start | bytes 921608 | tf_op jit(solution)/shard_map/ppermute | solution.py:163
  333.3 70.8 %collective-permute-start.58 = (bf16[4,160,1280]{2,1,0:T(8,128)(2,1)S(1)}, bf16[4,160,1280]{2,1,0:T(8,128)(2,1)S(1)}, u32[]{:S(2)}, u32[]{:S(2)}) collective-permute-start(bf16[4,160,1280]{2,1,0:T(8,128)(2,1)S(1)} %pad_maximum_fusion.6), channel_id=1, source_target_pairs={{0,8},{24,16},{1,9},{25,17},{2,10},{26,18},{3,11},{27,19},{4,12},{... | collective-permute-start | bytes 4915208 | tf_op jit(solution)/shard_map/ppermute | solution.py:199
  335.1 67.7 %collective-permute-start.47 = (bf16[4,160,960]{2,1,0:T(8,128)(2,1)S(1)}, bf16[4,160,960]{2,1,0:T(8,128)(2,1)S(1)}, u32[]{:S(2)}, u32[]{:S(2)}) collective-permute-start(bf16[4,160,960]{2,1,0:T(8,128)(2,1)S(1)} %pad_maximum_fusion.11), channel_id=1, source_target_pairs={{0,8},{24,16},{1,9},{25,17},{2,10},{26,18},{3,11},{27,19},{4,12},{... | collective-permute-start | bytes 3686408 | tf_op jit(solution)/shard_map/ppermute | solution.py:199
  341.7 64.2 %collective-permute-start.52 = (bf16[160,1280]{1,0:T(8,128)(2,1)S(1)}, bf16[160,1280]{1,0:T(8,128)(2,1)S(1)}, u32[]{:S(2)}, u32[]{:S(2)}) collective-permute-start(bf16[160,1280]{1,0:T(8,128)(2,1)S(1)} %add_convert_fusion.8), channel_id=1, source_target_pairs={{8,16},{16,8},{9,17},{17,9},{10,18},{18,10},{11,19},{19,11},{12,20... | collective-permute-start | bytes 1228808 | tf_op jit(solution)/shard_map/ppermute | solution.py:199
  342.8 66.9 %collective-permute-start.63 = (bf16[640,1280]{1,0:T(8,128)(2,1)S(1)}, bf16[640,1280]{1,0:T(8,128)(2,1)S(1)}, u32[]{:S(2)}, u32[]{:S(2)}) collective-permute-start(bf16[640,1280]{1,0:T(8,128)(2,1)S(1)} %add_convert_fusion.1), channel_id=1, source_target_pairs={{8,16},{16,8},{9,17},{17,9},{10,18},{18,10},{11,19},{19,11},{12,20... | collective-permute-start | bytes 4915208 | tf_op jit(solution)/shard_map/ppermute | solution.py:199
  408.4 62.8 %collective-permute-start.49 = (bf16[4,160,960]{2,1,0:T(8,128)(2,1)S(1)}, bf16[4,160,960]{2,1,0:T(8,128)(2,1)S(1)}, u32[]{:S(2)}, u32[]{:S(2)}) collective-permute-start(bf16[4,160,960]{2,1,0:T(8,128)(2,1)S(1)} %add_convert_fusion.4), channel_id=1, source_target_pairs={{8,0},{16,24},{9,1},{17,25},{10,2},{18,26},{11,3},{19,27},{12,4},{... | collective-permute-start | bytes 3686408 | tf_op jit(solution)/shard_map/ppermute | solution.py:199
  411.3 95.1 %collective-permute-start.64 = (bf16[640,1280]{1,0:T(8,128)(2,1)}, bf16[640,1280]{1,0:T(8,128)(2,1)}, u32[]{:S(2)}, u32[]{:S(2)}) collective-permute-start(bf16[640,1280]{1,0:T(8,128)(2,1)} %add_convert_fusion), channel_id=1, source_target_pairs={{8,0},{16,24},{9,1},{17,25},{10,2},{18,26},{11,3},{19,27},{12,4},{... | collective-permute-start | bytes 4915208 | tf_op jit(solution)/shard_map/ppermute | solution.py:199
  414.4 120.6 %collective-permute-start.60 = (bf16[4,160,1280]{2,1,0:T(8,128)(2,1)}, bf16[4,160,1280]{2,1,0:T(8,128)(2,1)}, u32[]{:S(2)}, u32[]{:S(2)}) collective-permute-start(bf16[4,160,1280]{2,1,0:T(8,128)(2,1)} %add_convert_fusion.2), channel_id=1, source_target_pairs={{8,0},{16,24},{9,1},{17,25},{10,2},{18,26},{11,3},{19,27},{12,4},{... | collective-permute-start | bytes 4915208 | tf_op jit(solution)/shard_map/ppermute | solution.py:199
  (83 other events, 850.2 us)

commit v2 on v1

v2 whole, which is shorter than its diff:
```python
import jax
import jax.numpy as jnp
from jax import lax
from jax.experimental import pallas as pl
from jax.experimental.pallas import tpu as pltpu
from jax.sharding import PartitionSpec as P

D = 1280
HEADS = 20
HEAD_DIM = 64
FF = 5120
CELLS_DEV = 2
EPS = 1e-05

TEAM = 8
CHIPS = 4
HEADS_CHIP = HEADS // CHIPS
D_CHIP = D // CHIPS
FF_CHIP = FF // CHIPS
SHARE = D // TEAM
FF_SHARE = FF // TEAM
SCALE = HEAD_DIM ** (-0.5)

GAIN1, BIAS1, BIAS_OUT, GAIN2, BIAS2, BIAS_DOWN, BIAS_UP, BIAS_QKV = range(8)
TABLE_ROWS = 8

COST = pl.CostEstimate(flops=1, bytes_accessed=1, transcendentals=0)
ANY = pl.BlockSpec(memory_space=pl.ANY)
SMEM = pl.BlockSpec(memory_space=pltpu.SMEM)
VMEM = pl.BlockSpec(memory_space=pltpu.VMEM)

f32 = jnp.float32
bf16 = jnp.bfloat16


def dot(a, b, dims):
    return lax.dot_general(a, b, (dims, ((), ())), preferred_element_type=f32)


def mm(a, b):
    return dot(a, b, ((1,), (0,)))


def mm_t(a, b):
    return dot(a, b, ((1,), (1,)))


def t_mm(a, b):
    return dot(a, b, ((0,), (0,)))


def normalize(values):
    center = jnp.mean(values, axis=-1, keepdims=True)
    centred = values - center
    spread = jnp.mean(centred * centred, axis=-1, keepdims=True)
    inverse = lax.rsqrt(spread + EPS)
    return centred * inverse, inverse


def norm_backward(grad_out, normed, inverse, norm_gain):
    grad_normed = grad_out * norm_gain
    first_mean = jnp.mean(grad_normed, axis=-1, keepdims=True)
    second_mean = jnp.mean(grad_normed * normed, axis=-1, keepdims=True)
    grad_in = inverse * (grad_normed - first_mean - normed * second_mean)
    gain_sum = jnp.sum(grad_out * normed, axis=0, keepdims=True)
    return grad_in, gain_sum, jnp.sum(grad_out, axis=0, keepdims=True)


def heads_of(projected, offset):
    return [
        projected[:, offset + i * HEAD_DIM : offset + (i + 1) * HEAD_DIM] for i in range(HEADS_CHIP)
    ]


def softmax_rows(queries, keys, keep):
    raw = jnp.concatenate([mm_t(q, k) for q, k in zip(queries, keys)], axis=0)
    masked = jnp.where(keep, raw * SCALE, -1e30)
    grown = jnp.exp(masked - jnp.max(masked, axis=-1, keepdims=True))
    return grown * (1.0 / jnp.sum(grown, axis=-1, keepdims=True))


def keep_of(mask):
    return jnp.concatenate([mask.astype(f32)] * HEADS_CHIP, axis=0) > 0.5


def attend(projected, mask):
    rows = mask.shape[0]
    probs = softmax_rows(heads_of(projected, 0), heads_of(projected, D_CHIP), keep_of(mask))
    probs = probs.astype(bf16)
    out = [
        mm(probs[i * rows : (i + 1) * rows], value)
        for i, value in enumerate(heads_of(projected, 2 * D_CHIP))
    ]
    return jnp.concatenate(out, axis=1).astype(bf16)


def attend_back(projected, mask, grad_context):
    rows = mask.shape[0]
    queries, keys, values = (heads_of(projected, i * D_CHIP) for i in range(3))
    grads = heads_of(grad_context, 0)
    probs = softmax_rows(queries, keys, keep_of(mask))
    grad_probs = jnp.concatenate([mm_t(g, v) for g, v in zip(grads, values)], axis=0)
    along = jnp.sum(grad_probs * probs, axis=-1, keepdims=True)
    grad_scores = (probs * (grad_probs - along) * SCALE).astype(bf16)
    probs = probs.astype(bf16)

    def cut(stack, i):
        return stack[i * rows : (i + 1) * rows]

    out = (
        [mm(cut(grad_scores, i), keys[i]) for i in range(HEADS_CHIP)]
        + [t_mm(cut(grad_scores, i), queries[i]) for i in range(HEADS_CHIP)]
        + [t_mm(cut(probs, i), grads[i]) for i in range(HEADS_CHIP)]
    )
    return jnp.concatenate(out, axis=1).astype(bf16)


HALF = SHARE // 2
EXTRA = 16
ROWS_Z = 2 * SHARE


def call(kernel, name, kinds, out_shapes, scratch=(), vmem=16):
    specs = {"s": SMEM, "a": ANY, "v": VMEM}
    return pl.pallas_call(
        kernel,
        in_specs=[specs[kind] for kind in kinds],
        out_specs=[VMEM] * len(out_shapes),
        out_shape=[jax.ShapeDtypeStruct(shape, kind) for shape, kind in out_shapes],
        scratch_shapes=list(scratch),
        compiler_params=pltpu.CompilerParams(vmem_limit_bytes=vmem * 2**20),
        cost_estimate=COST,
        name=name,
    )


def sems(count):
    return pltpu.SemaphoreType.DMA((count,))


def row_at(i, size):
    return pl.ds(pl.multiple_of(i * size, size), size)


def tiled(width, tile, body):
    @pl.loop(0, width // tile)
    def _(i):
        body(row_at(i, tile))


def stack_blocks(blocks, whole):
    rows = blocks[0].shape[0]
    for i, block in enumerate(blocks):
        whole[i * rows : (i + 1) * rows, :] = block[...]


def row_of(spot, i, of_core, half=None):
    row = (2 * (spot[0] ^ i) + of_core) * SHARE
    if half is None:
        return pl.ds(pl.multiple_of(row, SHARE), SHARE)
    return pl.ds(pl.multiple_of(row + half * HALF, HALF), HALF)


def stack_columns(spot, mine, other, whole):
    core, side = spot[1], spot[2]
    for of_core, (near, far) in ((core, mine), (1 - core, other)):
        whole[row_of(spot, 0, of_core), :] = near[:SHARE, :]
        for i in range(1, CHIPS):
            lo = SHARE + (i - 1) * HALF
            whole[row_of(spot, i, of_core, side), :] = near[lo : lo + HALF, :]
            lo = (i - 1) * HALF
            whole[row_of(spot, i, of_core, 1 - side), :] = far[lo : lo + HALF, :]


def by_core_copies(core, mine, other, whole, sem):
    size = mine.shape[0]
    return [
        pltpu.make_async_copy(mine, whole.at[row_at(core, size)], sem.at[0]),
        pltpu.make_async_copy(other, whole.at[row_at(1 - core, size)], sem.at[1]),
    ]


def start_all(copies):
    for copy in copies:
        copy.start()


def wait_all(copies):
    for copy in copies:
        copy.wait()


def chip_columns(weights, rows, chip):
    start = pl.multiple_of((chip * 5 // 2) * 128, 128)
    odd = lax.rem(chip, 2) == 1
    out = []
    for kind in range(3):
        window = weights[rows, pl.ds(kind * D + start, 384)]
        out.append(jnp.where(odd, window[:, 64 : 64 + D_CHIP], window[:, :D_CHIP]))
    return jnp.concatenate(out, axis=1)


def qkv_blocks_kernel(spot, lengths, padding, weights, *refs):
    vectors, own, sent = refs[:9], refs[9], refs[10 : 9 + CHIPS]
    held, marks, whole, vector_sems, sem = refs[9 + CHIPS : 18 + CHIPS], *refs[18 + CHIPS :]
    copies = [
        pltpu.make_async_copy(vector, here, vector_sems.at[i])
        for i, (vector, here) in enumerate(zip(vectors, held))
    ]
    copies.append(pltpu.make_async_copy(padding, marks, sem.at[0]))
    copies.append(pltpu.make_async_copy(weights, whole, sem.at[1]))
    start_all(copies)
    wait_all(copies)
    rows = padding.shape[-1]
    place = lax.broadcasted_iota(jnp.int32, (1, rows), 1)
    first = lengths[0, 0]
    member = (place >= first).astype(f32)
    leading = (place == 0) | (place == first)
    usable = jnp.where(leading | (marks[...].reshape(1, rows) > 0), 1.0, 0.0)
    code = 2.0 * member + usable
    width = 3 * D_CHIP
    lines = [v[...].astype(f32).reshape(1, -1) for v in held]
    extra = jnp.concatenate(
        [
            jnp.concatenate(lines[:6], axis=1),
            jnp.concatenate(lines[6:], axis=1),
            jnp.concatenate([code, jnp.zeros((1, width - rows), f32)], axis=1),
            jnp.zeros((EXTRA - 3, width), f32),
        ],
        axis=0,
    ).astype(bf16)
    own[:SHARE, :] = chip_columns(whole, slice(None), spot[0])
    own[SHARE:, :] = extra
    for i, block in enumerate(sent):
        block[:HALF, :] = chip_columns(whole, row_at(spot[2], HALF), spot[0] ^ (i + 1))
        block[HALF:, :] = extra


def qkv_blocks(spot, lengths, padding, weights, vectors):
    half = ((HALF + EXTRA, 3 * D_CHIP), bf16)
    return call(
        qkv_blocks_kernel,
        "qkv_blocks",
        "ss" + "a" * 11,
        [((SHARE + EXTRA, 3 * D_CHIP), bf16)] + [half] * (CHIPS - 1),
        [pltpu.VMEM(v.shape, v.dtype) for v in vectors]
        + [
            pltpu.VMEM(padding.shape, padding.dtype),
            pltpu.VMEM(weights.shape, weights.dtype),
            sems(9),
            sems(2),
        ],
    )(spot, lengths, padding, weights, *vectors)


def qkv_join_kernel(own, q1, q2, q3, near, near_half, extras):
    near[:SHARE, :] = own[:SHARE, :]
    extras[:EXTRA, :] = own[SHARE:, :]
    for i, block in enumerate((q1, q2, q3)):
        near[SHARE + i * HALF : SHARE + (i + 1) * HALF, :] = block[:HALF, :]
        near_half[i * HALF : (i + 1) * HALF, :] = block[:HALF, :]
        extras[(i + 1) * EXTRA : (i + 2) * EXTRA, :] = block[HALF:, :]


def qkv_join(blocks):
    width = blocks[0].shape[-1]
    return call(
        qkv_join_kernel,
        "qkv_join",
        "vvvv",
        [
            ((SHARE + 3 * HALF, width), bf16),
            ((3 * HALF, width), bf16),
            ((CHIPS * EXTRA, width), bf16),
        ],
    )(*blocks)


def up_blocks_kernel(spot, weights, cotangent, own, *sent):
    def columns(chip):
        return pl.ds(pl.multiple_of(chip * FF_CHIP, FF_CHIP), FF_CHIP)

    rows = cotangent.shape[0]
    own[...] = weights[:, columns(spot[0])]
    for i, block in enumerate(sent):
        block[:rows, :] = cotangent[...]
        block[rows:, :] = weights[row_at(spot[2], HALF), columns(spot[0] ^ (i + 1))]


def up_blocks(spot, weights, cotangent):
    half = ((cotangent.shape[0] + HALF, FF_CHIP), bf16)
    return call(
        up_blocks_kernel, "up_blocks", "svv", [((SHARE, FF_CHIP), bf16)] + [half] * (CHIPS - 1)
    )(spot, weights, cotangent)


def up_join_kernel(own, cotangent, u1, u2, u3, near, near_half, whole):
    rows = cotangent.shape[0]
    near[:SHARE, :] = own[...]
    whole[:rows, :] = cotangent[...]
    for i, block in enumerate((u1, u2, u3)):
        near[SHARE + i * HALF : SHARE + (i + 1) * HALF, :] = block[rows:, :]
        near_half[i * HALF : (i + 1) * HALF, :] = block[rows:, :]
        whole[(i + 1) * rows : (i + 2) * rows, :] = block[:rows, :]


def up_join(own, cotangent, blocks):
    return call(
        up_join_kernel,
        "up_join",
        "vvvvv",
        [
            ((SHARE + 3 * HALF, FF_CHIP), bf16),
            ((3 * HALF, FF_CHIP), bf16),
            ((CHIPS * cotangent.shape[0], D), bf16),
        ],
    )(own, cotangent, *blocks)


def fill_table(spot, extras, table, mask):
    chip, core = spot[0], spot[1]
    rows = mask.shape[1]
    table[...] = jnp.zeros_like(table)
    for team in range(TEAM):
        for i in range(6):
            table[i : i + 1, team * SHARE : (team + 1) * SHARE] = extras[
                team, 0:1, i * SHARE : (i + 1) * SHARE
            ]
    for half in range(2):
        line = extras[2 * chip + half, 1:2, :]
        lo = half * SHARE
        table[BIAS_QKV : BIAS_QKV + 1, lo : lo + SHARE] = line[:, :SHARE]
        table[BIAS_QKV : BIAS_QKV + 1, 2 * D_CHIP + lo : 2 * D_CHIP + lo + SHARE] = line[
            :, SHARE : 2 * SHARE
        ]
        table[BIAS_UP : BIAS_UP + 1, half * FF_SHARE : (half + 1) * FF_SHARE] = line[:, 2 * SHARE :]
    for i in range(CHIPS):
        code = extras[2 * (chip ^ i) + core, 2:3, :rows]
        of_key = jnp.broadcast_to(code, (rows, rows))
        cell_of_key = jnp.floor(of_key * 0.5)
        open_key = of_key - 2.0 * cell_of_key
        keep = jnp.where(cell_of_key == cell_of_key.T, open_key, 0.0)
        mask[i * rows : (i + 1) * rows, :] = keep.astype(bf16)


def token_norm_kernel(x0, x1, x2, x3, normed):
    rows = x0.shape[0]
    for i, x in enumerate((x0, x1, x2, x3)):
        normed[i * rows : (i + 1) * rows, :] = normalize(x[...].astype(f32))[0]


def token_norm(blocks):
    rows, width = blocks[0].shape
    return call(token_norm_kernel, "token_norm", "vvvv", [((CHIPS * rows, width), f32)])(*blocks)[0]


def enter_kernel(spot, normed, *refs):
    mine, other, refs = refs[:3], refs[3:6], refs[6:]
    out_mine, out_other, refs = *refs[:2], refs[2:]
    table, mask, qkv, out, first_low, projected, context = refs[:7]
    partials = refs[7 : 7 + CHIPS]
    extras, out_sems = refs[7 + CHIPS :]
    rows = mask.shape[1]
    out_copies = by_core_copies(spot[1], out_mine, out_other, out, out_sems)
    start_all(out_copies)
    for of_core, lines in ((spot[1], mine[2]), (1 - spot[1], other[2])):
        for i in range(CHIPS):
            extras[2 * (spot[0] ^ i) + of_core] = lines[i * EXTRA : (i + 1) * EXTRA, :].astype(f32)
    fill_table(spot, extras, table, mask)
    stack_columns(spot, mine[:2], other[:2], qkv)
    gain = table[GAIN1 : GAIN1 + 1, :]
    bias = table[BIAS1 : BIAS1 + 1, :]
    first_low[...] = (normed[...] * gain + bias).astype(bf16)
    for lo, hi in ((0, 384), (384, 768), (768, 960)):
        shift = table[BIAS_QKV : BIAS_QKV + 1, lo:hi]
        projected[:, lo:hi] = (mm(first_low[...], qkv[:, lo:hi]) + shift).astype(bf16)

    @pl.loop(0, CHIPS)
    def _(i):
        at = row_at(i, rows)
        context[at, :] = attend(projected[at, :], mask[at, :])

    wait_all(out_copies)

    def partial(at):
        whole = mm(context[...], out[:, at]).astype(bf16)
        for i, part in enumerate(partials):
            part[:, at] = whole[i * rows : (i + 1) * rows]

    tiled(D, 256, partial)


def enter(spot, normed, mine, other, out_mine, out_other):
    total = normed.shape[0]
    rows = total // CHIPS
    outs = call(
        enter_kernel,
        "enter",
        "sv" + "v" * 6 + "aa",
        [
            ((TABLE_ROWS, D), f32),
            ((total, rows), bf16),
            ((D, 3 * D_CHIP), bf16),
            ((D_CHIP, D), bf16),
            ((total, D), bf16),
            ((total, 3 * D_CHIP), bf16),
            ((total, D_CHIP), bf16),
        ]
        + [((rows, D), bf16)] * CHIPS,
        [pltpu.VMEM((TEAM, EXTRA, 3 * D_CHIP), f32), sems(2)],
    )(spot, normed, *mine, *other, out_mine, out_other)
    return outs[:7], outs[7:]


def leave_kernel(
    b0, b1, b2, b3, qkv, out, projected, mask, branch, grad_projected, bias_sum, *refs
):
    partials, grad_context = refs[:CHIPS], refs[CHIPS]
    rows = b0.shape[0]
    stack_blocks((b0, b1, b2, b3), branch)
    grad_context[...] = mm_t(branch[...], out[...]).astype(bf16)
    bias_sum[...] = jnp.zeros_like(bias_sum)

    @pl.loop(0, CHIPS)
    def _(i):
        at = row_at(i, rows)
        grad = attend_back(projected[at, :], mask[at, :], grad_context[at, :])
        grad_projected[at, :] = grad
        bias_sum[...] += jnp.sum(grad.astype(f32), axis=0, keepdims=True)

    def partial(at):
        whole = mm_t(grad_projected[...], qkv[at, :]).astype(bf16)
        for i, part in enumerate(partials):
            part[:, at] = whole[i * rows : (i + 1) * rows]

    tiled(D, 256, partial)


def leave(blocks, qkv, out, projected, mask):
    rows = blocks[0].shape[0]
    total = CHIPS * rows
    outs = call(
        leave_kernel,
        "leave",
        "v" * 8,
        [((total, D), bf16), ((total, 3 * D_CHIP), bf16), ((1, 3 * D_CHIP), f32)]
        + [((rows, D), bf16)] * CHIPS,
        [pltpu.VMEM((total, D_CHIP), bf16)],
    )(*blocks, qkv, out, projected, mask)
    return outs[:3], outs[3:]


def total_of(parts):
    total = parts[0][...].astype(f32)
    for part in parts[1:]:
        total = total + part[...].astype(f32)
    return total


def mix_kernel(p0, p1, p2, p3, tokens, table, mixed, second):
    total = total_of((p0, p1, p2, p3)) + tokens[...].astype(f32)
    total = total + table[BIAS_OUT : BIAS_OUT + 1, :]
    mixed[...] = total
    normed, _ = normalize(total)
    second[...] = (normed * table[GAIN2 : GAIN2 + 1, :] + table[BIAS2 : BIAS2 + 1, :]).astype(bf16)


def mix(parts, tokens, table):
    shape = tokens.shape
    return call(mix_kernel, "mix", "v" * 6, [(shape, f32), (shape, bf16)])(*parts, tokens, table)


def unmix_kernel(p0, p1, p2, p3, mixed, table, cotangent, grad_mixed, branch, sums):
    grad = total_of((p0, p1, p2, p3))
    normed, inverse = normalize(mixed[...])
    grad_in, gain_sum, bias_sum = norm_backward(grad, normed, inverse, table[GAIN2 : GAIN2 + 1, :])
    grad_out = cotangent[...].astype(f32)
    grad_in = grad_in + grad_out
    grad_mixed[...] = grad_in
    low = grad_in.astype(bf16)
    branch[...] = low
    sums[...] = jnp.zeros_like(sums)
    sums[0:1, :] = jnp.sum(low.astype(f32), axis=0, keepdims=True)
    sums[1:2, :] = gain_sum
    sums[2:3, :] = bias_sum
    sums[3:4, :] = jnp.sum(grad_out, axis=0, keepdims=True)


def unmix(parts, mixed, table, cotangent):
    shape = cotangent.shape
    return call(
        unmix_kernel, "unmix", "v" * 7, [(shape, f32), (shape, bf16), ((8, D), f32)]
    )(*parts, mixed, table, cotangent)


def act_grad_kernel(spot, whole, mine, other, grad_act, down, down_sems):
    copies = by_core_copies(spot[1], mine, other, down, down_sems)
    start_all(copies)
    wait_all(copies)

    def columns(at):
        grad_act[:, at] = mm_t(whole[...], down[at, :])

    tiled(FF_CHIP, 256, columns)


def act_grad(spot, cotangent, down_mine, down_other):
    return call(
        act_grad_kernel,
        "act_grad",
        "svaa",
        [((cotangent.shape[0], FF_CHIP), f32), ((FF_CHIP, D), bf16)],
        [sems(2)],
    )(spot, cotangent, down_mine, down_other)


def hidden_kernel(spot, s0, s1, s2, s3, grad_act, cotangent, table, *refs):
    mine, other, refs = refs[:2], refs[2:4], refs[4:]
    second, act, grad_pre, down_sent, bias_sum = refs[:5]
    partials = refs[5 : 5 + CHIPS]
    up, pre_act = refs[5 + CHIPS :]
    rows = s0.shape[0]
    stack_columns(spot, mine, other, up)
    stack_blocks((s0, s1, s2, s3), second)

    def columns(at):
        pre_act[:, at] = mm(second[...], up[:, at]) + table[BIAS_UP : BIAS_UP + 1, at]

    tiled(FF_CHIP, 256, columns)
    bias_sum[...] = jnp.zeros_like(bias_sum)

    def activate(at):
        pre = pre_act[at, :]
        below = 0.5 * (1.0 + lax.erf(pre * (0.5**0.5)))
        bell = jnp.exp(-0.5 * pre * pre) * 0.3989422804014327
        act[at, :] = (pre * below).astype(bf16)
        grad = (grad_act[at, :] * (below + pre * bell)).astype(bf16)
        grad_pre[at, :] = grad
        bias_sum[...] += jnp.sum(grad.astype(f32), axis=0, keepdims=True)

    tiled(second.shape[0], 64, activate)
    first = (1 - spot[1]) * FF_SHARE

    @pl.loop(0, FF_SHARE // 128)
    def _(i):
        columns_at = pl.ds(pl.multiple_of(first + i * 128, 128), 128)
        down_sent[row_at(i, 128), :] = t_mm(act[:, columns_at], cotangent[...]).astype(bf16)

    def partial(at):
        whole = mm_t(grad_pre[...], up[at, :]).astype(bf16)
        for i, part in enumerate(partials):
            part[:, at] = whole[i * rows : (i + 1) * rows]

    tiled(D, 256, partial)


def hidden(spot, blocks, grad_act, cotangent, table, mine, other):
    rows = blocks[0].shape[0]
    total = CHIPS * rows
    outs = call(
        hidden_kernel,
        "hidden",
        "svvvvvvv" + "v" * 4,
        [
            ((total, D), bf16),
            ((total, FF_CHIP), bf16),
            ((total, FF_CHIP), bf16),
            ((FF_SHARE, D), bf16),
            ((1, FF_CHIP), f32),
        ]
        + [((rows, D), bf16)] * CHIPS,
        [pltpu.VMEM((D, FF_CHIP), bf16), pltpu.VMEM((total, FF_CHIP), f32)],
    )(spot, *blocks, grad_act, cotangent, table, *mine, *other)
    return outs[:5], outs[5:]


def down_grad_kernel(spot, act, cotangent, got, first, second):
    kept = pl.ds(pl.multiple_of(spot[1] * FF_SHARE, 128), FF_SHARE)
    half = FF_SHARE // 2
    total = t_mm(act[:, kept], cotangent[...]) + got[...].astype(f32)
    first[...] = total[:half].astype(bf16)
    second[...] = total[half:].astype(bf16)


def down_grad_of(spot, act, cotangent, got):
    half = FF_SHARE // 2
    return call(
        down_grad_kernel, "down_grad", "svvv", [((half, D), bf16), ((half, D), bf16)]
    )(spot, act, cotangent, got)


def split_rows(core, whole, sent, kept):
    for k in range(CHIPS):
        targets = ((sent[k // 2], k % 2, 1 - core), (kept, k, core))
        for target, at, of_core in targets:
            start = pl.multiple_of((2 * k + of_core) * SHARE, SHARE)
            target[at] = whole[pl.ds(start, SHARE), :].astype(bf16)


def up_grad_kernel(spot, second, grad_pre, sent_a, sent_b, kept, whole):
    def columns(at):
        whole[at, :] = t_mm(second[:, at], grad_pre[...])

    tiled(D, 256, columns)
    split_rows(spot[1], whole, (sent_a, sent_b), kept)


def up_grad_of(spot, second, grad_pre):
    half = ((CHIPS // 2, SHARE, FF_CHIP), bf16)
    return call(
        up_grad_kernel,
        "up_grad",
        "svv",
        [half, half, ((CHIPS, SHARE, FF_CHIP), bf16)],
        [pltpu.VMEM((D, FF_CHIP), f32)],
    )(spot, second, grad_pre)


def result_kernel(act, down, *partials):
    rows = partials[0].shape[0]

    def columns(at):
        whole = mm(act[...], down[:, at]).astype(bf16)
        for i, part in enumerate(partials):
            part[:, at] = whole[i * rows : (i + 1) * rows]

    tiled(D, 256, columns)


def result_of(act, down):
    rows = act.shape[0] // CHIPS
    return call(result_kernel, "result", "vv", [((rows, D), bf16)] * CHIPS)(act, down)


def qkv_grad_kernel(
    spot,
    first_low,
    grad_projected,
    context,
    branch,
    sent_a,
    sent_b,
    kept,
    out_sent,
    out_kept,
    whole,
    out,
):
    core = spot[1]

    def columns(at):
        whole[at, :] = t_mm(first_low[:, at], grad_projected[...])

    tiled(D, 256, columns)
    split_rows(core, whole, (sent_a, sent_b), kept)
    out[...] = t_mm(context[...], branch[...])
    for target, of_core in ((out_sent, 1 - core), (out_kept, core)):
        target[...] = out[row_at(of_core, SHARE), :].astype(bf16)


def qkv_grad_of(spot, first_low, grad_projected, context, branch):
    half = ((CHIPS // 2, SHARE, 3 * D_CHIP), bf16)
    rows = ((SHARE, D), bf16)
    return call(
        qkv_grad_kernel,
        "qkv_grad",
        "svvvv",
        [half, half, ((CHIPS, SHARE, 3 * D_CHIP), bf16), rows, rows],
        [pltpu.VMEM((D, 3 * D_CHIP), f32), pltpu.VMEM((D_CHIP, D), f32)],
    )(spot, first_low, grad_projected, context, branch)


def add_kernel(*refs):
    count = len(refs) // 3
    for a, b, c in zip(refs[:count], refs[count : 2 * count], refs[2 * count :]):
        c[...] = (a[...].astype(f32) + b[...].astype(f32)).astype(c.dtype)


def add_all(left, right):
    shapes = [(a.shape, a.dtype) for a in left]
    return call(add_kernel, "add", "v" * (2 * len(left)), shapes)(*left, *right)


def split_add_kernel(kept, got_a, got_b, *halves):
    for i, (half, got) in enumerate(zip(halves, (got_a, got_b))):
        for j in range(CHIPS // 2):
            total = kept[i * CHIPS // 2 + j].astype(f32) + got[j].astype(f32)
            half[j * SHARE : (j + 1) * SHARE, :] = total.astype(bf16)


def split_add(kept, got_a, got_b):
    shape = (ROWS_Z, kept.shape[-1])
    return call(split_add_kernel, "split_add", "vvv", [(shape, bf16)] * 2)(kept, got_a, got_b)


PACKED = SHARE * 3 // 4
STEP = SHARE // 4


def pack_kernel(kept, got_a, got_b, out_kept, out_got, *chunks):
    for i, chunk in enumerate(chunks):
        for j in range(2):
            got = got_b if i else got_a
            total = (kept[2 * i + j].astype(f32) + got[j].astype(f32)).astype(bf16)
            lo = j * PACKED
            chunk[lo : lo + PACKED, : 3 * D_CHIP] = total[:PACKED]
            for part in range(3):
                at = lo + part * STEP
                chunk[at : at + STEP, 3 * D_CHIP :] = total[
                    PACKED:, part * D_CHIP : (part + 1) * D_CHIP
                ]
        rows = slice(i * HALF, (i + 1) * HALF)
        total = out_kept[rows, :].astype(f32) + out_got[rows, :].astype(f32)
        chunk[2 * PACKED :, :] = total.astype(bf16)


def pack(kept, got_a, got_b, out_kept, out_got):
    return call(pack_kernel, "pack", "vvvvv", [((ROWS_Z, D), bf16)] * 2)(
        kept, got_a, got_b, out_kept, out_got
    )


def unpacked(chunk, j):
    lo = j * PACKED
    tail = [
        chunk[lo + part * STEP : lo + (part + 1) * STEP, 3 * D_CHIP :] for part in range(3)
    ]
    return jnp.concatenate(
        [chunk[lo : lo + PACKED, : 3 * D_CHIP], jnp.concatenate(tail, axis=1)], axis=0
    )


def z_kernel(names, spot, *refs):
    ref = dict(zip(names, refs))
    middle = spot[3] > 0
    if "half" in ref:
        ref["half"][...] = (ref["low"][...].astype(f32) + ref["got_side"][...].astype(f32)).astype(
            bf16
        )
    if "send" in ref:
        sent = None
        if "half_before" in ref:
            sent = (
                ref["half_before"][...].astype(f32) + ref["got_middle"][...].astype(f32)
            ).astype(bf16)
        if "low_next" in ref:
            low_next = ref["low_next"][...]
            sent = low_next if sent is None else jnp.where(middle, sent, low_next)
        ref["send"][...] = sent
    if "final" in ref:
        ref["final"][...] = jnp.where(middle, ref["sent_before"][...], ref["got_side"][...])


def z_step(spot, inputs, outputs):
    inputs = {name: value for name, value in inputs.items() if value is not None}
    names = tuple(inputs) + tuple(outputs)
    shape = ((ROWS_Z, D), bf16)

    def kernel(*refs):
        z_kernel(names, *refs)

    done = call(kernel, "z_step", "s" + "v" * len(inputs), [shape] * len(outputs))(
        spot, *inputs.values()
    )
    return dict(zip(outputs, done))


def last_kernel(spot, down_a, sent, got, b0, b1, b2, b3, down, qkv, stack):
    down[:ROWS_Z, :] = down_a[...].astype(f32)
    down[ROWS_Z:, :] = jnp.where(spot[3] > 0, sent[...], got[...]).astype(f32)
    qkv_rows(spot, (b0, b1, b2, b3), qkv, stack)


def last(spot, down_a, sent, got, blocks):
    shape = blocks[0].shape
    return call(
        last_kernel,
        "last",
        "s" + "v" * 7,
        [((2 * ROWS_Z, D), f32), ((shape[0], 3 * D), f32)],
        [pltpu.VMEM((CHIPS,) + shape, bf16)],
    )(spot, down_a, sent, got, *blocks)


def up_exchange_kernel(spot, a, b, *blocks):
    chunks = (a, b)
    for i, block in enumerate(blocks):
        chip = spot[0] ^ i
        at = row_at(lax.rem(chip, 2), SHARE)
        block[...] = jnp.where(chip >= 2, chunks[1][at, :], chunks[0][at, :])


def up_exchange(spot, a, b):
    return call(up_exchange_kernel, "up_exchange", "svv", [((SHARE, FF_CHIP), bf16)] * CHIPS)(
        spot, a, b
    )


def qkv_exchange_kernel(spot, a, b, *refs):
    blocks, out_rows, stack = refs[:CHIPS], refs[CHIPS], refs[CHIPS + 1]
    for i, chunk in enumerate((a, b)):
        for j in range(2):
            stack[2 * i + j] = unpacked(chunk, j)
        out_rows[i * HALF : (i + 1) * HALF, :] = chunk[2 * PACKED :, :].astype(f32)
    for i, block in enumerate(blocks):
        block[...] = stack[spot[0] ^ i]


def qkv_exchange(spot, a, b):
    shape = (SHARE, 3 * D_CHIP)
    outs = call(
        qkv_exchange_kernel,
        "qkv_exchange",
        "svv",
        [(shape, bf16)] * CHIPS + [((SHARE, D), f32)],
        [pltpu.VMEM((CHIPS,) + shape, bf16)],
    )(spot, a, b)
    return outs[:CHIPS], outs[CHIPS]


def qkv_rows(spot, blocks, weights, stack):
    for i, block in enumerate(blocks):
        stack[spot[0] ^ i] = block[...]
    for chip in range(CHIPS):
        for kind in range(3):
            lo = kind * D + chip * D_CHIP
            weights[:, lo : lo + D_CHIP] = stack[
                chip, :, kind * D_CHIP : (kind + 1) * D_CHIP
            ].astype(f32)


def up_rows_kernel(spot, b0, b1, b2, b3, weights):
    for i, block in enumerate((b0, b1, b2, b3)):
        start = pl.multiple_of((spot[0] ^ i) * FF_CHIP, FF_CHIP)
        weights[:, pl.ds(start, FF_CHIP)] = block[...].astype(f32)


def up_rows(spot, blocks):
    return call(up_rows_kernel, "up_rows", "svvvv", [((SHARE, FF), f32)])(spot, *blocks)[0]


def end_kernel(
    spot,
    lengths,
    p0,
    p1,
    p2,
    p3,
    r0,
    r1,
    r2,
    r3,
    grad_mixed,
    tokens,
    table,
    mixed,
    mix_sums,
    qkv_sum,
    up_sum,
    layer_out,
    grad_tokens,
    sums,
):
    grad = total_of((p0, p1, p2, p3))
    normed, inverse = normalize(tokens[...].astype(f32))
    grad_in, gain_sum, bias_sum = norm_backward(grad, normed, inverse, table[GAIN1 : GAIN1 + 1, :])
    grad_tokens[...] = grad_mixed[...] + grad_in
    result = mixed[...] + total_of((r0, r1, r2, r3)) + table[BIAS_DOWN : BIAS_DOWN + 1, :]
    layer_out[...] = result.astype(bf16)
    place = lax.broadcasted_iota(jnp.int32, (result.shape[0], 1), 0)
    picked = jnp.where((place == 0) | (place == lengths[0, 0]), result, 0.0)
    sums[...] = jnp.zeros_like(sums)
    sums[0:1, :] = gain_sum
    sums[1:2, :] = bias_sum
    sums[2:6, :] = mix_sums[0:4, :]
    sums[6:7, :] = jnp.sum(picked, axis=0, keepdims=True)
    sums[7:8, :] = jnp.sum(picked * picked, axis=0, keepdims=True)
    for k in range(CHIPS):
        here = spot[0] == k
        sums[8 + k : 9 + k, :D_CHIP] = jnp.where(here, qkv_sum[:, :D_CHIP], 0.0)
        sums[12 + k : 13 + k, :D_CHIP] = jnp.where(here, qkv_sum[:, 2 * D_CHIP :], 0.0)
        sums[16 + k : 17 + k, :] = jnp.where(here, up_sum[...], 0.0)


def end(spot, lengths, parts, results, *rest):
    shape = parts[0].shape
    return call(
        end_kernel,
        "end",
        "ss" + "v" * 15,
        [(shape, bf16), (shape, f32), ((24, D), f32)],
    )(spot, lengths, *parts, *results, *rest)


def fence(*values):
    return lax.optimization_barrier(values)


def local(
    tokens,
    lengths,
    padding,
    ln1_gain,
    ln1_bias,
    w_qkv,
    b_query,
    b_value,
    w_out,
    b_out,
    ln2_gain,
    ln2_bias,
    w_up,
    b_up,
    w_down,
    b_down,
    cotangent,
):
    fsdp_count = lax.axis_size("fsdp")
    dp_count = lax.axis_size("dp")
    groups = fsdp_count // TEAM
    place = lax.axis_index("fsdp") // groups
    chip = place // 2
    core = place % 2
    depth = lax.axis_index("dp")
    middle = (depth == 1) | (depth == 2)
    spot = jnp.stack([chip, core, depth % 2, middle.astype(jnp.int32)]).astype(jnp.int32)

    def swap(value, mask):
        pairs = [
            (team * groups + group, (team ^ mask) * groups + group)
            for team in range(TEAM)
            for group in range(groups)
        ]
        return lax.ppermute(value, "fsdp", pairs)

    shard_groups = [[team * groups + group for group in range(groups)] for team in range(TEAM)]
    def gather_shards(value):
        if groups == 1:
            return value
        return lax.all_gather(value, "fsdp", axis=0, tiled=True, axis_index_groups=shard_groups)

    def scatter_shards(value):
        if groups == 1:
            return value
        return lax.psum_scatter(
            value, "fsdp", scatter_dimension=0, tiled=True, axis_index_groups=shard_groups
        )

    def along_z(pairs, value):
        return lax.ppermute(value, "dp", pairs)

    def z_swap(value):
        return along_z([(0, 1), (1, 0), (2, 3), (3, 2)], value)

    def z_middle(value):
        return along_z([(1, 2), (2, 1)], value)

    def from_chips(blocks):
        return [blocks[0]] + [swap(block, 2 * i) for i, block in enumerate(blocks) if i > 0]

    def fence_list(first, *others):
        done = fence(*first, *others)
        return list(done[: len(first)]), *done[len(first) :]

    w_qkv, w_out, w_up, w_down = (gather_shards(w) for w in (w_qkv, w_out, w_up, w_down))
    given = (ln1_gain, ln1_bias, b_out, ln2_gain, ln2_bias, b_down, b_query, b_value, b_up)
    qkv_sent = qkv_blocks(spot, lengths, padding, w_qkv, [gather_shards(v) for v in given])
    qkv_near, qkv_half, extras = qkv_join(from_chips(qkv_sent))
    qkv_far = z_swap(qkv_half)
    qkv_near_other, extras_other = swap(qkv_near, 1), swap(extras, 1)
    tokens_sent, extras = fence(tokens, extras)
    blocks = [tokens] + [swap(tokens_sent, 2 * i) for i in range(1, CHIPS)]
    normed = token_norm(blocks)
    normed, qkv_far, extras_other = fence(normed, qkv_far, extras_other)
    qkv_far_other = swap(qkv_far, 1)
    out_sent, normed = fence(w_out, normed)
    out_other = swap(out_sent, 1)
    up_own, *up_sent = up_blocks(spot, w_up, cotangent)
    up_sent, normed = fence_list(up_sent, normed)
    loads = [swap(block, 2 * i + 2) for i, block in enumerate(up_sent)]

    (table, mask, qkv, out, first_low, projected, context), partial_out = enter(
        spot,
        normed,
        [qkv_near, qkv_far, extras],
        [qkv_near_other, qkv_far_other, extras_other],
        w_out,
        out_other,
    )
    loads, *partial_out = fence_list(loads, *partial_out)
    out_parts = from_chips(partial_out)
    up_near, up_half, whole_cotangent = up_join(up_own, cotangent, loads)
    up_far = z_swap(up_half)
    down_sent, up_half = fence(w_down, up_half)
    down_other = swap(down_sent, 1)
    out_parts, down_other = fence_list(out_parts, down_other)
    mixed, second_own = mix(out_parts, tokens, table)
    second_blocks = from_chips([second_own] * CHIPS)
    up_near, up_far, second_own = fence(up_near, up_far, second_own)
    up_near_other, up_far_other = swap(up_near, 1), swap(up_far, 1)
    whole_cotangent, second_own = fence(whole_cotangent, second_own)
    grad_act, down = act_grad(spot, whole_cotangent, w_down, down_other)

    second_blocks, grad_act = fence_list(second_blocks, grad_act)
    (second_low, act_low, grad_pre, down_sent, up_bias_sum), partial_second = hidden(
        spot,
        second_blocks,
        grad_act,
        whole_cotangent,
        table,
        [up_near, up_far],
        [up_near_other, up_far_other],
    )
    down_got = swap(down_sent, 1)
    second_parts = from_chips(partial_second)
    down_a, down_b = down_grad_of(spot, act_low, whole_cotangent, down_got)
    side0 = z_swap(down_a)

    second_low, down_a = fence(second_low, down_a)
    up_sent_a, up_sent_b, up_kept = up_grad_of(spot, second_low, grad_pre)
    up_a, up_b = split_add(up_kept, swap(up_sent_a, 1), swap(up_sent_b, 1))

    second_parts, side0, up_a = fence_list(second_parts, side0, up_a)
    z = z_step(spot, dict(got_side=side0, low=down_a, low_next=up_a), ("half", "send"))
    half0, send1 = z["half"], z["send"]
    side1, middle1 = z_swap(send1), z_middle(half0)
    second_parts, half0 = fence_list(second_parts, half0)
    grad_mixed, branch_own, mix_sums = unmix(second_parts, mixed, table, cotangent)
    branch_blocks = from_chips([branch_own] * CHIPS)
    act_low, branch_own = fence(act_low, branch_own)
    partial_result = result_of(act_low, down)

    branch_blocks, side1, middle1, *partial_result = fence_list(
        branch_blocks, side1, middle1, *partial_result
    )
    z = z_step(
        spot,
        dict(got_side=side1, got_middle=middle1, low=up_a, half_before=half0, low_next=up_b),
        ("half", "send"),
    )
    half1, send2 = z["half"], z["send"]
    side2, middle2 = z_swap(send2), z_middle(half1)
    branch_blocks, half1 = fence_list(branch_blocks, half1)
    (whole_branch, grad_projected, qkv_bias_sum), partial_first = leave(
        branch_blocks, qkv, out, projected, mask
    )
    first_low, grad_projected = fence(first_low, grad_projected)
    qkv_sent_a, qkv_sent_b, qkv_kept, out_sent, out_kept = qkv_grad_of(
        spot, first_low, grad_projected, context, whole_branch
    )
    qkv_a, qkv_b = pack(
        qkv_kept, swap(qkv_sent_a, 1), swap(qkv_sent_b, 1), out_kept, swap(out_sent, 1)
    )

    side2, middle2, qkv_a = fence(side2, middle2, qkv_a)
    z = z_step(
        spot,
        dict(got_side=side2, got_middle=middle2, low=up_b, half_before=half1, low_next=qkv_a),
        ("half", "send"),
    )
    half2, send3 = z["half"], z["send"]
    side3, middle3 = z_swap(send3), z_middle(half2)
    *partial_first, half2 = fence(*partial_first, half2)
    first_parts = from_chips(partial_first)
    down_a_final = z_step(spot, dict(got_side=side2, sent_before=send2), ("final",))["final"]

    first_parts, side3, middle3 = fence_list(first_parts, side3, middle3)
    z = z_step(
        spot,
        dict(
            got_side=side3,
            got_middle=middle3,
            low=qkv_a,
            half_before=half2,
            low_next=qkv_b,
            sent_before=send3,
        ),
        ("half", "send", "final"),
    )
    half3, send4, up_a_final = z["half"], z["send"], z["final"]
    side4, middle4 = z_swap(send4), z_middle(half3)
    *partial_result, half3 = fence(*partial_result, half3)
    result_parts = from_chips(partial_result)

    result_parts, side4, middle4 = fence_list(result_parts, side4, middle4)
    z = z_step(
        spot,
        dict(
            got_side=side4,
            got_middle=middle4,
            low=qkv_b,
            half_before=half3,
            low_next=down_b,
            sent_before=send4,
        ),
        ("half", "send", "final"),
    )
    half4, send5, up_b_final = z["half"], z["send"], z["final"]
    side5, middle5 = z_swap(send5), z_middle(half4)
    result_parts, half4 = fence_list(result_parts, half4)
    layer_out, grad_tokens, sums = end(
        spot,
        lengths,
        first_parts,
        result_parts,
        grad_mixed,
        tokens,
        table,
        mixed,
        mix_sums,
        qkv_bias_sum,
        up_bias_sum,
    )
    for mask_bit in (1, 2, 4):
        (sums,) = add_all([sums], [swap(sums, mask_bit)])
    if groups > 1:
        sums = lax.psum(sums, "fsdp", axis_index_groups=shard_groups)
    sums_got = z_swap(sums)

    side5, middle5, sums_got = fence(side5, middle5, sums_got)
    z = z_step(
        spot,
        dict(
            got_side=side5,
            got_middle=middle5,
            low=down_b,
            half_before=half4,
            sent_before=send5,
        ),
        ("half", "send", "final"),
    )
    half5, send6, qkv_a_final = z["half"], z["send"], z["final"]
    side6, middle6 = z_swap(send6), z_middle(half5)
    up_a_final, half5 = fence(up_a_final, half5)
    up_total = from_chips(up_exchange(spot, up_a_final, up_b_final))
    (sums,) = add_all([sums], [sums_got])

    up_total, side6, middle6, sums = fence_list(up_total, side6, middle6, sums)
    z = z_step(
        spot,
        dict(got_side=side6, got_middle=middle6, half_before=half5, sent_before=send6),
        ("send", "final"),
    )
    send7, qkv_b_final = z["send"], z["final"]
    side7 = along_z([(1, 0), (2, 3)], send7)
    qkv_a_final, send7, sums = fence(qkv_a_final, send7, sums)
    qkv_last, out_grad = qkv_exchange(spot, qkv_a_final, qkv_b_final)
    qkv_total = from_chips(qkv_last)
    sums_got = along_z([(z, z ^ 2) for z in range(4)], sums)
    up_grad = up_rows(spot, up_total)
    qkv_total, side7, up_grad = fence_list(qkv_total, side7, up_grad)
    down_grad, qkv_grad = last(spot, down_a_final, send7, side7, qkv_total)
    (sums,) = add_all([sums], [sums_got])

    index = lax.axis_index("fsdp")
    size = D // fsdp_count

    def owned(row):
        return lax.dynamic_slice(sums, (row, index * size), (1, size)).reshape(size)

    def owned_at(row, width, share):
        start = index * share
        return lax.dynamic_slice(sums, (row + start // width, start % width), (1, share)).reshape(
            share
        )

    moments = sums[6:8] / (CELLS_DEV * dp_count * fsdp_count)
    cls_mean = moments[0]
    cls_var = moments[1] - cls_mean * cls_mean

    return (
        layer_out,
        grad_tokens,
        owned(0),
        owned(1),
        scatter_shards(qkv_grad),
        owned_at(8, D_CHIP, size),
        owned_at(12, D_CHIP, size),
        scatter_shards(out_grad),
        owned(2),
        owned(3),
        owned(4),
        scatter_shards(up_grad),
        owned_at(16, FF_CHIP, FF // fsdp_count),
        scatter_shards(down_grad),
        owned(5),
        cls_mean,
        cls_var,
    )


def solution(mesh):
    tokens_spec = P(("dp", "fsdp"), None)
    vector = P("fsdp")
    matrix = P("fsdp", None)
    in_specs = (
        tokens_spec,
        P(("dp", "fsdp"), None),
        P(("dp", "fsdp")),
        vector,
        vector,
        matrix,
        vector,
        vector,
        matrix,
        vector,
        vector,
        vector,
        matrix,
        vector,
        matrix,
        vector,
        tokens_spec,
    )
    out_specs = (
        tokens_spec,
        tokens_spec,
        vector,
        vector,
        matrix,
        vector,
        vector,
        matrix,
        vector,
        vector,
        vector,
        matrix,
        vector,
        matrix,
        vector,
        P(),
        P(),
    )
    return jax.shard_map(local, mesh=mesh, in_specs=in_specs, out_specs=out_specs, check_vma=False)
```

time: 548 us -> 308 us (0.56); the launches traced: 539 us -> 307 us
  waiting for transfers between devices: 306 us -> 151 us
  Pallas kernels: 21.5 us -> 63.6 us
  local copies, waits for them, and re-layouts: 55.4 us -> 14.4 us
  other arithmetic: 41.5 us -> 0.69 us
  matrix products: 37.1 us -> 0 us
    ppermute x16 -> x18, waiting for transfers between devices: 170 us -> 11 us  [along_z(): return lax.ppermute(value, 'dp', pairs)]
    pallas_call x2 -> x35, Pallas kernels: 21.5 us -> 63.6 us  [the longest x1 9.77 us: hidden(): call(hidden_kernel, 'hidden', 'svvvvvvv' + 'v' * 4, [((total, D), bf16),...]
    dot_general x12 -> x0, matrix products: 37.1 us -> none  [dot(): return lax.dot_general(a, b, (dims, ((), ())), preferred_element_type=f32)]
    convert_element_type x8 -> x0, local copies, waits for them, and re-layouts: 20.9 us -> none  [the longest x3 10.4 us: local(): qkv_total = qkv_total.reshape(CHIPS, share, 3, D_CHIP).transpose(1, 2, 0,...]
    convert_element_type x18 -> x0, other arithmetic: 18.5 us -> none  [the longest x2 4.55 us: own_core(): return (kept + swap(sent.astype(bf16), 1).astype(f32)).astype(bf16)]
    ppermute x16 -> x18, starting transfers between devices: 20.4 us -> 33.1 us  [along_z(): return lax.ppermute(value, 'dp', pairs)]
    ppermute x54 -> x49, starting transfers between devices: 54.9 us -> 43.6 us  [swap(): return lax.ppermute(value, 'fsdp', pairs)]
    reshape x10 -> x0, local copies, waits for them, and re-layouts: 8.58 us -> none  [the longest x3 5.56 us: local(): w_qkv.reshape(share, 3, CHIPS, D_CHIP).transpose(2, 0, 1, 3)]
  transfers between devices with their start and end apart: 70 -> 67, of which waited for: 39 -> 36; matrix products, arithmetic and copies ran while one was open for 22% -> 1% of each run, Pallas kernels for 4% -> 12%
where the time goes in v2:
time: 308 us; the launch traced here: 307 us
  waiting for transfers between devices  151 us (49%)
  starting transfers between devices  76.6 us (25%)
  Pallas kernels  63.6 us (21%)
  local copies, waits for them, and re-layouts  14.4 us (5%)
    ppermute x49, waiting for transfers between devices, swap(): return lax.ppermute(value, 'fsdp', pairs)  140 us
    ppermute x49, starting transfers between devices, swap(): return lax.ppermute(value, 'fsdp', pairs)  43.6 us
    ppermute x18, starting transfers between devices, along_z(): return lax.ppermute(value, 'dp', pairs)  33.1 us
    unnamed x58, local copies, waits for them, and re-layouts  13 us
    ppermute x18, waiting for transfers between devices, along_z(): return lax.ppermute(value, 'dp', pairs)  11 us
    pallas_call x1, Pallas kernels, hidden(): call(hidden_kernel, 'hidden', 'svvvvvvv' + 'v' * 4, [((total, D), bf16),...  9.77 us
    pallas_call x8, Pallas kernels, z_step(): call(kernel, 'z_step', 's' + 'v' * len(inputs), [shape] * len(outputs))  7.41 us
    pallas_call x1, Pallas kernels, enter(): call(enter_kernel, 'enter', 'sv' + 'v' * 6 + 'aa', [((TABLE_ROWS, D), f32...  7.32 us
  transfers between devices with their start and end apart: 67, of which 36 were waited for; matrix products, arithmetic and copies ran while one was open for 1% of the time, Pallas kernels for 12%

profile of v2, /device:TPU:0, one launch (start us, length us, event | category | flops | bytes accessed | tf_op | source)
XLA Modules:
  0.0 307.2 jit_solution(6448305809884443552)
XLA Ops:
  15.6 4.2 %collective-permute-done.q1 = bf16[96,960]{1,0:T(8,128)(2,1)S(1)} collective-permute-done((bf16[96,960]{1,0:T(8,128)(2,1)S(1)}, bf16[96,960]{1,0:T(8,128)(2,1)S(1)}, u32[]{:S(2)}, u32[]{:S(2)}) %collective-permute-start) | collective-permute-done | bytes 184352 | tf_op jit(solution)/shard_map/ppermute | solution.py:934
  19.8 4.8 %collective-permute-done.1.q2 = bf16[96,960]{1,0:T(8,128)(2,1)S(1)} collective-permute-done((bf16[96,960]{1,0:T(8,128)(2,1)S(1)}, bf16[96,960]{1,0:T(8,128)(2,1)S(1)}, u32[]{:S(2)}, u32[]{:S(2)}) %collective-permute-start.1) | collective-permute-done | bytes 184352 | tf_op jit(solution)/shard_map/ppermute | solution.py:934
  29.9 7.1 %collective-permute-done.3.x1 = bf16[128,1280]{1,0:T(8,128)(2,1)S(1)} collective-permute-done((bf16[128,1280]{1,0:T(8,128)(2,1)S(1)}, bf16[128,1280]{1,0:T(8,128)(2,1)S(1)}, u32[]{:S(2)}, u32[]{:S(2)}) %collective-permute-start.3) | collective-permute-done | bytes 327712 | tf_op jit(solution)/shard_map/ppermute | solution.py:934
  51.0 7.3 %enter.1 = (f32[8,1280]{1,0:T(8,128)S(1)}, bf16[512,128]{1,0:T(8,128)(2,1)S(1)}, bf16[1280,960]{1,0:T(8,128)(2,1)S(1)}, bf16[320,1280]{1,0:T(8,128)(2,1)S(1)}, b...) custom-call(s32[4]{0:T(128)S(1)} %pad_add_fusion.spot.refs_0_, ...), custom_call_target="tpu_custom_call" | custom-call | flops 1 | bytes 1 | tf_op jit(solution)/shard_map/enter/pallas_call | solution.py:396
  61.0 8.8 %collective-permute-done.8.u1 = bf16[208,1280]{1,0:T(8,128)(2,1)S(1)} collective-permute-done((bf16[208,1280]{1,0:T(8,128)(2,1)S(1)}, bf16[208,1280]{1,0:T(8,128)(2,1)S(1)}, u32[]{:S(2)}, u32[]{:S(2)}) %collective-permute-start.8) | collective-permute-done | bytes 532512 | tf_op jit(solution)/shard_map/ppermute | solution.py:934
  75.0 7.1 %collective-permute-done.14.p1 = bf16[128,1280]{1,0:T(8,128)(2,1)S(1)} collective-permute-done((bf16[128,1280]{1,0:T(8,128)(2,1)S(1)}, bf16[128,1280]{1,0:T(8,128)(2,1)S(1)}, u32[]{:S(2)}, u32[]{:S(2)}) %collective-permute-start.14) | collective-permute-done | bytes 327712 | tf_op jit(solution)/shard_map/ppermute | solution.py:934
  82.1 6.6 %collective-permute-done.15.p2 = bf16[128,1280]{1,0:T(8,128)(2,1)S(1)} collective-permute-done((bf16[128,1280]{1,0:T(8,128)(2,1)S(1)}, bf16[128,1280]{1,0:T(8,128)(2,1)S(1)}, u32[]{:S(2)}, u32[]{:S(2)}) %collective-permute-start.15) | collective-permute-done | bytes 327712 | tf_op jit(solution)/shard_map/ppermute | solution.py:934
  93.1 3.7 %act_grad.1 = (f32[512,1280]{1,0:T(8,128)S(1)}, bf16[1280,1280]{1,0:T(8,128)(2,1)S(1)}) custom-call(s32[4]{0:T(128)S(1)} %pad_add_fusion.spot.refs_0_, bf16[512,1280]{1,0:T(8,128)(2,1)S(1)} %get-tuple-element.268.whole.cotangent, bf16[640,1280]{1,0:T(8,128)(2,1)S(1)} %copy-done.3, bf16[640,1280]{1,0:T(8,128)(2,1)S(1)} %collective-permute-done.17.other), custom_call_target="tpu_custom_call" | custom-call | flops 1 | bytes 1 | tf_op jit(solution)/shard_map/act_grad/pallas_call | solution.py:508
  100.2 7.3 %collective-permute-done.19.s2 = bf16[128,1280]{1,0:T(8,128)(2,1)S(1)} collective-permute-done((bf16[128,1280]{1,0:T(8,128)(2,1)S(1)}, bf16[128,1280]{1,0:T(8,128)(2,1)S(1)}, u32[]{:S(2)}, u32[]{:S(2)}) %collective-permute-start.19) | collective-permute-done | bytes 327712 | tf_op jit(solution)/shard_map/ppermute | solution.py:934
  107.5 9.8 %hidden.1 = (bf16[512,1280]{1,0:T(8,128)(2,1)S(1)}, bf16[512,1280]{1,0:T(8,128)(2,1)S(1)}, bf16[512,1280]{1,0:T(8,128)(2,1)S(1)}, bf16[640,1280]{1,0:T(8,128)(2,...) custom-call(s32[4]{0:T(128)S(1)} %pad_add_fusion.spot.refs_0_, ...), custom_call_target="tpu_custom_call" | custom-call | flops 1 | bytes 1 | tf_op jit(solution)/shard_map/hidden/pallas_call | solution.py:560
  117.4 3.5 %collective-permute-done.27.got = bf16[640,1280]{1,0:T(8,128)(2,1)S(1)} collective-permute-done((bf16[640,1280]{1,0:T(8,128)(2,1)S(1)}, bf16[640,1280]{1,0:T(8,128)(2,1)S(1)}, u32[]{:S(2)}, u32[]{:S(2)}) %collective-permute-start.27) | collective-permute-done | bytes 1638432 | tf_op jit(solution)/shard_map/ppermute | solution.py:934
  122.5 3.6 %up_grad.1 = (bf16[2,160,1280]{2,1,0:T(8,128)(2,1)S(1)}, bf16[2,160,1280]{2,1,0:T(8,128)(2,1)S(1)}, bf16[4,160,1280]{2,1,0:T(8,128)(2,1)S(1)}) custom-call(s32[4]{0:T(128)S(1)} %pad_add_fusion.spot.refs_0_, bf16[512,1280]{1,0:T(8,128)(2,1)S(1)} %get-tuple-element.287.second, bf16[512,1280]{1,0:T(8,128)(2,1)S(1)} %get-tuple-element.288.grad_pre), custom_call_target="tpu_custom_call" | custom-call | flops 1 | bytes 1 | tf_op jit(solution)/shard_map/up_grad/pallas_call | solution.py:610
  132.2 6.7 %collective-permute-done.24.p1 = bf16[128,1280]{1,0:T(8,128)(2,1)S(1)} collective-permute-done((bf16[128,1280]{1,0:T(8,128)(2,1)S(1)}, bf16[128,1280]{1,0:T(8,128)(2,1)S(1)}, u32[]{:S(2)}, u32[]{:S(2)}) %collective-permute-start.24) | collective-permute-done | bytes 327712 | tf_op jit(solution)/shard_map/ppermute | solution.py:934
  138.9 6.2 %collective-permute-done.25.p2 = bf16[128,1280]{1,0:T(8,128)(2,1)S(1)} collective-permute-done((bf16[128,1280]{1,0:T(8,128)(2,1)S(1)}, bf16[128,1280]{1,0:T(8,128)(2,1)S(1)}, u32[]{:S(2)}, u32[]{:S(2)}) %collective-permute-start.25) | collective-permute-done | bytes 327712 | tf_op jit(solution)/shard_map/ppermute | solution.py:934
  157.2 4.6 %collective-permute-done.31.b1 = bf16[128,1280]{1,0:T(8,128)(2,1)S(1)} collective-permute-done((bf16[128,1280]{1,0:T(8,128)(2,1)S(1)}, bf16[128,1280]{1,0:T(8,128)(2,1)S(1)}, u32[]{:S(2)}, u32[]{:S(2)}) %collective-permute-start.31) | collective-permute-done | bytes 327712 | tf_op jit(solution)/shard_map/ppermute | solution.py:934
  161.8 5.3 %collective-permute-done.32.b2 = bf16[128,1280]{1,0:T(8,128)(2,1)S(1)} collective-permute-done((bf16[128,1280]{1,0:T(8,128)(2,1)S(1)}, bf16[128,1280]{1,0:T(8,128)(2,1)S(1)}, u32[]{:S(2)}, u32[]{:S(2)}) %collective-permute-start.32) | collective-permute-done | bytes 327712 | tf_op jit(solution)/shard_map/ppermute | solution.py:934
  168.3 4.8 %collective-permute-start.36 = (bf16[320,1280]{1,0:T(8,128)(2,1)S(1)}, bf16[320,1280]{1,0:T(8,128)(2,1)S(1)}, u32[]{:S(2)}, u32[]{:S(2)}) collective-permute-start(bf16[320,1280]{1,0:T(8,128)(2,1)S(1)} %get-tuple-element.335.refs_2_), channel_id=1, source_target_pairs={{0,8},{8,0},{16,24},{24,16},{1,9},{9,1},{17,25},{25,17},{2,10},{10... | collective-permute-start | bytes 2457608 | tf_op jit(solution)/shard_map/ppermute | solution.py:950
  173.9 6.8 %leave.1 = (bf16[512,1280]{1,0:T(8,128)(2,1)S(1)}, bf16[512,960]{1,0:T(8,128)(2,1)S(1)}, f32[1,960]{1,0:T(1,128)S(1)}, bf16[128,1280]{1,0:T(8,128)(2,1)S(1)}, bf...) custom-call(bf16[128,1280]{1,0:T(8,128)(2,1)S(1)} %get-tuple-element.323.b0, ...), custom_call_target="tpu_custom_call" | custom-call | flops 1 | bytes 1 | tf_op jit(solution)/shard_map/leave/pallas_call | solution.py:442
  180.7 3.8 %qkv_grad.1 = (bf16[2,160,960]{2,1,0:T(8,128)(2,1)S(1)}, bf16[2,160,960]{2,1,0:T(8,128)(2,1)S(1)}, bf16[4,160,960]{2,1,0:T(8,128)(2,1)S(1)}, bf16[160,1280]{1,0:T(8,128)(2,1)S(1)}, bf16[160,1280]{1,0:T(8,128)(2,1)S(1)}) custom-call(s32[4]{0:T(128)S(1)} %pad_add_fusion.spot.refs_0_, bf16[512,1280]{1,0:T(8,128)(2,1)S(1)} %get-tuple-element.338.first_low, ...), custom_call_target="tpu_custom_call" | custom-call | flops 1 | bytes 1 | tf_op jit(solution)/shard_map/qkv_grad/pallas_call | solution.py:664
  191.0 3.7 %collective-permute-start.44 = (bf16[320,1280]{1,0:T(8,128)(2,1)S(1)}, bf16[320,1280]{1,0:T(8,128)(2,1)S(1)}, u32[]{:S(2)}, u32[]{:S(2)}) collective-permute-start(bf16[320,1280]{1,0:T(8,128)(2,1)S(1)} %get-tuple-element.357.refs_6_), channel_id=1, source_target_pairs={{0,8},{8,0},{16,24},{24,16},{1,9},{9,1},{17,25},{25,17},{2,10},{10... | collective-permute-start | bytes 2457608 | tf_op jit(solution)/shard_map/ppermute | solution.py:950
  198.9 7.2 %collective-permute-done.41.p1 = bf16[128,1280]{1,0:T(8,128)(2,1)S(1)} collective-permute-done((bf16[128,1280]{1,0:T(8,128)(2,1)S(1)}, bf16[128,1280]{1,0:T(8,128)(2,1)S(1)}, u32[]{:S(2)}, u32[]{:S(2)}) %collective-permute-start.41) | collective-permute-done | bytes 327712 | tf_op jit(solution)/shard_map/ppermute | solution.py:934
  206.1 4.2 %collective-permute-done.42.p2 = bf16[128,1280]{1,0:T(8,128)(2,1)S(1)} collective-permute-done((bf16[128,1280]{1,0:T(8,128)(2,1)S(1)}, bf16[128,1280]{1,0:T(8,128)(2,1)S(1)}, u32[]{:S(2)}, u32[]{:S(2)}) %collective-permute-start.42) | collective-permute-done | bytes 327712 | tf_op jit(solution)/shard_map/ppermute | solution.py:934
  212.3 3.7 %collective-permute-start.49 = (bf16[320,1280]{1,0:T(8,128)(2,1)S(1)}, bf16[320,1280]{1,0:T(8,128)(2,1)S(1)}, u32[]{:S(2)}, u32[]{:S(2)}) collective-permute-start(bf16[320,1280]{1,0:T(8,128)(2,1)S(1)} %get-tuple-element.375.refs_6_), channel_id=1, source_target_pairs={{0,8},{8,0},{16,24},{24,16},{1,9},{9,1},{17,25},{25,17},{2,10},{10... | collective-permute-start | bytes 2457608 | tf_op jit(solution)/shard_map/ppermute | solution.py:950
  220.3 6.6 %collective-permute-done.46.r1 = bf16[128,1280]{1,0:T(8,128)(2,1)S(1)} collective-permute-done((bf16[128,1280]{1,0:T(8,128)(2,1)S(1)}, bf16[128,1280]{1,0:T(8,128)(2,1)S(1)}, u32[]{:S(2)}, u32[]{:S(2)}) %collective-permute-start.46) | collective-permute-done | bytes 327712 | tf_op jit(solution)/shard_map/ppermute | solution.py:934
  226.9 3.8 %collective-permute-done.47.r2 = bf16[128,1280]{1,0:T(8,128)(2,1)S(1)} collective-permute-done((bf16[128,1280]{1,0:T(8,128)(2,1)S(1)}, bf16[128,1280]{1,0:T(8,128)(2,1)S(1)}, u32[]{:S(2)}, u32[]{:S(2)}) %collective-permute-start.47) | collective-permute-done | bytes 327712 | tf_op jit(solution)/shard_map/ppermute | solution.py:934
  232.8 3.7 %collective-permute-start.51 = (bf16[320,1280]{1,0:T(8,128)(2,1)S(1)}, bf16[320,1280]{1,0:T(8,128)(2,1)S(1)}, u32[]{:S(2)}, u32[]{:S(2)}) collective-permute-start(bf16[320,1280]{1,0:T(8,128)(2,1)S(1)} %get-tuple-element.395.refs_5_), channel_id=1, source_target_pairs={{0,8},{8,0},{16,24},{24,16},{1,9},{9,1},{17,25},{25,17},{2,10},{10... | collective-permute-start | bytes 2457608 | tf_op jit(solution)/shard_map/ppermute | solution.py:950
  241.9 4.8 %collective-permute-done.54.refs_1_ = f32[24,1280]{1,0:T(8,128)S(1)} collective-permute-done((f32[24,1280]{1,0:T(8,128)S(1)}, f32[24,1280]{1,0:T(8,128)S(1)}, u32[]{:S(2)}, u32[]{:S(2)}) %collective-permute-start.54) | collective-permute-done | bytes 122912 | tf_op jit(solution)/shard_map/ppermute | solution.py:934
  247.4 4.3 %collective-permute-done.55.refs_1_ = f32[24,1280]{1,0:T(8,128)S(1)} collective-permute-done((f32[24,1280]{1,0:T(8,128)S(1)}, f32[24,1280]{1,0:T(8,128)S(1)}, u32[]{:S(2)}, u32[]{:S(2)}) %collective-permute-start.55) | collective-permute-done | bytes 122912 | tf_op jit(solution)/shard_map/ppermute | solution.py:934
  264.3 8.9 %collective-permute-done.57.b1 = bf16[160,1280]{1,0:T(8,128)(2,1)S(1)} collective-permute-done((bf16[160,1280]{1,0:T(8,128)(2,1)S(1)}, bf16[160,1280]{1,0:T(8,128)(2,1)S(1)}, u32[]{:S(2)}, u32[]{:S(2)}) %collective-permute-start.57) | collective-permute-done | bytes 409632 | tf_op jit(solution)/shard_map/ppermute | solution.py:934
  273.2 5.1 %collective-permute-done.58.b2 = bf16[160,1280]{1,0:T(8,128)(2,1)S(1)} collective-permute-done((bf16[160,1280]{1,0:T(8,128)(2,1)S(1)}, bf16[160,1280]{1,0:T(8,128)(2,1)S(1)}, u32[]{:S(2)}, u32[]{:S(2)}) %collective-permute-start.58) | collective-permute-done | bytes 409632 | tf_op jit(solution)/shard_map/ppermute | solution.py:934
  296.6 4.4 %collective-permute-done.64.b2 = bf16[160,960]{1,0:T(8,128)(2,1)S(1)} collective-permute-done((bf16[160,960]{1,0:T(8,128)(2,1)S(1)}, bf16[160,960]{1,0:T(8,128)(2,1)S(1)}, u32[]{:S(2)}, u32[]{:S(2)}) %collective-permute-start.64) | collective-permute-done | bytes 307232 | tf_op jit(solution)/shard_map/ppermute | solution.py:934
  303.5 3.7 %last.1 = (f32[640,1280]{1,0:T(8,128)}, f32[160,3840]{1,0:T(8,128)}) custom-call(s32[4]{0:T(128)S(1)} %pad_add_fusion.spot.refs_0_, bf16[320,1280]{1,0:T(8,128)(2,1)S(1)} %z_step.15.down_a, bf16[320,1280]{1,0:T(8,128)(2,1)S(1)} %copy-done.6, bf16[320,1280]{1,0:T(8,128)(2,1)S(1)} %collective-permute-done.66.got, bf16[160,960]{1,0:T(8,128)(2,1)S(1)} %get-tuple-element.429.b0, ...), custom_call_target="tpu_custom_call" | custom-call | flops 1 | bytes 1 | tf_op jit(solution)/shard_map/last/pallas_call | solution.py:776
  (201 shorter events, 129.9 us)
Async XLA Ops:
  24.7 23.9 %collective-permute-start.11 = (bf16[400,960]{1,0:T(8,128)(2,1)S(1)}, bf16[400,960]{1,0:T(8,128)(2,1)S(1)}, u32[]{:S(2)}, u32[]{:S(2)}) collective-permute-start(bf16[400,960]{1,0:T(8,128)(2,1)S(1)} %get-tuple-element.243.refs_0_), channel_id=1, source_target_pairs={{0,1},{1,0},{2,3},{3,2},{4,5},{5,4},{6,7},{7,6},{8,9},{9,8},{10,11... | collective-permute-start | bytes 2304008 | tf_op jit(solution)/shard_map/ppermute | solution.py:934
  24.8 20.2 %collective-permute-start.6 = (bf16[240,960]{1,0:T(8,128)(2,1)S(1)}, bf16[240,960]{1,0:T(8,128)(2,1)S(1)}, u32[]{:S(2)}, u32[]{:S(2)}) collective-permute-start(bf16[240,960]{1,0:T(8,128)(2,1)S(1)} %get-tuple-element.236), channel_id=1, source_target_pairs={{0,8},{8,0},{16,24},{24,16},{1,9},{9,1},{17,25},{25,17},{2,10},{10... | collective-permute-start | bytes 1382408 | tf_op jit(solution)/shard_map/ppermute | solution.py:950
  28.5 15.7 %collective-permute-start.5 = (bf16[128,1280]{1,0:T(8,128)(2,1)S(1)}, bf16[128,1280]{1,0:T(8,128)(2,1)S(1)}, u32[]{:S(2)}, u32[]{:S(2)}) collective-permute-start(bf16[128,1280]{1,0:T(8,128)(2,1)S(1)} %copy-done.1), channel_id=1, source_target_pairs={{0,6},{1,7},{2,4},{3,5},{4,2},{5,3},{6,0},{7,1},{8,14},{9,15},{10,... | collective-permute-start | bytes 983048 | tf_op jit(solution)/shard_map/ppermute | solution.py:934
  45.0 16.0 %collective-permute-start.10 = (bf16[208,1280]{1,0:T(8,128)(2,1)S(1)}, bf16[208,1280]{1,0:T(8,128)(2,1)S(1)}, u32[]{:S(2)}, u32[]{:S(2)}) collective-permute-start(bf16[208,1280]{1,0:T(8,128)(2,1)S(1)} %get-tuple-element.241), channel_id=1, source_target_pairs={{0,6},{1,7},{2,4},{3,5},{4,2},{5,3},{6,0},{7,1},{8,14},{9,15},{10,... | collective-permute-start | bytes 1597448 | tf_op jit(solution)/shard_map/ppermute | solution.py:934
  46.8 23.0 %collective-permute-start.8 = (bf16[208,1280]{1,0:T(8,128)(2,1)S(1)}, bf16[208,1280]{1,0:T(8,128)(2,1)S(1)}, u32[]{:S(2)}, u32[]{:S(2)}) collective-permute-start(bf16[208,1280]{1,0:T(8,128)(2,1)S(1)} %get-tuple-element.239), channel_id=1, source_target_pairs={{0,2},{1,3},{2,0},{3,1},{4,6},{5,7},{6,4},{7,5},{8,10},{9,11},{10,... | collective-permute-start | bytes 1597448 | tf_op jit(solution)/shard_map/ppermute | solution.py:934
  47.4 23.4 %collective-permute-start.9 = (bf16[208,1280]{1,0:T(8,128)(2,1)S(1)}, bf16[208,1280]{1,0:T(8,128)(2,1)S(1)}, u32[]{:S(2)}, u32[]{:S(2)}) collective-permute-start(bf16[208,1280]{1,0:T(8,128)(2,1)S(1)} %get-tuple-element.240), channel_id=1, source_target_pairs={{0,4},{1,5},{2,6},{3,7},{4,0},{5,1},{6,2},{7,3},{8,12},{9,13},{10,... | collective-permute-start | bytes 1597448 | tf_op jit(solution)/shard_map/ppermute | solution.py:934
  70.9 17.7 %collective-permute-start.17 = (bf16[640,1280]{1,0:T(8,128)(2,1)S(1)}, bf16[640,1280]{1,0:T(8,128)(2,1)S(1)}, u32[]{:S(2)}, u32[]{:S(2)}) collective-permute-start(bf16[640,1280]{1,0:T(8,128)(2,1)S(1)} %copy-done.3), channel_id=1, source_target_pairs={{0,1},{1,0},{2,3},{3,2},{4,5},{5,4},{6,7},{7,6},{8,9},{9,8},{10,11... | collective-permute-start | bytes 4915208 | tf_op jit(solution)/shard_map/ppermute | solution.py:934
  71.0 18.1 %collective-permute-start.21 = (bf16[240,1280]{1,0:T(8,128)(2,1)S(1)}, bf16[240,1280]{1,0:T(8,128)(2,1)S(1)}, u32[]{:S(2)}, u32[]{:S(2)}) collective-permute-start(bf16[240,1280]{1,0:T(8,128)(2,1)S(1)} %get-tuple-element.260), channel_id=1, source_target_pairs={{0,8},{8,0},{16,24},{24,16},{1,9},{9,1},{17,25},{25,17},{2,10},{10... | collective-permute-start | bytes 1843208 | tf_op jit(solution)/shard_map/ppermute | solution.py:950
  72.1 16.5 %collective-permute-start.15 = (bf16[128,1280]{1,0:T(8,128)(2,1)S(1)}, bf16[128,1280]{1,0:T(8,128)(2,1)S(1)}, u32[]{:S(2)}, u32[]{:S(2)}) collective-permute-start(bf16[128,1280]{1,0:T(8,128)(2,1)S(1)} %get-tuple-element.254), channel_id=1, source_target_pairs={{0,4},{1,5},{2,6},{3,7},{4,0},{5,1},{6,2},{7,3},{8,12},{9,13},{10,... | collective-permute-start | bytes 983048 | tf_op jit(solution)/shard_map/ppermute | solution.py:934
  73.3 15.3 %collective-permute-start.16 = (bf16[128,1280]{1,0:T(8,128)(2,1)S(1)}, bf16[128,1280]{1,0:T(8,128)(2,1)S(1)}, u32[]{:S(2)}, u32[]{:S(2)}) collective-permute-start(bf16[128,1280]{1,0:T(8,128)(2,1)S(1)} %get-tuple-element.255), channel_id=1, source_target_pairs={{0,6},{1,7},{2,4},{3,5},{4,2},{5,3},{6,0},{7,1},{8,14},{9,15},{10,... | collective-permute-start | bytes 983048 | tf_op jit(solution)/shard_map/ppermute | solution.py:934
  89.1 18.5 %collective-permute-start.22 = (bf16[400,1280]{1,0:T(8,128)(2,1)S(1)}, bf16[400,1280]{1,0:T(8,128)(2,1)S(1)}, u32[]{:S(2)}, u32[]{:S(2)}) collective-permute-start(bf16[400,1280]{1,0:T(8,128)(2,1)S(1)} %get-tuple-element.277.refs_0_), channel_id=1, source_target_pairs={{0,1},{1,0},{2,3},{3,2},{4,5},{5,4},{6,7},{7,6},{8,9},{9,8},{10,11... | collective-permute-start | bytes 3072008 | tf_op jit(solution)/shard_map/ppermute | solution.py:934
  89.2 18.4 %collective-permute-start.23 = (bf16[240,1280]{1,0:T(8,128)(2,1)S(1)}, bf16[240,1280]{1,0:T(8,128)(2,1)S(1)}, u32[]{:S(2)}, u32[]{:S(2)}) collective-permute-start(bf16[240,1280]{1,0:T(8,128)(2,1)S(1)} %collective-permute-done.21.refs_1_), channel_id=1, source_target_pairs={{0,1},{1,0},{2,3},{3,2},{4,5},{5,4},{6,7},{7,6},{8,9},{9,8},{10,11... | collective-permute-start | bytes 1843208 | tf_op jit(solution)/shard_map/ppermute | solution.py:934
  91.1 16.4 %collective-permute-start.19 = (bf16[128,1280]{1,0:T(8,128)(2,1)S(1)}, bf16[128,1280]{1,0:T(8,128)(2,1)S(1)}, u32[]{:S(2)}, u32[]{:S(2)}) collective-permute-start(bf16[128,1280]{1,0:T(8,128)(2,1)S(1)} %get-tuple-element.271.s0), channel_id=1, source_target_pairs={{0,4},{1,5},{2,6},{3,7},{4,0},{5,1},{6,2},{7,3},{8,12},{9,13},{10,... | collective-permute-start | bytes 983048 | tf_op jit(solution)/shard_map/ppermute | solution.py:934
  91.7 15.8 %collective-permute-start.20 = (bf16[128,1280]{1,0:T(8,128)(2,1)S(1)}, bf16[128,1280]{1,0:T(8,128)(2,1)S(1)}, u32[]{:S(2)}, u32[]{:S(2)}) collective-permute-start(bf16[128,1280]{1,0:T(8,128)(2,1)S(1)} %get-tuple-element.271.s0), channel_id=1, source_target_pairs={{0,6},{1,7},{2,4},{3,5},{4,2},{5,3},{6,0},{7,1},{8,14},{9,15},{10,... | collective-permute-start | bytes 983048 | tf_op jit(solution)/shard_map/ppermute | solution.py:934
  126.7 20.3 %collective-permute-start.28 = (bf16[320,1280]{1,0:T(8,128)(2,1)S(1)}, bf16[320,1280]{1,0:T(8,128)(2,1)S(1)}, u32[]{:S(2)}, u32[]{:S(2)}) collective-permute-start(bf16[320,1280]{1,0:T(8,128)(2,1)S(1)} %get-tuple-element.298.refs_2_), channel_id=1, source_target_pairs={{0,8},{8,0},{16,24},{24,16},{1,9},{9,1},{17,25},{25,17},{2,10},{10... | collective-permute-start | bytes 2457608 | tf_op jit(solution)/shard_map/ppermute | solution.py:950
  128.9 16.2 %collective-permute-start.25 = (bf16[128,1280]{1,0:T(8,128)(2,1)S(1)}, bf16[128,1280]{1,0:T(8,128)(2,1)S(1)}, u32[]{:S(2)}, u32[]{:S(2)}) collective-permute-start(bf16[128,1280]{1,0:T(8,128)(2,1)S(1)} %get-tuple-element.281), channel_id=1, source_target_pairs={{0,4},{1,5},{2,6},{3,7},{4,0},{5,1},{6,2},{7,3},{8,12},{9,13},{10,... | collective-permute-start | bytes 983048 | tf_op jit(solution)/shard_map/ppermute | solution.py:934
  147.8 19.5 %collective-permute-start.34 = (bf16[320,1280]{1,0:T(8,128)(2,1)S(1)}, bf16[320,1280]{1,0:T(8,128)(2,1)S(1)}, u32[]{:S(2)}, u32[]{:S(2)}) collective-permute-start(bf16[320,1280]{1,0:T(8,128)(2,1)S(1)} %get-tuple-element.307), channel_id=1, source_target_pairs={{0,8},{8,0},{16,24},{24,16},{1,9},{9,1},{17,25},{25,17},{2,10},{10... | collective-permute-start | bytes 2457608 | tf_op jit(solution)/shard_map/ppermute | solution.py:950
  149.4 17.9 %collective-permute-start.35 = (bf16[320,1280]{1,0:T(8,128)(2,1)S(1)}, bf16[320,1280]{1,0:T(8,128)(2,1)S(1)}, u32[]{:S(2)}, u32[]{:S(2)}) collective-permute-start(bf16[320,1280]{1,0:T(8,128)(2,1)S(1)} %get-tuple-element.320.refs_4_), channel_id=1, source_target_pairs={{8,16},{16,8},{9,17},{17,9},{10,18},{18,10},{11,19},{19,11},{12,20... | collective-permute-start | bytes 2457608 | tf_op jit(solution)/shard_map/ppermute | solution.py:950
  151.8 15.4 %collective-permute-start.32 = (bf16[128,1280]{1,0:T(8,128)(2,1)S(1)}, bf16[128,1280]{1,0:T(8,128)(2,1)S(1)}, u32[]{:S(2)}, u32[]{:S(2)}) collective-permute-start(bf16[128,1280]{1,0:T(8,128)(2,1)S(1)} %get-tuple-element.323.b0), channel_id=1, source_target_pairs={{0,4},{1,5},{2,6},{3,7},{4,0},{5,1},{6,2},{7,3},{8,12},{9,13},{10,... | collective-permute-start | bytes 983048 | tf_op jit(solution)/shard_map/ppermute | solution.py:934
  168.3 21.6 %collective-permute-start.36 = (bf16[320,1280]{1,0:T(8,128)(2,1)S(1)}, bf16[320,1280]{1,0:T(8,128)(2,1)S(1)}, u32[]{:S(2)}, u32[]{:S(2)}) collective-permute-start(bf16[320,1280]{1,0:T(8,128)(2,1)S(1)} %get-tuple-element.335.refs_2_), channel_id=1, source_target_pairs={{0,8},{8,0},{16,24},{24,16},{1,9},{9,1},{17,25},{25,17},{2,10},{10... | collective-permute-start | bytes 2457608 | tf_op jit(solution)/shard_map/ppermute | solution.py:950
  173.1 16.8 %collective-permute-start.37 = (bf16[320,1280]{1,0:T(8,128)(2,1)S(1)}, bf16[320,1280]{1,0:T(8,128)(2,1)S(1)}, u32[]{:S(2)}, u32[]{:S(2)}) collective-permute-start(bf16[320,1280]{1,0:T(8,128)(2,1)S(1)} %get-tuple-element.350.refs_4_), channel_id=1, source_target_pairs={{8,16},{16,8},{9,17},{17,9},{10,18},{18,10},{11,19},{19,11},{12,20... | collective-permute-start | bytes 2457608 | tf_op jit(solution)/shard_map/ppermute | solution.py:950
  191.0 20.3 %collective-permute-start.44 = (bf16[320,1280]{1,0:T(8,128)(2,1)S(1)}, bf16[320,1280]{1,0:T(8,128)(2,1)S(1)}, u32[]{:S(2)}, u32[]{:S(2)}) collective-permute-start(bf16[320,1280]{1,0:T(8,128)(2,1)S(1)} %get-tuple-element.357.refs_6_), channel_id=1, source_target_pairs={{0,8},{8,0},{16,24},{24,16},{1,9},{9,1},{17,25},{25,17},{2,10},{10... | collective-permute-start | bytes 2457608 | tf_op jit(solution)/shard_map/ppermute | solution.py:950
  194.7 16.6 %collective-permute-start.45 = (bf16[320,1280]{1,0:T(8,128)(2,1)S(1)}, bf16[320,1280]{1,0:T(8,128)(2,1)S(1)}, u32[]{:S(2)}, u32[]{:S(2)}) collective-permute-start(bf16[320,1280]{1,0:T(8,128)(2,1)S(1)} %get-tuple-element.368.refs_4_), channel_id=1, source_target_pairs={{8,16},{16,8},{9,17},{17,9},{10,18},{18,10},{11,19},{19,11},{12,20... | collective-permute-start | bytes 2457608 | tf_op jit(solution)/shard_map/ppermute | solution.py:950
  212.3 19.4 %collective-permute-start.49 = (bf16[320,1280]{1,0:T(8,128)(2,1)S(1)}, bf16[320,1280]{1,0:T(8,128)(2,1)S(1)}, u32[]{:S(2)}, u32[]{:S(2)}) collective-permute-start(bf16[320,1280]{1,0:T(8,128)(2,1)S(1)} %get-tuple-element.375.refs_6_), channel_id=1, source_target_pairs={{0,8},{8,0},{16,24},{24,16},{1,9},{9,1},{17,25},{25,17},{2,10},{10... | collective-permute-start | bytes 2457608 | tf_op jit(solution)/shard_map/ppermute | solution.py:950
  216.0 15.7 %collective-permute-start.50 = (bf16[320,1280]{1,0:T(8,128)(2,1)S(1)}, bf16[320,1280]{1,0:T(8,128)(2,1)S(1)}, u32[]{:S(2)}, u32[]{:S(2)}) collective-permute-start(bf16[320,1280]{1,0:T(8,128)(2,1)S(1)} %get-tuple-element.382.refs_4_), channel_id=1, source_target_pairs={{8,16},{16,8},{9,17},{17,9},{10,18},{18,10},{11,19},{19,11},{12,20... | collective-permute-start | bytes 2457608 | tf_op jit(solution)/shard_map/ppermute | solution.py:950
  232.8 23.8 %collective-permute-start.51 = (bf16[320,1280]{1,0:T(8,128)(2,1)S(1)}, bf16[320,1280]{1,0:T(8,128)(2,1)S(1)}, u32[]{:S(2)}, u32[]{:S(2)}) collective-permute-start(bf16[320,1280]{1,0:T(8,128)(2,1)S(1)} %get-tuple-element.395.refs_5_), channel_id=1, source_target_pairs={{0,8},{8,0},{16,24},{24,16},{1,9},{9,1},{17,25},{25,17},{2,10},{10... | collective-permute-start | bytes 2457608 | tf_op jit(solution)/shard_map/ppermute | solution.py:950
  236.5 20.1 %collective-permute-start.52 = (bf16[320,1280]{1,0:T(8,128)(2,1)S(1)}, bf16[320,1280]{1,0:T(8,128)(2,1)S(1)}, u32[]{:S(2)}, u32[]{:S(2)}) collective-permute-start(bf16[320,1280]{1,0:T(8,128)(2,1)S(1)} %get-tuple-element.399.refs_4_), channel_id=1, source_target_pairs={{8,16},{16,8},{9,17},{17,9},{10,18},{18,10},{11,19},{19,11},{12,20... | collective-permute-start | bytes 2457608 | tf_op jit(solution)/shard_map/ppermute | solution.py:950
  257.7 22.1 %collective-permute-start.60 = (bf16[320,1280]{1,0:T(8,128)(2,1)S(1)}, bf16[320,1280]{1,0:T(8,128)(2,1)S(1)}, u32[]{:S(2)}, u32[]{:S(2)}) collective-permute-start(bf16[320,1280]{1,0:T(8,128)(2,1)S(1)} %get-tuple-element.409.refs_4_), channel_id=1, source_target_pairs={{0,8},{8,0},{16,24},{24,16},{1,9},{9,1},{17,25},{25,17},{2,10},{10... | collective-permute-start | bytes 2457608 | tf_op jit(solution)/shard_map/ppermute | solution.py:950
  259.3 20.5 %collective-permute-start.61 = (bf16[320,1280]{1,0:T(8,128)(2,1)S(1)}, bf16[320,1280]{1,0:T(8,128)(2,1)S(1)}, u32[]{:S(2)}, u32[]{:S(2)}) collective-permute-start(bf16[320,1280]{1,0:T(8,128)(2,1)S(1)} %get-tuple-element.413.refs_3_), channel_id=1, source_target_pairs={{8,16},{16,8},{9,17},{17,9},{10,18},{18,10},{11,19},{19,11},{12,20... | collective-permute-start | bytes 2457608 | tf_op jit(solution)/shard_map/ppermute | solution.py:950
  261.3 16.9 %collective-permute-start.58 = (bf16[160,1280]{1,0:T(8,128)(2,1)S(1)}, bf16[160,1280]{1,0:T(8,128)(2,1)S(1)}, u32[]{:S(2)}, u32[]{:S(2)}) collective-permute-start(bf16[160,1280]{1,0:T(8,128)(2,1)S(1)} %get-tuple-element.407), channel_id=1, source_target_pairs={{0,4},{1,5},{2,6},{3,7},{4,0},{5,1},{6,2},{7,3},{8,12},{9,13},{10,... | collective-permute-start | bytes 1228808 | tf_op jit(solution)/shard_map/ppermute | solution.py:934
  262.5 16.5 %collective-permute-start.59 = (bf16[160,1280]{1,0:T(8,128)(2,1)S(1)}, bf16[160,1280]{1,0:T(8,128)(2,1)S(1)}, u32[]{:S(2)}, u32[]{:S(2)}) collective-permute-start(bf16[160,1280]{1,0:T(8,128)(2,1)S(1)} %get-tuple-element.408), channel_id=1, source_target_pairs={{0,6},{1,7},{2,4},{3,5},{4,2},{5,3},{6,0},{7,1},{8,14},{9,15},{10,... | collective-permute-start | bytes 1228808 | tf_op jit(solution)/shard_map/ppermute | solution.py:934
  285.6 17.9 %collective-permute-start.66 = (bf16[320,1280]{1,0:T(8,128)(2,1)S(1)}, bf16[320,1280]{1,0:T(8,128)(2,1)S(1)}, u32[]{:S(2)}, u32[]{:S(2)}) collective-permute-start(bf16[320,1280]{1,0:T(8,128)(2,1)S(1)} %copy-done.6), channel_id=1, source_target_pairs={{8,0},{16,24},{9,1},{17,25},{10,2},{18,26},{11,3},{19,27},{12,4},{... | collective-permute-start | bytes 2457608 | tf_op jit(solution)/shard_map/ppermute | solution.py:950
  (64 other events, 480.1 us)

commit v3 on v2

--- a/solution.py
+++ b/solution.py
@@ -23,10 +23,11 @@
 
 GAIN1, BIAS1, BIAS_OUT, GAIN2, BIAS2, BIAS_DOWN, BIAS_UP, BIAS_QKV = range(8)
 TABLE_ROWS = 8
+SUM_ROWS = 16
 
 COST = pl.CostEstimate(flops=1, bytes_accessed=1, transcendentals=0)
-ANY = pl.BlockSpec(memory_space=pl.ANY)
 SMEM = pl.BlockSpec(memory_space=pltpu.SMEM)
+HBM = pl.BlockSpec(memory_space=pltpu.HBM)
 VMEM = pl.BlockSpec(memory_space=pltpu.VMEM)
 
 f32 = jnp.float32
@@ -121,8 +122,8 @@
 
 
 def call(kernel, name, kinds, out_shapes, scratch=(), vmem=16):
-    specs = {"s": SMEM, "a": ANY, "v": VMEM}
-    return pl.pallas_call(
+    specs = {"s": SMEM, "h": HBM, "v": VMEM}
+    made = pl.pallas_call(
         kernel,
         in_specs=[specs[kind] for kind in kinds],
         out_specs=[VMEM] * len(out_shapes),
@@ -133,6 +134,15 @@
         name=name,
     )
 
+    def run(*args):
+        placed = [
+            pltpu.with_memory_space_constraint(arg, pltpu.HBM) if kind == "h" else arg
+            for kind, arg in zip(kinds, args, strict=True)
+        ]
+        return made(*placed)
+
+    return run
+
 
 def sems(count):
     return pltpu.SemaphoreType.DMA((count,))
@@ -163,13 +173,12 @@
 
 def stack_columns(spot, mine, other, whole):
     core, side = spot[1], spot[2]
-    for of_core, (near, far) in ((core, mine), (1 - core, other)):
-        whole[row_of(spot, 0, of_core), :] = near[:SHARE, :]
+    for of_core, (own, near, far) in ((core, mine), (1 - core, other)):
+        whole[row_of(spot, 0, of_core), :] = own[:SHARE, :]
         for i in range(1, CHIPS):
-            lo = SHARE + (i - 1) * HALF
-            whole[row_of(spot, i, of_core, side), :] = near[lo : lo + HALF, :]
-            lo = (i - 1) * HALF
-            whole[row_of(spot, i, of_core, 1 - side), :] = far[lo : lo + HALF, :]
+            rows = slice((i - 1) * HALF, i * HALF)
+            whole[row_of(spot, i, of_core, side), :] = near[rows, :]
+            whole[row_of(spot, i, of_core, 1 - side), :] = far[rows, :]
 
 
 def by_core_copies(core, mine, other, whole, sem):
@@ -241,7 +250,7 @@
     return call(
         qkv_blocks_kernel,
         "qkv_blocks",
-        "ss" + "a" * 11,
+        "ss" + "h" * 11,
         [((SHARE + EXTRA, 3 * D_CHIP), bf16)] + [half] * (CHIPS - 1),
         [pltpu.VMEM(v.shape, v.dtype) for v in vectors]
         + [
@@ -294,27 +303,50 @@
     )(spot, weights, cotangent)
 
 
-def up_join_kernel(own, cotangent, u1, u2, u3, near, near_half, whole):
+def up_join_kernel(cotangent, u1, u2, u3, half_a, half_b, whole):
     rows = cotangent.shape[0]
-    near[:SHARE, :] = own[...]
     whole[:rows, :] = cotangent[...]
+    size = half_a.shape[0]
+    near = []
     for i, block in enumerate((u1, u2, u3)):
-        near[SHARE + i * HALF : SHARE + (i + 1) * HALF, :] = block[rows:, :]
-        near_half[i * HALF : (i + 1) * HALF, :] = block[rows:, :]
+        near.append(block[rows:, :])
         whole[(i + 1) * rows : (i + 2) * rows, :] = block[:rows, :]
-
-
-def up_join(own, cotangent, blocks):
+    near = jnp.concatenate(near, axis=0)
+    half_a[...] = near[:size]
+    half_b[...] = near[size:]
+
+
+def up_join(cotangent, blocks):
+    half = ((3 * HALF // 2, FF_CHIP), bf16)
     return call(
         up_join_kernel,
         "up_join",
-        "vvvvv",
-        [
-            ((SHARE + 3 * HALF, FF_CHIP), bf16),
-            ((3 * HALF, FF_CHIP), bf16),
-            ((CHIPS * cotangent.shape[0], D), bf16),
-        ],
-    )(own, cotangent, *blocks)
+        "vvvv",
+        [half, half, ((CHIPS * cotangent.shape[0], D), bf16)],
+    )(cotangent, *blocks)
+
+
+def halves_kernel(whole, first, second):
+    size = first.shape[0]
+    first[...] = whole[:size, :]
+    second[...] = whole[size:, :]
+
+
+def halves(whole):
+    shape = (whole.shape[0] // 2, whole.shape[1])
+    return call(halves_kernel, "halves", "v", [(shape, whole.dtype)] * 2)(whole)
+
+
+def join_kernel(*refs):
+    stack_blocks(refs[:-1], refs[-1])
+
+
+def join(blocks):
+    rows, width = blocks[0].shape
+    count = len(blocks)
+    return call(join_kernel, "join", "v" * count, [((count * rows, width), blocks[0].dtype)])(
+        *blocks
+    )[0]
 
 
 def fill_table(spot, extras, table, mask):
@@ -367,7 +399,8 @@
         for i in range(CHIPS):
             extras[2 * (spot[0] ^ i) + of_core] = lines[i * EXTRA : (i + 1) * EXTRA, :].astype(f32)
     fill_table(spot, extras, table, mask)
-    stack_columns(spot, mine[:2], other[:2], qkv)
+    columns = [(near, near.at[SHARE:], far) for near, far, _ in (mine, other)]
+    stack_columns(spot, *columns, qkv)
     gain = table[GAIN1 : GAIN1 + 1, :]
     bias = table[BIAS1 : BIAS1 + 1, :]
     first_low[...] = (normed[...] * gain + bias).astype(bf16)
@@ -396,7 +429,7 @@
     outs = call(
         enter_kernel,
         "enter",
-        "sv" + "v" * 6 + "aa",
+        "sv" + "v" * 6 + "hv",
         [
             ((TABLE_ROWS, D), f32),
             ((total, rows), bf16),
@@ -508,43 +541,133 @@
     return call(
         act_grad_kernel,
         "act_grad",
-        "svaa",
+        "svhv",
         [((cotangent.shape[0], FF_CHIP), f32), ((FF_CHIP, D), bf16)],
         [sems(2)],
     )(spot, cotangent, down_mine, down_other)
 
 
-def hidden_kernel(spot, s0, s1, s2, s3, grad_act, cotangent, table, *refs):
-    mine, other, refs = refs[:2], refs[2:4], refs[4:]
-    second, act, grad_pre, down_sent, bias_sum = refs[:5]
-    partials = refs[5 : 5 + CHIPS]
-    up, pre_act = refs[5 + CHIPS :]
-    rows = s0.shape[0]
-    stack_columns(spot, mine, other, up)
-    stack_blocks((s0, s1, s2, s3), second)
-
-    def columns(at):
-        pre_act[:, at] = mm(second[...], up[:, at]) + table[BIAS_UP : BIAS_UP + 1, at]
+def hidden_rows(at, second, up, table, grad_act, pre_act, act, grad_pre, bias_sum):
+    size = at.stop - at.start
+
+    def columns(tile):
+        pre_act[at, tile] = mm(second[at, :], up[:, tile]) + table[BIAS_UP : BIAS_UP + 1, tile]
 
     tiled(FF_CHIP, 256, columns)
-    bias_sum[...] = jnp.zeros_like(bias_sum)
-
-    def activate(at):
-        pre = pre_act[at, :]
+
+    @pl.loop(0, size // 64)
+    def _(i):
+        rows = pl.ds(pl.multiple_of(at.start + i * 64, 64), 64)
+        pre = pre_act[rows, :]
         below = 0.5 * (1.0 + lax.erf(pre * (0.5**0.5)))
         bell = jnp.exp(-0.5 * pre * pre) * 0.3989422804014327
-        act[at, :] = (pre * below).astype(bf16)
-        grad = (grad_act[at, :] * (below + pre * bell)).astype(bf16)
-        grad_pre[at, :] = grad
+        act[rows, :] = (pre * below).astype(bf16)
+        grad = (grad_act[rows, :] * (below + pre * bell)).astype(bf16)
+        grad_pre[rows, :] = grad
         bias_sum[...] += jnp.sum(grad.astype(f32), axis=0, keepdims=True)
 
-    tiled(second.shape[0], 64, activate)
-    first = (1 - spot[1]) * FF_SHARE
-
-    @pl.loop(0, FF_SHARE // 128)
-    def _(i):
-        columns_at = pl.ds(pl.multiple_of(first + i * 128, 128), 128)
-        down_sent[row_at(i, 128), :] = t_mm(act[:, columns_at], cotangent[...]).astype(bf16)
+
+def hidden_first_kernel(spot, s0, s1, s2, grad_act, table, *refs):
+    columns = [(own, rest, rest.at[3 * HALF :]) for own, rest in (refs[:2], refs[2:4])]
+    second, act, grad_pre, bias_sum, up, pre_act = refs[4:]
+    rows = s0.shape[0]
+    stack_columns(spot, *columns, up)
+    stack_blocks((s0, s1, s2), second)
+    bias_sum[...] = jnp.zeros_like(bias_sum)
+    hidden_rows(
+        slice(0, 3 * rows), second, up, table, grad_act, pre_act, act, grad_pre, bias_sum
+    )
+
+
+def hidden_first(spot, blocks, grad_act, table, mine, other):
+    total = grad_act.shape[0]
+    return call(
+        hidden_first_kernel,
+        "hidden_first",
+        "svvvvv" + "v" * 4,
+        [
+            ((total, D), bf16),
+            ((total, FF_CHIP), bf16),
+            ((total, FF_CHIP), bf16),
+            ((1, FF_CHIP), f32),
+            ((D, FF_CHIP), bf16),
+        ],
+        [pltpu.VMEM((total, FF_CHIP), f32)],
+    )(spot, *blocks, grad_act, table, *mine, *other)
+
+
+def hidden_last_kernel(
+    spot,
+    s3,
+    grad_act,
+    table,
+    cotangent,
+    up,
+    second_in,
+    act_in,
+    grad_pre_in,
+    bias_in,
+    second,
+    act,
+    grad_pre,
+    bias_sum,
+    down_sent,
+    pre_act,
+):
+    del second_in, act_in, grad_pre_in
+    rows = s3.shape[0]
+    at = slice(3 * rows, 4 * rows)
+    second[at, :] = s3[...]
+    bias_sum[...] = bias_in[...]
+    hidden_rows(at, second, up, table, grad_act, pre_act, act, grad_pre, bias_sum)
+    down_product(act, cotangent, 1 - spot[1], 0, down_sent)
+
+
+def down_product(act, cotangent, of_core, half, target):
+    low = half * ROWS_Z
+    aligned = low // 128 * 128
+    if half == 0:
+        units = pl.ds(pl.multiple_of(of_core * FF_SHARE, 128), ROWS_Z)
+        target[...] = t_mm(act[:, units], cotangent[...]).astype(target.dtype)
+    else:
+        units = pl.ds(pl.multiple_of(of_core * FF_SHARE + aligned, 128), FF_SHARE - aligned)
+        window = act[:, units][:, low - aligned :]
+        target[...] = t_mm(window, cotangent[...]).astype(target.dtype)
+
+
+def up_product(second, grad_pre, pair, of_core, target, work):
+    for i in range(2):
+        first = (2 * (2 * pair + i) + of_core) * SHARE
+        aligned = pl.multiple_of(first // 128 * 128, 128)
+        work[...] = t_mm(second[:, pl.ds(aligned, 256)], grad_pre[...])
+        start = pl.multiple_of(lax.rem(first, 128), 32)
+        target[i * SHARE : (i + 1) * SHARE, :] = work[pl.ds(start, SHARE), :].astype(target.dtype)
+
+
+def hidden_last(spot, block, grad_act, table, cotangent, up, second, act, grad_pre, bias_sum):
+    total = second.shape[0]
+    return pl.pallas_call(
+        hidden_last_kernel,
+        in_specs=[SMEM] + [VMEM] * 9,
+        out_specs=[VMEM] * 5,
+        out_shape=[
+            jax.ShapeDtypeStruct(second.shape, bf16),
+            jax.ShapeDtypeStruct(act.shape, bf16),
+            jax.ShapeDtypeStruct(grad_pre.shape, bf16),
+            jax.ShapeDtypeStruct(bias_sum.shape, f32),
+            jax.ShapeDtypeStruct((ROWS_Z, D), bf16),
+        ],
+        scratch_shapes=[pltpu.VMEM((total, FF_CHIP), f32)],
+        input_output_aliases={6: 0, 7: 1, 8: 2},
+        compiler_params=pltpu.CompilerParams(vmem_limit_bytes=16 * 2**20),
+        cost_estimate=COST,
+        name="hidden_last",
+    )(spot, block, grad_act, table, cotangent, up, second, act, grad_pre, bias_sum)
+
+
+def second_grad_kernel(spot, grad_pre, up, second, *refs):
+    partials, up_sent, work = refs[:CHIPS], refs[CHIPS], refs[CHIPS + 1]
+    rows = partials[0].shape[0]
 
     def partial(at):
         whole = mm_t(grad_pre[...], up[at, :]).astype(bf16)
@@ -552,41 +675,19 @@
             part[:, at] = whole[i * rows : (i + 1) * rows]
 
     tiled(D, 256, partial)
-
-
-def hidden(spot, blocks, grad_act, cotangent, table, mine, other):
-    rows = blocks[0].shape[0]
-    total = CHIPS * rows
+    up_product(second, grad_pre, 0, 1 - spot[1], up_sent, work)
+
+
+def second_grad(spot, grad_pre, up, second):
+    rows = grad_pre.shape[0] // CHIPS
     outs = call(
-        hidden_kernel,
-        "hidden",
-        "svvvvvvv" + "v" * 4,
-        [
-            ((total, D), bf16),
-            ((total, FF_CHIP), bf16),
-            ((total, FF_CHIP), bf16),
-            ((FF_SHARE, D), bf16),
-            ((1, FF_CHIP), f32),
-        ]
-        + [((rows, D), bf16)] * CHIPS,
-        [pltpu.VMEM((D, FF_CHIP), bf16), pltpu.VMEM((total, FF_CHIP), f32)],
-    )(spot, *blocks, grad_act, cotangent, table, *mine, *other)
-    return outs[:5], outs[5:]
-
-
-def down_grad_kernel(spot, act, cotangent, got, first, second):
-    kept = pl.ds(pl.multiple_of(spot[1] * FF_SHARE, 128), FF_SHARE)
-    half = FF_SHARE // 2
-    total = t_mm(act[:, kept], cotangent[...]) + got[...].astype(f32)
-    first[...] = total[:half].astype(bf16)
-    second[...] = total[half:].astype(bf16)
-
-
-def down_grad_of(spot, act, cotangent, got):
-    half = FF_SHARE // 2
-    return call(
-        down_grad_kernel, "down_grad", "svvv", [((half, D), bf16), ((half, D), bf16)]
-    )(spot, act, cotangent, got)
+        second_grad_kernel,
+        "second_grad",
+        "svvv",
+        [((rows, D), bf16)] * CHIPS + [((ROWS_Z, FF_CHIP), bf16)],
+        [pltpu.VMEM((256, FF_CHIP), f32)],
+    )(spot, grad_pre, up, second)
+    return outs[:CHIPS], outs[CHIPS]
 
 
 def split_rows(core, whole, sent, kept):
@@ -597,23 +698,36 @@
             target[at] = whole[pl.ds(start, SHARE), :].astype(bf16)
 
 
-def up_grad_kernel(spot, second, grad_pre, sent_a, sent_b, kept, whole):
-    def columns(at):
-        whole[at, :] = t_mm(second[:, at], grad_pre[...])
-
-    tiled(D, 256, columns)
-    split_rows(spot[1], whole, (sent_a, sent_b), kept)
-
-
-def up_grad_of(spot, second, grad_pre):
-    half = ((CHIPS // 2, SHARE, FF_CHIP), bf16)
+def down_grad_kernel(spot, act, cotangent, got, total):
+    down_product(act, cotangent, spot[1], 0, total)
+    total[...] = (total[...].astype(f32) + got[...].astype(f32)).astype(bf16)
+
+
+def down_grad_of(spot, act, cotangent, got):
+    return call(down_grad_kernel, "down_grad", "svvv", [((ROWS_Z, D), bf16)])(
+        spot, act, cotangent, got
+    )[0]
+
+
+def rest_kernel(
+    spot, second, grad_pre, act, cotangent, up_a, up_b, up_sent, down_b, down_sent, work
+):
+    core = spot[1]
+    up_product(second, grad_pre, 0, core, up_a, work)
+    up_product(second, grad_pre, 1, 1 - core, up_sent, work)
+    up_product(second, grad_pre, 1, core, up_b, work)
+    down_product(act, cotangent, 1 - core, 1, down_sent)
+    down_product(act, cotangent, core, 1, down_b)
+
+
+def rest_of_grads(spot, second, grad_pre, act, cotangent):
     return call(
-        up_grad_kernel,
-        "up_grad",
-        "svv",
-        [half, half, ((CHIPS, SHARE, FF_CHIP), bf16)],
-        [pltpu.VMEM((D, FF_CHIP), f32)],
-    )(spot, second, grad_pre)
+        rest_kernel,
+        "rest",
+        "svvvv",
+        [((ROWS_Z, D), bf16)] * 5,
+        [pltpu.VMEM((256, FF_CHIP), f32)],
+    )(spot, second, grad_pre, act, cotangent)
 
 
 def result_kernel(act, down, *partials):
@@ -681,20 +795,17 @@
     return call(add_kernel, "add", "v" * (2 * len(left)), shapes)(*left, *right)
 
 
-def split_add_kernel(kept, got_a, got_b, *halves):
-    for i, (half, got) in enumerate(zip(halves, (got_a, got_b))):
-        for j in range(CHIPS // 2):
-            total = kept[i * CHIPS // 2 + j].astype(f32) + got[j].astype(f32)
-            half[j * SHARE : (j + 1) * SHARE, :] = total.astype(bf16)
-
-
-def split_add(kept, got_a, got_b):
-    shape = (ROWS_Z, kept.shape[-1])
-    return call(split_add_kernel, "split_add", "vvv", [(shape, bf16)] * 2)(kept, got_a, got_b)
-
-
 PACKED = SHARE * 3 // 4
 STEP = SHARE // 4
+
+
+def sum_all_kernel(a, b, c, d, total):
+    total[...] = (a[...] + b[...]) + (c[...] + d[...])
+
+
+def sum_all(parts):
+    shape = (parts[0].shape, parts[0].dtype)
+    return call(sum_all_kernel, "sum_all", "vvvv", [shape])(*parts)[0]
 
 
 def pack_kernel(kept, got_a, got_b, out_kept, out_got, *chunks):
@@ -730,56 +841,130 @@
     )
 
 
-def z_kernel(names, spot, *refs):
-    ref = dict(zip(names, refs))
-    middle = spot[3] > 0
-    if "half" in ref:
-        ref["half"][...] = (ref["low"][...].astype(f32) + ref["got_side"][...].astype(f32)).astype(
-            bf16
-        )
-    if "send" in ref:
-        sent = None
-        if "half_before" in ref:
-            sent = (
-                ref["half_before"][...].astype(f32) + ref["got_middle"][...].astype(f32)
-            ).astype(bf16)
-        if "low_next" in ref:
-            low_next = ref["low_next"][...]
-            sent = low_next if sent is None else jnp.where(middle, sent, low_next)
-        ref["send"][...] = sent
-    if "final" in ref:
-        ref["final"][...] = jnp.where(middle, ref["sent_before"][...], ref["got_side"][...])
-
-
-def z_step(spot, inputs, outputs):
-    inputs = {name: value for name, value in inputs.items() if value is not None}
-    names = tuple(inputs) + tuple(outputs)
-    shape = ((ROWS_Z, D), bf16)
+def z_half(low, got_side):
+    return add_all([low], [got_side])[0]
+
+
+def z_send_kernel(spot, half, got_middle, low, sent):
+    whole = (half[...].astype(f32) + got_middle[...].astype(f32)).astype(bf16)
+    sent[...] = jnp.where(spot[3] > 0, whole, low[...])
+
+
+def z_send(spot, half, got_middle, low):
+    return call(z_send_kernel, "z_send", "svvv", [(low.shape, bf16)])(spot, half, got_middle, low)[0]
+
+
+def z_final_kernel(spot, sent, got_side, final):
+    final[...] = jnp.where(spot[3] > 0, sent[...], got_side[...])
+
+
+def z_final(spot, sent, got_side):
+    return call(z_final_kernel, "z_final", "svv", [(sent.shape, bf16)])(spot, sent, got_side)[0]
+
+
+def first_down_kernel(spot, sent, got, down, here, sem):
+    here[...] = jnp.where(spot[3] > 0, sent[...], got[...]).astype(f32)
+    copy = pltpu.make_async_copy(here, down.at[:ROWS_Z], sem.at[0])
+    copy.start()
+    copy.wait()
+
+
+def first_down(spot, sent, got):
+    return pl.pallas_call(
+        first_down_kernel,
+        in_specs=[SMEM, VMEM, VMEM],
+        out_specs=HBM,
+        out_shape=pltpu.HBM((2 * ROWS_Z, D), f32),
+        scratch_shapes=[pltpu.VMEM((ROWS_Z, D), f32), sems(1)],
+        compiler_params=pltpu.CompilerParams(vmem_limit_bytes=16 * 2**20),
+        cost_estimate=COST,
+        name="first_down",
+    )(spot, sent, got)
+
+
+def second_down_kernel(spot, sent, got, before, down, here, sem):
+    del before
+    here[...] = jnp.where(spot[3] > 0, sent[...], got[...]).astype(f32)
+    copy = pltpu.make_async_copy(here, down.at[ROWS_Z:], sem.at[0])
+    copy.start()
+    copy.wait()
+
+
+def second_down(spot, sent, got, down):
+    return pl.pallas_call(
+        second_down_kernel,
+        in_specs=[SMEM, VMEM, VMEM, HBM],
+        out_specs=HBM,
+        out_shape=pltpu.HBM((2 * ROWS_Z, D), f32),
+        scratch_shapes=[pltpu.VMEM((ROWS_Z, D), f32), sems(1)],
+        input_output_aliases={3: 0},
+        compiler_params=pltpu.CompilerParams(vmem_limit_bytes=16 * 2**20),
+        cost_estimate=COST,
+        name="second_down",
+    )(spot, sent, got, pltpu.with_memory_space_constraint(down, pltpu.HBM))
+
+
+def qkv_rows_kernel(spot, b0, b1, b2, b3, qkv, rows, stack, sem):
+    for i, block in enumerate((b0, b1, b2, b3)):
+        stack[spot[0] ^ i] = block[...]
+    copies = []
+    for kind in range(3):
+        for chip in range(CHIPS):
+            lo = kind * D + chip * D_CHIP
+            rows[:, lo : lo + D_CHIP] = stack[
+                chip, :, kind * D_CHIP : (kind + 1) * D_CHIP
+            ].astype(f32)
+        at = slice(kind * D, (kind + 1) * D)
+        copies.append(pltpu.make_async_copy(rows.at[:, at], qkv.at[:, at], sem.at[kind]))
+        copies[-1].start()
+    wait_all(copies)
+
+
+def qkv_rows(spot, blocks):
+    shape = blocks[0].shape
+    return pl.pallas_call(
+        qkv_rows_kernel,
+        in_specs=[SMEM] + [VMEM] * 4,
+        out_specs=HBM,
+        out_shape=pltpu.HBM((shape[0], 3 * D), f32),
+        scratch_shapes=[
+            pltpu.VMEM((shape[0], 3 * D), f32),
+            pltpu.VMEM((CHIPS,) + shape, bf16),
+            sems(3),
+        ],
+        compiler_params=pltpu.CompilerParams(vmem_limit_bytes=16 * 2**20),
+        cost_estimate=COST,
+        name="qkv_rows",
+    )(spot, *blocks)
+
+
+def owned_kernel(count, place, sums, got, *outs):
+    total = sums[...] + got[...]
+    index = place[0]
+    size = outs[0].shape[0]
+    mine = pltpu.roll(total, D - index * size, 1)
+    for i, row in enumerate((0, 1, 2, 3, 4, 5, 8, 9)):
+        outs[i][...] = mine[row : row + 1, :size].reshape(size)
+    wide = outs[8].shape[0]
+    first = index * wide
+    row = first // D
+    line = total[10:11, :]
+    for k in range(1, CHIPS):
+        line = jnp.where(row == k, total[10 + k : 11 + k, :], line)
+    line = pltpu.roll(jnp.broadcast_to(line, (8, D)), D - lax.rem(first, D), 1)
+    outs[8][...] = line[0:1, :wide].reshape(wide)
+    mean = total[6:7, :] / count
+    outs[9][...] = mean.reshape(D)
+    outs[10][...] = (total[7:8, :] / count - mean * mean).reshape(D)
+
+
+def owned(place, count, fsdp_count, sums, got):
+    sizes = [D // fsdp_count] * 8 + [FF // fsdp_count, D, D]
 
     def kernel(*refs):
-        z_kernel(names, *refs)
-
-    done = call(kernel, "z_step", "s" + "v" * len(inputs), [shape] * len(outputs))(
-        spot, *inputs.values()
-    )
-    return dict(zip(outputs, done))
-
-
-def last_kernel(spot, down_a, sent, got, b0, b1, b2, b3, down, qkv, stack):
-    down[:ROWS_Z, :] = down_a[...].astype(f32)
-    down[ROWS_Z:, :] = jnp.where(spot[3] > 0, sent[...], got[...]).astype(f32)
-    qkv_rows(spot, (b0, b1, b2, b3), qkv, stack)
-
-
-def last(spot, down_a, sent, got, blocks):
-    shape = blocks[0].shape
-    return call(
-        last_kernel,
-        "last",
-        "s" + "v" * 7,
-        [((2 * ROWS_Z, D), f32), ((shape[0], 3 * D), f32)],
-        [pltpu.VMEM((CHIPS,) + shape, bf16)],
-    )(spot, down_a, sent, got, *blocks)
+        owned_kernel(count, *refs)
+
+    return call(kernel, "owned", "svv", [((size,), f32) for size in sizes])(place, sums, got)
 
 
 def up_exchange_kernel(spot, a, b, *blocks):
@@ -796,37 +981,44 @@
     )
 
 
-def qkv_exchange_kernel(spot, a, b, *refs):
+def qkv_unpack_kernel(spot, sent, got_side, blocks, out_rows):
+    chunk = jnp.where(spot[3] > 0, sent[...], got_side[...])
+    for j in range(2):
+        blocks[j] = unpacked(chunk, j)
+    out_rows[...] = chunk[2 * PACKED :, :].astype(f32)
+
+
+def qkv_unpack(spot, sent, got_side):
+    return call(
+        qkv_unpack_kernel,
+        "qkv_unpack",
+        "svv",
+        [((2, SHARE, 3 * D_CHIP), bf16), ((HALF, D), f32)],
+    )(spot, sent, got_side)
+
+
+def qkv_exchange_kernel(spot, blocks_a, rows_a, sent, got_side, *refs):
     blocks, out_rows, stack = refs[:CHIPS], refs[CHIPS], refs[CHIPS + 1]
-    for i, chunk in enumerate((a, b)):
-        for j in range(2):
-            stack[2 * i + j] = unpacked(chunk, j)
-        out_rows[i * HALF : (i + 1) * HALF, :] = chunk[2 * PACKED :, :].astype(f32)
+    chunk = jnp.where(spot[3] > 0, sent[...], got_side[...])
+    stack[:2] = blocks_a[...]
+    for j in range(2):
+        stack[2 + j] = unpacked(chunk, j)
+    out_rows[:HALF, :] = rows_a[...]
+    out_rows[HALF:, :] = chunk[2 * PACKED :, :].astype(f32)
     for i, block in enumerate(blocks):
         block[...] = stack[spot[0] ^ i]
 
 
-def qkv_exchange(spot, a, b):
+def qkv_exchange(spot, blocks_a, rows_a, sent, got_side):
     shape = (SHARE, 3 * D_CHIP)
     outs = call(
         qkv_exchange_kernel,
         "qkv_exchange",
-        "svv",
+        "svvvv",
         [(shape, bf16)] * CHIPS + [((SHARE, D), f32)],
         [pltpu.VMEM((CHIPS,) + shape, bf16)],
-    )(spot, a, b)
+    )(spot, blocks_a, rows_a, sent, got_side)
     return outs[:CHIPS], outs[CHIPS]
-
-
-def qkv_rows(spot, blocks, weights, stack):
-    for i, block in enumerate(blocks):
-        stack[spot[0] ^ i] = block[...]
-    for chip in range(CHIPS):
-        for kind in range(3):
-            lo = kind * D + chip * D_CHIP
-            weights[:, lo : lo + D_CHIP] = stack[
-                chip, :, kind * D_CHIP : (kind + 1) * D_CHIP
-            ].astype(f32)
 
 
 def up_rows_kernel(spot, b0, b1, b2, b3, weights):
@@ -877,9 +1069,10 @@
     sums[7:8, :] = jnp.sum(picked * picked, axis=0, keepdims=True)
     for k in range(CHIPS):
         here = spot[0] == k
-        sums[8 + k : 9 + k, :D_CHIP] = jnp.where(here, qkv_sum[:, :D_CHIP], 0.0)
-        sums[12 + k : 13 + k, :D_CHIP] = jnp.where(here, qkv_sum[:, 2 * D_CHIP :], 0.0)
-        sums[16 + k : 17 + k, :] = jnp.where(here, up_sum[...], 0.0)
+        lo = k * D_CHIP
+        sums[8:9, lo : lo + D_CHIP] = jnp.where(here, qkv_sum[:, :D_CHIP], 0.0)
+        sums[9:10, lo : lo + D_CHIP] = jnp.where(here, qkv_sum[:, 2 * D_CHIP :], 0.0)
+        sums[10 + k : 11 + k, :] = jnp.where(here, up_sum[...], 0.0)
 
 
 def end(spot, lengths, parts, results, *rest):
@@ -888,7 +1081,7 @@
         end_kernel,
         "end",
         "ss" + "v" * 15,
-        [(shape, bf16), (shape, f32), ((24, D), f32)],
+        [(shape, bf16), (shape, f32), ((SUM_ROWS, D), f32)],
     )(spot, lengths, *parts, *results, *rest)
 
 
@@ -965,19 +1158,24 @@
     w_qkv, w_out, w_up, w_down = (gather_shards(w) for w in (w_qkv, w_out, w_up, w_down))
     given = (ln1_gain, ln1_bias, b_out, ln2_gain, ln2_bias, b_down, b_query, b_value, b_up)
     qkv_sent = qkv_blocks(spot, lengths, padding, w_qkv, [gather_shards(v) for v in given])
-    qkv_near, qkv_half, extras = qkv_join(from_chips(qkv_sent))
+    qkv_got = from_chips(qkv_sent)
+    x1, x2, *qkv_got = fence(swap(tokens, 2), swap(tokens, 4), *qkv_got)
+    qkv_near, qkv_half, extras = qkv_join(qkv_got)
     qkv_far = z_swap(qkv_half)
     qkv_near_other, extras_other = swap(qkv_near, 1), swap(extras, 1)
     tokens_sent, extras = fence(tokens, extras)
-    blocks = [tokens] + [swap(tokens_sent, 2 * i) for i in range(1, CHIPS)]
+    blocks = [tokens, x1, x2, swap(tokens_sent, 6)]
     normed = token_norm(blocks)
-    normed, qkv_far, extras_other = fence(normed, qkv_far, extras_other)
-    qkv_far_other = swap(qkv_far, 1)
-    out_sent, normed = fence(w_out, normed)
+    out_sent, _ = fence(w_out, extras)
     out_other = swap(out_sent, 1)
     up_own, *up_sent = up_blocks(spot, w_up, cotangent)
-    up_sent, normed = fence_list(up_sent, normed)
+    up_own, *up_sent = fence(up_own, *up_sent, extras)[:-1]
+    up_own_other = swap(up_own, 1)
     loads = [swap(block, 2 * i + 2) for i, block in enumerate(up_sent)]
+    normed, qkv_far, extras_other, qkv_near_other, out_other, up_own_other = fence(
+        normed, qkv_far, extras_other, qkv_near_other, out_other, up_own_other
+    )
+    qkv_far_other = join([swap(half, 1) for half in halves(qkv_far)])
 
     (table, mask, qkv, out, first_low, projected, context), partial_out = enter(
         spot,
@@ -987,58 +1185,67 @@
         w_out,
         out_other,
     )
-    loads, *partial_out = fence_list(loads, *partial_out)
     out_parts = from_chips(partial_out)
-    up_near, up_half, whole_cotangent = up_join(up_own, cotangent, loads)
-    up_far = z_swap(up_half)
-    down_sent, up_half = fence(w_down, up_half)
-    down_other = swap(down_sent, 1)
-    out_parts, down_other = fence_list(out_parts, down_other)
+    cotangent_late, _ = fence(cotangent, partial_out[0])
+    up_half_a, up_half_b, whole_cotangent = up_join(cotangent_late, loads)
+    up_far = [z_swap(up_half_a), z_swap(up_half_b)]
+    up_far, *out_parts = fence_list(up_far, *out_parts)
     mixed, second_own = mix(out_parts, tokens, table)
     second_blocks = from_chips([second_own] * CHIPS)
-    up_near, up_far, second_own = fence(up_near, up_far, second_own)
-    up_near_other, up_far_other = swap(up_near, 1), swap(up_far, 1)
-    whole_cotangent, second_own = fence(whole_cotangent, second_own)
+    up_far, _ = fence_list(up_far, second_own)
+    up_rest = join([up_half_a, up_half_b] + up_far)
+    up_other = [up_own_other, swap(up_rest, 1)]
+    down_sent, _ = fence(w_down, second_own)
+    down_other = swap(down_sent, 1)
+    whole_cotangent, down_other = fence(whole_cotangent, down_other)
     grad_act, down = act_grad(spot, whole_cotangent, w_down, down_other)
 
-    second_blocks, grad_act = fence_list(second_blocks, grad_act)
-    (second_low, act_low, grad_pre, down_sent, up_bias_sum), partial_second = hidden(
+    second_low, act_low, grad_pre, up_bias_sum, up = hidden_first(
         spot,
-        second_blocks,
+        second_blocks[:3],
         grad_act,
-        whole_cotangent,
         table,
-        [up_near, up_far],
-        [up_near_other, up_far_other],
+        [up_own, up_rest],
+        up_other,
+    )
+    block, up_bias_sum = fence(second_blocks[3], up_bias_sum)
+    second_low, act_low, grad_pre, up_bias_sum, down_sent = hidden_last(
+        spot, block, grad_act, table, whole_cotangent, up, second_low, act_low, grad_pre, up_bias_sum
     )
     down_got = swap(down_sent, 1)
+    partial_second, up_sent = second_grad(spot, grad_pre, up, second_low)
+    up_got = swap(up_sent, 1)
+    act_low, up_sent = fence(act_low, up_sent)
+    down_a = down_grad_of(spot, act_low, whole_cotangent, down_got)
+    side0 = z_swap(down_a)
+    *partial_second, down_a = fence(*partial_second, down_a)
     second_parts = from_chips(partial_second)
-    down_a, down_b = down_grad_of(spot, act_low, whole_cotangent, down_got)
-    side0 = z_swap(down_a)
-
     second_low, down_a = fence(second_low, down_a)
-    up_sent_a, up_sent_b, up_kept = up_grad_of(spot, second_low, grad_pre)
-    up_a, up_b = split_add(up_kept, swap(up_sent_a, 1), swap(up_sent_b, 1))
+    up_a, up_b, up_sent, down_b, down_sent = rest_of_grads(
+        spot, second_low, grad_pre, act_low, whole_cotangent
+    )
+    up_got, up_sent = fence(up_got, up_sent)
+    (up_a,) = add_all([up_a], [up_got])
+    up_got = swap(up_sent, 1)
 
     second_parts, side0, up_a = fence_list(second_parts, side0, up_a)
-    z = z_step(spot, dict(got_side=side0, low=down_a, low_next=up_a), ("half", "send"))
-    half0, send1 = z["half"], z["send"]
+    half0, send1 = z_half(down_a, side0), up_a
+    send1, _ = fence(send1, half0)
     side1, middle1 = z_swap(send1), z_middle(half0)
     second_parts, half0 = fence_list(second_parts, half0)
     grad_mixed, branch_own, mix_sums = unmix(second_parts, mixed, table, cotangent)
     branch_blocks = from_chips([branch_own] * CHIPS)
     act_low, branch_own = fence(act_low, branch_own)
-    partial_result = result_of(act_low, down)
-
-    branch_blocks, side1, middle1, *partial_result = fence_list(
-        branch_blocks, side1, middle1, *partial_result
-    )
-    z = z_step(
-        spot,
-        dict(got_side=side1, got_middle=middle1, low=up_a, half_before=half0, low_next=up_b),
-        ("half", "send"),
-    )
-    half1, send2 = z["half"], z["send"]
+    partial_result = list(result_of(act_low, down))
+
+    up_got, partial_result[0] = fence(up_got, partial_result[0])
+    (up_b,) = add_all([up_b], [up_got])
+    branch_blocks, side1, middle1, *partial_result, up_b = fence_list(
+        branch_blocks, side1, middle1, *partial_result, up_b
+    )
+    half1 = z_half(up_a, side1)
+    middle1, _ = fence(middle1, half1)
+    send2 = z_send(spot, half0, middle1, up_b)
     side2, middle2 = z_swap(send2), z_middle(half1)
     branch_blocks, half1 = fence_list(branch_blocks, half1)
     (whole_branch, grad_projected, qkv_bias_sum), partial_first = leave(
@@ -1053,49 +1260,32 @@
     )
 
     side2, middle2, qkv_a = fence(side2, middle2, qkv_a)
-    z = z_step(
-        spot,
-        dict(got_side=side2, got_middle=middle2, low=up_b, half_before=half1, low_next=qkv_a),
-        ("half", "send"),
-    )
-    half2, send3 = z["half"], z["send"]
+    half2 = z_half(up_b, side2)
+    middle2, _ = fence(middle2, half2)
+    send3 = z_send(spot, half1, middle2, qkv_a)
     side3, middle3 = z_swap(send3), z_middle(half2)
-    *partial_first, half2 = fence(*partial_first, half2)
+    down_sent, _ = fence(down_sent, send3)
+    (down_b,) = add_all([down_b], [swap(down_sent, 1)])
+    *partial_first, down_b = fence(*partial_first, down_b)
     first_parts = from_chips(partial_first)
-    down_a_final = z_step(spot, dict(got_side=side2, sent_before=send2), ("final",))["final"]
+    down_grad = first_down(spot, send2, side2)
 
     first_parts, side3, middle3 = fence_list(first_parts, side3, middle3)
-    z = z_step(
-        spot,
-        dict(
-            got_side=side3,
-            got_middle=middle3,
-            low=qkv_a,
-            half_before=half2,
-            low_next=qkv_b,
-            sent_before=send3,
-        ),
-        ("half", "send", "final"),
-    )
-    half3, send4, up_a_final = z["half"], z["send"], z["final"]
+    half3 = z_half(qkv_a, side3)
+    middle3, _ = fence(middle3, half3)
+    send4 = z_send(spot, half2, middle3, qkv_b)
+    sent, _ = fence(send3, send4)
+    up_a_final = z_final(spot, sent, side3)
     side4, middle4 = z_swap(send4), z_middle(half3)
     *partial_result, half3 = fence(*partial_result, half3)
     result_parts = from_chips(partial_result)
 
     result_parts, side4, middle4 = fence_list(result_parts, side4, middle4)
-    z = z_step(
-        spot,
-        dict(
-            got_side=side4,
-            got_middle=middle4,
-            low=qkv_b,
-            half_before=half3,
-            low_next=down_b,
-            sent_before=send4,
-        ),
-        ("half", "send", "final"),
-    )
-    half4, send5, up_b_final = z["half"], z["send"], z["final"]
+    half4 = z_half(qkv_b, side4)
+    middle4, _ = fence(middle4, half4)
+    send5 = z_send(spot, half3, middle4, down_b)
+    sent, _ = fence(send4, send5)
+    up_b_final = z_final(spot, sent, side4)
     side5, middle5 = z_swap(send5), z_middle(half4)
     result_parts, half4 = fence_list(result_parts, half4)
     layer_out, grad_tokens, sums = end(
@@ -1111,81 +1301,59 @@
         qkv_bias_sum,
         up_bias_sum,
     )
-    for mask_bit in (1, 2, 4):
-        (sums,) = add_all([sums], [swap(sums, mask_bit)])
+    (sums,) = add_all([sums], [swap(sums, 1)])
+    sums = sum_all(from_chips([sums] * CHIPS))
     if groups > 1:
         sums = lax.psum(sums, "fsdp", axis_index_groups=shard_groups)
     sums_got = z_swap(sums)
-
-    side5, middle5, sums_got = fence(side5, middle5, sums_got)
-    z = z_step(
-        spot,
-        dict(
-            got_side=side5,
-            got_middle=middle5,
-            low=down_b,
-            half_before=half4,
-            sent_before=send5,
-        ),
-        ("half", "send", "final"),
-    )
-    half5, send6, qkv_a_final = z["half"], z["send"], z["final"]
+    up_a_final, _ = fence(up_a_final, sums)
+    up_ready = up_exchange(spot, up_a_final, up_b_final)
+
+    side5, middle5, sums_got, _ = fence(side5, middle5, sums_got, up_ready[0])
+    half5 = z_half(down_b, side5)
+    middle5, _ = fence(middle5, half5)
+    send6 = z_half(half4, middle5)
+    sent, _ = fence(send5, send6)
+    qkv_ready, rows_ready = qkv_unpack(spot, sent, side5)
     side6, middle6 = z_swap(send6), z_middle(half5)
-    up_a_final, half5 = fence(up_a_final, half5)
-    up_total = from_chips(up_exchange(spot, up_a_final, up_b_final))
+    up_ready, _ = fence_list(up_ready, send6)
+    up_total = from_chips(up_ready)
     (sums,) = add_all([sums], [sums_got])
 
     up_total, side6, middle6, sums = fence_list(up_total, side6, middle6, sums)
-    z = z_step(
-        spot,
-        dict(got_side=side6, got_middle=middle6, half_before=half5, sent_before=send6),
-        ("send", "final"),
-    )
-    send7, qkv_b_final = z["send"], z["final"]
+    middle6, _ = fence(middle6, side6)
+    send7 = z_half(half5, middle6)
     side7 = along_z([(1, 0), (2, 3)], send7)
-    qkv_a_final, send7, sums = fence(qkv_a_final, send7, sums)
-    qkv_last, out_grad = qkv_exchange(spot, qkv_a_final, qkv_b_final)
+    sent, send7, sums = fence(send6, send7, sums)
+    qkv_last, out_grad = qkv_exchange(spot, qkv_ready, rows_ready, sent, side6)
     qkv_total = from_chips(qkv_last)
     sums_got = along_z([(z, z ^ 2) for z in range(4)], sums)
     up_grad = up_rows(spot, up_total)
-    qkv_total, side7, up_grad = fence_list(qkv_total, side7, up_grad)
-    down_grad, qkv_grad = last(spot, down_a_final, send7, side7, qkv_total)
-    (sums,) = add_all([sums], [sums_got])
-
-    index = lax.axis_index("fsdp")
-    size = D // fsdp_count
-
-    def owned(row):
-        return lax.dynamic_slice(sums, (row, index * size), (1, size)).reshape(size)
-
-    def owned_at(row, width, share):
-        start = index * share
-        return lax.dynamic_slice(sums, (row + start // width, start % width), (1, share)).reshape(
-            share
-        )
-
-    moments = sums[6:8] / (CELLS_DEV * dp_count * fsdp_count)
-    cls_mean = moments[0]
-    cls_var = moments[1] - cls_mean * cls_mean
+    place_in = jnp.stack([lax.axis_index("fsdp")]).astype(jnp.int32)
+    vectors = list(owned(place_in, CELLS_DEV * dp_count * fsdp_count, fsdp_count, sums, sums_got))
+    qkv_total, up_grad, vectors[0] = fence_list(qkv_total, up_grad, vectors[0])
+    qkv_grad = qkv_rows(spot, qkv_total)
+    side7, qkv_grad = fence(side7, qkv_grad)
+    down_grad = second_down(spot, send7, side7, down_grad)
 
     return (
         layer_out,
         grad_tokens,
-        owned(0),
-        owned(1),
+        vectors[0],
+        vectors[1],
         scatter_shards(qkv_grad),
-        owned_at(8, D_CHIP, size),
-        owned_at(12, D_CHIP, size),
+        vectors[6],
+        vectors[7],
         scatter_shards(out_grad),
-        owned(2),
-        owned(3),
-        owned(4),
+        vectors[2],
+        vectors[3],
+        vectors[4],
         scatter_shards(up_grad),
-        owned_at(16, FF_CHIP, FF // fsdp_count),
+        vectors[8],
         scatter_shards(down_grad),
-        owned(5),
-        cls_mean,
-        cls_var,
+        vectors[5],
+        vectors[9],
+        vectors[10],
     )
 
 

time: 308 us -> 282 us (0.916)
  waiting for transfers between devices: 151 us -> 126 us
  local copies, waits for them, and re-layouts: 14.4 us -> 0.79 us
  starting transfers between devices: 76.6 us -> 84 us
  Pallas kernels: 63.6 us -> 69.4 us
    ppermute x49 -> x52, waiting for transfers between devices: 140 us -> 89.4 us  [swap(): return lax.ppermute(value, 'fsdp', pairs)]
    ppermute x18 -> x19, waiting for transfers between devices: 11 us -> 36.2 us  [along_z(): return lax.ppermute(value, 'dp', pairs)]
    unnamed x58 -> x14, local copies, waits for them, and re-layouts: 13 us -> 0.79 us
    pallas_call x35 -> x50, Pallas kernels: 63.6 us -> 69.4 us  [the longest x46 60.6 us: run(): return made(*placed)]
    ppermute x49 -> x52, starting transfers between devices: 43.6 us -> 49.3 us  [swap(): return lax.ppermute(value, 'fsdp', pairs)]
    ppermute x18 -> x19, starting transfers between devices: 33.1 us -> 34.7 us  [along_z(): return lax.ppermute(value, 'dp', pairs)]
  transfers between devices with their start and end apart: 67 -> 71, of which waited for: 36 -> 33; matrix products, arithmetic and copies ran while one was open for 1% -> 0% of each run, Pallas kernels for 12% -> 21%
where the time goes in v3:
time: 282 us; the launch traced here: 281 us
  waiting for transfers between devices  126 us (45%)
  starting transfers between devices  84 us (30%)
  Pallas kernels  69.4 us (25%)
    ppermute x52, waiting for transfers between devices, swap(): return lax.ppermute(value, 'fsdp', pairs)  89.4 us
    pallas_call x46, Pallas kernels, run(): return made(*placed)  60.6 us
    ppermute x52, starting transfers between devices, swap(): return lax.ppermute(value, 'fsdp', pairs)  49.3 us
    ppermute x19, waiting for transfers between devices, along_z(): return lax.ppermute(value, 'dp', pairs)  36.2 us
    ppermute x19, starting transfers between devices, along_z(): return lax.ppermute(value, 'dp', pairs)  34.7 us
  transfers between devices with their start and end apart: 71, of which 33 were waited for; matrix products, arithmetic and copies ran while one was open for 0% of the time, Pallas kernels for 21%

profile of v3, /device:TPU:0, one launch (start us, length us, event | category | flops | bytes accessed | tf_op | source)
XLA Modules:
  0.0 281.3 jit_solution(13805348427104713810)
XLA Ops:
  0.7 3.0 %collective-permute-start.1 = (bf16[128,1280]{1,0:T(8,128)(2,1)}, bf16[128,1280]{1,0:T(8,128)(2,1)S(1)}, u32[]{:S(2)}, u32[]{:S(2)}) collective-permute-start(bf16[128,1280]{1,0:T(8,128)(2,1)} %tokens.3), channel_id=1, source_target_pairs={{0,4},{1,5},{2,6},{3,7},{4,0},{5,1},{6,2},{7,3},{8,12},{9,13},{10,... | collective-permute-start | bytes 983048 | tf_op jit(solution)/shard_map/ppermute | solution.py:1127
  5.9 2.7 qkv_blocks.1
  9.4 2.9 %collective-permute-start.4 = (bf16[96,960]{1,0:T(8,128)(2,1)S(1)}, bf16[96,960]{1,0:T(8,128)(2,1)S(1)}, u32[]{:S(2)}, u32[]{:S(2)}) collective-permute-start(bf16[96,960]{1,0:T(8,128)(2,1)S(1)} %get-tuple-element.259), channel_id=1, source_target_pairs={{0,6},{1,7},{2,4},{3,5},{4,2},{5,3},{6,0},{7,1},{8,14},{9,15},{10,... | collective-permute-start | bytes 552968 | tf_op jit(solution)/shard_map/ppermute | solution.py:1127
  12.2 6.5 %collective-permute-done.2.q1 = bf16[96,960]{1,0:T(8,128)(2,1)S(1)} collective-permute-done((bf16[96,960]{1,0:T(8,128)(2,1)S(1)}, bf16[96,960]{1,0:T(8,128)(2,1)S(1)}, u32[]{:S(2)}, u32[]{:S(2)}) %collective-permute-start.2) | collective-permute-done | bytes 184352 | tf_op jit(solution)/shard_map/ppermute | solution.py:1127
  28.4 5.4 %collective-permute-done.5.x3 = bf16[128,1280]{1,0:T(8,128)(2,1)S(1)} collective-permute-done((bf16[128,1280]{1,0:T(8,128)(2,1)S(1)}, bf16[128,1280]{1,0:T(8,128)(2,1)S(1)}, u32[]{:S(2)}, u32[]{:S(2)}) %collective-permute-start.5) | collective-permute-done | bytes 327712 | tf_op jit(solution)/shard_map/ppermute | solution.py:1127
  42.1 7.3 %enter.1 = (f32[8,1280]{1,0:T(8,128)S(1)}, bf16[512,128]{1,0:T(8,128)(2,1)S(1)}, bf16[1280,960]{1,0:T(8,128)(2,1)S(1)}, bf16[320,1280]{1,0:T(8,128)(2,1)S(1)}, b...) custom-call(s32[4]{0:T(128)S(1)} %pad_add_fusion.spot, ...), custom_call_target="tpu_custom_call" | custom-call | flops 1 | bytes 1 | tf_op jit(solution)/shard_map/enter/pallas_call | solution.py:142
  53.0 7.6 %collective-permute-done.14.u2 = bf16[208,1280]{1,0:T(8,128)(2,1)S(1)} collective-permute-done((bf16[208,1280]{1,0:T(8,128)(2,1)S(1)}, bf16[208,1280]{1,0:T(8,128)(2,1)S(1)}, u32[]{:S(2)}, u32[]{:S(2)}) %collective-permute-start.14) | collective-permute-done | bytes 532512 | tf_op jit(solution)/shard_map/ppermute | solution.py:1127
  63.6 7.9 %collective-permute-done.16.refs_2_ = bf16[120,1280]{1,0:T(8,128)(2,1)S(1)} collective-permute-done((bf16[120,1280]{1,0:T(8,128)(2,1)S(1)}, bf16[120,1280]{1,0:T(8,128)(2,1)S(1)}, u32[]{:S(2)}, u32[]{:S(2)}) %collective-permute-start.16) | collective-permute-done | bytes 307232 | tf_op jit(solution)/shard_map/ppermute | solution.py:1143
  71.5 3.3 %collective-permute-done.17.refs_3_ = bf16[120,1280]{1,0:T(8,128)(2,1)S(1)} collective-permute-done((bf16[120,1280]{1,0:T(8,128)(2,1)S(1)}, bf16[120,1280]{1,0:T(8,128)(2,1)S(1)}, u32[]{:S(2)}, u32[]{:S(2)}) %collective-permute-start.17) | collective-permute-done | bytes 307232 | tf_op jit(solution)/shard_map/ppermute | solution.py:1143
  79.4 4.7 %act_grad.1 = (f32[512,1280]{1,0:T(8,128)S(1)}, bf16[1280,1280]{1,0:T(8,128)(2,1)S(1)}) custom-call(s32[4]{0:T(128)S(1)} %pad_add_fusion.spot, bf16[512,1280]{1,0:T(8,128)(2,1)S(1)} %get-tuple-element.302.whole.cotangent, bf16[640,1280]{1,0:T(8,128)(2,1)} %mine.1, bf16[640,1280]{1,0:T(8,128)(2,1)S(1)} %collective-permute-done.24.other), custom_call_target="tpu_custom_call" | custom-call | flops 1 | bytes 1 | tf_op jit(solution)/shard_map/act_grad/pallas_call | solution.py:142
  87.6 4.3 %hidden_first.1 = (bf16[512,1280]{1,0:T(8,128)(2,1)S(1)}, bf16[512,1280]{1,0:T(8,128)(2,1)S(1)}, bf16[512,1280]{1,0:T(8,128)(2,1)S(1)}, f32[1,1280]{1,0:T(1,128)S(1)}, bf16[1280,1280]{1,0:T(8,128)(2,1)S(1)}) custom-call(s32[4]{0:T(128)S(1)} %pad_add_fusion.spot, bf16[128,1280]{1,0:T(8,128)(2,1)S(1)} %get-tuple-element.299.s0, ...), custom_call_target="tpu_custom_call" | custom-call | flops 1 | bytes 1 | tf_op jit(solution)/shard_map/hidden_first/pallas_call | solution.py:142
  93.8 2.9 %hidden_last.1 = (bf16[512,1280]{1,0:T(8,128)(2,1)S(1)}, bf16[512,1280]{1,0:T(8,128)(2,1)S(1)}, bf16[512,1280]{1,0:T(8,128)(2,1)S(1)}, f32[1,1280]{1,0:T(1,128)S(1)}, bf16[320,1280]{1,0:T(8,128)(2,1)S(1)}) custom-call(s32[4]{0:T(128)S(1)} %pad_add_fusion.spot, ...), custom_call_target="tpu_custom_call", output_to_operand_aliasing={{0}: (6, {}), {1}: (7, {}), {2}: (8, {})} | custom-call | flops 1 | bytes 1 | tf_op jit(solution)/shard_map/hidden_last/pallas_call | solution.py:649
  96.8 4.2 %second_grad.1 = (bf16[128,1280]{1,0:T(8,128)(2,1)S(1)}, bf16[128,1280]{1,0:T(8,128)(2,1)S(1)}, bf16[128,1280]{1,0:T(8,128)(2,1)S(1)}, bf16[128,1280]{1,0:T(8,128)(2,1)S(1)}, bf16[320,1280]{1,0:T(8,128)(2,1)S(1)}) custom-call(s32[4]{0:T(128)S(1)} %pad_add_fusion.spot, bf16[512,1280]{1,0:T(8,128)(2,1)S(1)} %get-tuple-element.317.grad_pre, ...), custom_call_target="tpu_custom_call" | custom-call | flops 1 | bytes 1 | tf_op jit(solution)/shard_map/second_grad/pallas_call | solution.py:142
  108.0 3.9 %rest.1 = (bf16[320,1280]{1,0:T(8,128)(2,1)S(1)}, bf16[320,1280]{1,0:T(8,128)(2,1)S(1)}, bf16[320,1280]{1,0:T(8,128)(2,1)S(1)}, bf16[320,1280]{1,0:T(8,128)(2,1)S(1)}, bf16[320,1280]{1,0:T(8,128)(2,1)S(1)}) custom-call(s32[4]{0:T(128)S(1)} %pad_add_fusion.spot, bf16[512,1280]{1,0:T(8,128)(2,1)S(1)} %get-tuple-element.332.second, ...), custom_call_target="tpu_custom_call" | custom-call | flops 1 | bytes 1 | tf_op jit(solution)/shard_map/rest/pallas_call | solution.py:142
  112.1 3.0 %collective-permute-done.27.p1 = bf16[128,1280]{1,0:T(8,128)(2,1)S(1)} collective-permute-done((bf16[128,1280]{1,0:T(8,128)(2,1)S(1)}, bf16[128,1280]{1,0:T(8,128)(2,1)S(1)}, u32[]{:S(2)}, u32[]{:S(2)}) %collective-permute-start.27) | collective-permute-done | bytes 327712 | tf_op jit(solution)/shard_map/ppermute | solution.py:1127
  115.1 7.0 %collective-permute-done.28.p2 = bf16[128,1280]{1,0:T(8,128)(2,1)S(1)} collective-permute-done((bf16[128,1280]{1,0:T(8,128)(2,1)S(1)}, bf16[128,1280]{1,0:T(8,128)(2,1)S(1)}, u32[]{:S(2)}, u32[]{:S(2)}) %collective-permute-start.28) | collective-permute-done | bytes 327712 | tf_op jit(solution)/shard_map/ppermute | solution.py:1127
  133.0 5.3 %collective-permute-done.34.b3 = bf16[128,1280]{1,0:T(8,128)(2,1)S(1)} collective-permute-done((bf16[128,1280]{1,0:T(8,128)(2,1)S(1)}, bf16[128,1280]{1,0:T(8,128)(2,1)S(1)}, u32[]{:S(2)}, u32[]{:S(2)}) %collective-permute-start.34) | collective-permute-done | bytes 327712 | tf_op jit(solution)/shard_map/ppermute | solution.py:1127
  138.3 4.9 %collective-permute-done.33.b2 = bf16[128,1280]{1,0:T(8,128)(2,1)S(1)} collective-permute-done((bf16[128,1280]{1,0:T(8,128)(2,1)S(1)}, bf16[128,1280]{1,0:T(8,128)(2,1)S(1)}, u32[]{:S(2)}, u32[]{:S(2)}) %collective-permute-start.33) | collective-permute-done | bytes 327712 | tf_op jit(solution)/shard_map/ppermute | solution.py:1127
  144.2 4.2 %collective-permute-start.38 = (bf16[320,1280]{1,0:T(8,128)(2,1)S(1)}, bf16[320,1280]{1,0:T(8,128)(2,1)S(1)}, u32[]{:S(2)}, u32[]{:S(2)}) collective-permute-start(bf16[320,1280]{1,0:T(8,128)(2,1)S(1)} %z_send.4.sent), channel_id=1, source_target_pairs={{0,8},{8,0},{16,24},{24,16},{1,9},{9,1},{17,25},{25,17},{2,10},{10... | collective-permute-start | bytes 2457608 | tf_op jit(solution)/shard_map/ppermute | solution.py:1143
  149.0 6.8 %leave.1 = (bf16[512,1280]{1,0:T(8,128)(2,1)S(1)}, bf16[512,960]{1,0:T(8,128)(2,1)S(1)}, f32[1,960]{1,0:T(1,128)S(1)}, bf16[128,1280]{1,0:T(8,128)(2,1)S(1)}, bf...) custom-call(bf16[128,1280]{1,0:T(8,128)(2,1)S(1)} %get-tuple-element.365.b0, ...), custom_call_target="tpu_custom_call" | custom-call | flops 1 | bytes 1 | tf_op jit(solution)/shard_map/leave/pallas_call | solution.py:142
  155.9 3.9 %qkv_grad.1 = (bf16[2,160,960]{2,1,0:T(8,128)(2,1)S(1)}, bf16[2,160,960]{2,1,0:T(8,128)(2,1)S(1)}, bf16[4,160,960]{2,1,0:T(8,128)(2,1)S(1)}, bf16[160,1280]{1,0:T(8,128)(2,1)S(1)}, bf16[160,1280]{1,0:T(8,128)(2,1)S(1)}) custom-call(s32[4]{0:T(128)S(1)} %pad_add_fusion.spot, bf16[512,1280]{1,0:T(8,128)(2,1)S(1)} %get-tuple-element.386.first_low, ...), custom_call_target="tpu_custom_call" | custom-call | flops 1 | bytes 1 | tf_op jit(solution)/shard_map/qkv_grad/pallas_call | solution.py:142
  160.4 3.0 %collective-permute-done.42.out_got = bf16[160,1280]{1,0:T(8,128)(2,1)S(1)} collective-permute-done((bf16[160,1280]{1,0:T(8,128)(2,1)S(1)}, bf16[160,1280]{1,0:T(8,128)(2,1)S(1)}, u32[]{:S(2)}, u32[]{:S(2)}) %collective-permute-start.42) | collective-permute-done | bytes 409632 | tf_op jit(solution)/shard_map/ppermute | solution.py:1127
  167.8 3.7 %collective-permute-start.47 = (bf16[320,1280]{1,0:T(8,128)(2,1)S(1)}, bf16[320,1280]{1,0:T(8,128)(2,1)S(1)}, u32[]{:S(2)}, u32[]{:S(2)}) collective-permute-start(bf16[320,1280]{1,0:T(8,128)(2,1)S(1)} %z_send.5.sent), channel_id=1, source_target_pairs={{0,8},{8,0},{16,24},{24,16},{1,9},{9,1},{17,25},{25,17},{2,10},{10... | collective-permute-start | bytes 2457608 | tf_op jit(solution)/shard_map/ppermute | solution.py:1143
  176.0 14.4 %collective-permute-done.47.refs_1_.got_side = bf16[320,1280]{1,0:T(8,128)(2,1)S(1)} collective-permute-done((bf16[320,1280]{1,0:T(8,128)(2,1)S(1)}, bf16[320,1280]{1,0:T(8,128)(2,1)S(1)}, u32[]{:S(2)}, u32[]{:S(2)}) %collective-permute-start.47) | collective-permute-done | bytes 819232 | tf_op jit(solution)/shard_map/ppermute | solution.py:1143
  191.4 3.7 %collective-permute-start.52 = (bf16[320,1280]{1,0:T(8,128)(2,1)S(1)}, bf16[320,1280]{1,0:T(8,128)(2,1)S(1)}, u32[]{:S(2)}, u32[]{:S(2)}) collective-permute-start(bf16[320,1280]{1,0:T(8,128)(2,1)S(1)} %z_send.6.sent), channel_id=1, source_target_pairs={{0,8},{8,0},{16,24},{24,16},{1,9},{9,1},{17,25},{25,17},{2,10},{10... | collective-permute-start | bytes 2457608 | tf_op jit(solution)/shard_map/ppermute | solution.py:1143
  199.4 7.2 %collective-permute-done.49.r1 = bf16[128,1280]{1,0:T(8,128)(2,1)S(1)} collective-permute-done((bf16[128,1280]{1,0:T(8,128)(2,1)S(1)}, bf16[128,1280]{1,0:T(8,128)(2,1)S(1)}, u32[]{:S(2)}, u32[]{:S(2)}) %collective-permute-start.49) | collective-permute-done | bytes 327712 | tf_op jit(solution)/shard_map/ppermute | solution.py:1127
  206.5 6.2 %collective-permute-done.50.r2 = bf16[128,1280]{1,0:T(8,128)(2,1)S(1)} collective-permute-done((bf16[128,1280]{1,0:T(8,128)(2,1)S(1)}, bf16[128,1280]{1,0:T(8,128)(2,1)S(1)}, u32[]{:S(2)}, u32[]{:S(2)}) %collective-permute-start.50) | collective-permute-done | bytes 327712 | tf_op jit(solution)/shard_map/ppermute | solution.py:1127
  214.1 3.7 %collective-permute-start.54 = (bf16[320,1280]{1,0:T(8,128)(2,1)S(1)}, bf16[320,1280]{1,0:T(8,128)(2,1)S(1)}, u32[]{:S(2)}, u32[]{:S(2)}) collective-permute-start(bf16[320,1280]{1,0:T(8,128)(2,1)S(1)} %z_send.7.sent), channel_id=1, source_target_pairs={{0,8},{8,0},{16,24},{24,16},{1,9},{9,1},{17,25},{25,17},{2,10},{10... | collective-permute-start | bytes 2457608 | tf_op jit(solution)/shard_map/ppermute | solution.py:1143
  233.3 3.5 %collective-permute-done.60.refs_1_ = f32[16,1280]{1,0:T(8,128)S(1)} collective-permute-done((f32[16,1280]{1,0:T(8,128)S(1)}, f32[16,1280]{1,0:T(8,128)S(1)}, u32[]{:S(2)}, u32[]{:S(2)}) %collective-permute-start.60) | collective-permute-done | bytes 81952 | tf_op jit(solution)/shard_map/ppermute | solution.py:1143
  243.4 8.9 %collective-permute-done.61.b1 = bf16[160,1280]{1,0:T(8,128)(2,1)S(1)} collective-permute-done((bf16[160,1280]{1,0:T(8,128)(2,1)S(1)}, bf16[160,1280]{1,0:T(8,128)(2,1)S(1)}, u32[]{:S(2)}, u32[]{:S(2)}) %collective-permute-start.61) | collective-permute-done | bytes 409632 | tf_op jit(solution)/shard_map/ppermute | solution.py:1127
  252.3 6.1 %collective-permute-done.62.b2 = bf16[160,1280]{1,0:T(8,128)(2,1)S(1)} collective-permute-done((bf16[160,1280]{1,0:T(8,128)(2,1)S(1)}, bf16[160,1280]{1,0:T(8,128)(2,1)S(1)}, u32[]{:S(2)}, u32[]{:S(2)}) %collective-permute-start.62) | collective-permute-done | bytes 409632 | tf_op jit(solution)/shard_map/ppermute | solution.py:1127
  265.8 3.2 %collective-permute-start.69 = (f32[16,1280]{1,0:T(8,128)S(1)}, f32[16,1280]{1,0:T(8,128)S(1)}, u32[]{:S(2)}, u32[]{:S(2)}) collective-permute-start(f32[16,1280]{1,0:T(8,128)S(1)} %add.41.refs_1_), channel_id=1, source_target_pairs={{0,16},{8,24},{16,0},{24,8},{1,17},{9,25},{17,1},{25,9},{2,18},{10... | collective-permute-start | bytes 245768 | tf_op jit(solution)/shard_map/ppermute | solution.py:1143
  (175 shorter events, 114.7 us)
Async XLA Ops:
  0.7 20.6 %collective-permute-start.1 = (bf16[128,1280]{1,0:T(8,128)(2,1)}, bf16[128,1280]{1,0:T(8,128)(2,1)S(1)}, u32[]{:S(2)}, u32[]{:S(2)}) collective-permute-start(bf16[128,1280]{1,0:T(8,128)(2,1)} %tokens.3), channel_id=1, source_target_pairs={{0,4},{1,5},{2,6},{3,7},{4,0},{5,1},{6,2},{7,3},{8,12},{9,13},{10,... | collective-permute-start | bytes 983048 | tf_op jit(solution)/shard_map/ppermute | solution.py:1127
  3.7 17.6 %collective-permute-start = (bf16[128,1280]{1,0:T(8,128)(2,1)}, bf16[128,1280]{1,0:T(8,128)(2,1)S(1)}, u32[]{:S(2)}, u32[]{:S(2)}) collective-permute-start(bf16[128,1280]{1,0:T(8,128)(2,1)} %tokens.3), channel_id=1, source_target_pairs={{0,2},{1,3},{2,0},{3,1},{4,6},{5,7},{6,4},{7,5},{8,10},{9,11},{10,... | collective-permute-start | bytes 983048 | tf_op jit(solution)/shard_map/ppermute | solution.py:1127
  21.4 18.7 %collective-permute-start.8 = (bf16[400,960]{1,0:T(8,128)(2,1)S(1)}, bf16[400,960]{1,0:T(8,128)(2,1)S(1)}, u32[]{:S(2)}, u32[]{:S(2)}) collective-permute-start(bf16[400,960]{1,0:T(8,128)(2,1)S(1)} %get-tuple-element.269.refs_0_), channel_id=1, source_target_pairs={{0,1},{1,0},{2,3},{3,2},{4,5},{5,4},{6,7},{7,6},{8,9},{9,8},{10,11... | collective-permute-start | bytes 2304008 | tf_op jit(solution)/shard_map/ppermute | solution.py:1127
  33.8 17.2 %collective-permute-start.13 = (bf16[208,1280]{1,0:T(8,128)(2,1)S(1)}, bf16[208,1280]{1,0:T(8,128)(2,1)S(1)}, u32[]{:S(2)}, u32[]{:S(2)}) collective-permute-start(bf16[208,1280]{1,0:T(8,128)(2,1)S(1)} %get-tuple-element.286), channel_id=1, source_target_pairs={{0,2},{1,3},{2,0},{3,1},{4,6},{5,7},{6,4},{7,5},{8,10},{9,11},{10,... | collective-permute-start | bytes 1597448 | tf_op jit(solution)/shard_map/ppermute | solution.py:1127
  35.5 25.1 %collective-permute-start.14 = (bf16[208,1280]{1,0:T(8,128)(2,1)S(1)}, bf16[208,1280]{1,0:T(8,128)(2,1)S(1)}, u32[]{:S(2)}, u32[]{:S(2)}) collective-permute-start(bf16[208,1280]{1,0:T(8,128)(2,1)S(1)} %get-tuple-element.287), channel_id=1, source_target_pairs={{0,4},{1,5},{2,6},{3,7},{4,0},{5,1},{6,2},{7,3},{8,12},{9,13},{10,... | collective-permute-start | bytes 1597448 | tf_op jit(solution)/shard_map/ppermute | solution.py:1127
  37.0 24.4 %collective-permute-start.15 = (bf16[208,1280]{1,0:T(8,128)(2,1)S(1)}, bf16[208,1280]{1,0:T(8,128)(2,1)S(1)}, u32[]{:S(2)}, u32[]{:S(2)}) collective-permute-start(bf16[208,1280]{1,0:T(8,128)(2,1)S(1)} %get-tuple-element.288), channel_id=1, source_target_pairs={{0,6},{1,7},{2,4},{3,5},{4,2},{5,3},{6,0},{7,1},{8,14},{9,15},{10,... | collective-permute-start | bytes 1597448 | tf_op jit(solution)/shard_map/ppermute | solution.py:1127
  49.4 25.3 %collective-permute-start.18 = (bf16[128,1280]{1,0:T(8,128)(2,1)S(1)}, bf16[128,1280]{1,0:T(8,128)(2,1)S(1)}, u32[]{:S(2)}, u32[]{:S(2)}) collective-permute-start(bf16[128,1280]{1,0:T(8,128)(2,1)S(1)} %get-tuple-element.291), channel_id=1, source_target_pairs={{0,2},{1,3},{2,0},{3,1},{4,6},{5,7},{6,4},{7,5},{8,10},{9,11},{10,... | collective-permute-start | bytes 983048 | tf_op jit(solution)/shard_map/ppermute | solution.py:1127
  50.0 24.8 %collective-permute-start.19 = (bf16[128,1280]{1,0:T(8,128)(2,1)S(1)}, bf16[128,1280]{1,0:T(8,128)(2,1)S(1)}, u32[]{:S(2)}, u32[]{:S(2)}) collective-permute-start(bf16[128,1280]{1,0:T(8,128)(2,1)S(1)} %get-tuple-element.292), channel_id=1, source_target_pairs={{0,4},{1,5},{2,6},{3,7},{4,0},{5,1},{6,2},{7,3},{8,12},{9,13},{10,... | collective-permute-start | bytes 983048 | tf_op jit(solution)/shard_map/ppermute | solution.py:1127
  51.0 23.8 %collective-permute-start.20 = (bf16[128,1280]{1,0:T(8,128)(2,1)S(1)}, bf16[128,1280]{1,0:T(8,128)(2,1)S(1)}, u32[]{:S(2)}, u32[]{:S(2)}) collective-permute-start(bf16[128,1280]{1,0:T(8,128)(2,1)S(1)} %get-tuple-element.293), channel_id=1, source_target_pairs={{0,6},{1,7},{2,4},{3,5},{4,2},{5,3},{6,0},{7,1},{8,14},{9,15},{10,... | collective-permute-start | bytes 983048 | tf_op jit(solution)/shard_map/ppermute | solution.py:1127
  77.9 15.9 %collective-permute-start.21 = (bf16[128,1280]{1,0:T(8,128)(2,1)S(1)}, bf16[128,1280]{1,0:T(8,128)(2,1)S(1)}, u32[]{:S(2)}, u32[]{:S(2)}) collective-permute-start(bf16[128,1280]{1,0:T(8,128)(2,1)S(1)} %get-tuple-element.299.s0), channel_id=1, source_target_pairs={{0,6},{1,7},{2,4},{3,5},{4,2},{5,3},{6,0},{7,1},{8,14},{9,15},{10,... | collective-permute-start | bytes 983048 | tf_op jit(solution)/shard_map/ppermute | solution.py:1127
  102.8 20.2 %collective-permute-start.30 = (bf16[320,1280]{1,0:T(8,128)(2,1)S(1)}, bf16[320,1280]{1,0:T(8,128)(2,1)S(1)}, u32[]{:S(2)}, u32[]{:S(2)}) collective-permute-start(bf16[320,1280]{1,0:T(8,128)(2,1)S(1)} %down_grad.1.refs_0_), channel_id=1, source_target_pairs={{0,8},{8,0},{16,24},{24,16},{1,9},{9,1},{17,25},{25,17},{2,10},{10... | collective-permute-start | bytes 2457608 | tf_op jit(solution)/shard_map/ppermute | solution.py:1143
  106.0 16.1 %collective-permute-start.28 = (bf16[128,1280]{1,0:T(8,128)(2,1)S(1)}, bf16[128,1280]{1,0:T(8,128)(2,1)S(1)}, u32[]{:S(2)}, u32[]{:S(2)}) collective-permute-start(bf16[128,1280]{1,0:T(8,128)(2,1)S(1)} %get-tuple-element.329), channel_id=1, source_target_pairs={{0,4},{1,5},{2,6},{3,7},{4,0},{5,1},{6,2},{7,3},{8,12},{9,13},{10,... | collective-permute-start | bytes 983048 | tf_op jit(solution)/shard_map/ppermute | solution.py:1127
  111.8 17.9 %collective-permute-start.37 = (bf16[320,1280]{1,0:T(8,128)(2,1)S(1)}, bf16[320,1280]{1,0:T(8,128)(2,1)S(1)}, u32[]{:S(2)}, u32[]{:S(2)}) collective-permute-start(bf16[320,1280]{1,0:T(8,128)(2,1)S(1)} %get-tuple-element.350), channel_id=1, source_target_pairs={{0,1},{1,0},{2,3},{3,2},{4,5},{5,4},{6,7},{7,6},{8,9},{9,8},{10,11... | collective-permute-start | bytes 2457608 | tf_op jit(solution)/shard_map/ppermute | solution.py:1127
  123.3 19.9 %collective-permute-start.35 = (bf16[320,1280]{1,0:T(8,128)(2,1)S(1)}, bf16[320,1280]{1,0:T(8,128)(2,1)S(1)}, u32[]{:S(2)}, u32[]{:S(2)}) collective-permute-start(bf16[320,1280]{1,0:T(8,128)(2,1)S(1)} %add.30.refs_0_), channel_id=1, source_target_pairs={{0,8},{8,0},{16,24},{24,16},{1,9},{9,1},{17,25},{25,17},{2,10},{10... | collective-permute-start | bytes 2457608 | tf_op jit(solution)/shard_map/ppermute | solution.py:1143
  124.9 18.3 %collective-permute-start.36 = (bf16[320,1280]{1,0:T(8,128)(2,1)S(1)}, bf16[320,1280]{1,0:T(8,128)(2,1)S(1)}, u32[]{:S(2)}, u32[]{:S(2)}) collective-permute-start(bf16[320,1280]{1,0:T(8,128)(2,1)S(1)} %add.31.half), channel_id=1, source_target_pairs={{8,16},{16,8},{9,17},{17,9},{10,18},{18,10},{11,19},{19,11},{12,20... | collective-permute-start | bytes 2457608 | tf_op jit(solution)/shard_map/ppermute | solution.py:1143
  144.2 22.6 %collective-permute-start.38 = (bf16[320,1280]{1,0:T(8,128)(2,1)S(1)}, bf16[320,1280]{1,0:T(8,128)(2,1)S(1)}, u32[]{:S(2)}, u32[]{:S(2)}) collective-permute-start(bf16[320,1280]{1,0:T(8,128)(2,1)S(1)} %z_send.4.sent), channel_id=1, source_target_pairs={{0,8},{8,0},{16,24},{24,16},{1,9},{9,1},{17,25},{25,17},{2,10},{10... | collective-permute-start | bytes 2457608 | tf_op jit(solution)/shard_map/ppermute | solution.py:1143
  148.3 18.4 %collective-permute-start.39 = (bf16[320,1280]{1,0:T(8,128)(2,1)S(1)}, bf16[320,1280]{1,0:T(8,128)(2,1)S(1)}, u32[]{:S(2)}, u32[]{:S(2)}) collective-permute-start(bf16[320,1280]{1,0:T(8,128)(2,1)S(1)} %add.33.half), channel_id=1, source_target_pairs={{8,16},{16,8},{9,17},{17,9},{10,18},{18,10},{11,19},{19,11},{12,20... | collective-permute-start | bytes 2457608 | tf_op jit(solution)/shard_map/ppermute | solution.py:1143
  167.8 22.5 %collective-permute-start.47 = (bf16[320,1280]{1,0:T(8,128)(2,1)S(1)}, bf16[320,1280]{1,0:T(8,128)(2,1)S(1)}, u32[]{:S(2)}, u32[]{:S(2)}) collective-permute-start(bf16[320,1280]{1,0:T(8,128)(2,1)S(1)} %z_send.5.sent), channel_id=1, source_target_pairs={{0,8},{8,0},{16,24},{24,16},{1,9},{9,1},{17,25},{25,17},{2,10},{10... | collective-permute-start | bytes 2457608 | tf_op jit(solution)/shard_map/ppermute | solution.py:1143
  171.5 18.8 %collective-permute-start.48 = (bf16[320,1280]{1,0:T(8,128)(2,1)S(1)}, bf16[320,1280]{1,0:T(8,128)(2,1)S(1)}, u32[]{:S(2)}, u32[]{:S(2)}) collective-permute-start(bf16[320,1280]{1,0:T(8,128)(2,1)S(1)} %add.34.half), channel_id=1, source_target_pairs={{8,16},{16,8},{9,17},{17,9},{10,18},{18,10},{11,19},{19,11},{12,20... | collective-permute-start | bytes 2457608 | tf_op jit(solution)/shard_map/ppermute | solution.py:1143
  172.4 17.9 %collective-permute-start.44 = (bf16[128,1280]{1,0:T(8,128)(2,1)S(1)}, bf16[128,1280]{1,0:T(8,128)(2,1)S(1)}, u32[]{:S(2)}, u32[]{:S(2)}) collective-permute-start(bf16[128,1280]{1,0:T(8,128)(2,1)S(1)} %get-tuple-element.402), channel_id=1, source_target_pairs={{0,2},{1,3},{2,0},{3,1},{4,6},{5,7},{6,4},{7,5},{8,10},{9,11},{10,... | collective-permute-start | bytes 983048 | tf_op jit(solution)/shard_map/ppermute | solution.py:1127
  173.7 16.7 %collective-permute-start.45 = (bf16[128,1280]{1,0:T(8,128)(2,1)S(1)}, bf16[128,1280]{1,0:T(8,128)(2,1)S(1)}, u32[]{:S(2)}, u32[]{:S(2)}) collective-permute-start(bf16[128,1280]{1,0:T(8,128)(2,1)S(1)} %get-tuple-element.403), channel_id=1, source_target_pairs={{0,4},{1,5},{2,6},{3,7},{4,0},{5,1},{6,2},{7,3},{8,12},{9,13},{10,... | collective-permute-start | bytes 983048 | tf_op jit(solution)/shard_map/ppermute | solution.py:1127
  174.5 15.9 %collective-permute-start.46 = (bf16[128,1280]{1,0:T(8,128)(2,1)S(1)}, bf16[128,1280]{1,0:T(8,128)(2,1)S(1)}, u32[]{:S(2)}, u32[]{:S(2)}) collective-permute-start(bf16[128,1280]{1,0:T(8,128)(2,1)S(1)} %get-tuple-element.404), channel_id=1, source_target_pairs={{0,6},{1,7},{2,4},{3,5},{4,2},{5,3},{6,0},{7,1},{8,14},{9,15},{10,... | collective-permute-start | bytes 983048 | tf_op jit(solution)/shard_map/ppermute | solution.py:1127
  191.4 21.7 %collective-permute-start.52 = (bf16[320,1280]{1,0:T(8,128)(2,1)S(1)}, bf16[320,1280]{1,0:T(8,128)(2,1)S(1)}, u32[]{:S(2)}, u32[]{:S(2)}) collective-permute-start(bf16[320,1280]{1,0:T(8,128)(2,1)S(1)} %z_send.6.sent), channel_id=1, source_target_pairs={{0,8},{8,0},{16,24},{24,16},{1,9},{9,1},{17,25},{25,17},{2,10},{10... | collective-permute-start | bytes 2457608 | tf_op jit(solution)/shard_map/ppermute | solution.py:1143
  195.1 18.0 %collective-permute-start.53 = (bf16[320,1280]{1,0:T(8,128)(2,1)S(1)}, bf16[320,1280]{1,0:T(8,128)(2,1)S(1)}, u32[]{:S(2)}, u32[]{:S(2)}) collective-permute-start(bf16[320,1280]{1,0:T(8,128)(2,1)S(1)} %add.36.half), channel_id=1, source_target_pairs={{8,16},{16,8},{9,17},{17,9},{10,18},{18,10},{11,19},{19,11},{12,20... | collective-permute-start | bytes 2457608 | tf_op jit(solution)/shard_map/ppermute | solution.py:1143
  197.0 15.7 %collective-permute-start.50 = (bf16[128,1280]{1,0:T(8,128)(2,1)S(1)}, bf16[128,1280]{1,0:T(8,128)(2,1)S(1)}, u32[]{:S(2)}, u32[]{:S(2)}) collective-permute-start(bf16[128,1280]{1,0:T(8,128)(2,1)S(1)} %get-tuple-element.416), channel_id=1, source_target_pairs={{0,4},{1,5},{2,6},{3,7},{4,0},{5,1},{6,2},{7,3},{8,12},{9,13},{10,... | collective-permute-start | bytes 983048 | tf_op jit(solution)/shard_map/ppermute | solution.py:1127
  214.1 22.6 %collective-permute-start.54 = (bf16[320,1280]{1,0:T(8,128)(2,1)S(1)}, bf16[320,1280]{1,0:T(8,128)(2,1)S(1)}, u32[]{:S(2)}, u32[]{:S(2)}) collective-permute-start(bf16[320,1280]{1,0:T(8,128)(2,1)S(1)} %z_send.7.sent), channel_id=1, source_target_pairs={{0,8},{8,0},{16,24},{24,16},{1,9},{9,1},{17,25},{25,17},{2,10},{10... | collective-permute-start | bytes 2457608 | tf_op jit(solution)/shard_map/ppermute | solution.py:1143
  217.9 18.9 %collective-permute-start.55 = (bf16[320,1280]{1,0:T(8,128)(2,1)S(1)}, bf16[320,1280]{1,0:T(8,128)(2,1)S(1)}, u32[]{:S(2)}, u32[]{:S(2)}) collective-permute-start(bf16[320,1280]{1,0:T(8,128)(2,1)S(1)} %add.37.refs_0_), channel_id=1, source_target_pairs={{8,16},{16,8},{9,17},{17,9},{10,18},{18,10},{11,19},{19,11},{12,20... | collective-permute-start | bytes 2457608 | tf_op jit(solution)/shard_map/ppermute | solution.py:1143
  237.2 21.3 %collective-permute-start.64 = (bf16[320,1280]{1,0:T(8,128)(2,1)S(1)}, bf16[320,1280]{1,0:T(8,128)(2,1)S(1)}, u32[]{:S(2)}, u32[]{:S(2)}) collective-permute-start(bf16[320,1280]{1,0:T(8,128)(2,1)S(1)} %add.40.sent), channel_id=1, source_target_pairs={{0,8},{8,0},{16,24},{24,16},{1,9},{9,1},{17,25},{25,17},{2,10},{10... | collective-permute-start | bytes 2457608 | tf_op jit(solution)/shard_map/ppermute | solution.py:1143
  239.1 19.3 %collective-permute-start.65 = (bf16[320,1280]{1,0:T(8,128)(2,1)S(1)}, bf16[320,1280]{1,0:T(8,128)(2,1)S(1)}, u32[]{:S(2)}, u32[]{:S(2)}) collective-permute-start(bf16[320,1280]{1,0:T(8,128)(2,1)S(1)} %add.39.refs_0_), channel_id=1, source_target_pairs={{8,16},{16,8},{9,17},{17,9},{10,18},{18,10},{11,19},{19,11},{12,20... | collective-permute-start | bytes 2457608 | tf_op jit(solution)/shard_map/ppermute | solution.py:1143
  241.0 17.4 %collective-permute-start.62 = (bf16[160,1280]{1,0:T(8,128)(2,1)S(1)}, bf16[160,1280]{1,0:T(8,128)(2,1)S(1)}, u32[]{:S(2)}, u32[]{:S(2)}) collective-permute-start(bf16[160,1280]{1,0:T(8,128)(2,1)S(1)} %get-tuple-element.457), channel_id=1, source_target_pairs={{0,4},{1,5},{2,6},{3,7},{4,0},{5,1},{6,2},{7,3},{8,12},{9,13},{10,... | collective-permute-start | bytes 1228808 | tf_op jit(solution)/shard_map/ppermute | solution.py:1127
  241.9 16.5 %collective-permute-start.63 = (bf16[160,1280]{1,0:T(8,128)(2,1)S(1)}, bf16[160,1280]{1,0:T(8,128)(2,1)S(1)}, u32[]{:S(2)}, u32[]{:S(2)}) collective-permute-start(bf16[160,1280]{1,0:T(8,128)(2,1)S(1)} %get-tuple-element.458), channel_id=1, source_target_pairs={{0,6},{1,7},{2,4},{3,5},{4,2},{5,3},{6,0},{7,1},{8,14},{9,15},{10,... | collective-permute-start | bytes 1228808 | tf_op jit(solution)/shard_map/ppermute | solution.py:1127
  258.6 20.7 %collective-permute-start.70 = (bf16[320,1280]{1,0:T(8,128)(2,1)S(1)}, bf16[320,1280]{1,0:T(8,128)(2,1)S(1)}, u32[]{:S(2)}, u32[]{:S(2)}) collective-permute-start(bf16[320,1280]{1,0:T(8,128)(2,1)S(1)} %add.42.sent), channel_id=1, source_target_pairs={{8,0},{16,24},{9,1},{17,25},{10,2},{18,26},{11,3},{19,27},{12,4},{... | collective-permute-start | bytes 2457608 | tf_op jit(solution)/shard_map/ppermute | solution.py:1143
  (46 other events, 413.1 us)

commit v4 on v3

--- a/solution.py
+++ b/solution.py
@@ -117,7 +117,7 @@
 
 
 HALF = SHARE // 2
-EXTRA = 16
+EXTRA = 8
 ROWS_Z = 2 * SHARE
 
 
@@ -262,67 +262,77 @@
     )(spot, lengths, padding, weights, *vectors)
 
 
-def qkv_join_kernel(own, q1, q2, q3, near, near_half, extras):
+def qkv_join_kernel(own, q1, q2, q3, x1, x2, near, near_half, first, second):
+    size = first.shape[0]
+    first[...] = x1[:size, :]
+    second[...] = x2[size:, :]
     near[:SHARE, :] = own[:SHARE, :]
-    extras[:EXTRA, :] = own[SHARE:, :]
+    low = SHARE + 3 * HALF
+    near[low : low + EXTRA, :] = own[SHARE:, :]
     for i, block in enumerate((q1, q2, q3)):
         near[SHARE + i * HALF : SHARE + (i + 1) * HALF, :] = block[:HALF, :]
         near_half[i * HALF : (i + 1) * HALF, :] = block[:HALF, :]
-        extras[(i + 1) * EXTRA : (i + 2) * EXTRA, :] = block[HALF:, :]
-
-
-def qkv_join(blocks):
+        low += EXTRA
+        near[low : low + EXTRA, :] = block[HALF:, :]
+
+
+def qkv_join(blocks, x1, x2):
     width = blocks[0].shape[-1]
+    half = ((x1.shape[0] // 2, x1.shape[1]), x1.dtype)
     return call(
         qkv_join_kernel,
         "qkv_join",
-        "vvvv",
+        "v" * 6,
         [
-            ((SHARE + 3 * HALF, width), bf16),
+            ((SHARE + 3 * HALF + CHIPS * EXTRA, width), bf16),
             ((3 * HALF, width), bf16),
-            ((CHIPS * EXTRA, width), bf16),
+            half,
+            half,
         ],
-    )(*blocks)
+    )(*blocks, x1, x2)
 
 
 def up_blocks_kernel(spot, weights, cotangent, own, *sent):
     def columns(chip):
         return pl.ds(pl.multiple_of(chip * FF_CHIP, FF_CHIP), FF_CHIP)
 
-    rows = cotangent.shape[0]
     own[...] = weights[:, columns(spot[0])]
     for i, block in enumerate(sent):
-        block[:rows, :] = cotangent[...]
-        block[rows:, :] = weights[row_at(spot[2], HALF), columns(spot[0] ^ (i + 1))]
+        block[:HALF, :] = weights[row_at(spot[2], HALF), columns(spot[0] ^ (i + 1))]
+    for block in sent[:2]:
+        block[HALF:, :] = cotangent[...]
 
 
 def up_blocks(spot, weights, cotangent):
-    half = ((cotangent.shape[0] + HALF, FF_CHIP), bf16)
-    return call(
-        up_blocks_kernel, "up_blocks", "svv", [((SHARE, FF_CHIP), bf16)] + [half] * (CHIPS - 1)
-    )(spot, weights, cotangent)
-
-
-def up_join_kernel(cotangent, u1, u2, u3, half_a, half_b, whole):
+    both = HALF + cotangent.shape[0]
+    sizes = (SHARE, both, both, HALF)
+    return call(up_blocks_kernel, "up_blocks", "svv", [((size, FF_CHIP), bf16) for size in sizes])(
+        spot, weights, cotangent
+    )
+
+
+def up_join_kernel(cotangent, u1, u2, u3, half_a, half_b, whole, first, second):
     rows = cotangent.shape[0]
-    whole[:rows, :] = cotangent[...]
+    for i, block in enumerate((cotangent, u1.at[HALF:], u2.at[HALF:])):
+        whole[i * rows : (i + 1) * rows, :] = block[...]
+    near = jnp.concatenate([block[:HALF, :] for block in (u1, u2, u3)], axis=0)
     size = half_a.shape[0]
-    near = []
-    for i, block in enumerate((u1, u2, u3)):
-        near.append(block[rows:, :])
-        whole[(i + 1) * rows : (i + 2) * rows, :] = block[:rows, :]
-    near = jnp.concatenate(near, axis=0)
     half_a[...] = near[:size]
     half_b[...] = near[size:]
+    half = rows // 2
+    first[...] = u1[HALF : HALF + half, :]
+    second[...] = u2[HALF + half :, :]
 
 
 def up_join(cotangent, blocks):
+    rows = cotangent.shape[0]
     half = ((3 * HALF // 2, FF_CHIP), bf16)
+    passed = ((rows // 2, D), bf16)
     return call(
         up_join_kernel,
         "up_join",
         "vvvv",
-        [half, half, ((CHIPS * cotangent.shape[0], D), bf16)],
+        [half, half, (((CHIPS - 1) * rows, D), bf16), passed, passed],
     )(cotangent, *blocks)
 
 
@@ -375,19 +385,23 @@
         mask[i * rows : (i + 1) * rows, :] = keep.astype(bf16)
 
 
-def token_norm_kernel(x0, x1, x2, x3, normed):
-    rows = x0.shape[0]
-    for i, x in enumerate((x0, x1, x2, x3)):
-        normed[i * rows : (i + 1) * rows, :] = normalize(x[...].astype(f32))[0]
+def token_norm_kernel(*refs):
+    blocks, normed = refs[:-1], refs[-1]
+    at = 0
+    for x in blocks:
+        rows = x.shape[0]
+        normed[at : at + rows, :] = normalize(x[...].astype(f32))[0]
+        at += rows
 
 
 def token_norm(blocks):
     rows, width = blocks[0].shape
-    return call(token_norm_kernel, "token_norm", "vvvv", [((CHIPS * rows, width), f32)])(*blocks)[0]
+    shape = (CHIPS * rows, width)
+    return call(token_norm_kernel, "token_norm", "v" * len(blocks), [(shape, f32)])(*blocks)[0]
 
 
 def enter_kernel(spot, normed, *refs):
-    mine, other, refs = refs[:3], refs[3:6], refs[6:]
+    mine, other, refs = refs[:2], refs[2:4], refs[4:]
     out_mine, out_other, refs = *refs[:2], refs[2:]
     table, mask, qkv, out, first_low, projected, context = refs[:7]
     partials = refs[7 : 7 + CHIPS]
@@ -395,11 +409,13 @@
     rows = mask.shape[1]
     out_copies = by_core_copies(spot[1], out_mine, out_other, out, out_sems)
     start_all(out_copies)
-    for of_core, lines in ((spot[1], mine[2]), (1 - spot[1], other[2])):
+    low = SHARE + 3 * HALF
+    for of_core, lines in ((spot[1], mine[0]), (1 - spot[1], other[0])):
         for i in range(CHIPS):
-            extras[2 * (spot[0] ^ i) + of_core] = lines[i * EXTRA : (i + 1) * EXTRA, :].astype(f32)
+            at = slice(low + i * EXTRA, low + (i + 1) * EXTRA)
+            extras[2 * (spot[0] ^ i) + of_core] = lines[at, :].astype(f32)
     fill_table(spot, extras, table, mask)
-    columns = [(near, near.at[SHARE:], far) for near, far, _ in (mine, other)]
+    columns = [(near, near.at[SHARE:], far) for near, far in (mine, other)]
     stack_columns(spot, *columns, qkv)
     gain = table[GAIN1 : GAIN1 + 1, :]
     bias = table[BIAS1 : BIAS1 + 1, :]
@@ -429,7 +445,7 @@
     outs = call(
         enter_kernel,
         "enter",
-        "sv" + "v" * 6 + "hv",
+        "sv" + "v" * 4 + "hv",
         [
             ((TABLE_ROWS, D), f32),
             ((total, rows), bf16),
@@ -526,9 +542,13 @@
     )(*parts, mixed, table, cotangent)
 
 
-def act_grad_kernel(spot, whole, mine, other, grad_act, down, down_sems):
+def act_grad_kernel(spot, part, g1, g2, mine, other, grad_act, down, whole, down_sems):
     copies = by_core_copies(spot[1], mine, other, down, down_sems)
     start_all(copies)
+    at = 0
+    for block in (part, g1, g2):
+        whole[at : at + block.shape[0], :] = block[...]
+        at += block.shape[0]
     wait_all(copies)
 
     def columns(at):
@@ -537,14 +557,15 @@
     tiled(FF_CHIP, 256, columns)
 
 
-def act_grad(spot, cotangent, down_mine, down_other):
+def act_grad(spot, part, passed, down_mine, down_other):
+    total = part.shape[0] // (CHIPS - 1) * CHIPS
     return call(
         act_grad_kernel,
         "act_grad",
-        "svhv",
-        [((cotangent.shape[0], FF_CHIP), f32), ((FF_CHIP, D), bf16)],
+        "svvvhv",
+        [((total, FF_CHIP), f32), ((FF_CHIP, D), bf16), ((total, D), bf16)],
         [sems(2)],
-    )(spot, cotangent, down_mine, down_other)
+    )(spot, part, *passed, down_mine, down_other)
 
 
 def hidden_rows(at, second, up, table, grad_act, pre_act, act, grad_pre, bias_sum):
@@ -846,8 +867,16 @@
 
 
 def z_send_kernel(spot, half, got_middle, low, sent):
-    whole = (half[...].astype(f32) + got_middle[...].astype(f32)).astype(bf16)
-    sent[...] = jnp.where(spot[3] > 0, whole, low[...])
+    middle = spot[3] > 0
+
+    @pl.when(middle)
+    def _():
+        whole = half[...].astype(f32) + got_middle[...].astype(f32)
+        sent[...] = whole.astype(bf16)
+
+    @pl.when(jnp.logical_not(middle))
+    def _():
+        sent[...] = low[...]
 
 
 def z_send(spot, half, got_middle, low):
@@ -1160,45 +1189,43 @@
     qkv_sent = qkv_blocks(spot, lengths, padding, w_qkv, [gather_shards(v) for v in given])
     qkv_got = from_chips(qkv_sent)
     x1, x2, *qkv_got = fence(swap(tokens, 2), swap(tokens, 4), *qkv_got)
-    qkv_near, qkv_half, extras = qkv_join(qkv_got)
+    qkv_near, qkv_half, x1_half, x2_half = qkv_join(qkv_got, x1, x2)
     qkv_far = z_swap(qkv_half)
-    qkv_near_other, extras_other = swap(qkv_near, 1), swap(extras, 1)
-    tokens_sent, extras = fence(tokens, extras)
-    blocks = [tokens, x1, x2, swap(tokens_sent, 6)]
+    qkv_near_other = swap(qkv_near, 1)
+    blocks = [tokens, x1, x2, swap(x1_half, 4), swap(x2_half, 2)]
     normed = token_norm(blocks)
-    out_sent, _ = fence(w_out, extras)
+    out_sent, _ = fence(w_out, qkv_near)
     out_other = swap(out_sent, 1)
     up_own, *up_sent = up_blocks(spot, w_up, cotangent)
-    up_own, *up_sent = fence(up_own, *up_sent, extras)[:-1]
-    up_own_other = swap(up_own, 1)
+    up_own, *up_sent = fence(up_own, *up_sent, qkv_near)[:-1]
     loads = [swap(block, 2 * i + 2) for i, block in enumerate(up_sent)]
-    normed, qkv_far, extras_other, qkv_near_other, out_other, up_own_other = fence(
-        normed, qkv_far, extras_other, qkv_near_other, out_other, up_own_other
-    )
+    normed, qkv_far, qkv_near_other, out_other = fence(normed, qkv_far, qkv_near_other, out_other)
     qkv_far_other = join([swap(half, 1) for half in halves(qkv_far)])
 
     (table, mask, qkv, out, first_low, projected, context), partial_out = enter(
         spot,
         normed,
-        [qkv_near, qkv_far, extras],
-        [qkv_near_other, qkv_far_other, extras_other],
+        [qkv_near, qkv_far],
+        [qkv_near_other, qkv_far_other],
         w_out,
         out_other,
     )
     out_parts = from_chips(partial_out)
     cotangent_late, _ = fence(cotangent, partial_out[0])
-    up_half_a, up_half_b, whole_cotangent = up_join(cotangent_late, loads)
+    up_half_a, up_half_b, part, first, second = up_join(cotangent_late, loads)
     up_far = [z_swap(up_half_a), z_swap(up_half_b)]
-    up_far, *out_parts = fence_list(up_far, *out_parts)
+    passed = [swap(first, 4), swap(second, 2)]
+    passed, up_far[0], up_far[1], *out_parts = fence_list(passed, *up_far, *out_parts)
     mixed, second_own = mix(out_parts, tokens, table)
     second_blocks = from_chips([second_own] * CHIPS)
     up_far, _ = fence_list(up_far, second_own)
     up_rest = join([up_half_a, up_half_b] + up_far)
-    up_other = [up_own_other, swap(up_rest, 1)]
+    up_own_sent, _ = fence(up_own, second_own)
+    up_other = [swap(up_own_sent, 1), swap(up_rest, 1)]
     down_sent, _ = fence(w_down, second_own)
     down_other = swap(down_sent, 1)
-    whole_cotangent, down_other = fence(whole_cotangent, down_other)
-    grad_act, down = act_grad(spot, whole_cotangent, w_down, down_other)
+    part, down_other = fence(part, down_other)
+    grad_act, down, whole_cotangent = act_grad(spot, part, passed, w_down, down_other)
 
     second_low, act_low, grad_pre, up_bias_sum, up = hidden_first(
         spot,

time: 282 us -> 275 us (0.975)
  waiting for transfers between devices: 126 us -> 116 us
  starting transfers between devices: 84 us -> 87.2 us
    ppermute x52 -> x54, waiting for transfers between devices: 89.4 us -> 76.4 us  [swap(): return lax.ppermute(value, 'fsdp', pairs)]
    ppermute x19, waiting for transfers between devices: 36.2 us -> 39.9 us  [along_z(): return lax.ppermute(value, 'dp', pairs)]
    ppermute x52 -> x54, starting transfers between devices: 49.3 us -> 50.9 us  [swap(): return lax.ppermute(value, 'fsdp', pairs)]
  transfers between devices with their start and end apart: 71 -> 73, of which waited for: 33 -> 35; matrix products, arithmetic and copies ran while one was open for 0% -> 0% of each run, Pallas kernels for 21% -> 22%
where the time goes in v4:
time: 275 us; the launch traced here: 274 us
  waiting for transfers between devices  116 us (42%)
  starting transfers between devices  87.2 us (32%)
  Pallas kernels  68.8 us (25%)
    ppermute x54, waiting for transfers between devices, swap(): return lax.ppermute(value, 'fsdp', pairs)  76.4 us
    pallas_call x46, Pallas kernels, run(): return made(*placed)  60 us
    ppermute x54, starting transfers between devices, swap(): return lax.ppermute(value, 'fsdp', pairs)  50.9 us
    ppermute x19, waiting for transfers between devices, along_z(): return lax.ppermute(value, 'dp', pairs)  39.9 us
    ppermute x19, starting transfers between devices, along_z(): return lax.ppermute(value, 'dp', pairs)  36.3 us
  transfers between devices with their start and end apart: 73, of which 35 were waited for; matrix products, arithmetic and copies ran while one was open for 0% of the time, Pallas kernels for 22%

profile of v4, /device:TPU:0, one launch (start us, length us, event | category | flops | bytes accessed | tf_op | source)
XLA Modules:
  0.0 274.4 jit_solution(10365300613838377522)
XLA Ops:
  0.7 3.0 %collective-permute-start.1 = (bf16[128,1280]{1,0:T(8,128)(2,1)}, bf16[128,1280]{1,0:T(8,128)(2,1)S(1)}, u32[]{:S(2)}, u32[]{:S(2)}) collective-permute-start(bf16[128,1280]{1,0:T(8,128)(2,1)} %tokens.3), channel_id=1, source_target_pairs={{0,4},{1,5},{2,6},{3,7},{4,0},{5,1},{6,2},{7,3},{8,12},{9,13},{10,... | collective-permute-start | bytes 983048 | tf_op jit(solution)/shard_map/ppermute | solution.py:1156
  5.9 2.9 %qkv_blocks.1 = (bf16[168,960]{1,0:T(8,128)(2,1)S(1)}, bf16[88,960]{1,0:T(8,128)(2,1)S(1)}, bf16[88,960]{1,0:T(8,128)(2,1)S(1)}, bf16[88,960]{1,0:T(8,128)(2,1)S(1)}) custom-call(s32[4]{0:T(128)S(1)} %pad_add_fusion.spot, s32[1,2]{1,0:T(1,128)S(1)} %copy-done.3, s32[128]{0:T(128)} %padding.1, bf16[160,3840]{1,0:T(8,128)(2,1)} %weights.2, ...), custom_call_target="tpu_custom_call" | custom-call | flops 1 | bytes 1 | tf_op jit(solution)/shard_map/qkv_blocks/pallas_call | solution.py:142
  9.5 2.9 %collective-permute-start.4 = (bf16[88,960]{1,0:T(8,128)(2,1)S(1)}, bf16[88,960]{1,0:T(8,128)(2,1)S(1)}, u32[]{:S(2)}, u32[]{:S(2)}) collective-permute-start(bf16[88,960]{1,0:T(8,128)(2,1)S(1)} %get-tuple-element.262), channel_id=1, source_target_pairs={{0,6},{1,7},{2,4},{3,5},{4,2},{5,3},{6,0},{7,1},{8,14},{9,15},{10,... | collective-permute-start | bytes 506888 | tf_op jit(solution)/shard_map/ppermute | solution.py:1156
  12.4 6.0 %collective-permute-done.2.q1 = bf16[88,960]{1,0:T(8,128)(2,1)S(1)} collective-permute-done((bf16[88,960]{1,0:T(8,128)(2,1)S(1)}, bf16[88,960]{1,0:T(8,128)(2,1)S(1)}, u32[]{:S(2)}, u32[]{:S(2)}) %collective-permute-start.2) | collective-permute-done | bytes 168992 | tf_op jit(solution)/shard_map/ppermute | solution.py:1156
  31.4 5.7 %collective-permute-done.7.whole.refs_1_ = bf16[240,960]{1,0:T(8,128)(2,1)S(1)} collective-permute-done((bf16[240,960]{1,0:T(8,128)(2,1)S(1)}, bf16[240,960]{1,0:T(8,128)(2,1)S(1)}, u32[]{:S(2)}, u32[]{:S(2)}) %collective-permute-start.7) | collective-permute-done | bytes 460832 | tf_op jit(solution)/shard_map/ppermute | solution.py:1172
  39.0 7.3 %enter.1 = (f32[8,1280]{1,0:T(8,128)S(1)}, bf16[512,128]{1,0:T(8,128)(2,1)S(1)}, bf16[1280,960]{1,0:T(8,128)(2,1)S(1)}, bf16[320,1280]{1,0:T(8,128)(2,1)S(1)}, b...) custom-call(s32[4]{0:T(128)S(1)} %pad_add_fusion.spot, ...), custom_call_target="tpu_custom_call" | custom-call | flops 1 | bytes 1 | tf_op jit(solution)/shard_map/enter/pallas_call | solution.py:142
  57.3 6.9 %collective-permute-done.17.refs_2_ = bf16[120,1280]{1,0:T(8,128)(2,1)S(1)} collective-permute-done((bf16[120,1280]{1,0:T(8,128)(2,1)S(1)}, bf16[120,1280]{1,0:T(8,128)(2,1)S(1)}, u32[]{:S(2)}, u32[]{:S(2)}) %collective-permute-start.17) | collective-permute-done | bytes 307232 | tf_op jit(solution)/shard_map/ppermute | solution.py:1172
  64.2 3.3 %collective-permute-done.18.refs_3_ = bf16[120,1280]{1,0:T(8,128)(2,1)S(1)} collective-permute-done((bf16[120,1280]{1,0:T(8,128)(2,1)S(1)}, bf16[120,1280]{1,0:T(8,128)(2,1)S(1)}, u32[]{:S(2)}, u32[]{:S(2)}) %collective-permute-start.18) | collective-permute-done | bytes 307232 | tf_op jit(solution)/shard_map/ppermute | solution.py:1172
  73.3 4.7 %act_grad.1 = (f32[512,1280]{1,0:T(8,128)S(1)}, bf16[1280,1280]{1,0:T(8,128)(2,1)S(1)}, bf16[512,1280]{1,0:T(8,128)(2,1)S(1)}) custom-call(s32[4]{0:T(128)S(1)} %pad_add_fusion.spot, bf16[384,1280]{1,0:T(8,128)(2,1)S(1)} %get-tuple-element.304.part, bf16[64,1280]{1,0:T(8,128)(2,1)S(1)} %collective-permute-done.15.g1, ...), custom_call_target="tpu_custom_call" | custom-call | flops 1 | bytes 1 | tf_op jit(solution)/shard_map/act_grad/pallas_call | solution.py:142
  80.4 4.3 %hidden_first.1 = (bf16[512,1280]{1,0:T(8,128)(2,1)S(1)}, bf16[512,1280]{1,0:T(8,128)(2,1)S(1)}, bf16[512,1280]{1,0:T(8,128)(2,1)S(1)}, f32[1,1280]{1,0:T(1,128)S(1)}, bf16[1280,1280]{1,0:T(8,128)(2,1)S(1)}) custom-call(s32[4]{0:T(128)S(1)} %pad_add_fusion.spot, bf16[128,1280]{1,0:T(8,128)(2,1)S(1)} %get-tuple-element.301.s0, ...), custom_call_target="tpu_custom_call" | custom-call | flops 1 | bytes 1 | tf_op jit(solution)/shard_map/hidden_first/pallas_call | solution.py:142
  84.7 2.9 %collective-permute-done.22.s3 = bf16[128,1280]{1,0:T(8,128)(2,1)S(1)} collective-permute-done((bf16[128,1280]{1,0:T(8,128)(2,1)S(1)}, bf16[128,1280]{1,0:T(8,128)(2,1)S(1)}, u32[]{:S(2)}, u32[]{:S(2)}) %collective-permute-start.22) | collective-permute-done | bytes 327712 | tf_op jit(solution)/shard_map/ppermute | solution.py:1156
  87.6 2.9 %hidden_last.1 = (bf16[512,1280]{1,0:T(8,128)(2,1)S(1)}, bf16[512,1280]{1,0:T(8,128)(2,1)S(1)}, bf16[512,1280]{1,0:T(8,128)(2,1)S(1)}, f32[1,1280]{1,0:T(1,128)S(1)}, bf16[320,1280]{1,0:T(8,128)(2,1)S(1)}) custom-call(s32[4]{0:T(128)S(1)} %pad_add_fusion.spot, ...), custom_call_target="tpu_custom_call", output_to_operand_aliasing={{0}: (6, {}), {1}: (7, {}), {2}: (8, {})} | custom-call | flops 1 | bytes 1 | tf_op jit(solution)/shard_map/hidden_last/pallas_call | solution.py:670
  90.6 4.2 %second_grad.1 = (bf16[128,1280]{1,0:T(8,128)(2,1)S(1)}, bf16[128,1280]{1,0:T(8,128)(2,1)S(1)}, bf16[128,1280]{1,0:T(8,128)(2,1)S(1)}, bf16[128,1280]{1,0:T(8,128)(2,1)S(1)}, bf16[320,1280]{1,0:T(8,128)(2,1)S(1)}) custom-call(s32[4]{0:T(128)S(1)} %pad_add_fusion.spot, bf16[512,1280]{1,0:T(8,128)(2,1)S(1)} %get-tuple-element.323.grad_pre, ...), custom_call_target="tpu_custom_call" | custom-call | flops 1 | bytes 1 | tf_op jit(solution)/shard_map/second_grad/pallas_call | solution.py:142
  101.7 3.9 %rest.1 = (bf16[320,1280]{1,0:T(8,128)(2,1)S(1)}, bf16[320,1280]{1,0:T(8,128)(2,1)S(1)}, bf16[320,1280]{1,0:T(8,128)(2,1)S(1)}, bf16[320,1280]{1,0:T(8,128)(2,1)S(1)}, bf16[320,1280]{1,0:T(8,128)(2,1)S(1)}) custom-call(s32[4]{0:T(128)S(1)} %pad_add_fusion.spot, bf16[512,1280]{1,0:T(8,128)(2,1)S(1)} %get-tuple-element.338.second, ...), custom_call_target="tpu_custom_call" | custom-call | flops 1 | bytes 1 | tf_op jit(solution)/shard_map/rest/pallas_call | solution.py:142
  105.9 3.0 %collective-permute-done.29.p1 = bf16[128,1280]{1,0:T(8,128)(2,1)S(1)} collective-permute-done((bf16[128,1280]{1,0:T(8,128)(2,1)S(1)}, bf16[128,1280]{1,0:T(8,128)(2,1)S(1)}, u32[]{:S(2)}, u32[]{:S(2)}) %collective-permute-start.29) | collective-permute-done | bytes 327712 | tf_op jit(solution)/shard_map/ppermute | solution.py:1156
  108.8 6.1 %collective-permute-done.30.p2 = bf16[128,1280]{1,0:T(8,128)(2,1)S(1)} collective-permute-done((bf16[128,1280]{1,0:T(8,128)(2,1)S(1)}, bf16[128,1280]{1,0:T(8,128)(2,1)S(1)}, u32[]{:S(2)}, u32[]{:S(2)}) %collective-permute-start.30) | collective-permute-done | bytes 327712 | tf_op jit(solution)/shard_map/ppermute | solution.py:1156
  126.7 5.3 %collective-permute-done.36.b3 = bf16[128,1280]{1,0:T(8,128)(2,1)S(1)} collective-permute-done((bf16[128,1280]{1,0:T(8,128)(2,1)S(1)}, bf16[128,1280]{1,0:T(8,128)(2,1)S(1)}, u32[]{:S(2)}, u32[]{:S(2)}) %collective-permute-start.36) | collective-permute-done | bytes 327712 | tf_op jit(solution)/shard_map/ppermute | solution.py:1156
  132.0 4.9 %collective-permute-done.35.b2 = bf16[128,1280]{1,0:T(8,128)(2,1)S(1)} collective-permute-done((bf16[128,1280]{1,0:T(8,128)(2,1)S(1)}, bf16[128,1280]{1,0:T(8,128)(2,1)S(1)}, u32[]{:S(2)}, u32[]{:S(2)}) %collective-permute-start.35) | collective-permute-done | bytes 327712 | tf_op jit(solution)/shard_map/ppermute | solution.py:1156
  137.7 4.3 %collective-permute-start.40 = (bf16[320,1280]{1,0:T(8,128)(2,1)S(1)}, bf16[320,1280]{1,0:T(8,128)(2,1)S(1)}, u32[]{:S(2)}, u32[]{:S(2)}) collective-permute-start(bf16[320,1280]{1,0:T(8,128)(2,1)S(1)} %z_send.4.sent), channel_id=1, source_target_pairs={{0,8},{8,0},{16,24},{24,16},{1,9},{9,1},{17,25},{25,17},{2,10},{10... | collective-permute-start | bytes 2457608 | tf_op jit(solution)/shard_map/ppermute | solution.py:1172
  142.7 6.8 %leave.1 = (bf16[512,1280]{1,0:T(8,128)(2,1)S(1)}, bf16[512,960]{1,0:T(8,128)(2,1)S(1)}, f32[1,960]{1,0:T(1,128)S(1)}, bf16[128,1280]{1,0:T(8,128)(2,1)S(1)}, bf...) custom-call(bf16[128,1280]{1,0:T(8,128)(2,1)S(1)} %get-tuple-element.371.b0, ...), custom_call_target="tpu_custom_call" | custom-call | flops 1 | bytes 1 | tf_op jit(solution)/shard_map/leave/pallas_call | solution.py:142
  149.6 3.9 %qkv_grad.1 = (bf16[2,160,960]{2,1,0:T(8,128)(2,1)S(1)}, bf16[2,160,960]{2,1,0:T(8,128)(2,1)S(1)}, bf16[4,160,960]{2,1,0:T(8,128)(2,1)S(1)}, bf16[160,1280]{1,0:T(8,128)(2,1)S(1)}, bf16[160,1280]{1,0:T(8,128)(2,1)S(1)}) custom-call(s32[4]{0:T(128)S(1)} %pad_add_fusion.spot, bf16[512,1280]{1,0:T(8,128)(2,1)S(1)} %get-tuple-element.392.first_low, ...), custom_call_target="tpu_custom_call" | custom-call | flops 1 | bytes 1 | tf_op jit(solution)/shard_map/qkv_grad/pallas_call | solution.py:142
  154.1 3.0 %collective-permute-done.44.out_got = bf16[160,1280]{1,0:T(8,128)(2,1)S(1)} collective-permute-done((bf16[160,1280]{1,0:T(8,128)(2,1)S(1)}, bf16[160,1280]{1,0:T(8,128)(2,1)S(1)}, u32[]{:S(2)}, u32[]{:S(2)}) %collective-permute-start.44) | collective-permute-done | bytes 409632 | tf_op jit(solution)/shard_map/ppermute | solution.py:1156
  161.3 3.8 %collective-permute-start.49 = (bf16[320,1280]{1,0:T(8,128)(2,1)S(1)}, bf16[320,1280]{1,0:T(8,128)(2,1)S(1)}, u32[]{:S(2)}, u32[]{:S(2)}) collective-permute-start(bf16[320,1280]{1,0:T(8,128)(2,1)S(1)} %z_send.5.sent), channel_id=1, source_target_pairs={{0,8},{8,0},{16,24},{24,16},{1,9},{9,1},{17,25},{25,17},{2,10},{10... | collective-permute-start | bytes 2457608 | tf_op jit(solution)/shard_map/ppermute | solution.py:1172
  169.6 14.4 %collective-permute-done.49.refs_1_.got_side = bf16[320,1280]{1,0:T(8,128)(2,1)S(1)} collective-permute-done((bf16[320,1280]{1,0:T(8,128)(2,1)S(1)}, bf16[320,1280]{1,0:T(8,128)(2,1)S(1)}, u32[]{:S(2)}, u32[]{:S(2)}) %collective-permute-start.49) | collective-permute-done | bytes 819232 | tf_op jit(solution)/shard_map/ppermute | solution.py:1172
  184.9 3.8 %collective-permute-start.54 = (bf16[320,1280]{1,0:T(8,128)(2,1)S(1)}, bf16[320,1280]{1,0:T(8,128)(2,1)S(1)}, u32[]{:S(2)}, u32[]{:S(2)}) collective-permute-start(bf16[320,1280]{1,0:T(8,128)(2,1)S(1)} %z_send.6.sent), channel_id=1, source_target_pairs={{0,8},{8,0},{16,24},{24,16},{1,9},{9,1},{17,25},{25,17},{2,10},{10... | collective-permute-start | bytes 2457608 | tf_op jit(solution)/shard_map/ppermute | solution.py:1172
  193.0 7.2 %collective-permute-done.51.r1 = bf16[128,1280]{1,0:T(8,128)(2,1)S(1)} collective-permute-done((bf16[128,1280]{1,0:T(8,128)(2,1)S(1)}, bf16[128,1280]{1,0:T(8,128)(2,1)S(1)}, u32[]{:S(2)}, u32[]{:S(2)}) %collective-permute-start.51) | collective-permute-done | bytes 327712 | tf_op jit(solution)/shard_map/ppermute | solution.py:1156
  200.1 5.6 %collective-permute-done.52.r2 = bf16[128,1280]{1,0:T(8,128)(2,1)S(1)} collective-permute-done((bf16[128,1280]{1,0:T(8,128)(2,1)S(1)}, bf16[128,1280]{1,0:T(8,128)(2,1)S(1)}, u32[]{:S(2)}, u32[]{:S(2)}) %collective-permute-start.52) | collective-permute-done | bytes 327712 | tf_op jit(solution)/shard_map/ppermute | solution.py:1156
  207.6 3.8 %collective-permute-start.56 = (bf16[320,1280]{1,0:T(8,128)(2,1)S(1)}, bf16[320,1280]{1,0:T(8,128)(2,1)S(1)}, u32[]{:S(2)}, u32[]{:S(2)}) collective-permute-start(bf16[320,1280]{1,0:T(8,128)(2,1)S(1)} %z_send.7.sent), channel_id=1, source_target_pairs={{0,8},{8,0},{16,24},{24,16},{1,9},{9,1},{17,25},{25,17},{2,10},{10... | collective-permute-start | bytes 2457608 | tf_op jit(solution)/shard_map/ppermute | solution.py:1172
  226.8 3.5 %collective-permute-done.62.refs_1_ = f32[16,1280]{1,0:T(8,128)S(1)} collective-permute-done((f32[16,1280]{1,0:T(8,128)S(1)}, f32[16,1280]{1,0:T(8,128)S(1)}, u32[]{:S(2)}, u32[]{:S(2)}) %collective-permute-start.62) | collective-permute-done | bytes 81952 | tf_op jit(solution)/shard_map/ppermute | solution.py:1172
  236.9 8.9 %collective-permute-done.63.b1 = bf16[160,1280]{1,0:T(8,128)(2,1)S(1)} collective-permute-done((bf16[160,1280]{1,0:T(8,128)(2,1)S(1)}, bf16[160,1280]{1,0:T(8,128)(2,1)S(1)}, u32[]{:S(2)}, u32[]{:S(2)}) %collective-permute-start.63) | collective-permute-done | bytes 409632 | tf_op jit(solution)/shard_map/ppermute | solution.py:1156
  245.8 5.6 %collective-permute-done.64.b2 = bf16[160,1280]{1,0:T(8,128)(2,1)S(1)} collective-permute-done((bf16[160,1280]{1,0:T(8,128)(2,1)S(1)}, bf16[160,1280]{1,0:T(8,128)(2,1)S(1)}, u32[]{:S(2)}, u32[]{:S(2)}) %collective-permute-start.64) | collective-permute-done | bytes 409632 | tf_op jit(solution)/shard_map/ppermute | solution.py:1156
  258.8 3.2 %collective-permute-start.71 = (f32[16,1280]{1,0:T(8,128)S(1)}, f32[16,1280]{1,0:T(8,128)S(1)}, u32[]{:S(2)}, u32[]{:S(2)}) collective-permute-start(f32[16,1280]{1,0:T(8,128)S(1)} %add.41.refs_1_), channel_id=1, source_target_pairs={{0,16},{8,24},{16,0},{24,8},{1,17},{9,25},{17,1},{25,9},{2,18},{10... | collective-permute-start | bytes 245768 | tf_op jit(solution)/shard_map/ppermute | solution.py:1172
  (179 shorter events, 115.0 us)
Async XLA Ops:
  0.7 19.9 %collective-permute-start.1 = (bf16[128,1280]{1,0:T(8,128)(2,1)}, bf16[128,1280]{1,0:T(8,128)(2,1)S(1)}, u32[]{:S(2)}, u32[]{:S(2)}) collective-permute-start(bf16[128,1280]{1,0:T(8,128)(2,1)} %tokens.3), channel_id=1, source_target_pairs={{0,4},{1,5},{2,6},{3,7},{4,0},{5,1},{6,2},{7,3},{8,12},{9,13},{10,... | collective-permute-start | bytes 983048 | tf_op jit(solution)/shard_map/ppermute | solution.py:1156
  3.7 16.9 %collective-permute-start = (bf16[128,1280]{1,0:T(8,128)(2,1)}, bf16[128,1280]{1,0:T(8,128)(2,1)S(1)}, u32[]{:S(2)}, u32[]{:S(2)}) collective-permute-start(bf16[128,1280]{1,0:T(8,128)(2,1)} %tokens.3), channel_id=1, source_target_pairs={{0,2},{1,3},{2,0},{3,1},{4,6},{5,7},{6,4},{7,5},{8,10},{9,11},{10,... | collective-permute-start | bytes 983048 | tf_op jit(solution)/shard_map/ppermute | solution.py:1156
  20.7 16.3 %collective-permute-start.8 = (bf16[432,960]{1,0:T(8,128)(2,1)S(1)}, bf16[432,960]{1,0:T(8,128)(2,1)S(1)}, u32[]{:S(2)}, u32[]{:S(2)}) collective-permute-start(bf16[432,960]{1,0:T(8,128)(2,1)S(1)} %get-tuple-element.272.refs_0_), channel_id=1, source_target_pairs={{0,1},{1,0},{2,3},{3,2},{4,5},{5,4},{6,7},{7,6},{8,9},{9,8},{10,11... | collective-permute-start | bytes 2488328 | tf_op jit(solution)/shard_map/ppermute | solution.py:1156
  27.4 19.3 %collective-permute-start.12 = (bf16[208,1280]{1,0:T(8,128)(2,1)S(1)}, bf16[208,1280]{1,0:T(8,128)(2,1)S(1)}, u32[]{:S(2)}, u32[]{:S(2)}) collective-permute-start(bf16[208,1280]{1,0:T(8,128)(2,1)S(1)} %get-tuple-element.286), channel_id=1, source_target_pairs={{0,2},{1,3},{2,0},{3,1},{4,6},{5,7},{6,4},{7,5},{8,10},{9,11},{10,... | collective-permute-start | bytes 1597448 | tf_op jit(solution)/shard_map/ppermute | solution.py:1156
  29.1 17.8 %collective-permute-start.13 = (bf16[208,1280]{1,0:T(8,128)(2,1)S(1)}, bf16[208,1280]{1,0:T(8,128)(2,1)S(1)}, u32[]{:S(2)}, u32[]{:S(2)}) collective-permute-start(bf16[208,1280]{1,0:T(8,128)(2,1)S(1)} %get-tuple-element.287), channel_id=1, source_target_pairs={{0,4},{1,5},{2,6},{3,7},{4,0},{5,1},{6,2},{7,3},{8,12},{9,13},{10,... | collective-permute-start | bytes 1597448 | tf_op jit(solution)/shard_map/ppermute | solution.py:1156
  49.1 18.4 %collective-permute-start.19 = (bf16[128,1280]{1,0:T(8,128)(2,1)S(1)}, bf16[128,1280]{1,0:T(8,128)(2,1)S(1)}, u32[]{:S(2)}, u32[]{:S(2)}) collective-permute-start(bf16[128,1280]{1,0:T(8,128)(2,1)S(1)} %get-tuple-element.293), channel_id=1, source_target_pairs={{0,2},{1,3},{2,0},{3,1},{4,6},{5,7},{6,4},{7,5},{8,10},{9,11},{10,... | collective-permute-start | bytes 983048 | tf_op jit(solution)/shard_map/ppermute | solution.py:1156
  50.6 16.9 %collective-permute-start.20 = (bf16[128,1280]{1,0:T(8,128)(2,1)S(1)}, bf16[128,1280]{1,0:T(8,128)(2,1)S(1)}, u32[]{:S(2)}, u32[]{:S(2)}) collective-permute-start(bf16[128,1280]{1,0:T(8,128)(2,1)S(1)} %get-tuple-element.294), channel_id=1, source_target_pairs={{0,4},{1,5},{2,6},{3,7},{4,0},{5,1},{6,2},{7,3},{8,12},{9,13},{10,... | collective-permute-start | bytes 983048 | tf_op jit(solution)/shard_map/ppermute | solution.py:1156
  51.1 17.0 %collective-permute-start.21 = (bf16[128,1280]{1,0:T(8,128)(2,1)S(1)}, bf16[128,1280]{1,0:T(8,128)(2,1)S(1)}, u32[]{:S(2)}, u32[]{:S(2)}) collective-permute-start(bf16[128,1280]{1,0:T(8,128)(2,1)S(1)} %get-tuple-element.295), channel_id=1, source_target_pairs={{0,6},{1,7},{2,4},{3,5},{4,2},{5,3},{6,0},{7,1},{8,14},{9,15},{10,... | collective-permute-start | bytes 983048 | tf_op jit(solution)/shard_map/ppermute | solution.py:1156
  72.1 15.5 %collective-permute-start.22 = (bf16[128,1280]{1,0:T(8,128)(2,1)S(1)}, bf16[128,1280]{1,0:T(8,128)(2,1)S(1)}, u32[]{:S(2)}, u32[]{:S(2)}) collective-permute-start(bf16[128,1280]{1,0:T(8,128)(2,1)S(1)} %get-tuple-element.301.s0), channel_id=1, source_target_pairs={{0,6},{1,7},{2,4},{3,5},{4,2},{5,3},{6,0},{7,1},{8,14},{9,15},{10,... | collective-permute-start | bytes 983048 | tf_op jit(solution)/shard_map/ppermute | solution.py:1156
  96.6 20.2 %collective-permute-start.32 = (bf16[320,1280]{1,0:T(8,128)(2,1)S(1)}, bf16[320,1280]{1,0:T(8,128)(2,1)S(1)}, u32[]{:S(2)}, u32[]{:S(2)}) collective-permute-start(bf16[320,1280]{1,0:T(8,128)(2,1)S(1)} %down_grad.1.refs_0_), channel_id=1, source_target_pairs={{0,8},{8,0},{16,24},{24,16},{1,9},{9,1},{17,25},{25,17},{2,10},{10... | collective-permute-start | bytes 2457608 | tf_op jit(solution)/shard_map/ppermute | solution.py:1172
  98.8 16.1 %collective-permute-start.30 = (bf16[128,1280]{1,0:T(8,128)(2,1)S(1)}, bf16[128,1280]{1,0:T(8,128)(2,1)S(1)}, u32[]{:S(2)}, u32[]{:S(2)}) collective-permute-start(bf16[128,1280]{1,0:T(8,128)(2,1)S(1)} %get-tuple-element.335), channel_id=1, source_target_pairs={{0,4},{1,5},{2,6},{3,7},{4,0},{5,1},{6,2},{7,3},{8,12},{9,13},{10,... | collective-permute-start | bytes 983048 | tf_op jit(solution)/shard_map/ppermute | solution.py:1156
  105.6 16.9 %collective-permute-start.39 = (bf16[320,1280]{1,0:T(8,128)(2,1)S(1)}, bf16[320,1280]{1,0:T(8,128)(2,1)S(1)}, u32[]{:S(2)}, u32[]{:S(2)}) collective-permute-start(bf16[320,1280]{1,0:T(8,128)(2,1)S(1)} %get-tuple-element.356), channel_id=1, source_target_pairs={{0,1},{1,0},{2,3},{3,2},{4,5},{5,4},{6,7},{7,6},{8,9},{9,8},{10,11... | collective-permute-start | bytes 2457608 | tf_op jit(solution)/shard_map/ppermute | solution.py:1156
  117.0 19.9 %collective-permute-start.37 = (bf16[320,1280]{1,0:T(8,128)(2,1)S(1)}, bf16[320,1280]{1,0:T(8,128)(2,1)S(1)}, u32[]{:S(2)}, u32[]{:S(2)}) collective-permute-start(bf16[320,1280]{1,0:T(8,128)(2,1)S(1)} %add.30.refs_0_), channel_id=1, source_target_pairs={{0,8},{8,0},{16,24},{24,16},{1,9},{9,1},{17,25},{25,17},{2,10},{10... | collective-permute-start | bytes 2457608 | tf_op jit(solution)/shard_map/ppermute | solution.py:1172
  118.7 18.3 %collective-permute-start.38 = (bf16[320,1280]{1,0:T(8,128)(2,1)S(1)}, bf16[320,1280]{1,0:T(8,128)(2,1)S(1)}, u32[]{:S(2)}, u32[]{:S(2)}) collective-permute-start(bf16[320,1280]{1,0:T(8,128)(2,1)S(1)} %add.31.half), channel_id=1, source_target_pairs={{8,16},{16,8},{9,17},{17,9},{10,18},{18,10},{11,19},{19,11},{12,20... | collective-permute-start | bytes 2457608 | tf_op jit(solution)/shard_map/ppermute | solution.py:1172
  121.7 15.2 %collective-permute-start.35 = (bf16[128,1280]{1,0:T(8,128)(2,1)S(1)}, bf16[128,1280]{1,0:T(8,128)(2,1)S(1)}, u32[]{:S(2)}, u32[]{:S(2)}) collective-permute-start(bf16[128,1280]{1,0:T(8,128)(2,1)S(1)} %get-tuple-element.371.b0), channel_id=1, source_target_pairs={{0,4},{1,5},{2,6},{3,7},{4,0},{5,1},{6,2},{7,3},{8,12},{9,13},{10,... | collective-permute-start | bytes 983048 | tf_op jit(solution)/shard_map/ppermute | solution.py:1156
  137.7 22.7 %collective-permute-start.40 = (bf16[320,1280]{1,0:T(8,128)(2,1)S(1)}, bf16[320,1280]{1,0:T(8,128)(2,1)S(1)}, u32[]{:S(2)}, u32[]{:S(2)}) collective-permute-start(bf16[320,1280]{1,0:T(8,128)(2,1)S(1)} %z_send.4.sent), channel_id=1, source_target_pairs={{0,8},{8,0},{16,24},{24,16},{1,9},{9,1},{17,25},{25,17},{2,10},{10... | collective-permute-start | bytes 2457608 | tf_op jit(solution)/shard_map/ppermute | solution.py:1172
  142.0 18.4 %collective-permute-start.41 = (bf16[320,1280]{1,0:T(8,128)(2,1)S(1)}, bf16[320,1280]{1,0:T(8,128)(2,1)S(1)}, u32[]{:S(2)}, u32[]{:S(2)}) collective-permute-start(bf16[320,1280]{1,0:T(8,128)(2,1)S(1)} %add.33.half), channel_id=1, source_target_pairs={{8,16},{16,8},{9,17},{17,9},{10,18},{18,10},{11,19},{19,11},{12,20... | collective-permute-start | bytes 2457608 | tf_op jit(solution)/shard_map/ppermute | solution.py:1172
  161.3 22.7 %collective-permute-start.49 = (bf16[320,1280]{1,0:T(8,128)(2,1)S(1)}, bf16[320,1280]{1,0:T(8,128)(2,1)S(1)}, u32[]{:S(2)}, u32[]{:S(2)}) collective-permute-start(bf16[320,1280]{1,0:T(8,128)(2,1)S(1)} %z_send.5.sent), channel_id=1, source_target_pairs={{0,8},{8,0},{16,24},{24,16},{1,9},{9,1},{17,25},{25,17},{2,10},{10... | collective-permute-start | bytes 2457608 | tf_op jit(solution)/shard_map/ppermute | solution.py:1172
  165.2 18.8 %collective-permute-start.50 = (bf16[320,1280]{1,0:T(8,128)(2,1)S(1)}, bf16[320,1280]{1,0:T(8,128)(2,1)S(1)}, u32[]{:S(2)}, u32[]{:S(2)}) collective-permute-start(bf16[320,1280]{1,0:T(8,128)(2,1)S(1)} %add.34.half), channel_id=1, source_target_pairs={{8,16},{16,8},{9,17},{17,9},{10,18},{18,10},{11,19},{19,11},{12,20... | collective-permute-start | bytes 2457608 | tf_op jit(solution)/shard_map/ppermute | solution.py:1172
  166.1 17.9 %collective-permute-start.46 = (bf16[128,1280]{1,0:T(8,128)(2,1)S(1)}, bf16[128,1280]{1,0:T(8,128)(2,1)S(1)}, u32[]{:S(2)}, u32[]{:S(2)}) collective-permute-start(bf16[128,1280]{1,0:T(8,128)(2,1)S(1)} %get-tuple-element.408), channel_id=1, source_target_pairs={{0,2},{1,3},{2,0},{3,1},{4,6},{5,7},{6,4},{7,5},{8,10},{9,11},{10,... | collective-permute-start | bytes 983048 | tf_op jit(solution)/shard_map/ppermute | solution.py:1156
  166.7 17.3 %collective-permute-start.47 = (bf16[128,1280]{1,0:T(8,128)(2,1)S(1)}, bf16[128,1280]{1,0:T(8,128)(2,1)S(1)}, u32[]{:S(2)}, u32[]{:S(2)}) collective-permute-start(bf16[128,1280]{1,0:T(8,128)(2,1)S(1)} %get-tuple-element.409), channel_id=1, source_target_pairs={{0,4},{1,5},{2,6},{3,7},{4,0},{5,1},{6,2},{7,3},{8,12},{9,13},{10,... | collective-permute-start | bytes 983048 | tf_op jit(solution)/shard_map/ppermute | solution.py:1156
  168.0 16.1 %collective-permute-start.48 = (bf16[128,1280]{1,0:T(8,128)(2,1)S(1)}, bf16[128,1280]{1,0:T(8,128)(2,1)S(1)}, u32[]{:S(2)}, u32[]{:S(2)}) collective-permute-start(bf16[128,1280]{1,0:T(8,128)(2,1)S(1)} %get-tuple-element.410), channel_id=1, source_target_pairs={{0,6},{1,7},{2,4},{3,5},{4,2},{5,3},{6,0},{7,1},{8,14},{9,15},{10,... | collective-permute-start | bytes 983048 | tf_op jit(solution)/shard_map/ppermute | solution.py:1156
  184.9 21.9 %collective-permute-start.54 = (bf16[320,1280]{1,0:T(8,128)(2,1)S(1)}, bf16[320,1280]{1,0:T(8,128)(2,1)S(1)}, u32[]{:S(2)}, u32[]{:S(2)}) collective-permute-start(bf16[320,1280]{1,0:T(8,128)(2,1)S(1)} %z_send.6.sent), channel_id=1, source_target_pairs={{0,8},{8,0},{16,24},{24,16},{1,9},{9,1},{17,25},{25,17},{2,10},{10... | collective-permute-start | bytes 2457608 | tf_op jit(solution)/shard_map/ppermute | solution.py:1172
  188.7 18.0 %collective-permute-start.55 = (bf16[320,1280]{1,0:T(8,128)(2,1)S(1)}, bf16[320,1280]{1,0:T(8,128)(2,1)S(1)}, u32[]{:S(2)}, u32[]{:S(2)}) collective-permute-start(bf16[320,1280]{1,0:T(8,128)(2,1)S(1)} %add.36.half), channel_id=1, source_target_pairs={{8,16},{16,8},{9,17},{17,9},{10,18},{18,10},{11,19},{19,11},{12,20... | collective-permute-start | bytes 2457608 | tf_op jit(solution)/shard_map/ppermute | solution.py:1172
  190.0 15.7 %collective-permute-start.52 = (bf16[128,1280]{1,0:T(8,128)(2,1)S(1)}, bf16[128,1280]{1,0:T(8,128)(2,1)S(1)}, u32[]{:S(2)}, u32[]{:S(2)}) collective-permute-start(bf16[128,1280]{1,0:T(8,128)(2,1)S(1)} %get-tuple-element.422), channel_id=1, source_target_pairs={{0,4},{1,5},{2,6},{3,7},{4,0},{5,1},{6,2},{7,3},{8,12},{9,13},{10,... | collective-permute-start | bytes 983048 | tf_op jit(solution)/shard_map/ppermute | solution.py:1156
  207.6 22.7 %collective-permute-start.56 = (bf16[320,1280]{1,0:T(8,128)(2,1)S(1)}, bf16[320,1280]{1,0:T(8,128)(2,1)S(1)}, u32[]{:S(2)}, u32[]{:S(2)}) collective-permute-start(bf16[320,1280]{1,0:T(8,128)(2,1)S(1)} %z_send.7.sent), channel_id=1, source_target_pairs={{0,8},{8,0},{16,24},{24,16},{1,9},{9,1},{17,25},{25,17},{2,10},{10... | collective-permute-start | bytes 2457608 | tf_op jit(solution)/shard_map/ppermute | solution.py:1172
  211.4 18.9 %collective-permute-start.57 = (bf16[320,1280]{1,0:T(8,128)(2,1)S(1)}, bf16[320,1280]{1,0:T(8,128)(2,1)S(1)}, u32[]{:S(2)}, u32[]{:S(2)}) collective-permute-start(bf16[320,1280]{1,0:T(8,128)(2,1)S(1)} %add.37.refs_0_), channel_id=1, source_target_pairs={{8,16},{16,8},{9,17},{17,9},{10,18},{18,10},{11,19},{19,11},{12,20... | collective-permute-start | bytes 2457608 | tf_op jit(solution)/shard_map/ppermute | solution.py:1172
  230.7 20.7 %collective-permute-start.66 = (bf16[320,1280]{1,0:T(8,128)(2,1)S(1)}, bf16[320,1280]{1,0:T(8,128)(2,1)S(1)}, u32[]{:S(2)}, u32[]{:S(2)}) collective-permute-start(bf16[320,1280]{1,0:T(8,128)(2,1)S(1)} %add.40.sent), channel_id=1, source_target_pairs={{0,8},{8,0},{16,24},{24,16},{1,9},{9,1},{17,25},{25,17},{2,10},{10... | collective-permute-start | bytes 2457608 | tf_op jit(solution)/shard_map/ppermute | solution.py:1172
  232.7 18.8 %collective-permute-start.67 = (bf16[320,1280]{1,0:T(8,128)(2,1)S(1)}, bf16[320,1280]{1,0:T(8,128)(2,1)S(1)}, u32[]{:S(2)}, u32[]{:S(2)}) collective-permute-start(bf16[320,1280]{1,0:T(8,128)(2,1)S(1)} %add.39.refs_0_), channel_id=1, source_target_pairs={{8,16},{16,8},{9,17},{17,9},{10,18},{18,10},{11,19},{19,11},{12,20... | collective-permute-start | bytes 2457608 | tf_op jit(solution)/shard_map/ppermute | solution.py:1172
  234.0 17.4 %collective-permute-start.64 = (bf16[160,1280]{1,0:T(8,128)(2,1)S(1)}, bf16[160,1280]{1,0:T(8,128)(2,1)S(1)}, u32[]{:S(2)}, u32[]{:S(2)}) collective-permute-start(bf16[160,1280]{1,0:T(8,128)(2,1)S(1)} %get-tuple-element.463), channel_id=1, source_target_pairs={{0,4},{1,5},{2,6},{3,7},{4,0},{5,1},{6,2},{7,3},{8,12},{9,13},{10,... | collective-permute-start | bytes 1228808 | tf_op jit(solution)/shard_map/ppermute | solution.py:1156
  235.2 16.2 %collective-permute-start.65 = (bf16[160,1280]{1,0:T(8,128)(2,1)S(1)}, bf16[160,1280]{1,0:T(8,128)(2,1)S(1)}, u32[]{:S(2)}, u32[]{:S(2)}) collective-permute-start(bf16[160,1280]{1,0:T(8,128)(2,1)S(1)} %get-tuple-element.464), channel_id=1, source_target_pairs={{0,6},{1,7},{2,4},{3,5},{4,2},{5,3},{6,0},{7,1},{8,14},{9,15},{10,... | collective-permute-start | bytes 1228808 | tf_op jit(solution)/shard_map/ppermute | solution.py:1156
  251.6 20.7 %collective-permute-start.72 = (bf16[320,1280]{1,0:T(8,128)(2,1)S(1)}, bf16[320,1280]{1,0:T(8,128)(2,1)S(1)}, u32[]{:S(2)}, u32[]{:S(2)}) collective-permute-start(bf16[320,1280]{1,0:T(8,128)(2,1)S(1)} %add.42.sent), channel_id=1, source_target_pairs={{8,0},{16,24},{9,1},{17,25},{10,2},{18,26},{11,3},{19,27},{12,4},{... | collective-permute-start | bytes 2457608 | tf_op jit(solution)/shard_map/ppermute | solution.py:1172
  (48 other events, 443.7 us)

commit v5 on v4

--- a/solution.py
+++ b/solution.py
@@ -311,14 +311,12 @@
     )
 
 
-def up_join_kernel(cotangent, u1, u2, u3, half_a, half_b, whole, first, second):
+def up_join_kernel(cotangent, u1, u2, u3, near, whole, first, second):
     rows = cotangent.shape[0]
     for i, block in enumerate((cotangent, u1.at[HALF:], u2.at[HALF:])):
         whole[i * rows : (i + 1) * rows, :] = block[...]
-    near = jnp.concatenate([block[:HALF, :] for block in (u1, u2, u3)], axis=0)
-    size = half_a.shape[0]
-    half_a[...] = near[:size]
-    half_b[...] = near[size:]
+    for i, block in enumerate((u1, u2, u3)):
+        near[i * HALF : (i + 1) * HALF, :] = block[:HALF, :]
     half = rows // 2
     first[...] = u1[HALF : HALF + half, :]
     second[...] = u2[HALF + half :, :]
@@ -326,13 +324,13 @@
 
 def up_join(cotangent, blocks):
     rows = cotangent.shape[0]
-    half = ((3 * HALF // 2, FF_CHIP), bf16)
+    near = ((3 * HALF, FF_CHIP), bf16)
     passed = ((rows // 2, D), bf16)
     return call(
         up_join_kernel,
         "up_join",
         "vvvv",
-        [half, half, (((CHIPS - 1) * rows, D), bf16), passed, passed],
+        [near, (((CHIPS - 1) * rows, D), bf16), passed, passed],
     )(cotangent, *blocks)
 
 
@@ -404,8 +402,8 @@
     mine, other, refs = refs[:2], refs[2:4], refs[4:]
     out_mine, out_other, refs = *refs[:2], refs[2:]
     table, mask, qkv, out, first_low, projected, context = refs[:7]
-    partials = refs[7 : 7 + CHIPS]
-    extras, out_sems = refs[7 + CHIPS :]
+    partials = refs[7 : 8 + CHIPS]
+    extras, out_sems = refs[8 + CHIPS :]
     rows = mask.shape[1]
     out_copies = by_core_copies(spot[1], out_mine, out_other, out, out_sems)
     start_all(out_copies)
@@ -433,8 +431,10 @@
 
     def partial(at):
         whole = mm(context[...], out[:, at]).astype(bf16)
-        for i, part in enumerate(partials):
-            part[:, at] = whole[i * rows : (i + 1) * rows]
+        lo = 0
+        for part in partials:
+            part[:, at] = whole[lo : lo + part.shape[0]]
+            lo += part.shape[0]
 
     tiled(D, 256, partial)
 
@@ -455,7 +455,8 @@
             ((total, 3 * D_CHIP), bf16),
             ((total, D_CHIP), bf16),
         ]
-        + [((rows, D), bf16)] * CHIPS,
+        + [((rows, D), bf16)] * (CHIPS - 1)
+        + [((rows // 2, D), bf16)] * 2,
         [pltpu.VMEM((TEAM, EXTRA, 3 * D_CHIP), f32), sems(2)],
     )(spot, normed, *mine, *other, out_mine, out_other)
     return outs[:7], outs[7:]
@@ -506,8 +507,20 @@
     return total
 
 
-def mix_kernel(p0, p1, p2, p3, tokens, table, mixed, second):
-    total = total_of((p0, p1, p2, p3)) + tokens[...].astype(f32)
+def pass_on_kernel(p1, p2, h1, h2, sum1, sum2):
+    size = h1.shape[0]
+    sum1[:size, :] = (p1[:size, :].astype(f32) + h1[...].astype(f32)).astype(bf16)
+    sum1[size:, :] = p1[size:, :]
+    sum2[:size, :] = p2[:size, :]
+    sum2[size:, :] = (p2[size:, :].astype(f32) + h2[...].astype(f32)).astype(bf16)
+
+
+def pass_on(p1, p2, h1, h2):
+    return call(pass_on_kernel, "pass_on", "vvvv", [(p1.shape, bf16)] * 2)(p1, p2, h1, h2)
+
+
+def mix_kernel(p0, p1, p2, tokens, table, mixed, second):
+    total = total_of((p0, p1, p2)) + tokens[...].astype(f32)
     total = total + table[BIAS_OUT : BIAS_OUT + 1, :]
     mixed[...] = total
     normed, _ = normalize(total)
@@ -516,7 +529,7 @@
 
 def mix(parts, tokens, table):
     shape = tokens.shape
-    return call(mix_kernel, "mix", "v" * 6, [(shape, f32), (shape, bf16)])(*parts, tokens, table)
+    return call(mix_kernel, "mix", "v" * 5, [(shape, f32), (shape, bf16)])(*parts, tokens, table)
 
 
 def unmix_kernel(p0, p1, p2, p3, mixed, table, cotangent, grad_mixed, branch, sums):
@@ -590,7 +603,8 @@
 
 def hidden_first_kernel(spot, s0, s1, s2, grad_act, table, *refs):
     columns = [(own, rest, rest.at[3 * HALF :]) for own, rest in (refs[:2], refs[2:4])]
-    second, act, grad_pre, bias_sum, up, pre_act = refs[4:]
+    second, act, grad_pre, bias_sum, up = refs[4:9]
+    partials, pre_act = refs[9:12], refs[12]
     rows = s0.shape[0]
     stack_columns(spot, *columns, up)
     stack_blocks((s0, s1, s2), second)
@@ -598,6 +612,18 @@
     hidden_rows(
         slice(0, 3 * rows), second, up, table, grad_act, pre_act, act, grad_pre, bias_sum
     )
+    second_partials(slice(0, 3 * rows), grad_pre, up, partials)
+
+
+def second_partials(at, grad_pre, up, partials):
+    rows = partials[0].shape[0]
+
+    def columns(tile):
+        whole = mm_t(grad_pre[at, :], up[tile, :]).astype(bf16)
+        for i, part in enumerate(partials):
+            part[:, tile] = whole[i * rows : (i + 1) * rows]
+
+    tiled(D, 256, columns)
 
 
 def hidden_first(spot, blocks, grad_act, table, mine, other):
@@ -612,7 +638,8 @@
             ((total, FF_CHIP), bf16),
             ((1, FF_CHIP), f32),
             ((D, FF_CHIP), bf16),
-        ],
+        ]
+        + [((total // CHIPS, D), bf16)] * 3,
         [pltpu.VMEM((total, FF_CHIP), f32)],
     )(spot, *blocks, grad_act, table, *mine, *other)
 
@@ -686,29 +713,28 @@
     )(spot, block, grad_act, table, cotangent, up, second, act, grad_pre, bias_sum)
 
 
-def second_grad_kernel(spot, grad_pre, up, second, *refs):
-    partials, up_sent, work = refs[:CHIPS], refs[CHIPS], refs[CHIPS + 1]
-    rows = partials[0].shape[0]
-
-    def partial(at):
-        whole = mm_t(grad_pre[...], up[at, :]).astype(bf16)
-        for i, part in enumerate(partials):
-            part[:, at] = whole[i * rows : (i + 1) * rows]
-
-    tiled(D, 256, partial)
+def second_last_kernel(grad_pre, up, partial):
+    rows = partial.shape[0]
+    second_partials(slice(grad_pre.shape[0] - rows, grad_pre.shape[0]), grad_pre, up, (partial,))
+
+
+def second_last(grad_pre, up):
+    rows = grad_pre.shape[0] // CHIPS
+    return call(second_last_kernel, "second_last", "vv", [((rows, D), bf16)])(grad_pre, up)[0]
+
+
+def up_sent_kernel(spot, grad_pre, second, up_sent, work):
     up_product(second, grad_pre, 0, 1 - spot[1], up_sent, work)
 
 
-def second_grad(spot, grad_pre, up, second):
-    rows = grad_pre.shape[0] // CHIPS
-    outs = call(
-        second_grad_kernel,
-        "second_grad",
-        "svvv",
-        [((rows, D), bf16)] * CHIPS + [((ROWS_Z, FF_CHIP), bf16)],
+def up_sent_of(spot, grad_pre, second):
+    return call(
+        up_sent_kernel,
+        "up_sent",
+        "svv",
+        [((ROWS_Z, FF_CHIP), bf16)],
         [pltpu.VMEM((256, FF_CHIP), f32)],
-    )(spot, grad_pre, up, second)
-    return outs[:CHIPS], outs[CHIPS]
+    )(spot, grad_pre, second)[0]
 
 
 def split_rows(core, whole, sent, kept):
@@ -1210,16 +1236,18 @@
         w_out,
         out_other,
     )
-    out_parts = from_chips(partial_out)
+    p0, p1, p2, h1, h2 = partial_out
+    p1, p2 = pass_on(p1, p2, swap(h1, 4), swap(h2, 2))
+    out_parts = [p0, swap(p1, 2), swap(p2, 4)]
     cotangent_late, _ = fence(cotangent, partial_out[0])
-    up_half_a, up_half_b, part, first, second = up_join(cotangent_late, loads)
-    up_far = [z_swap(up_half_a), z_swap(up_half_b)]
+    up_near, part, first, second = up_join(cotangent_late, loads)
+    up_far = z_swap(up_near)
     passed = [swap(first, 4), swap(second, 2)]
-    passed, up_far[0], up_far[1], *out_parts = fence_list(passed, *up_far, *out_parts)
+    passed, up_far, *out_parts = fence_list(passed, up_far, *out_parts)
     mixed, second_own = mix(out_parts, tokens, table)
     second_blocks = from_chips([second_own] * CHIPS)
-    up_far, _ = fence_list(up_far, second_own)
-    up_rest = join([up_half_a, up_half_b] + up_far)
+    up_far, _ = fence(up_far, second_own)
+    up_rest = join([up_near, up_far])
     up_own_sent, _ = fence(up_own, second_own)
     up_other = [swap(up_own_sent, 1), swap(up_rest, 1)]
     down_sent, _ = fence(w_down, second_own)
@@ -1227,7 +1255,7 @@
     part, down_other = fence(part, down_other)
     grad_act, down, whole_cotangent = act_grad(spot, part, passed, w_down, down_other)
 
-    second_low, act_low, grad_pre, up_bias_sum, up = hidden_first(
+    second_low, act_low, grad_pre, up_bias_sum, up, *partial_second = hidden_first(
         spot,
         second_blocks[:3],
         grad_act,
@@ -1240,14 +1268,15 @@
         spot, block, grad_act, table, whole_cotangent, up, second_low, act_low, grad_pre, up_bias_sum
     )
     down_got = swap(down_sent, 1)
-    partial_second, up_sent = second_grad(spot, grad_pre, up, second_low)
+    up_sent = up_sent_of(spot, grad_pre, second_low)
     up_got = swap(up_sent, 1)
     act_low, up_sent = fence(act_low, up_sent)
     down_a = down_grad_of(spot, act_low, whole_cotangent, down_got)
     side0 = z_swap(down_a)
-    *partial_second, down_a = fence(*partial_second, down_a)
+    up_late, _ = fence(up, down_a)
+    partial_second = partial_second + [second_last(grad_pre, up_late)]
     second_parts = from_chips(partial_second)
-    second_low, down_a = fence(second_low, down_a)
+    second_low, _ = fence(second_low, partial_second[3])
     up_a, up_b, up_sent, down_b, down_sent = rest_of_grads(
         spot, second_low, grad_pre, act_low, whole_cotangent
     )
@@ -1347,7 +1376,9 @@
     up_total = from_chips(up_ready)
     (sums,) = add_all([sums], [sums_got])
 
-    up_total, side6, middle6, sums = fence_list(up_total, side6, middle6, sums)
+    up_total, side6, middle6, sums, qkv_ready = fence_list(
+        up_total, side6, middle6, sums, qkv_ready
+    )
     middle6, _ = fence(middle6, side6)
     send7 = z_half(half5, middle6)
     side7 = along_z([(1, 0), (2, 3)], send7)

time: 275 us -> 270 us (0.982)
  waiting for transfers between devices: 116 us -> 113 us
    ppermute x19 -> x18, waiting for transfers between devices: 39.9 us -> 30.4 us  [along_z(): return lax.ppermute(value, 'dp', pairs)]
    ppermute x54 -> x55, waiting for transfers between devices: 76.4 us -> 82.2 us  [swap(): return lax.ppermute(value, 'fsdp', pairs)]
    ppermute x19 -> x18, starting transfers between devices: 36.3 us -> 32.6 us  [along_z(): return lax.ppermute(value, 'dp', pairs)]
    ppermute x54 -> x55, starting transfers between devices: 50.9 us -> 52.5 us  [swap(): return lax.ppermute(value, 'fsdp', pairs)]
    pallas_call x46 -> x48, Pallas kernels: 60 us -> 61.5 us  [run(): return made(*placed)]
  transfers between devices with their start and end apart: 73 -> 73, of which waited for: 35 -> 36; matrix products, arithmetic and copies ran while one was open for 0% -> 0% of each run, Pallas kernels for 22% -> 23%
where the time goes in v5:
time: 270 us
  waiting for transfers between devices  113 us (42%)
  starting transfers between devices  85.1 us (32%)
  Pallas kernels  70.3 us (26%)
    ppermute x55, waiting for transfers between devices, swap(): return lax.ppermute(value, 'fsdp', pairs)  82.2 us
    pallas_call x48, Pallas kernels, run(): return made(*placed)  61.5 us
    ppermute x55, starting transfers between devices, swap(): return lax.ppermute(value, 'fsdp', pairs)  52.5 us
    ppermute x18, starting transfers between devices, along_z(): return lax.ppermute(value, 'dp', pairs)  32.6 us
    ppermute x18, waiting for transfers between devices, along_z(): return lax.ppermute(value, 'dp', pairs)  30.4 us
  transfers between devices with their start and end apart: 73, of which 36 were waited for; matrix products, arithmetic and copies ran while one was open for 0% of the time, Pallas kernels for 23%

profile of v5, /device:TPU:0, one launch (start us, length us, event | category | flops | bytes accessed | tf_op | source)
XLA Modules:
  0.0 270.1 jit_solution(10622560816187165757)
XLA Ops:
  0.7 3.0 %collective-permute-start.1 = (bf16[128,1280]{1,0:T(8,128)(2,1)}, bf16[128,1280]{1,0:T(8,128)(2,1)S(1)}, u32[]{:S(2)}, u32[]{:S(2)}) collective-permute-start(bf16[128,1280]{1,0:T(8,128)(2,1)} %tokens.3), channel_id=1, source_target_pairs={{0,4},{1,5},{2,6},{3,7},{4,0},{5,1},{6,2},{7,3},{8,12},{9,13},{10,... | collective-permute-start | bytes 983048 | tf_op jit(solution)/shard_map/ppermute | solution.py:1182
  5.9 2.9 %qkv_blocks.1 = (bf16[168,960]{1,0:T(8,128)(2,1)S(1)}, bf16[88,960]{1,0:T(8,128)(2,1)S(1)}, bf16[88,960]{1,0:T(8,128)(2,1)S(1)}, bf16[88,960]{1,0:T(8,128)(2,1)S(1)}) custom-call(s32[4]{0:T(128)S(1)} %pad_add_fusion.spot, s32[1,2]{1,0:T(1,128)S(1)} %copy-done.3, s32[128]{0:T(128)} %padding.1, bf16[160,3840]{1,0:T(8,128)(2,1)} %weights.2, ...), custom_call_target="tpu_custom_call" | custom-call | flops 1 | bytes 1 | tf_op jit(solution)/shard_map/qkv_blocks/pallas_call | solution.py:142
  9.5 2.9 %collective-permute-start.4 = (bf16[88,960]{1,0:T(8,128)(2,1)S(1)}, bf16[88,960]{1,0:T(8,128)(2,1)S(1)}, u32[]{:S(2)}, u32[]{:S(2)}) collective-permute-start(bf16[88,960]{1,0:T(8,128)(2,1)S(1)} %get-tuple-element.255), channel_id=1, source_target_pairs={{0,6},{1,7},{2,4},{3,5},{4,2},{5,3},{6,0},{7,1},{8,14},{9,15},{10,... | collective-permute-start | bytes 506888 | tf_op jit(solution)/shard_map/ppermute | solution.py:1182
  12.4 6.0 %collective-permute-done.2.q1 = bf16[88,960]{1,0:T(8,128)(2,1)S(1)} collective-permute-done((bf16[88,960]{1,0:T(8,128)(2,1)S(1)}, bf16[88,960]{1,0:T(8,128)(2,1)S(1)}, u32[]{:S(2)}, u32[]{:S(2)}) %collective-permute-start.2) | collective-permute-done | bytes 168992 | tf_op jit(solution)/shard_map/ppermute | solution.py:1182
  31.4 5.7 %collective-permute-done.7.whole.refs_1_ = bf16[240,960]{1,0:T(8,128)(2,1)S(1)} collective-permute-done((bf16[240,960]{1,0:T(8,128)(2,1)S(1)}, bf16[240,960]{1,0:T(8,128)(2,1)S(1)}, u32[]{:S(2)}, u32[]{:S(2)}) %collective-permute-start.7) | collective-permute-done | bytes 460832 | tf_op jit(solution)/shard_map/ppermute | solution.py:1198
  39.0 7.3 %enter.1 = (f32[8,1280]{1,0:T(8,128)S(1)}, bf16[512,128]{1,0:T(8,128)(2,1)S(1)}, bf16[1280,960]{1,0:T(8,128)(2,1)S(1)}, bf16[320,1280]{1,0:T(8,128)(2,1)S(1)}, b...) custom-call(s32[4]{0:T(128)S(1)} %pad_add_fusion.spot, ...), custom_call_target="tpu_custom_call" | custom-call | flops 1 | bytes 1 | tf_op jit(solution)/shard_map/enter/pallas_call | solution.py:142
  50.7 3.5 %collective-permute-done.18.h1 = bf16[64,1280]{1,0:T(8,128)(2,1)S(1)} collective-permute-done((bf16[64,1280]{1,0:T(8,128)(2,1)S(1)}, bf16[64,1280]{1,0:T(8,128)(2,1)S(1)}, u32[]{:S(2)}, u32[]{:S(2)}) %collective-permute-start.18) | collective-permute-done | bytes 163872 | tf_op jit(solution)/shard_map/ppermute | solution.py:1182
  59.7 7.4 %collective-permute-done.15.g1 = bf16[64,1280]{1,0:T(8,128)(2,1)S(1)} collective-permute-done((bf16[64,1280]{1,0:T(8,128)(2,1)S(1)}, bf16[64,1280]{1,0:T(8,128)(2,1)S(1)}, u32[]{:S(2)}, u32[]{:S(2)}) %collective-permute-start.15) | collective-permute-done | bytes 163872 | tf_op jit(solution)/shard_map/ppermute | solution.py:1182
  72.7 4.7 %act_grad.1 = (f32[512,1280]{1,0:T(8,128)S(1)}, bf16[1280,1280]{1,0:T(8,128)(2,1)S(1)}, bf16[512,1280]{1,0:T(8,128)(2,1)S(1)}) custom-call(s32[4]{0:T(128)S(1)} %pad_add_fusion.spot, bf16[384,1280]{1,0:T(8,128)(2,1)S(1)} %get-tuple-element.298.part, bf16[64,1280]{1,0:T(8,128)(2,1)S(1)} %collective-permute-done.15.g1, ...), custom_call_target="tpu_custom_call" | custom-call | flops 1 | bytes 1 | tf_op jit(solution)/shard_map/act_grad/pallas_call | solution.py:142
  79.6 6.5 %hidden_first.1 = (bf16[512,1280]{1,0:T(8,128)(2,1)S(1)}, bf16[512,1280]{1,0:T(8,128)(2,1)S(1)}, bf16[512,1280]{1,0:T(8,128)(2,1)S(1)}, f32[1,1280]{1,0:T(1,128)...) custom-call(s32[4]{0:T(128)S(1)} %pad_add_fusion.spot, ...), custom_call_target="tpu_custom_call" | custom-call | flops 1 | bytes 1 | tf_op jit(solution)/shard_map/hidden_first/pallas_call | solution.py:142
  86.5 2.9 %hidden_last.1 = (bf16[512,1280]{1,0:T(8,128)(2,1)S(1)}, bf16[512,1280]{1,0:T(8,128)(2,1)S(1)}, bf16[512,1280]{1,0:T(8,128)(2,1)S(1)}, f32[1,1280]{1,0:T(1,128)S(1)}, bf16[320,1280]{1,0:T(8,128)(2,1)S(1)}) custom-call(s32[4]{0:T(128)S(1)} %pad_add_fusion.spot, ...), custom_call_target="tpu_custom_call", output_to_operand_aliasing={{0}: (6, {}), {1}: (7, {}), {2}: (8, {})} | custom-call | flops 1 | bytes 1 | tf_op jit(solution)/shard_map/hidden_last/pallas_call | solution.py:697
  98.9 3.9 %rest.1 = (bf16[320,1280]{1,0:T(8,128)(2,1)S(1)}, bf16[320,1280]{1,0:T(8,128)(2,1)S(1)}, bf16[320,1280]{1,0:T(8,128)(2,1)S(1)}, bf16[320,1280]{1,0:T(8,128)(2,1)S(1)}, bf16[320,1280]{1,0:T(8,128)(2,1)S(1)}) custom-call(s32[4]{0:T(128)S(1)} %pad_add_fusion.spot, bf16[512,1280]{1,0:T(8,128)(2,1)S(1)} %get-tuple-element.324.second, ...), custom_call_target="tpu_custom_call" | custom-call | flops 1 | bytes 1 | tf_op jit(solution)/shard_map/rest/pallas_call | solution.py:142
  104.1 6.8 %collective-permute-done.28.p2 = bf16[128,1280]{1,0:T(8,128)(2,1)S(1)} collective-permute-done((bf16[128,1280]{1,0:T(8,128)(2,1)S(1)}, bf16[128,1280]{1,0:T(8,128)(2,1)S(1)}, u32[]{:S(2)}, u32[]{:S(2)}) %collective-permute-start.28) | collective-permute-done | bytes 327712 | tf_op jit(solution)/shard_map/ppermute | solution.py:1182
  110.9 2.5 collective-permute-done.32.refs_1_
  119.4 2.6 result.1
  122.2 5.3 %collective-permute-done.36.b3 = bf16[128,1280]{1,0:T(8,128)(2,1)S(1)} collective-permute-done((bf16[128,1280]{1,0:T(8,128)(2,1)S(1)}, bf16[128,1280]{1,0:T(8,128)(2,1)S(1)}, u32[]{:S(2)}, u32[]{:S(2)}) %collective-permute-start.36) | collective-permute-done | bytes 327712 | tf_op jit(solution)/shard_map/ppermute | solution.py:1182
  127.5 5.0 %collective-permute-done.35.b2 = bf16[128,1280]{1,0:T(8,128)(2,1)S(1)} collective-permute-done((bf16[128,1280]{1,0:T(8,128)(2,1)S(1)}, bf16[128,1280]{1,0:T(8,128)(2,1)S(1)}, u32[]{:S(2)}, u32[]{:S(2)}) %collective-permute-start.35) | collective-permute-done | bytes 327712 | tf_op jit(solution)/shard_map/ppermute | solution.py:1182
  133.9 3.9 %collective-permute-start.40 = (bf16[320,1280]{1,0:T(8,128)(2,1)S(1)}, bf16[320,1280]{1,0:T(8,128)(2,1)S(1)}, u32[]{:S(2)}, u32[]{:S(2)}) collective-permute-start(bf16[320,1280]{1,0:T(8,128)(2,1)S(1)} %z_send.4.sent), channel_id=1, source_target_pairs={{0,8},{8,0},{16,24},{24,16},{1,9},{9,1},{17,25},{25,17},{2,10},{10... | collective-permute-start | bytes 2457608 | tf_op jit(solution)/shard_map/ppermute | solution.py:1198
  138.5 6.9 %leave.1 = (bf16[512,1280]{1,0:T(8,128)(2,1)S(1)}, bf16[512,960]{1,0:T(8,128)(2,1)S(1)}, f32[1,960]{1,0:T(1,128)S(1)}, bf16[128,1280]{1,0:T(8,128)(2,1)S(1)}, bf...) custom-call(bf16[128,1280]{1,0:T(8,128)(2,1)S(1)} %get-tuple-element.356.b0, ...), custom_call_target="tpu_custom_call" | custom-call | flops 1 | bytes 1 | tf_op jit(solution)/shard_map/leave/pallas_call | solution.py:142
  145.4 3.9 %qkv_grad.1 = (bf16[2,160,960]{2,1,0:T(8,128)(2,1)S(1)}, bf16[2,160,960]{2,1,0:T(8,128)(2,1)S(1)}, bf16[4,160,960]{2,1,0:T(8,128)(2,1)S(1)}, bf16[160,1280]{1,0:T(8,128)(2,1)S(1)}, bf16[160,1280]{1,0:T(8,128)(2,1)S(1)}) custom-call(s32[4]{0:T(128)S(1)} %pad_add_fusion.spot, bf16[512,1280]{1,0:T(8,128)(2,1)S(1)} %get-tuple-element.377.first_low, ...), custom_call_target="tpu_custom_call" | custom-call | flops 1 | bytes 1 | tf_op jit(solution)/shard_map/qkv_grad/pallas_call | solution.py:142
  149.9 3.0 %collective-permute-done.44.out_got = bf16[160,1280]{1,0:T(8,128)(2,1)S(1)} collective-permute-done((bf16[160,1280]{1,0:T(8,128)(2,1)S(1)}, bf16[160,1280]{1,0:T(8,128)(2,1)S(1)}, u32[]{:S(2)}, u32[]{:S(2)}) %collective-permute-start.44) | collective-permute-done | bytes 409632 | tf_op jit(solution)/shard_map/ppermute | solution.py:1182
  156.7 3.8 %collective-permute-start.49 = (bf16[320,1280]{1,0:T(8,128)(2,1)S(1)}, bf16[320,1280]{1,0:T(8,128)(2,1)S(1)}, u32[]{:S(2)}, u32[]{:S(2)}) collective-permute-start(bf16[320,1280]{1,0:T(8,128)(2,1)S(1)} %z_send.5.sent), channel_id=1, source_target_pairs={{0,8},{8,0},{16,24},{24,16},{1,9},{9,1},{17,25},{25,17},{2,10},{10... | collective-permute-start | bytes 2457608 | tf_op jit(solution)/shard_map/ppermute | solution.py:1198
  165.0 14.4 %collective-permute-done.49.refs_1_.got_side = bf16[320,1280]{1,0:T(8,128)(2,1)S(1)} collective-permute-done((bf16[320,1280]{1,0:T(8,128)(2,1)S(1)}, bf16[320,1280]{1,0:T(8,128)(2,1)S(1)}, u32[]{:S(2)}, u32[]{:S(2)}) %collective-permute-start.49) | collective-permute-done | bytes 819232 | tf_op jit(solution)/shard_map/ppermute | solution.py:1198
  180.2 3.8 %collective-permute-start.54 = (bf16[320,1280]{1,0:T(8,128)(2,1)S(1)}, bf16[320,1280]{1,0:T(8,128)(2,1)S(1)}, u32[]{:S(2)}, u32[]{:S(2)}) collective-permute-start(bf16[320,1280]{1,0:T(8,128)(2,1)S(1)} %z_send.6.sent), channel_id=1, source_target_pairs={{0,8},{8,0},{16,24},{24,16},{1,9},{9,1},{17,25},{25,17},{2,10},{10... | collective-permute-start | bytes 2457608 | tf_op jit(solution)/shard_map/ppermute | solution.py:1198
  188.3 7.2 %collective-permute-done.51.r1 = bf16[128,1280]{1,0:T(8,128)(2,1)S(1)} collective-permute-done((bf16[128,1280]{1,0:T(8,128)(2,1)S(1)}, bf16[128,1280]{1,0:T(8,128)(2,1)S(1)}, u32[]{:S(2)}, u32[]{:S(2)}) %collective-permute-start.51) | collective-permute-done | bytes 327712 | tf_op jit(solution)/shard_map/ppermute | solution.py:1182
  195.5 6.2 %collective-permute-done.52.r2 = bf16[128,1280]{1,0:T(8,128)(2,1)S(1)} collective-permute-done((bf16[128,1280]{1,0:T(8,128)(2,1)S(1)}, bf16[128,1280]{1,0:T(8,128)(2,1)S(1)}, u32[]{:S(2)}, u32[]{:S(2)}) %collective-permute-start.52) | collective-permute-done | bytes 327712 | tf_op jit(solution)/shard_map/ppermute | solution.py:1182
  202.9 3.8 %collective-permute-start.60 = (bf16[320,1280]{1,0:T(8,128)(2,1)S(1)}, bf16[320,1280]{1,0:T(8,128)(2,1)S(1)}, u32[]{:S(2)}, u32[]{:S(2)}) collective-permute-start(bf16[320,1280]{1,0:T(8,128)(2,1)S(1)} %z_send.7.sent), channel_id=1, source_target_pairs={{0,8},{8,0},{16,24},{24,16},{1,9},{9,1},{17,25},{25,17},{2,10},{10... | collective-permute-start | bytes 2457608 | tf_op jit(solution)/shard_map/ppermute | solution.py:1198
  207.5 2.6 end.1
  222.4 3.3 %collective-permute-done.62.refs_1_ = f32[16,1280]{1,0:T(8,128)S(1)} collective-permute-done((f32[16,1280]{1,0:T(8,128)S(1)}, f32[16,1280]{1,0:T(8,128)S(1)}, u32[]{:S(2)}, u32[]{:S(2)}) %collective-permute-start.62) | collective-permute-done | bytes 81952 | tf_op jit(solution)/shard_map/ppermute | solution.py:1198
  233.2 8.2 %collective-permute-done.63.b1 = bf16[160,1280]{1,0:T(8,128)(2,1)S(1)} collective-permute-done((bf16[160,1280]{1,0:T(8,128)(2,1)S(1)}, bf16[160,1280]{1,0:T(8,128)(2,1)S(1)}, u32[]{:S(2)}, u32[]{:S(2)}) %collective-permute-start.63) | collective-permute-done | bytes 409632 | tf_op jit(solution)/shard_map/ppermute | solution.py:1182
  241.4 6.1 %collective-permute-done.64.b2 = bf16[160,1280]{1,0:T(8,128)(2,1)S(1)} collective-permute-done((bf16[160,1280]{1,0:T(8,128)(2,1)S(1)}, bf16[160,1280]{1,0:T(8,128)(2,1)S(1)}, u32[]{:S(2)}, u32[]{:S(2)}) %collective-permute-start.64) | collective-permute-done | bytes 409632 | tf_op jit(solution)/shard_map/ppermute | solution.py:1182
  254.3 3.2 %collective-permute-start.71 = (f32[16,1280]{1,0:T(8,128)S(1)}, f32[16,1280]{1,0:T(8,128)S(1)}, u32[]{:S(2)}, u32[]{:S(2)}) collective-permute-start(f32[16,1280]{1,0:T(8,128)S(1)} %add.41.refs_1_), channel_id=1, source_target_pairs={{0,16},{8,24},{16,0},{24,8},{1,17},{9,25},{17,1},{25,9},{2,18},{10... | collective-permute-start | bytes 245768 | tf_op jit(solution)/shard_map/ppermute | solution.py:1198
  (181 shorter events, 109.7 us)
Async XLA Ops:
  0.7 19.9 %collective-permute-start.1 = (bf16[128,1280]{1,0:T(8,128)(2,1)}, bf16[128,1280]{1,0:T(8,128)(2,1)S(1)}, u32[]{:S(2)}, u32[]{:S(2)}) collective-permute-start(bf16[128,1280]{1,0:T(8,128)(2,1)} %tokens.3), channel_id=1, source_target_pairs={{0,4},{1,5},{2,6},{3,7},{4,0},{5,1},{6,2},{7,3},{8,12},{9,13},{10,... | collective-permute-start | bytes 983048 | tf_op jit(solution)/shard_map/ppermute | solution.py:1182
  3.7 16.9 %collective-permute-start = (bf16[128,1280]{1,0:T(8,128)(2,1)}, bf16[128,1280]{1,0:T(8,128)(2,1)S(1)}, u32[]{:S(2)}, u32[]{:S(2)}) collective-permute-start(bf16[128,1280]{1,0:T(8,128)(2,1)} %tokens.3), channel_id=1, source_target_pairs={{0,2},{1,3},{2,0},{3,1},{4,6},{5,7},{6,4},{7,5},{8,10},{9,11},{10,... | collective-permute-start | bytes 983048 | tf_op jit(solution)/shard_map/ppermute | solution.py:1182
  20.7 16.3 %collective-permute-start.8 = (bf16[432,960]{1,0:T(8,128)(2,1)S(1)}, bf16[432,960]{1,0:T(8,128)(2,1)S(1)}, u32[]{:S(2)}, u32[]{:S(2)}) collective-permute-start(bf16[432,960]{1,0:T(8,128)(2,1)S(1)} %get-tuple-element.265.refs_0_), channel_id=1, source_target_pairs={{0,1},{1,0},{2,3},{3,2},{4,5},{5,4},{6,7},{7,6},{8,9},{9,8},{10,11... | collective-permute-start | bytes 2488328 | tf_op jit(solution)/shard_map/ppermute | solution.py:1182
  27.4 19.3 %collective-permute-start.12 = (bf16[208,1280]{1,0:T(8,128)(2,1)S(1)}, bf16[208,1280]{1,0:T(8,128)(2,1)S(1)}, u32[]{:S(2)}, u32[]{:S(2)}) collective-permute-start(bf16[208,1280]{1,0:T(8,128)(2,1)S(1)} %get-tuple-element.279), channel_id=1, source_target_pairs={{0,2},{1,3},{2,0},{3,1},{4,6},{5,7},{6,4},{7,5},{8,10},{9,11},{10,... | collective-permute-start | bytes 1597448 | tf_op jit(solution)/shard_map/ppermute | solution.py:1182
  29.1 17.8 %collective-permute-start.13 = (bf16[208,1280]{1,0:T(8,128)(2,1)S(1)}, bf16[208,1280]{1,0:T(8,128)(2,1)S(1)}, u32[]{:S(2)}, u32[]{:S(2)}) collective-permute-start(bf16[208,1280]{1,0:T(8,128)(2,1)S(1)} %get-tuple-element.280), channel_id=1, source_target_pairs={{0,4},{1,5},{2,6},{3,7},{4,0},{5,1},{6,2},{7,3},{8,12},{9,13},{10,... | collective-permute-start | bytes 1597448 | tf_op jit(solution)/shard_map/ppermute | solution.py:1182
  47.0 20.1 %collective-permute-start.17 = (bf16[240,1280]{1,0:T(8,128)(2,1)S(1)}, bf16[240,1280]{1,0:T(8,128)(2,1)S(1)}, u32[]{:S(2)}, u32[]{:S(2)}) collective-permute-start(bf16[240,1280]{1,0:T(8,128)(2,1)S(1)} %get-tuple-element.284.refs_0_), channel_id=1, source_target_pairs={{0,8},{8,0},{16,24},{24,16},{1,9},{9,1},{17,25},{25,17},{2,10},{10... | collective-permute-start | bytes 1843208 | tf_op jit(solution)/shard_map/ppermute | solution.py:1198
  71.0 15.5 %collective-permute-start.29 = (bf16[128,1280]{1,0:T(8,128)(2,1)S(1)}, bf16[128,1280]{1,0:T(8,128)(2,1)S(1)}, u32[]{:S(2)}, u32[]{:S(2)}) collective-permute-start(bf16[128,1280]{1,0:T(8,128)(2,1)S(1)} %get-tuple-element.295.s0), channel_id=1, source_target_pairs={{0,6},{1,7},{2,4},{3,5},{4,2},{5,3},{6,0},{7,1},{8,14},{9,15},{10,... | collective-permute-start | bytes 983048 | tf_op jit(solution)/shard_map/ppermute | solution.py:1182
  93.0 20.4 %collective-permute-start.32 = (bf16[320,1280]{1,0:T(8,128)(2,1)S(1)}, bf16[320,1280]{1,0:T(8,128)(2,1)S(1)}, u32[]{:S(2)}, u32[]{:S(2)}) collective-permute-start(bf16[320,1280]{1,0:T(8,128)(2,1)S(1)} %down_grad.1.refs_0_), channel_id=1, source_target_pairs={{0,8},{8,0},{16,24},{24,16},{1,9},{9,1},{17,25},{25,17},{2,10},{10... | collective-permute-start | bytes 2457608 | tf_op jit(solution)/shard_map/ppermute | solution.py:1198
  94.7 16.2 %collective-permute-start.28 = (bf16[128,1280]{1,0:T(8,128)(2,1)S(1)}, bf16[128,1280]{1,0:T(8,128)(2,1)S(1)}, u32[]{:S(2)}, u32[]{:S(2)}) collective-permute-start(bf16[128,1280]{1,0:T(8,128)(2,1)S(1)} %get-tuple-element.309), channel_id=1, source_target_pairs={{0,4},{1,5},{2,6},{3,7},{4,0},{5,1},{6,2},{7,3},{8,12},{9,13},{10,... | collective-permute-start | bytes 983048 | tf_op jit(solution)/shard_map/ppermute | solution.py:1182
  102.8 15.7 %collective-permute-start.39 = (bf16[320,1280]{1,0:T(8,128)(2,1)S(1)}, bf16[320,1280]{1,0:T(8,128)(2,1)S(1)}, u32[]{:S(2)}, u32[]{:S(2)}) collective-permute-start(bf16[320,1280]{1,0:T(8,128)(2,1)S(1)} %get-tuple-element.341), channel_id=1, source_target_pairs={{0,1},{1,0},{2,3},{3,2},{4,5},{5,4},{6,7},{7,6},{8,9},{9,8},{10,11... | collective-permute-start | bytes 2457608 | tf_op jit(solution)/shard_map/ppermute | solution.py:1182
  113.6 19.5 %collective-permute-start.37 = (bf16[320,1280]{1,0:T(8,128)(2,1)S(1)}, bf16[320,1280]{1,0:T(8,128)(2,1)S(1)}, u32[]{:S(2)}, u32[]{:S(2)}) collective-permute-start(bf16[320,1280]{1,0:T(8,128)(2,1)S(1)} %add.30.refs_0_), channel_id=1, source_target_pairs={{0,8},{8,0},{16,24},{24,16},{1,9},{9,1},{17,25},{25,17},{2,10},{10... | collective-permute-start | bytes 2457608 | tf_op jit(solution)/shard_map/ppermute | solution.py:1198
  114.1 19.0 %collective-permute-start.38 = (bf16[320,1280]{1,0:T(8,128)(2,1)S(1)}, bf16[320,1280]{1,0:T(8,128)(2,1)S(1)}, u32[]{:S(2)}, u32[]{:S(2)}) collective-permute-start(bf16[320,1280]{1,0:T(8,128)(2,1)S(1)} %add.31.half), channel_id=1, source_target_pairs={{8,16},{16,8},{9,17},{17,9},{10,18},{18,10},{11,19},{19,11},{12,20... | collective-permute-start | bytes 2457608 | tf_op jit(solution)/shard_map/ppermute | solution.py:1198
  117.6 14.9 %collective-permute-start.35 = (bf16[128,1280]{1,0:T(8,128)(2,1)S(1)}, bf16[128,1280]{1,0:T(8,128)(2,1)S(1)}, u32[]{:S(2)}, u32[]{:S(2)}) collective-permute-start(bf16[128,1280]{1,0:T(8,128)(2,1)S(1)} %get-tuple-element.356.b0), channel_id=1, source_target_pairs={{0,4},{1,5},{2,6},{3,7},{4,0},{5,1},{6,2},{7,3},{8,12},{9,13},{10,... | collective-permute-start | bytes 983048 | tf_op jit(solution)/shard_map/ppermute | solution.py:1182
  118.5 14.0 %collective-permute-start.34 = (bf16[128,1280]{1,0:T(8,128)(2,1)S(1)}, bf16[128,1280]{1,0:T(8,128)(2,1)S(1)}, u32[]{:S(2)}, u32[]{:S(2)}) collective-permute-start(bf16[128,1280]{1,0:T(8,128)(2,1)S(1)} %get-tuple-element.356.b0), channel_id=1, source_target_pairs={{0,2},{1,3},{2,0},{3,1},{4,6},{5,7},{6,4},{7,5},{8,10},{9,11},{10,... | collective-permute-start | bytes 983048 | tf_op jit(solution)/shard_map/ppermute | solution.py:1182
  133.9 21.9 %collective-permute-start.40 = (bf16[320,1280]{1,0:T(8,128)(2,1)S(1)}, bf16[320,1280]{1,0:T(8,128)(2,1)S(1)}, u32[]{:S(2)}, u32[]{:S(2)}) collective-permute-start(bf16[320,1280]{1,0:T(8,128)(2,1)S(1)} %z_send.4.sent), channel_id=1, source_target_pairs={{0,8},{8,0},{16,24},{24,16},{1,9},{9,1},{17,25},{25,17},{2,10},{10... | collective-permute-start | bytes 2457608 | tf_op jit(solution)/shard_map/ppermute | solution.py:1198
  137.8 18.0 %collective-permute-start.41 = (bf16[320,1280]{1,0:T(8,128)(2,1)S(1)}, bf16[320,1280]{1,0:T(8,128)(2,1)S(1)}, u32[]{:S(2)}, u32[]{:S(2)}) collective-permute-start(bf16[320,1280]{1,0:T(8,128)(2,1)S(1)} %add.33.half), channel_id=1, source_target_pairs={{8,16},{16,8},{9,17},{17,9},{10,18},{18,10},{11,19},{19,11},{12,20... | collective-permute-start | bytes 2457608 | tf_op jit(solution)/shard_map/ppermute | solution.py:1198
  156.7 22.7 %collective-permute-start.49 = (bf16[320,1280]{1,0:T(8,128)(2,1)S(1)}, bf16[320,1280]{1,0:T(8,128)(2,1)S(1)}, u32[]{:S(2)}, u32[]{:S(2)}) collective-permute-start(bf16[320,1280]{1,0:T(8,128)(2,1)S(1)} %z_send.5.sent), channel_id=1, source_target_pairs={{0,8},{8,0},{16,24},{24,16},{1,9},{9,1},{17,25},{25,17},{2,10},{10... | collective-permute-start | bytes 2457608 | tf_op jit(solution)/shard_map/ppermute | solution.py:1198
  160.5 18.8 %collective-permute-start.50 = (bf16[320,1280]{1,0:T(8,128)(2,1)S(1)}, bf16[320,1280]{1,0:T(8,128)(2,1)S(1)}, u32[]{:S(2)}, u32[]{:S(2)}) collective-permute-start(bf16[320,1280]{1,0:T(8,128)(2,1)S(1)} %add.34.half), channel_id=1, source_target_pairs={{8,16},{16,8},{9,17},{17,9},{10,18},{18,10},{11,19},{19,11},{12,20... | collective-permute-start | bytes 2457608 | tf_op jit(solution)/shard_map/ppermute | solution.py:1198
  161.4 17.9 %collective-permute-start.46 = (bf16[128,1280]{1,0:T(8,128)(2,1)S(1)}, bf16[128,1280]{1,0:T(8,128)(2,1)S(1)}, u32[]{:S(2)}, u32[]{:S(2)}) collective-permute-start(bf16[128,1280]{1,0:T(8,128)(2,1)S(1)} %get-tuple-element.393), channel_id=1, source_target_pairs={{0,2},{1,3},{2,0},{3,1},{4,6},{5,7},{6,4},{7,5},{8,10},{9,11},{10,... | collective-permute-start | bytes 983048 | tf_op jit(solution)/shard_map/ppermute | solution.py:1182
  162.6 16.7 %collective-permute-start.47 = (bf16[128,1280]{1,0:T(8,128)(2,1)S(1)}, bf16[128,1280]{1,0:T(8,128)(2,1)S(1)}, u32[]{:S(2)}, u32[]{:S(2)}) collective-permute-start(bf16[128,1280]{1,0:T(8,128)(2,1)S(1)} %get-tuple-element.394), channel_id=1, source_target_pairs={{0,4},{1,5},{2,6},{3,7},{4,0},{5,1},{6,2},{7,3},{8,12},{9,13},{10,... | collective-permute-start | bytes 983048 | tf_op jit(solution)/shard_map/ppermute | solution.py:1182
  163.8 15.6 %collective-permute-start.48 = (bf16[128,1280]{1,0:T(8,128)(2,1)S(1)}, bf16[128,1280]{1,0:T(8,128)(2,1)S(1)}, u32[]{:S(2)}, u32[]{:S(2)}) collective-permute-start(bf16[128,1280]{1,0:T(8,128)(2,1)S(1)} %get-tuple-element.395), channel_id=1, source_target_pairs={{0,6},{1,7},{2,4},{3,5},{4,2},{5,3},{6,0},{7,1},{8,14},{9,15},{10,... | collective-permute-start | bytes 983048 | tf_op jit(solution)/shard_map/ppermute | solution.py:1182
  180.2 21.9 %collective-permute-start.54 = (bf16[320,1280]{1,0:T(8,128)(2,1)S(1)}, bf16[320,1280]{1,0:T(8,128)(2,1)S(1)}, u32[]{:S(2)}, u32[]{:S(2)}) collective-permute-start(bf16[320,1280]{1,0:T(8,128)(2,1)S(1)} %z_send.6.sent), channel_id=1, source_target_pairs={{0,8},{8,0},{16,24},{24,16},{1,9},{9,1},{17,25},{25,17},{2,10},{10... | collective-permute-start | bytes 2457608 | tf_op jit(solution)/shard_map/ppermute | solution.py:1198
  184.0 18.0 %collective-permute-start.55 = (bf16[320,1280]{1,0:T(8,128)(2,1)S(1)}, bf16[320,1280]{1,0:T(8,128)(2,1)S(1)}, u32[]{:S(2)}, u32[]{:S(2)}) collective-permute-start(bf16[320,1280]{1,0:T(8,128)(2,1)S(1)} %add.36.half), channel_id=1, source_target_pairs={{8,16},{16,8},{9,17},{17,9},{10,18},{18,10},{11,19},{19,11},{12,20... | collective-permute-start | bytes 2457608 | tf_op jit(solution)/shard_map/ppermute | solution.py:1198
  186.0 15.7 %collective-permute-start.52 = (bf16[128,1280]{1,0:T(8,128)(2,1)S(1)}, bf16[128,1280]{1,0:T(8,128)(2,1)S(1)}, u32[]{:S(2)}, u32[]{:S(2)}) collective-permute-start(bf16[128,1280]{1,0:T(8,128)(2,1)S(1)} %get-tuple-element.407), channel_id=1, source_target_pairs={{0,4},{1,5},{2,6},{3,7},{4,0},{5,1},{6,2},{7,3},{8,12},{9,13},{10,... | collective-permute-start | bytes 983048 | tf_op jit(solution)/shard_map/ppermute | solution.py:1182
  187.1 14.6 %collective-permute-start.53 = (bf16[128,1280]{1,0:T(8,128)(2,1)S(1)}, bf16[128,1280]{1,0:T(8,128)(2,1)S(1)}, u32[]{:S(2)}, u32[]{:S(2)}) collective-permute-start(bf16[128,1280]{1,0:T(8,128)(2,1)S(1)} %get-tuple-element.408), channel_id=1, source_target_pairs={{0,6},{1,7},{2,4},{3,5},{4,2},{5,3},{6,0},{7,1},{8,14},{9,15},{10,... | collective-permute-start | bytes 983048 | tf_op jit(solution)/shard_map/ppermute | solution.py:1182
  202.9 22.7 %collective-permute-start.60 = (bf16[320,1280]{1,0:T(8,128)(2,1)S(1)}, bf16[320,1280]{1,0:T(8,128)(2,1)S(1)}, u32[]{:S(2)}, u32[]{:S(2)}) collective-permute-start(bf16[320,1280]{1,0:T(8,128)(2,1)S(1)} %z_send.7.sent), channel_id=1, source_target_pairs={{0,8},{8,0},{16,24},{24,16},{1,9},{9,1},{17,25},{25,17},{2,10},{10... | collective-permute-start | bytes 2457608 | tf_op jit(solution)/shard_map/ppermute | solution.py:1198
  206.8 18.9 %collective-permute-start.61 = (bf16[320,1280]{1,0:T(8,128)(2,1)S(1)}, bf16[320,1280]{1,0:T(8,128)(2,1)S(1)}, u32[]{:S(2)}, u32[]{:S(2)}) collective-permute-start(bf16[320,1280]{1,0:T(8,128)(2,1)S(1)} %add.37.refs_0_), channel_id=1, source_target_pairs={{8,16},{16,8},{9,17},{17,9},{10,18},{18,10},{11,19},{19,11},{12,20... | collective-permute-start | bytes 2457608 | tf_op jit(solution)/shard_map/ppermute | solution.py:1198
  226.1 21.5 %collective-permute-start.66 = (bf16[320,1280]{1,0:T(8,128)(2,1)S(1)}, bf16[320,1280]{1,0:T(8,128)(2,1)S(1)}, u32[]{:S(2)}, u32[]{:S(2)}) collective-permute-start(bf16[320,1280]{1,0:T(8,128)(2,1)S(1)} %add.40.sent), channel_id=1, source_target_pairs={{0,8},{8,0},{16,24},{24,16},{1,9},{9,1},{17,25},{25,17},{2,10},{10... | collective-permute-start | bytes 2457608 | tf_op jit(solution)/shard_map/ppermute | solution.py:1198
  228.0 19.6 %collective-permute-start.67 = (bf16[320,1280]{1,0:T(8,128)(2,1)S(1)}, bf16[320,1280]{1,0:T(8,128)(2,1)S(1)}, u32[]{:S(2)}, u32[]{:S(2)}) collective-permute-start(bf16[320,1280]{1,0:T(8,128)(2,1)S(1)} %add.39.refs_0_), channel_id=1, source_target_pairs={{8,16},{16,8},{9,17},{17,9},{10,18},{18,10},{11,19},{19,11},{12,20... | collective-permute-start | bytes 2457608 | tf_op jit(solution)/shard_map/ppermute | solution.py:1198
  230.2 17.4 %collective-permute-start.64 = (bf16[160,1280]{1,0:T(8,128)(2,1)S(1)}, bf16[160,1280]{1,0:T(8,128)(2,1)S(1)}, u32[]{:S(2)}, u32[]{:S(2)}) collective-permute-start(bf16[160,1280]{1,0:T(8,128)(2,1)S(1)} %get-tuple-element.445), channel_id=1, source_target_pairs={{0,4},{1,5},{2,6},{3,7},{4,0},{5,1},{6,2},{7,3},{8,12},{9,13},{10,... | collective-permute-start | bytes 1228808 | tf_op jit(solution)/shard_map/ppermute | solution.py:1182
  231.3 16.3 %collective-permute-start.65 = (bf16[160,1280]{1,0:T(8,128)(2,1)S(1)}, bf16[160,1280]{1,0:T(8,128)(2,1)S(1)}, u32[]{:S(2)}, u32[]{:S(2)}) collective-permute-start(bf16[160,1280]{1,0:T(8,128)(2,1)S(1)} %get-tuple-element.446), channel_id=1, source_target_pairs={{0,6},{1,7},{2,4},{3,5},{4,2},{5,3},{6,0},{7,1},{8,14},{9,15},{10,... | collective-permute-start | bytes 1228808 | tf_op jit(solution)/shard_map/ppermute | solution.py:1182
  247.8 20.3 %collective-permute-start.72 = (bf16[320,1280]{1,0:T(8,128)(2,1)S(1)}, bf16[320,1280]{1,0:T(8,128)(2,1)S(1)}, u32[]{:S(2)}, u32[]{:S(2)}) collective-permute-start(bf16[320,1280]{1,0:T(8,128)(2,1)S(1)} %add.42.sent), channel_id=1, source_target_pairs={{8,0},{16,24},{9,1},{17,25},{10,2},{18,26},{11,3},{19,27},{12,4},{... | collective-permute-start | bytes 2457608 | tf_op jit(solution)/shard_map/ppermute | solution.py:1198
  (48 other events, 424.6 us)

commit v6 on v5

--- a/solution.py
+++ b/solution.py
@@ -939,10 +939,14 @@
 
 def second_down_kernel(spot, sent, got, before, down, here, sem):
     del before
-    here[...] = jnp.where(spot[3] > 0, sent[...], got[...]).astype(f32)
-    copy = pltpu.make_async_copy(here, down.at[ROWS_Z:], sem.at[0])
-    copy.start()
-    copy.wait()
+    copies = []
+    for i in range(2):
+        rows = slice(i * SHARE, (i + 1) * SHARE)
+        here[rows, :] = jnp.where(spot[3] > 0, sent[rows, :], got[rows, :]).astype(f32)
+        target = down.at[ROWS_Z + i * SHARE : ROWS_Z + (i + 1) * SHARE]
+        copies.append(pltpu.make_async_copy(here.at[rows], target, sem.at[i]))
+        copies[-1].start()
+    wait_all(copies)
 
 
 def second_down(spot, sent, got, down):
@@ -951,7 +955,7 @@
         in_specs=[SMEM, VMEM, VMEM, HBM],
         out_specs=HBM,
         out_shape=pltpu.HBM((2 * ROWS_Z, D), f32),
-        scratch_shapes=[pltpu.VMEM((ROWS_Z, D), f32), sems(1)],
+        scratch_shapes=[pltpu.VMEM((ROWS_Z, D), f32), sems(2)],
         input_output_aliases={3: 0},
         compiler_params=pltpu.CompilerParams(vmem_limit_bytes=16 * 2**20),
         cost_estimate=COST,
@@ -1237,13 +1241,15 @@
         out_other,
     )
     p0, p1, p2, h1, h2 = partial_out
-    p1, p2 = pass_on(p1, p2, swap(h1, 4), swap(h2, 2))
-    out_parts = [p0, swap(p1, 2), swap(p2, 4)]
+    h1, h2 = swap(h1, 4), swap(h2, 2)
     cotangent_late, _ = fence(cotangent, partial_out[0])
     up_near, part, first, second = up_join(cotangent_late, loads)
     up_far = z_swap(up_near)
     passed = [swap(first, 4), swap(second, 2)]
-    passed, up_far, *out_parts = fence_list(passed, up_far, *out_parts)
+    passed, h1, h2 = fence_list(passed, h1, h2)
+    p1, p2 = pass_on(p1, p2, h1, h2)
+    out_parts = [p0, swap(p1, 2), swap(p2, 4)]
+    up_far, *out_parts = fence(up_far, *out_parts)
     mixed, second_own = mix(out_parts, tokens, table)
     second_blocks = from_chips([second_own] * CHIPS)
     up_far, _ = fence(up_far, second_own)
@@ -1284,12 +1290,12 @@
     (up_a,) = add_all([up_a], [up_got])
     up_got = swap(up_sent, 1)
 
-    second_parts, side0, up_a = fence_list(second_parts, side0, up_a)
-    half0, send1 = z_half(down_a, side0), up_a
-    send1, _ = fence(send1, half0)
+    second_parts, up_a = fence_list(second_parts, up_a)
+    grad_mixed, branch_own, mix_sums = unmix(second_parts, mixed, table, cotangent)
+    side0, _ = fence(side0, branch_own)
+    half0 = z_half(down_a, side0)
+    send1, _ = fence(up_a, half0)
     side1, middle1 = z_swap(send1), z_middle(half0)
-    second_parts, half0 = fence_list(second_parts, half0)
-    grad_mixed, branch_own, mix_sums = unmix(second_parts, mixed, table, cotangent)
     branch_blocks = from_chips([branch_own] * CHIPS)
     act_low, branch_own = fence(act_low, branch_own)
     partial_result = list(result_of(act_low, down))

time: 270 us -> 268 us (level)
  waiting for transfers between devices: 113 us -> 109 us
  transfers between devices with their start and end apart: 73 -> 73, of which waited for: 36 -> 39; matrix products, arithmetic and copies ran while one was open for 0% -> 0% of each run, Pallas kernels for 23% -> 23%
where the time goes in v6:
time: 268 us
  waiting for transfers between devices  109 us (41%)
  starting transfers between devices  86 us (32%)
  Pallas kernels  70.4 us (26%)
    ppermute x55, waiting for transfers between devices, swap(): return lax.ppermute(value, 'fsdp', pairs)  80.4 us
    pallas_call x48, Pallas kernels, run(): return made(*placed)  61.6 us
    ppermute x55, starting transfers between devices, swap(): return lax.ppermute(value, 'fsdp', pairs)  53.1 us
    ppermute x18, starting transfers between devices, along_z(): return lax.ppermute(value, 'dp', pairs)  32.9 us
    ppermute x18, waiting for transfers between devices, along_z(): return lax.ppermute(value, 'dp', pairs)  29.1 us
  transfers between devices with their start and end apart: 73, of which 39 were waited for; matrix products, arithmetic and copies ran while one was open for 0% of the time, Pallas kernels for 23%

profile of v6, /device:TPU:0, one launch (start us, length us, event | category | flops | bytes accessed | tf_op | source)
XLA Modules:
  0.0 268.0 jit_solution(5593078030561296646)
XLA Ops:
  0.7 3.0 %collective-permute-start.1 = (bf16[128,1280]{1,0:T(8,128)(2,1)}, bf16[128,1280]{1,0:T(8,128)(2,1)S(1)}, u32[]{:S(2)}, u32[]{:S(2)}) collective-permute-start(bf16[128,1280]{1,0:T(8,128)(2,1)} %tokens.3), channel_id=1, source_target_pairs={{0,4},{1,5},{2,6},{3,7},{4,0},{5,1},{6,2},{7,3},{8,12},{9,13},{10,... | collective-permute-start | bytes 983048 | tf_op jit(solution)/shard_map/ppermute | solution.py:1186
  5.9 2.9 %qkv_blocks.1 = (bf16[168,960]{1,0:T(8,128)(2,1)S(1)}, bf16[88,960]{1,0:T(8,128)(2,1)S(1)}, bf16[88,960]{1,0:T(8,128)(2,1)S(1)}, bf16[88,960]{1,0:T(8,128)(2,1)S(1)}) custom-call(s32[4]{0:T(128)S(1)} %pad_add_fusion.spot, s32[1,2]{1,0:T(1,128)S(1)} %copy-done.3, s32[128]{0:T(128)} %padding.1, bf16[160,3840]{1,0:T(8,128)(2,1)} %weights.2, ...), custom_call_target="tpu_custom_call" | custom-call | flops 1 | bytes 1 | tf_op jit(solution)/shard_map/qkv_blocks/pallas_call | solution.py:142
  9.5 2.9 %collective-permute-start.4 = (bf16[88,960]{1,0:T(8,128)(2,1)S(1)}, bf16[88,960]{1,0:T(8,128)(2,1)S(1)}, u32[]{:S(2)}, u32[]{:S(2)}) collective-permute-start(bf16[88,960]{1,0:T(8,128)(2,1)S(1)} %get-tuple-element.252), channel_id=1, source_target_pairs={{0,6},{1,7},{2,4},{3,5},{4,2},{5,3},{6,0},{7,1},{8,14},{9,15},{10,... | collective-permute-start | bytes 506888 | tf_op jit(solution)/shard_map/ppermute | solution.py:1186
  12.4 6.0 %collective-permute-done.2.q1 = bf16[88,960]{1,0:T(8,128)(2,1)S(1)} collective-permute-done((bf16[88,960]{1,0:T(8,128)(2,1)S(1)}, bf16[88,960]{1,0:T(8,128)(2,1)S(1)}, u32[]{:S(2)}, u32[]{:S(2)}) %collective-permute-start.2) | collective-permute-done | bytes 168992 | tf_op jit(solution)/shard_map/ppermute | solution.py:1186
  31.4 5.7 %collective-permute-done.7.whole.refs_1_ = bf16[240,960]{1,0:T(8,128)(2,1)S(1)} collective-permute-done((bf16[240,960]{1,0:T(8,128)(2,1)S(1)}, bf16[240,960]{1,0:T(8,128)(2,1)S(1)}, u32[]{:S(2)}, u32[]{:S(2)}) %collective-permute-start.7) | collective-permute-done | bytes 460832 | tf_op jit(solution)/shard_map/ppermute | solution.py:1202
  39.0 7.1 %enter.1 = (f32[8,1280]{1,0:T(8,128)S(1)}, bf16[512,128]{1,0:T(8,128)(2,1)S(1)}, bf16[1280,960]{1,0:T(8,128)(2,1)S(1)}, bf16[320,1280]{1,0:T(8,128)(2,1)S(1)}, b...) custom-call(s32[4]{0:T(128)S(1)} %pad_add_fusion.spot, ...), custom_call_target="tpu_custom_call" | custom-call | flops 1 | bytes 1 | tf_op jit(solution)/shard_map/enter/pallas_call | solution.py:142
  52.7 3.1 %collective-permute-done.18.h1 = bf16[64,1280]{1,0:T(8,128)(2,1)S(1)} collective-permute-done((bf16[64,1280]{1,0:T(8,128)(2,1)S(1)}, bf16[64,1280]{1,0:T(8,128)(2,1)S(1)}, u32[]{:S(2)}, u32[]{:S(2)}) %collective-permute-start.18) | collective-permute-done | bytes 163872 | tf_op jit(solution)/shard_map/ppermute | solution.py:1186
  59.9 5.7 %collective-permute-done.20.p1 = bf16[128,1280]{1,0:T(8,128)(2,1)S(1)} collective-permute-done((bf16[128,1280]{1,0:T(8,128)(2,1)S(1)}, bf16[128,1280]{1,0:T(8,128)(2,1)S(1)}, u32[]{:S(2)}, u32[]{:S(2)}) %collective-permute-start.20) | collective-permute-done | bytes 327712 | tf_op jit(solution)/shard_map/ppermute | solution.py:1186
  72.2 4.7 %act_grad.1 = (f32[512,1280]{1,0:T(8,128)S(1)}, bf16[1280,1280]{1,0:T(8,128)(2,1)S(1)}, bf16[512,1280]{1,0:T(8,128)(2,1)S(1)}) custom-call(s32[4]{0:T(128)S(1)} %pad_add_fusion.spot, bf16[384,1280]{1,0:T(8,128)(2,1)S(1)} %get-tuple-element.297.part, bf16[64,1280]{1,0:T(8,128)(2,1)S(1)} %collective-permute-done.16.g1, ...), custom_call_target="tpu_custom_call" | custom-call | flops 1 | bytes 1 | tf_op jit(solution)/shard_map/act_grad/pallas_call | solution.py:142
  78.9 6.5 %hidden_first.1 = (bf16[512,1280]{1,0:T(8,128)(2,1)S(1)}, bf16[512,1280]{1,0:T(8,128)(2,1)S(1)}, bf16[512,1280]{1,0:T(8,128)(2,1)S(1)}, f32[1,1280]{1,0:T(1,128)...) custom-call(s32[4]{0:T(128)S(1)} %pad_add_fusion.spot, ...), custom_call_target="tpu_custom_call" | custom-call | flops 1 | bytes 1 | tf_op jit(solution)/shard_map/hidden_first/pallas_call | solution.py:142
  85.7 2.9 %hidden_last.1 = (bf16[512,1280]{1,0:T(8,128)(2,1)S(1)}, bf16[512,1280]{1,0:T(8,128)(2,1)S(1)}, bf16[512,1280]{1,0:T(8,128)(2,1)S(1)}, f32[1,1280]{1,0:T(1,128)S(1)}, bf16[320,1280]{1,0:T(8,128)(2,1)S(1)}) custom-call(s32[4]{0:T(128)S(1)} %pad_add_fusion.spot, ...), custom_call_target="tpu_custom_call", output_to_operand_aliasing={{0}: (6, {}), {1}: (7, {}), {2}: (8, {})} | custom-call | flops 1 | bytes 1 | tf_op jit(solution)/shard_map/hidden_last/pallas_call | solution.py:697
  98.3 3.9 %rest.1 = (bf16[320,1280]{1,0:T(8,128)(2,1)S(1)}, bf16[320,1280]{1,0:T(8,128)(2,1)S(1)}, bf16[320,1280]{1,0:T(8,128)(2,1)S(1)}, bf16[320,1280]{1,0:T(8,128)(2,1)S(1)}, bf16[320,1280]{1,0:T(8,128)(2,1)S(1)}) custom-call(s32[4]{0:T(128)S(1)} %pad_add_fusion.spot, bf16[512,1280]{1,0:T(8,128)(2,1)S(1)} %get-tuple-element.323.second, ...), custom_call_target="tpu_custom_call" | custom-call | flops 1 | bytes 1 | tf_op jit(solution)/shard_map/rest/pallas_call | solution.py:142
  103.3 7.0 %collective-permute-done.28.p2 = bf16[128,1280]{1,0:T(8,128)(2,1)S(1)} collective-permute-done((bf16[128,1280]{1,0:T(8,128)(2,1)S(1)}, bf16[128,1280]{1,0:T(8,128)(2,1)S(1)}, u32[]{:S(2)}, u32[]{:S(2)}) %collective-permute-start.28) | collective-permute-done | bytes 327712 | tf_op jit(solution)/shard_map/ppermute | solution.py:1186
  117.6 2.6 result.1
  120.3 5.3 %collective-permute-done.35.b3 = bf16[128,1280]{1,0:T(8,128)(2,1)S(1)} collective-permute-done((bf16[128,1280]{1,0:T(8,128)(2,1)S(1)}, bf16[128,1280]{1,0:T(8,128)(2,1)S(1)}, u32[]{:S(2)}, u32[]{:S(2)}) %collective-permute-start.35) | collective-permute-done | bytes 327712 | tf_op jit(solution)/shard_map/ppermute | solution.py:1186
  125.7 5.0 %collective-permute-done.34.b2 = bf16[128,1280]{1,0:T(8,128)(2,1)S(1)} collective-permute-done((bf16[128,1280]{1,0:T(8,128)(2,1)S(1)}, bf16[128,1280]{1,0:T(8,128)(2,1)S(1)}, u32[]{:S(2)}, u32[]{:S(2)}) %collective-permute-start.34) | collective-permute-done | bytes 327712 | tf_op jit(solution)/shard_map/ppermute | solution.py:1186
  133.1 3.8 %collective-permute-start.40 = (bf16[320,1280]{1,0:T(8,128)(2,1)S(1)}, bf16[320,1280]{1,0:T(8,128)(2,1)S(1)}, u32[]{:S(2)}, u32[]{:S(2)}) collective-permute-start(bf16[320,1280]{1,0:T(8,128)(2,1)S(1)} %z_send.4.sent), channel_id=1, source_target_pairs={{0,8},{8,0},{16,24},{24,16},{1,9},{9,1},{17,25},{25,17},{2,10},{10... | collective-permute-start | bytes 2457608 | tf_op jit(solution)/shard_map/ppermute | solution.py:1202
  137.7 6.9 %leave.1 = (bf16[512,1280]{1,0:T(8,128)(2,1)S(1)}, bf16[512,960]{1,0:T(8,128)(2,1)S(1)}, f32[1,960]{1,0:T(1,128)S(1)}, bf16[128,1280]{1,0:T(8,128)(2,1)S(1)}, bf...) custom-call(bf16[128,1280]{1,0:T(8,128)(2,1)S(1)} %get-tuple-element.351.b0, ...), custom_call_target="tpu_custom_call" | custom-call | flops 1 | bytes 1 | tf_op jit(solution)/shard_map/leave/pallas_call | solution.py:142
  144.5 3.9 %qkv_grad.1 = (bf16[2,160,960]{2,1,0:T(8,128)(2,1)S(1)}, bf16[2,160,960]{2,1,0:T(8,128)(2,1)S(1)}, bf16[4,160,960]{2,1,0:T(8,128)(2,1)S(1)}, bf16[160,1280]{1,0:T(8,128)(2,1)S(1)}, bf16[160,1280]{1,0:T(8,128)(2,1)S(1)}) custom-call(s32[4]{0:T(128)S(1)} %pad_add_fusion.spot, bf16[512,1280]{1,0:T(8,128)(2,1)S(1)} %get-tuple-element.371.first_low, ...), custom_call_target="tpu_custom_call" | custom-call | flops 1 | bytes 1 | tf_op jit(solution)/shard_map/qkv_grad/pallas_call | solution.py:142
  149.0 3.0 %collective-permute-done.44.out_got = bf16[160,1280]{1,0:T(8,128)(2,1)S(1)} collective-permute-done((bf16[160,1280]{1,0:T(8,128)(2,1)S(1)}, bf16[160,1280]{1,0:T(8,128)(2,1)S(1)}, u32[]{:S(2)}, u32[]{:S(2)}) %collective-permute-start.44) | collective-permute-done | bytes 409632 | tf_op jit(solution)/shard_map/ppermute | solution.py:1186
  155.0 3.8 %collective-permute-start.49 = (bf16[320,1280]{1,0:T(8,128)(2,1)S(1)}, bf16[320,1280]{1,0:T(8,128)(2,1)S(1)}, u32[]{:S(2)}, u32[]{:S(2)}) collective-permute-start(bf16[320,1280]{1,0:T(8,128)(2,1)S(1)} %z_send.5.sent), channel_id=1, source_target_pairs={{0,8},{8,0},{16,24},{24,16},{1,9},{9,1},{17,25},{25,17},{2,10},{10... | collective-permute-start | bytes 2457608 | tf_op jit(solution)/shard_map/ppermute | solution.py:1202
  163.4 14.4 %collective-permute-done.49.refs_1_.got_side = bf16[320,1280]{1,0:T(8,128)(2,1)S(1)} collective-permute-done((bf16[320,1280]{1,0:T(8,128)(2,1)S(1)}, bf16[320,1280]{1,0:T(8,128)(2,1)S(1)}, u32[]{:S(2)}, u32[]{:S(2)}) %collective-permute-start.49) | collective-permute-done | bytes 819232 | tf_op jit(solution)/shard_map/ppermute | solution.py:1202
  178.6 3.8 %collective-permute-start.54 = (bf16[320,1280]{1,0:T(8,128)(2,1)S(1)}, bf16[320,1280]{1,0:T(8,128)(2,1)S(1)}, u32[]{:S(2)}, u32[]{:S(2)}) collective-permute-start(bf16[320,1280]{1,0:T(8,128)(2,1)S(1)} %z_send.6.sent), channel_id=1, source_target_pairs={{0,8},{8,0},{16,24},{24,16},{1,9},{9,1},{17,25},{25,17},{2,10},{10... | collective-permute-start | bytes 2457608 | tf_op jit(solution)/shard_map/ppermute | solution.py:1202
  186.7 7.2 %collective-permute-done.51.r1 = bf16[128,1280]{1,0:T(8,128)(2,1)S(1)} collective-permute-done((bf16[128,1280]{1,0:T(8,128)(2,1)S(1)}, bf16[128,1280]{1,0:T(8,128)(2,1)S(1)}, u32[]{:S(2)}, u32[]{:S(2)}) %collective-permute-start.51) | collective-permute-done | bytes 327712 | tf_op jit(solution)/shard_map/ppermute | solution.py:1186
  193.8 5.9 %collective-permute-done.52.r2 = bf16[128,1280]{1,0:T(8,128)(2,1)S(1)} collective-permute-done((bf16[128,1280]{1,0:T(8,128)(2,1)S(1)}, bf16[128,1280]{1,0:T(8,128)(2,1)S(1)}, u32[]{:S(2)}, u32[]{:S(2)}) %collective-permute-start.52) | collective-permute-done | bytes 327712 | tf_op jit(solution)/shard_map/ppermute | solution.py:1186
  201.5 3.8 %collective-permute-start.60 = (bf16[320,1280]{1,0:T(8,128)(2,1)S(1)}, bf16[320,1280]{1,0:T(8,128)(2,1)S(1)}, u32[]{:S(2)}, u32[]{:S(2)}) collective-permute-start(bf16[320,1280]{1,0:T(8,128)(2,1)S(1)} %z_send.7.sent), channel_id=1, source_target_pairs={{0,8},{8,0},{16,24},{24,16},{1,9},{9,1},{17,25},{25,17},{2,10},{10... | collective-permute-start | bytes 2457608 | tf_op jit(solution)/shard_map/ppermute | solution.py:1202
  206.1 2.6 end.1
  221.5 2.7 %collective-permute-done.62.refs_1_ = f32[16,1280]{1,0:T(8,128)S(1)} collective-permute-done((f32[16,1280]{1,0:T(8,128)S(1)}, f32[16,1280]{1,0:T(8,128)S(1)}, u32[]{:S(2)}, u32[]{:S(2)}) %collective-permute-start.62) | collective-permute-done | bytes 81952 | tf_op jit(solution)/shard_map/ppermute | solution.py:1202
  231.6 8.2 %collective-permute-done.63.b1 = bf16[160,1280]{1,0:T(8,128)(2,1)S(1)} collective-permute-done((bf16[160,1280]{1,0:T(8,128)(2,1)S(1)}, bf16[160,1280]{1,0:T(8,128)(2,1)S(1)}, u32[]{:S(2)}, u32[]{:S(2)}) %collective-permute-start.63) | collective-permute-done | bytes 409632 | tf_op jit(solution)/shard_map/ppermute | solution.py:1186
  239.8 5.9 %collective-permute-done.64.b2 = bf16[160,1280]{1,0:T(8,128)(2,1)S(1)} collective-permute-done((bf16[160,1280]{1,0:T(8,128)(2,1)S(1)}, bf16[160,1280]{1,0:T(8,128)(2,1)S(1)}, u32[]{:S(2)}, u32[]{:S(2)}) %collective-permute-start.64) | collective-permute-done | bytes 409632 | tf_op jit(solution)/shard_map/ppermute | solution.py:1186
  252.3 3.6 %collective-permute-start.71 = (f32[16,1280]{1,0:T(8,128)S(1)}, f32[16,1280]{1,0:T(8,128)S(1)}, u32[]{:S(2)}, u32[]{:S(2)}) collective-permute-start(f32[16,1280]{1,0:T(8,128)S(1)} %add.41.refs_1_), channel_id=1, source_target_pairs={{0,16},{8,24},{16,0},{24,8},{1,17},{9,25},{17,1},{25,9},{2,18},{10... | collective-permute-start | bytes 245768 | tf_op jit(solution)/shard_map/ppermute | solution.py:1202
  257.7 2.5 up_rows.1
  (181 shorter events, 110.4 us)
Async XLA Ops:
  0.7 19.9 %collective-permute-start.1 = (bf16[128,1280]{1,0:T(8,128)(2,1)}, bf16[128,1280]{1,0:T(8,128)(2,1)S(1)}, u32[]{:S(2)}, u32[]{:S(2)}) collective-permute-start(bf16[128,1280]{1,0:T(8,128)(2,1)} %tokens.3), channel_id=1, source_target_pairs={{0,4},{1,5},{2,6},{3,7},{4,0},{5,1},{6,2},{7,3},{8,12},{9,13},{10,... | collective-permute-start | bytes 983048 | tf_op jit(solution)/shard_map/ppermute | solution.py:1186
  3.7 16.9 %collective-permute-start = (bf16[128,1280]{1,0:T(8,128)(2,1)}, bf16[128,1280]{1,0:T(8,128)(2,1)S(1)}, u32[]{:S(2)}, u32[]{:S(2)}) collective-permute-start(bf16[128,1280]{1,0:T(8,128)(2,1)} %tokens.3), channel_id=1, source_target_pairs={{0,2},{1,3},{2,0},{3,1},{4,6},{5,7},{6,4},{7,5},{8,10},{9,11},{10,... | collective-permute-start | bytes 983048 | tf_op jit(solution)/shard_map/ppermute | solution.py:1186
  20.7 16.3 %collective-permute-start.8 = (bf16[432,960]{1,0:T(8,128)(2,1)S(1)}, bf16[432,960]{1,0:T(8,128)(2,1)S(1)}, u32[]{:S(2)}, u32[]{:S(2)}) collective-permute-start(bf16[432,960]{1,0:T(8,128)(2,1)S(1)} %get-tuple-element.262.refs_0_), channel_id=1, source_target_pairs={{0,1},{1,0},{2,3},{3,2},{4,5},{5,4},{6,7},{7,6},{8,9},{9,8},{10,11... | collective-permute-start | bytes 2488328 | tf_op jit(solution)/shard_map/ppermute | solution.py:1186
  27.4 19.3 %collective-permute-start.12 = (bf16[208,1280]{1,0:T(8,128)(2,1)S(1)}, bf16[208,1280]{1,0:T(8,128)(2,1)S(1)}, u32[]{:S(2)}, u32[]{:S(2)}) collective-permute-start(bf16[208,1280]{1,0:T(8,128)(2,1)S(1)} %get-tuple-element.276), channel_id=1, source_target_pairs={{0,2},{1,3},{2,0},{3,1},{4,6},{5,7},{6,4},{7,5},{8,10},{9,11},{10,... | collective-permute-start | bytes 1597448 | tf_op jit(solution)/shard_map/ppermute | solution.py:1186
  29.1 17.8 %collective-permute-start.13 = (bf16[208,1280]{1,0:T(8,128)(2,1)S(1)}, bf16[208,1280]{1,0:T(8,128)(2,1)S(1)}, u32[]{:S(2)}, u32[]{:S(2)}) collective-permute-start(bf16[208,1280]{1,0:T(8,128)(2,1)S(1)} %get-tuple-element.277), channel_id=1, source_target_pairs={{0,4},{1,5},{2,6},{3,7},{4,0},{5,1},{6,2},{7,3},{8,12},{9,13},{10,... | collective-permute-start | bytes 1597448 | tf_op jit(solution)/shard_map/ppermute | solution.py:1186
  47.0 19.3 %collective-permute-start.15 = (bf16[240,1280]{1,0:T(8,128)(2,1)S(1)}, bf16[240,1280]{1,0:T(8,128)(2,1)S(1)}, u32[]{:S(2)}, u32[]{:S(2)}) collective-permute-start(bf16[240,1280]{1,0:T(8,128)(2,1)S(1)} %get-tuple-element.279.refs_0_), channel_id=1, source_target_pairs={{0,8},{8,0},{16,24},{24,16},{1,9},{9,1},{17,25},{25,17},{2,10},{10... | collective-permute-start | bytes 1843208 | tf_op jit(solution)/shard_map/ppermute | solution.py:1202
  70.2 15.5 %collective-permute-start.29 = (bf16[128,1280]{1,0:T(8,128)(2,1)S(1)}, bf16[128,1280]{1,0:T(8,128)(2,1)S(1)}, u32[]{:S(2)}, u32[]{:S(2)}) collective-permute-start(bf16[128,1280]{1,0:T(8,128)(2,1)S(1)} %get-tuple-element.294.s0), channel_id=1, source_target_pairs={{0,6},{1,7},{2,4},{3,5},{4,2},{5,3},{6,0},{7,1},{8,14},{9,15},{10,... | collective-permute-start | bytes 983048 | tf_op jit(solution)/shard_map/ppermute | solution.py:1186
  92.2 20.4 %collective-permute-start.36 = (bf16[320,1280]{1,0:T(8,128)(2,1)S(1)}, bf16[320,1280]{1,0:T(8,128)(2,1)S(1)}, u32[]{:S(2)}, u32[]{:S(2)}) collective-permute-start(bf16[320,1280]{1,0:T(8,128)(2,1)S(1)} %down_grad.1.refs_0_), channel_id=1, source_target_pairs={{0,8},{8,0},{16,24},{24,16},{1,9},{9,1},{17,25},{25,17},{2,10},{10... | collective-permute-start | bytes 2457608 | tf_op jit(solution)/shard_map/ppermute | solution.py:1202
  94.1 16.2 %collective-permute-start.28 = (bf16[128,1280]{1,0:T(8,128)(2,1)S(1)}, bf16[128,1280]{1,0:T(8,128)(2,1)S(1)}, u32[]{:S(2)}, u32[]{:S(2)}) collective-permute-start(bf16[128,1280]{1,0:T(8,128)(2,1)S(1)} %get-tuple-element.308), channel_id=1, source_target_pairs={{0,4},{1,5},{2,6},{3,7},{4,0},{5,1},{6,2},{7,3},{8,12},{9,13},{10,... | collective-permute-start | bytes 983048 | tf_op jit(solution)/shard_map/ppermute | solution.py:1186
  102.2 14.8 %collective-permute-start.39 = (bf16[320,1280]{1,0:T(8,128)(2,1)S(1)}, bf16[320,1280]{1,0:T(8,128)(2,1)S(1)}, u32[]{:S(2)}, u32[]{:S(2)}) collective-permute-start(bf16[320,1280]{1,0:T(8,128)(2,1)S(1)} %get-tuple-element.336), channel_id=1, source_target_pairs={{0,1},{1,0},{2,3},{3,2},{4,5},{5,4},{6,7},{7,6},{8,9},{9,8},{10,11... | collective-permute-start | bytes 2457608 | tf_op jit(solution)/shard_map/ppermute | solution.py:1186
  112.8 19.5 %collective-permute-start.37 = (bf16[320,1280]{1,0:T(8,128)(2,1)S(1)}, bf16[320,1280]{1,0:T(8,128)(2,1)S(1)}, u32[]{:S(2)}, u32[]{:S(2)}) collective-permute-start(bf16[320,1280]{1,0:T(8,128)(2,1)S(1)} %add.30.refs_0_), channel_id=1, source_target_pairs={{0,8},{8,0},{16,24},{24,16},{1,9},{9,1},{17,25},{25,17},{2,10},{10... | collective-permute-start | bytes 2457608 | tf_op jit(solution)/shard_map/ppermute | solution.py:1202
  113.3 19.0 %collective-permute-start.38 = (bf16[320,1280]{1,0:T(8,128)(2,1)S(1)}, bf16[320,1280]{1,0:T(8,128)(2,1)S(1)}, u32[]{:S(2)}, u32[]{:S(2)}) collective-permute-start(bf16[320,1280]{1,0:T(8,128)(2,1)S(1)} %add.31.half), channel_id=1, source_target_pairs={{8,16},{16,8},{9,17},{17,9},{10,18},{18,10},{11,19},{19,11},{12,20... | collective-permute-start | bytes 2457608 | tf_op jit(solution)/shard_map/ppermute | solution.py:1202
  116.1 14.6 %collective-permute-start.34 = (bf16[128,1280]{1,0:T(8,128)(2,1)S(1)}, bf16[128,1280]{1,0:T(8,128)(2,1)S(1)}, u32[]{:S(2)}, u32[]{:S(2)}) collective-permute-start(bf16[128,1280]{1,0:T(8,128)(2,1)S(1)} %get-tuple-element.351.b0), channel_id=1, source_target_pairs={{0,4},{1,5},{2,6},{3,7},{4,0},{5,1},{6,2},{7,3},{8,12},{9,13},{10,... | collective-permute-start | bytes 983048 | tf_op jit(solution)/shard_map/ppermute | solution.py:1186
  116.9 13.7 %collective-permute-start.33 = (bf16[128,1280]{1,0:T(8,128)(2,1)S(1)}, bf16[128,1280]{1,0:T(8,128)(2,1)S(1)}, u32[]{:S(2)}, u32[]{:S(2)}) collective-permute-start(bf16[128,1280]{1,0:T(8,128)(2,1)S(1)} %get-tuple-element.351.b0), channel_id=1, source_target_pairs={{0,2},{1,3},{2,0},{3,1},{4,6},{5,7},{6,4},{7,5},{8,10},{9,11},{10,... | collective-permute-start | bytes 983048 | tf_op jit(solution)/shard_map/ppermute | solution.py:1186
  133.1 21.0 %collective-permute-start.40 = (bf16[320,1280]{1,0:T(8,128)(2,1)S(1)}, bf16[320,1280]{1,0:T(8,128)(2,1)S(1)}, u32[]{:S(2)}, u32[]{:S(2)}) collective-permute-start(bf16[320,1280]{1,0:T(8,128)(2,1)S(1)} %z_send.4.sent), channel_id=1, source_target_pairs={{0,8},{8,0},{16,24},{24,16},{1,9},{9,1},{17,25},{25,17},{2,10},{10... | collective-permute-start | bytes 2457608 | tf_op jit(solution)/shard_map/ppermute | solution.py:1202
  136.9 17.2 %collective-permute-start.41 = (bf16[320,1280]{1,0:T(8,128)(2,1)S(1)}, bf16[320,1280]{1,0:T(8,128)(2,1)S(1)}, u32[]{:S(2)}, u32[]{:S(2)}) collective-permute-start(bf16[320,1280]{1,0:T(8,128)(2,1)S(1)} %add.33.half), channel_id=1, source_target_pairs={{8,16},{16,8},{9,17},{17,9},{10,18},{18,10},{11,19},{19,11},{12,20... | collective-permute-start | bytes 2457608 | tf_op jit(solution)/shard_map/ppermute | solution.py:1202
  155.0 22.7 %collective-permute-start.49 = (bf16[320,1280]{1,0:T(8,128)(2,1)S(1)}, bf16[320,1280]{1,0:T(8,128)(2,1)S(1)}, u32[]{:S(2)}, u32[]{:S(2)}) collective-permute-start(bf16[320,1280]{1,0:T(8,128)(2,1)S(1)} %z_send.5.sent), channel_id=1, source_target_pairs={{0,8},{8,0},{16,24},{24,16},{1,9},{9,1},{17,25},{25,17},{2,10},{10... | collective-permute-start | bytes 2457608 | tf_op jit(solution)/shard_map/ppermute | solution.py:1202
  158.9 18.8 %collective-permute-start.50 = (bf16[320,1280]{1,0:T(8,128)(2,1)S(1)}, bf16[320,1280]{1,0:T(8,128)(2,1)S(1)}, u32[]{:S(2)}, u32[]{:S(2)}) collective-permute-start(bf16[320,1280]{1,0:T(8,128)(2,1)S(1)} %add.34.half), channel_id=1, source_target_pairs={{8,16},{16,8},{9,17},{17,9},{10,18},{18,10},{11,19},{19,11},{12,20... | collective-permute-start | bytes 2457608 | tf_op jit(solution)/shard_map/ppermute | solution.py:1202
  159.8 17.9 %collective-permute-start.46 = (bf16[128,1280]{1,0:T(8,128)(2,1)S(1)}, bf16[128,1280]{1,0:T(8,128)(2,1)S(1)}, u32[]{:S(2)}, u32[]{:S(2)}) collective-permute-start(bf16[128,1280]{1,0:T(8,128)(2,1)S(1)} %get-tuple-element.387), channel_id=1, source_target_pairs={{0,2},{1,3},{2,0},{3,1},{4,6},{5,7},{6,4},{7,5},{8,10},{9,11},{10,... | collective-permute-start | bytes 983048 | tf_op jit(solution)/shard_map/ppermute | solution.py:1186
  160.7 17.0 %collective-permute-start.47 = (bf16[128,1280]{1,0:T(8,128)(2,1)S(1)}, bf16[128,1280]{1,0:T(8,128)(2,1)S(1)}, u32[]{:S(2)}, u32[]{:S(2)}) collective-permute-start(bf16[128,1280]{1,0:T(8,128)(2,1)S(1)} %get-tuple-element.388), channel_id=1, source_target_pairs={{0,4},{1,5},{2,6},{3,7},{4,0},{5,1},{6,2},{7,3},{8,12},{9,13},{10,... | collective-permute-start | bytes 983048 | tf_op jit(solution)/shard_map/ppermute | solution.py:1186
  161.9 15.8 %collective-permute-start.48 = (bf16[128,1280]{1,0:T(8,128)(2,1)S(1)}, bf16[128,1280]{1,0:T(8,128)(2,1)S(1)}, u32[]{:S(2)}, u32[]{:S(2)}) collective-permute-start(bf16[128,1280]{1,0:T(8,128)(2,1)S(1)} %get-tuple-element.389), channel_id=1, source_target_pairs={{0,6},{1,7},{2,4},{3,5},{4,2},{5,3},{6,0},{7,1},{8,14},{9,15},{10,... | collective-permute-start | bytes 983048 | tf_op jit(solution)/shard_map/ppermute | solution.py:1186
  178.6 21.9 %collective-permute-start.54 = (bf16[320,1280]{1,0:T(8,128)(2,1)S(1)}, bf16[320,1280]{1,0:T(8,128)(2,1)S(1)}, u32[]{:S(2)}, u32[]{:S(2)}) collective-permute-start(bf16[320,1280]{1,0:T(8,128)(2,1)S(1)} %z_send.6.sent), channel_id=1, source_target_pairs={{0,8},{8,0},{16,24},{24,16},{1,9},{9,1},{17,25},{25,17},{2,10},{10... | collective-permute-start | bytes 2457608 | tf_op jit(solution)/shard_map/ppermute | solution.py:1202
  182.4 18.0 %collective-permute-start.55 = (bf16[320,1280]{1,0:T(8,128)(2,1)S(1)}, bf16[320,1280]{1,0:T(8,128)(2,1)S(1)}, u32[]{:S(2)}, u32[]{:S(2)}) collective-permute-start(bf16[320,1280]{1,0:T(8,128)(2,1)S(1)} %add.36.half), channel_id=1, source_target_pairs={{8,16},{16,8},{9,17},{17,9},{10,18},{18,10},{11,19},{19,11},{12,20... | collective-permute-start | bytes 2457608 | tf_op jit(solution)/shard_map/ppermute | solution.py:1202
  184.0 15.7 %collective-permute-start.52 = (bf16[128,1280]{1,0:T(8,128)(2,1)S(1)}, bf16[128,1280]{1,0:T(8,128)(2,1)S(1)}, u32[]{:S(2)}, u32[]{:S(2)}) collective-permute-start(bf16[128,1280]{1,0:T(8,128)(2,1)S(1)} %get-tuple-element.401), channel_id=1, source_target_pairs={{0,4},{1,5},{2,6},{3,7},{4,0},{5,1},{6,2},{7,3},{8,12},{9,13},{10,... | collective-permute-start | bytes 983048 | tf_op jit(solution)/shard_map/ppermute | solution.py:1186
  185.2 14.5 %collective-permute-start.53 = (bf16[128,1280]{1,0:T(8,128)(2,1)S(1)}, bf16[128,1280]{1,0:T(8,128)(2,1)S(1)}, u32[]{:S(2)}, u32[]{:S(2)}) collective-permute-start(bf16[128,1280]{1,0:T(8,128)(2,1)S(1)} %get-tuple-element.402), channel_id=1, source_target_pairs={{0,6},{1,7},{2,4},{3,5},{4,2},{5,3},{6,0},{7,1},{8,14},{9,15},{10,... | collective-permute-start | bytes 983048 | tf_op jit(solution)/shard_map/ppermute | solution.py:1186
  201.5 22.7 %collective-permute-start.60 = (bf16[320,1280]{1,0:T(8,128)(2,1)S(1)}, bf16[320,1280]{1,0:T(8,128)(2,1)S(1)}, u32[]{:S(2)}, u32[]{:S(2)}) collective-permute-start(bf16[320,1280]{1,0:T(8,128)(2,1)S(1)} %z_send.7.sent), channel_id=1, source_target_pairs={{0,8},{8,0},{16,24},{24,16},{1,9},{9,1},{17,25},{25,17},{2,10},{10... | collective-permute-start | bytes 2457608 | tf_op jit(solution)/shard_map/ppermute | solution.py:1202
  205.3 18.9 %collective-permute-start.61 = (bf16[320,1280]{1,0:T(8,128)(2,1)S(1)}, bf16[320,1280]{1,0:T(8,128)(2,1)S(1)}, u32[]{:S(2)}, u32[]{:S(2)}) collective-permute-start(bf16[320,1280]{1,0:T(8,128)(2,1)S(1)} %add.37.refs_0_), channel_id=1, source_target_pairs={{8,16},{16,8},{9,17},{17,9},{10,18},{18,10},{11,19},{19,11},{12,20... | collective-permute-start | bytes 2457608 | tf_op jit(solution)/shard_map/ppermute | solution.py:1202
  224.6 21.0 %collective-permute-start.66 = (bf16[320,1280]{1,0:T(8,128)(2,1)S(1)}, bf16[320,1280]{1,0:T(8,128)(2,1)S(1)}, u32[]{:S(2)}, u32[]{:S(2)}) collective-permute-start(bf16[320,1280]{1,0:T(8,128)(2,1)S(1)} %add.40.sent), channel_id=1, source_target_pairs={{0,8},{8,0},{16,24},{24,16},{1,9},{9,1},{17,25},{25,17},{2,10},{10... | collective-permute-start | bytes 2457608 | tf_op jit(solution)/shard_map/ppermute | solution.py:1202
  226.6 19.0 %collective-permute-start.67 = (bf16[320,1280]{1,0:T(8,128)(2,1)S(1)}, bf16[320,1280]{1,0:T(8,128)(2,1)S(1)}, u32[]{:S(2)}, u32[]{:S(2)}) collective-permute-start(bf16[320,1280]{1,0:T(8,128)(2,1)S(1)} %add.39.refs_0_), channel_id=1, source_target_pairs={{8,16},{16,8},{9,17},{17,9},{10,18},{18,10},{11,19},{19,11},{12,20... | collective-permute-start | bytes 2457608 | tf_op jit(solution)/shard_map/ppermute | solution.py:1202
  228.2 17.4 %collective-permute-start.64 = (bf16[160,1280]{1,0:T(8,128)(2,1)S(1)}, bf16[160,1280]{1,0:T(8,128)(2,1)S(1)}, u32[]{:S(2)}, u32[]{:S(2)}) collective-permute-start(bf16[160,1280]{1,0:T(8,128)(2,1)S(1)} %get-tuple-element.439), channel_id=1, source_target_pairs={{0,4},{1,5},{2,6},{3,7},{4,0},{5,1},{6,2},{7,3},{8,12},{9,13},{10,... | collective-permute-start | bytes 1228808 | tf_op jit(solution)/shard_map/ppermute | solution.py:1186
  229.4 16.2 %collective-permute-start.65 = (bf16[160,1280]{1,0:T(8,128)(2,1)S(1)}, bf16[160,1280]{1,0:T(8,128)(2,1)S(1)}, u32[]{:S(2)}, u32[]{:S(2)}) collective-permute-start(bf16[160,1280]{1,0:T(8,128)(2,1)S(1)} %get-tuple-element.440), channel_id=1, source_target_pairs={{0,6},{1,7},{2,4},{3,5},{4,2},{5,3},{6,0},{7,1},{8,14},{9,15},{10,... | collective-permute-start | bytes 1228808 | tf_op jit(solution)/shard_map/ppermute | solution.py:1186
  245.8 20.3 %collective-permute-start.72 = (bf16[320,1280]{1,0:T(8,128)(2,1)S(1)}, bf16[320,1280]{1,0:T(8,128)(2,1)S(1)}, u32[]{:S(2)}, u32[]{:S(2)}) collective-permute-start(bf16[320,1280]{1,0:T(8,128)(2,1)S(1)} %add.42.sent), channel_id=1, source_target_pairs={{8,0},{16,24},{9,1},{17,25},{10,2},{18,26},{11,3},{19,27},{12,4},{... | collective-permute-start | bytes 2457608 | tf_op jit(solution)/shard_map/ppermute | solution.py:1202
  (48 other events, 414.0 us)

commit v7 on v6

--- a/solution.py
+++ b/solution.py
@@ -118,6 +118,7 @@
 
 HALF = SHARE // 2
 EXTRA = 8
+FLAG_ROWS = 16
 ROWS_Z = 2 * SHARE
 
 
@@ -210,8 +211,9 @@
 
 
 def qkv_blocks_kernel(spot, lengths, padding, weights, *refs):
-    vectors, own, sent = refs[:9], refs[9], refs[10 : 9 + CHIPS]
-    held, marks, whole, vector_sems, sem = refs[9 + CHIPS : 18 + CHIPS], *refs[18 + CHIPS :]
+    vectors, own, sent, flag = refs[:9], refs[9], refs[10 : 9 + CHIPS], refs[9 + CHIPS]
+    held, marks, whole, vector_sems, sem = refs[10 + CHIPS : 19 + CHIPS], *refs[19 + CHIPS :]
+    flag[...] = jnp.full(flag.shape, spot[3].astype(f32), f32).astype(bf16)
     copies = [
         pltpu.make_async_copy(vector, here, vector_sems.at[i])
         for i, (vector, here) in enumerate(zip(vectors, held))
@@ -251,7 +253,7 @@
         qkv_blocks_kernel,
         "qkv_blocks",
         "ss" + "h" * 11,
-        [((SHARE + EXTRA, 3 * D_CHIP), bf16)] + [half] * (CHIPS - 1),
+        [((SHARE + EXTRA, 3 * D_CHIP), bf16)] + [half] * (CHIPS - 1) + [((FLAG_ROWS, D), bf16)],
         [pltpu.VMEM(v.shape, v.dtype) for v in vectors]
         + [
             pltpu.VMEM(padding.shape, padding.dtype),
@@ -587,7 +589,7 @@
     def columns(tile):
         pre_act[at, tile] = mm(second[at, :], up[:, tile]) + table[BIAS_UP : BIAS_UP + 1, tile]
 
-    tiled(FF_CHIP, 256, columns)
+    tiled(FF_CHIP, 640, columns)
 
     @pl.loop(0, size // 64)
     def _(i):
@@ -623,7 +625,7 @@
         for i, part in enumerate(partials):
             part[:, tile] = whole[i * rows : (i + 1) * rows]
 
-    tiled(D, 256, columns)
+    tiled(D, 640, columns)
 
 
 def hidden_first(spot, blocks, grad_act, table, mine, other):
@@ -834,7 +836,7 @@
 def add_kernel(*refs):
     count = len(refs) // 3
     for a, b, c in zip(refs[:count], refs[count : 2 * count], refs[2 * count :]):
-        c[...] = (a[...].astype(f32) + b[...].astype(f32)).astype(c.dtype)
+        c[...] = a[...] + b[...]
 
 
 def add_all(left, right):
@@ -892,21 +894,15 @@
     return add_all([low], [got_side])[0]
 
 
-def z_send_kernel(spot, half, got_middle, low, sent):
-    middle = spot[3] > 0
-
-    @pl.when(middle)
-    def _():
-        whole = half[...].astype(f32) + got_middle[...].astype(f32)
-        sent[...] = whole.astype(bf16)
-
-    @pl.when(jnp.logical_not(middle))
-    def _():
-        sent[...] = low[...]
-
-
-def z_send(spot, half, got_middle, low):
-    return call(z_send_kernel, "z_send", "svvv", [(low.shape, bf16)])(spot, half, got_middle, low)[0]
+def z_send_kernel(flag, half, got_middle, low, sent):
+    middle = flag[...] > 0.5
+    for i in range(ROWS_Z // FLAG_ROWS):
+        rows = slice(i * FLAG_ROWS, (i + 1) * FLAG_ROWS)
+        sent[rows, :] = jnp.where(middle, half[rows, :] + got_middle[rows, :], low[rows, :])
+
+
+def z_send(flag, half, got_middle, low):
+    return call(z_send_kernel, "z_send", "vvvv", [(low.shape, bf16)])(flag, half, got_middle, low)[0]
 
 
 def z_final_kernel(spot, sent, got_side, final):
@@ -937,22 +933,25 @@
     )(spot, sent, got)
 
 
-def second_down_kernel(spot, sent, got, before, down, here, sem):
+def second_down_kernel(flag, sent, got, before, down, here, sem):
     del before
     copies = []
+    middle = flag[...] > 0.5
     for i in range(2):
+        for lo in range(i * SHARE, (i + 1) * SHARE, FLAG_ROWS):
+            rows = slice(lo, lo + FLAG_ROWS)
+            here[rows, :] = jnp.where(middle, sent[rows, :], got[rows, :]).astype(f32)
         rows = slice(i * SHARE, (i + 1) * SHARE)
-        here[rows, :] = jnp.where(spot[3] > 0, sent[rows, :], got[rows, :]).astype(f32)
         target = down.at[ROWS_Z + i * SHARE : ROWS_Z + (i + 1) * SHARE]
         copies.append(pltpu.make_async_copy(here.at[rows], target, sem.at[i]))
         copies[-1].start()
     wait_all(copies)
 
 
-def second_down(spot, sent, got, down):
+def second_down(flag, sent, got, down):
     return pl.pallas_call(
         second_down_kernel,
-        in_specs=[SMEM, VMEM, VMEM, HBM],
+        in_specs=[VMEM, VMEM, VMEM, HBM],
         out_specs=HBM,
         out_shape=pltpu.HBM((2 * ROWS_Z, D), f32),
         scratch_shapes=[pltpu.VMEM((ROWS_Z, D), f32), sems(2)],
@@ -960,7 +959,7 @@
         compiler_params=pltpu.CompilerParams(vmem_limit_bytes=16 * 2**20),
         cost_estimate=COST,
         name="second_down",
-    )(spot, sent, got, pltpu.with_memory_space_constraint(down, pltpu.HBM))
+    )(flag, sent, got, pltpu.with_memory_space_constraint(down, pltpu.HBM))
 
 
 def qkv_rows_kernel(spot, b0, b1, b2, b3, qkv, rows, stack, sem):
@@ -1216,7 +1215,7 @@
 
     w_qkv, w_out, w_up, w_down = (gather_shards(w) for w in (w_qkv, w_out, w_up, w_down))
     given = (ln1_gain, ln1_bias, b_out, ln2_gain, ln2_bias, b_down, b_query, b_value, b_up)
-    qkv_sent = qkv_blocks(spot, lengths, padding, w_qkv, [gather_shards(v) for v in given])
+    *qkv_sent, flag = qkv_blocks(spot, lengths, padding, w_qkv, [gather_shards(v) for v in given])
     qkv_got = from_chips(qkv_sent)
     x1, x2, *qkv_got = fence(swap(tokens, 2), swap(tokens, 4), *qkv_got)
     qkv_near, qkv_half, x1_half, x2_half = qkv_join(qkv_got, x1, x2)
@@ -1307,7 +1306,7 @@
     )
     half1 = z_half(up_a, side1)
     middle1, _ = fence(middle1, half1)
-    send2 = z_send(spot, half0, middle1, up_b)
+    send2 = z_send(flag, half0, middle1, up_b)
     side2, middle2 = z_swap(send2), z_middle(half1)
     branch_blocks, half1 = fence_list(branch_blocks, half1)
     (whole_branch, grad_projected, qkv_bias_sum), partial_first = leave(
@@ -1324,7 +1323,7 @@
     side2, middle2, qkv_a = fence(side2, middle2, qkv_a)
     half2 = z_half(up_b, side2)
     middle2, _ = fence(middle2, half2)
-    send3 = z_send(spot, half1, middle2, qkv_a)
+    send3 = z_send(flag, half1, middle2, qkv_a)
     side3, middle3 = z_swap(send3), z_middle(half2)
     down_sent, _ = fence(down_sent, send3)
     (down_b,) = add_all([down_b], [swap(down_sent, 1)])
@@ -1335,7 +1334,7 @@
     first_parts, side3, middle3 = fence_list(first_parts, side3, middle3)
     half3 = z_half(qkv_a, side3)
     middle3, _ = fence(middle3, half3)
-    send4 = z_send(spot, half2, middle3, qkv_b)
+    send4 = z_send(flag, half2, middle3, qkv_b)
     sent, _ = fence(send3, send4)
     up_a_final = z_final(spot, sent, side3)
     side4, middle4 = z_swap(send4), z_middle(half3)
@@ -1345,7 +1344,7 @@
     result_parts, side4, middle4 = fence_list(result_parts, side4, middle4)
     half4 = z_half(qkv_b, side4)
     middle4, _ = fence(middle4, half4)
-    send5 = z_send(spot, half3, middle4, down_b)
+    send5 = z_send(flag, half3, middle4, down_b)
     sent, _ = fence(send4, send5)
     up_b_final = z_final(spot, sent, side4)
     side5, middle5 = z_swap(send5), z_middle(half4)
@@ -1398,7 +1397,7 @@
     qkv_total, up_grad, vectors[0] = fence_list(qkv_total, up_grad, vectors[0])
     qkv_grad = qkv_rows(spot, qkv_total)
     side7, qkv_grad = fence(side7, qkv_grad)
-    down_grad = second_down(spot, send7, side7, down_grad)
+    down_grad = second_down(flag, send7, side7, down_grad)
 
     return (
         layer_out,

time: 268 us -> 265 us (0.989)
  Pallas kernels: 70.4 us -> 65.3 us
  waiting for transfers between devices: 109 us -> 112 us
    pallas_call x48, Pallas kernels: 61.6 us -> 57.5 us  [run(): return made(*placed)]
where the time goes in v7:
time: 265 us
  waiting for transfers between devices  112 us (42%)
  starting transfers between devices  85.2 us (32%)
  Pallas kernels  65.3 us (25%)
    ppermute x55, waiting for transfers between devices, swap(): return lax.ppermute(value, 'fsdp', pairs)  82.6 us
    pallas_call x48, Pallas kernels, run(): return made(*placed)  57.5 us
    ppermute x55, starting transfers between devices, swap(): return lax.ppermute(value, 'fsdp', pairs)  53 us
    ppermute x18, starting transfers between devices, along_z(): return lax.ppermute(value, 'dp', pairs)  32.2 us
    ppermute x18, waiting for transfers between devices, along_z(): return lax.ppermute(value, 'dp', pairs)  29.2 us
  transfers between devices with their start and end apart: 73, of which 39 were waited for; matrix products, arithmetic and copies ran while one was open for 0% of the time, Pallas kernels for 23%

profile of v7, /device:TPU:0, one launch (start us, length us, event | category | flops | bytes accessed | tf_op | source)
XLA Modules:
  0.0 264.5 jit_solution(4483988422976325813)
XLA Ops:
  0.7 3.0 %collective-permute-start.1 = (bf16[128,1280]{1,0:T(8,128)(2,1)}, bf16[128,1280]{1,0:T(8,128)(2,1)S(1)}, u32[]{:S(2)}, u32[]{:S(2)}) collective-permute-start(bf16[128,1280]{1,0:T(8,128)(2,1)} %tokens.3), channel_id=1, source_target_pairs={{0,4},{1,5},{2,6},{3,7},{4,0},{5,1},{6,2},{7,3},{8,12},{9,13},{10,... | collective-permute-start | bytes 983048 | tf_op jit(solution)/shard_map/ppermute | solution.py:1185
  5.9 2.9 %qkv_blocks.1 = (bf16[168,960]{1,0:T(8,128)(2,1)S(1)}, bf16[88,960]{1,0:T(8,128)(2,1)S(1)}, bf16[88,960]{1,0:T(8,128)(2,1)S(1)}, bf16[88,960]{1,0:T(8,128)(2,1)S(1)}, bf16[16,1280]{1,0:T(8,128)(2,1)S(1)}) custom-call(s32[4]{0:T(128)S(1)} %pad_add_fusion.spot, s32[1,2]{1,0:T(1,128)S(1)} %copy-done.3, s32[128]{0:T(128)} %padding.1, bf16[160,3840]{1,0:T(8,128)(2,1)} %weights.2, ...), custom_call_target="tpu_custom_call" | custom-call | flops 1 | bytes 1 | tf_op jit(solution)/shard_map/qkv_blocks/pallas_call | solution.py:143
  9.5 2.9 %collective-permute-start.4 = (bf16[88,960]{1,0:T(8,128)(2,1)S(1)}, bf16[88,960]{1,0:T(8,128)(2,1)S(1)}, u32[]{:S(2)}, u32[]{:S(2)}) collective-permute-start(bf16[88,960]{1,0:T(8,128)(2,1)S(1)} %get-tuple-element.253), channel_id=1, source_target_pairs={{0,6},{1,7},{2,4},{3,5},{4,2},{5,3},{6,0},{7,1},{8,14},{9,15},{10,... | collective-permute-start | bytes 506888 | tf_op jit(solution)/shard_map/ppermute | solution.py:1185
  12.4 6.0 %collective-permute-done.2.q1 = bf16[88,960]{1,0:T(8,128)(2,1)S(1)} collective-permute-done((bf16[88,960]{1,0:T(8,128)(2,1)S(1)}, bf16[88,960]{1,0:T(8,128)(2,1)S(1)}, u32[]{:S(2)}, u32[]{:S(2)}) %collective-permute-start.2) | collective-permute-done | bytes 168992 | tf_op jit(solution)/shard_map/ppermute | solution.py:1185
  31.4 5.7 %collective-permute-done.7.whole.refs_1_ = bf16[240,960]{1,0:T(8,128)(2,1)S(1)} collective-permute-done((bf16[240,960]{1,0:T(8,128)(2,1)S(1)}, bf16[240,960]{1,0:T(8,128)(2,1)S(1)}, u32[]{:S(2)}, u32[]{:S(2)}) %collective-permute-start.7) | collective-permute-done | bytes 460832 | tf_op jit(solution)/shard_map/ppermute | solution.py:1201
  39.0 7.3 %enter.1 = (f32[8,1280]{1,0:T(8,128)S(1)}, bf16[512,128]{1,0:T(8,128)(2,1)S(1)}, bf16[1280,960]{1,0:T(8,128)(2,1)S(1)}, bf16[320,1280]{1,0:T(8,128)(2,1)S(1)}, b...) custom-call(s32[4]{0:T(128)S(1)} %pad_add_fusion.spot, ...), custom_call_target="tpu_custom_call" | custom-call | flops 1 | bytes 1 | tf_op jit(solution)/shard_map/enter/pallas_call | solution.py:143
  52.7 3.1 %collective-permute-done.18.h1 = bf16[64,1280]{1,0:T(8,128)(2,1)S(1)} collective-permute-done((bf16[64,1280]{1,0:T(8,128)(2,1)S(1)}, bf16[64,1280]{1,0:T(8,128)(2,1)S(1)}, u32[]{:S(2)}, u32[]{:S(2)}) %collective-permute-start.18) | collective-permute-done | bytes 163872 | tf_op jit(solution)/shard_map/ppermute | solution.py:1185
  60.1 5.8 %collective-permute-done.20.p1 = bf16[128,1280]{1,0:T(8,128)(2,1)S(1)} collective-permute-done((bf16[128,1280]{1,0:T(8,128)(2,1)S(1)}, bf16[128,1280]{1,0:T(8,128)(2,1)S(1)}, u32[]{:S(2)}, u32[]{:S(2)}) %collective-permute-start.20) | collective-permute-done | bytes 327712 | tf_op jit(solution)/shard_map/ppermute | solution.py:1185
  72.5 4.7 %act_grad.1 = (f32[512,1280]{1,0:T(8,128)S(1)}, bf16[1280,1280]{1,0:T(8,128)(2,1)S(1)}, bf16[512,1280]{1,0:T(8,128)(2,1)S(1)}) custom-call(s32[4]{0:T(128)S(1)} %pad_add_fusion.spot, bf16[384,1280]{1,0:T(8,128)(2,1)S(1)} %get-tuple-element.298.part, bf16[64,1280]{1,0:T(8,128)(2,1)S(1)} %collective-permute-done.16.g1, ...), custom_call_target="tpu_custom_call" | custom-call | flops 1 | bytes 1 | tf_op jit(solution)/shard_map/act_grad/pallas_call | solution.py:143
  79.2 5.9 %hidden_first.1 = (bf16[512,1280]{1,0:T(8,128)(2,1)S(1)}, bf16[512,1280]{1,0:T(8,128)(2,1)S(1)}, bf16[512,1280]{1,0:T(8,128)(2,1)S(1)}, f32[1,1280]{1,0:T(1,128)...) custom-call(s32[4]{0:T(128)S(1)} %pad_add_fusion.spot, ...), custom_call_target="tpu_custom_call" | custom-call | flops 1 | bytes 1 | tf_op jit(solution)/shard_map/hidden_first/pallas_call | solution.py:143
  86.1 2.5 hidden_last.1
  97.8 3.9 %rest.1 = (bf16[320,1280]{1,0:T(8,128)(2,1)S(1)}, bf16[320,1280]{1,0:T(8,128)(2,1)S(1)}, bf16[320,1280]{1,0:T(8,128)(2,1)S(1)}, bf16[320,1280]{1,0:T(8,128)(2,1)S(1)}, bf16[320,1280]{1,0:T(8,128)(2,1)S(1)}) custom-call(s32[4]{0:T(128)S(1)} %pad_add_fusion.spot, bf16[512,1280]{1,0:T(8,128)(2,1)S(1)} %get-tuple-element.324.second, ...), custom_call_target="tpu_custom_call" | custom-call | flops 1 | bytes 1 | tf_op jit(solution)/shard_map/rest/pallas_call | solution.py:143
  103.3 6.7 %collective-permute-done.28.p2 = bf16[128,1280]{1,0:T(8,128)(2,1)S(1)} collective-permute-done((bf16[128,1280]{1,0:T(8,128)(2,1)S(1)}, bf16[128,1280]{1,0:T(8,128)(2,1)S(1)}, u32[]{:S(2)}, u32[]{:S(2)}) %collective-permute-start.28) | collective-permute-done | bytes 327712 | tf_op jit(solution)/shard_map/ppermute | solution.py:1185
  117.4 2.6 result.1
  120.1 5.4 %collective-permute-done.35.b3 = bf16[128,1280]{1,0:T(8,128)(2,1)S(1)} collective-permute-done((bf16[128,1280]{1,0:T(8,128)(2,1)S(1)}, bf16[128,1280]{1,0:T(8,128)(2,1)S(1)}, u32[]{:S(2)}, u32[]{:S(2)}) %collective-permute-start.35) | collective-permute-done | bytes 327712 | tf_op jit(solution)/shard_map/ppermute | solution.py:1185
  125.5 5.0 %collective-permute-done.34.b2 = bf16[128,1280]{1,0:T(8,128)(2,1)S(1)} collective-permute-done((bf16[128,1280]{1,0:T(8,128)(2,1)S(1)}, bf16[128,1280]{1,0:T(8,128)(2,1)S(1)}, u32[]{:S(2)}, u32[]{:S(2)}) %collective-permute-start.34) | collective-permute-done | bytes 327712 | tf_op jit(solution)/shard_map/ppermute | solution.py:1185
  132.4 3.7 %collective-permute-start.40 = (bf16[320,1280]{1,0:T(8,128)(2,1)S(1)}, bf16[320,1280]{1,0:T(8,128)(2,1)S(1)}, u32[]{:S(2)}, u32[]{:S(2)}) collective-permute-start(bf16[320,1280]{1,0:T(8,128)(2,1)S(1)} %z_send.4.sent), channel_id=1, source_target_pairs={{0,8},{8,0},{16,24},{24,16},{1,9},{9,1},{17,25},{25,17},{2,10},{10... | collective-permute-start | bytes 2457608 | tf_op jit(solution)/shard_map/ppermute | solution.py:1201
  136.8 6.8 %leave.1 = (bf16[512,1280]{1,0:T(8,128)(2,1)S(1)}, bf16[512,960]{1,0:T(8,128)(2,1)S(1)}, f32[1,960]{1,0:T(1,128)S(1)}, bf16[128,1280]{1,0:T(8,128)(2,1)S(1)}, bf...) custom-call(bf16[128,1280]{1,0:T(8,128)(2,1)S(1)} %get-tuple-element.352.b0, ...), custom_call_target="tpu_custom_call" | custom-call | flops 1 | bytes 1 | tf_op jit(solution)/shard_map/leave/pallas_call | solution.py:143
  143.7 3.8 %qkv_grad.1 = (bf16[2,160,960]{2,1,0:T(8,128)(2,1)S(1)}, bf16[2,160,960]{2,1,0:T(8,128)(2,1)S(1)}, bf16[4,160,960]{2,1,0:T(8,128)(2,1)S(1)}, bf16[160,1280]{1,0:T(8,128)(2,1)S(1)}, bf16[160,1280]{1,0:T(8,128)(2,1)S(1)}) custom-call(s32[4]{0:T(128)S(1)} %pad_add_fusion.spot, bf16[512,1280]{1,0:T(8,128)(2,1)S(1)} %get-tuple-element.373.first_low, ...), custom_call_target="tpu_custom_call" | custom-call | flops 1 | bytes 1 | tf_op jit(solution)/shard_map/qkv_grad/pallas_call | solution.py:143
  148.2 3.0 %collective-permute-done.44.out_got = bf16[160,1280]{1,0:T(8,128)(2,1)S(1)} collective-permute-done((bf16[160,1280]{1,0:T(8,128)(2,1)S(1)}, bf16[160,1280]{1,0:T(8,128)(2,1)S(1)}, u32[]{:S(2)}, u32[]{:S(2)}) %collective-permute-start.44) | collective-permute-done | bytes 409632 | tf_op jit(solution)/shard_map/ppermute | solution.py:1185
  153.6 3.7 %collective-permute-start.49 = (bf16[320,1280]{1,0:T(8,128)(2,1)S(1)}, bf16[320,1280]{1,0:T(8,128)(2,1)S(1)}, u32[]{:S(2)}, u32[]{:S(2)}) collective-permute-start(bf16[320,1280]{1,0:T(8,128)(2,1)S(1)} %z_send.5.sent), channel_id=1, source_target_pairs={{0,8},{8,0},{16,24},{24,16},{1,9},{9,1},{17,25},{25,17},{2,10},{10... | collective-permute-start | bytes 2457608 | tf_op jit(solution)/shard_map/ppermute | solution.py:1201
  161.7 14.5 %collective-permute-done.49.refs_1_.got_side = bf16[320,1280]{1,0:T(8,128)(2,1)S(1)} collective-permute-done((bf16[320,1280]{1,0:T(8,128)(2,1)S(1)}, bf16[320,1280]{1,0:T(8,128)(2,1)S(1)}, u32[]{:S(2)}, u32[]{:S(2)}) %collective-permute-start.49) | collective-permute-done | bytes 819232 | tf_op jit(solution)/shard_map/ppermute | solution.py:1201
  176.5 3.7 %collective-permute-start.54 = (bf16[320,1280]{1,0:T(8,128)(2,1)S(1)}, bf16[320,1280]{1,0:T(8,128)(2,1)S(1)}, u32[]{:S(2)}, u32[]{:S(2)}) collective-permute-start(bf16[320,1280]{1,0:T(8,128)(2,1)S(1)} %z_send.6.sent), channel_id=1, source_target_pairs={{0,8},{8,0},{16,24},{24,16},{1,9},{9,1},{17,25},{25,17},{2,10},{10... | collective-permute-start | bytes 2457608 | tf_op jit(solution)/shard_map/ppermute | solution.py:1201
  184.4 7.2 %collective-permute-done.51.r1 = bf16[128,1280]{1,0:T(8,128)(2,1)S(1)} collective-permute-done((bf16[128,1280]{1,0:T(8,128)(2,1)S(1)}, bf16[128,1280]{1,0:T(8,128)(2,1)S(1)}, u32[]{:S(2)}, u32[]{:S(2)}) %collective-permute-start.51) | collective-permute-done | bytes 327712 | tf_op jit(solution)/shard_map/ppermute | solution.py:1185
  191.6 6.1 %collective-permute-done.52.r2 = bf16[128,1280]{1,0:T(8,128)(2,1)S(1)} collective-permute-done((bf16[128,1280]{1,0:T(8,128)(2,1)S(1)}, bf16[128,1280]{1,0:T(8,128)(2,1)S(1)}, u32[]{:S(2)}, u32[]{:S(2)}) %collective-permute-start.52) | collective-permute-done | bytes 327712 | tf_op jit(solution)/shard_map/ppermute | solution.py:1185
  198.5 3.7 %collective-permute-start.60 = (bf16[320,1280]{1,0:T(8,128)(2,1)S(1)}, bf16[320,1280]{1,0:T(8,128)(2,1)S(1)}, u32[]{:S(2)}, u32[]{:S(2)}) collective-permute-start(bf16[320,1280]{1,0:T(8,128)(2,1)S(1)} %z_send.7.sent), channel_id=1, source_target_pairs={{0,8},{8,0},{16,24},{24,16},{1,9},{9,1},{17,25},{25,17},{2,10},{10... | collective-permute-start | bytes 2457608 | tf_op jit(solution)/shard_map/ppermute | solution.py:1201
  203.1 2.6 end.1
  218.4 2.6 collective-permute-done.62.refs_1_
  228.2 8.2 %collective-permute-done.63.b1 = bf16[160,1280]{1,0:T(8,128)(2,1)S(1)} collective-permute-done((bf16[160,1280]{1,0:T(8,128)(2,1)S(1)}, bf16[160,1280]{1,0:T(8,128)(2,1)S(1)}, u32[]{:S(2)}, u32[]{:S(2)}) %collective-permute-start.63) | collective-permute-done | bytes 409632 | tf_op jit(solution)/shard_map/ppermute | solution.py:1185
  236.4 6.3 %collective-permute-done.64.b2 = bf16[160,1280]{1,0:T(8,128)(2,1)S(1)} collective-permute-done((bf16[160,1280]{1,0:T(8,128)(2,1)S(1)}, bf16[160,1280]{1,0:T(8,128)(2,1)S(1)}, u32[]{:S(2)}, u32[]{:S(2)}) %collective-permute-start.64) | collective-permute-done | bytes 409632 | tf_op jit(solution)/shard_map/ppermute | solution.py:1185
  249.3 3.3 %collective-permute-start.71 = (f32[16,1280]{1,0:T(8,128)S(1)}, f32[16,1280]{1,0:T(8,128)S(1)}, u32[]{:S(2)}, u32[]{:S(2)}) collective-permute-start(f32[16,1280]{1,0:T(8,128)S(1)} %add.41.refs_1_), channel_id=1, source_target_pairs={{0,16},{8,24},{16,0},{24,8},{1,17},{9,25},{17,1},{25,9},{2,18},{10... | collective-permute-start | bytes 245768 | tf_op jit(solution)/shard_map/ppermute | solution.py:1201
  254.4 2.5 up_rows.1
  (181 shorter events, 108.0 us)
Async XLA Ops:
  0.7 19.9 %collective-permute-start.1 = (bf16[128,1280]{1,0:T(8,128)(2,1)}, bf16[128,1280]{1,0:T(8,128)(2,1)S(1)}, u32[]{:S(2)}, u32[]{:S(2)}) collective-permute-start(bf16[128,1280]{1,0:T(8,128)(2,1)} %tokens.3), channel_id=1, source_target_pairs={{0,4},{1,5},{2,6},{3,7},{4,0},{5,1},{6,2},{7,3},{8,12},{9,13},{10,... | collective-permute-start | bytes 983048 | tf_op jit(solution)/shard_map/ppermute | solution.py:1185
  3.7 16.9 %collective-permute-start = (bf16[128,1280]{1,0:T(8,128)(2,1)}, bf16[128,1280]{1,0:T(8,128)(2,1)S(1)}, u32[]{:S(2)}, u32[]{:S(2)}) collective-permute-start(bf16[128,1280]{1,0:T(8,128)(2,1)} %tokens.3), channel_id=1, source_target_pairs={{0,2},{1,3},{2,0},{3,1},{4,6},{5,7},{6,4},{7,5},{8,10},{9,11},{10,... | collective-permute-start | bytes 983048 | tf_op jit(solution)/shard_map/ppermute | solution.py:1185
  20.7 16.3 %collective-permute-start.8 = (bf16[432,960]{1,0:T(8,128)(2,1)S(1)}, bf16[432,960]{1,0:T(8,128)(2,1)S(1)}, u32[]{:S(2)}, u32[]{:S(2)}) collective-permute-start(bf16[432,960]{1,0:T(8,128)(2,1)S(1)} %get-tuple-element.263.refs_0_), channel_id=1, source_target_pairs={{0,1},{1,0},{2,3},{3,2},{4,5},{5,4},{6,7},{7,6},{8,9},{9,8},{10,11... | collective-permute-start | bytes 2488328 | tf_op jit(solution)/shard_map/ppermute | solution.py:1185
  27.4 19.3 %collective-permute-start.12 = (bf16[208,1280]{1,0:T(8,128)(2,1)S(1)}, bf16[208,1280]{1,0:T(8,128)(2,1)S(1)}, u32[]{:S(2)}, u32[]{:S(2)}) collective-permute-start(bf16[208,1280]{1,0:T(8,128)(2,1)S(1)} %get-tuple-element.277), channel_id=1, source_target_pairs={{0,2},{1,3},{2,0},{3,1},{4,6},{5,7},{6,4},{7,5},{8,10},{9,11},{10,... | collective-permute-start | bytes 1597448 | tf_op jit(solution)/shard_map/ppermute | solution.py:1185
  29.1 17.8 %collective-permute-start.13 = (bf16[208,1280]{1,0:T(8,128)(2,1)S(1)}, bf16[208,1280]{1,0:T(8,128)(2,1)S(1)}, u32[]{:S(2)}, u32[]{:S(2)}) collective-permute-start(bf16[208,1280]{1,0:T(8,128)(2,1)S(1)} %get-tuple-element.278), channel_id=1, source_target_pairs={{0,4},{1,5},{2,6},{3,7},{4,0},{5,1},{6,2},{7,3},{8,12},{9,13},{10,... | collective-permute-start | bytes 1597448 | tf_op jit(solution)/shard_map/ppermute | solution.py:1185
  47.0 19.6 %collective-permute-start.15 = (bf16[240,1280]{1,0:T(8,128)(2,1)S(1)}, bf16[240,1280]{1,0:T(8,128)(2,1)S(1)}, u32[]{:S(2)}, u32[]{:S(2)}) collective-permute-start(bf16[240,1280]{1,0:T(8,128)(2,1)S(1)} %get-tuple-element.280.refs_0_), channel_id=1, source_target_pairs={{0,8},{8,0},{16,24},{24,16},{1,9},{9,1},{17,25},{25,17},{2,10},{10... | collective-permute-start | bytes 1843208 | tf_op jit(solution)/shard_map/ppermute | solution.py:1201
  70.6 15.5 %collective-permute-start.29 = (bf16[128,1280]{1,0:T(8,128)(2,1)S(1)}, bf16[128,1280]{1,0:T(8,128)(2,1)S(1)}, u32[]{:S(2)}, u32[]{:S(2)}) collective-permute-start(bf16[128,1280]{1,0:T(8,128)(2,1)S(1)} %get-tuple-element.295.s0), channel_id=1, source_target_pairs={{0,6},{1,7},{2,4},{3,5},{4,2},{5,3},{6,0},{7,1},{8,14},{9,15},{10,... | collective-permute-start | bytes 983048 | tf_op jit(solution)/shard_map/ppermute | solution.py:1185
  92.2 20.4 %collective-permute-start.36 = (bf16[320,1280]{1,0:T(8,128)(2,1)S(1)}, bf16[320,1280]{1,0:T(8,128)(2,1)S(1)}, u32[]{:S(2)}, u32[]{:S(2)}) collective-permute-start(bf16[320,1280]{1,0:T(8,128)(2,1)S(1)} %down_grad.1.refs_0_), channel_id=1, source_target_pairs={{0,8},{8,0},{16,24},{24,16},{1,9},{9,1},{17,25},{25,17},{2,10},{10... | collective-permute-start | bytes 2457608 | tf_op jit(solution)/shard_map/ppermute | solution.py:1201
  93.8 16.2 %collective-permute-start.28 = (bf16[128,1280]{1,0:T(8,128)(2,1)S(1)}, bf16[128,1280]{1,0:T(8,128)(2,1)S(1)}, u32[]{:S(2)}, u32[]{:S(2)}) collective-permute-start(bf16[128,1280]{1,0:T(8,128)(2,1)S(1)} %get-tuple-element.309), channel_id=1, source_target_pairs={{0,4},{1,5},{2,6},{3,7},{4,0},{5,1},{6,2},{7,3},{8,12},{9,13},{10,... | collective-permute-start | bytes 983048 | tf_op jit(solution)/shard_map/ppermute | solution.py:1185
  101.6 14.8 %collective-permute-start.39 = (bf16[320,1280]{1,0:T(8,128)(2,1)S(1)}, bf16[320,1280]{1,0:T(8,128)(2,1)S(1)}, u32[]{:S(2)}, u32[]{:S(2)}) collective-permute-start(bf16[320,1280]{1,0:T(8,128)(2,1)S(1)} %get-tuple-element.337), channel_id=1, source_target_pairs={{0,1},{1,0},{2,3},{3,2},{4,5},{5,4},{6,7},{7,6},{8,9},{9,8},{10,11... | collective-permute-start | bytes 2457608 | tf_op jit(solution)/shard_map/ppermute | solution.py:1185
  112.7 19.5 %collective-permute-start.37 = (bf16[320,1280]{1,0:T(8,128)(2,1)S(1)}, bf16[320,1280]{1,0:T(8,128)(2,1)S(1)}, u32[]{:S(2)}, u32[]{:S(2)}) collective-permute-start(bf16[320,1280]{1,0:T(8,128)(2,1)S(1)} %add.30.refs_0_), channel_id=1, source_target_pairs={{0,8},{8,0},{16,24},{24,16},{1,9},{9,1},{17,25},{25,17},{2,10},{10... | collective-permute-start | bytes 2457608 | tf_op jit(solution)/shard_map/ppermute | solution.py:1201
  113.2 19.0 %collective-permute-start.38 = (bf16[320,1280]{1,0:T(8,128)(2,1)S(1)}, bf16[320,1280]{1,0:T(8,128)(2,1)S(1)}, u32[]{:S(2)}, u32[]{:S(2)}) collective-permute-start(bf16[320,1280]{1,0:T(8,128)(2,1)S(1)} %add.31.half), channel_id=1, source_target_pairs={{8,16},{16,8},{9,17},{17,9},{10,18},{18,10},{11,19},{19,11},{12,20... | collective-permute-start | bytes 2457608 | tf_op jit(solution)/shard_map/ppermute | solution.py:1201
  115.9 14.6 %collective-permute-start.34 = (bf16[128,1280]{1,0:T(8,128)(2,1)S(1)}, bf16[128,1280]{1,0:T(8,128)(2,1)S(1)}, u32[]{:S(2)}, u32[]{:S(2)}) collective-permute-start(bf16[128,1280]{1,0:T(8,128)(2,1)S(1)} %get-tuple-element.352.b0), channel_id=1, source_target_pairs={{0,4},{1,5},{2,6},{3,7},{4,0},{5,1},{6,2},{7,3},{8,12},{9,13},{10,... | collective-permute-start | bytes 983048 | tf_op jit(solution)/shard_map/ppermute | solution.py:1185
  116.5 14.0 %collective-permute-start.33 = (bf16[128,1280]{1,0:T(8,128)(2,1)S(1)}, bf16[128,1280]{1,0:T(8,128)(2,1)S(1)}, u32[]{:S(2)}, u32[]{:S(2)}) collective-permute-start(bf16[128,1280]{1,0:T(8,128)(2,1)S(1)} %get-tuple-element.352.b0), channel_id=1, source_target_pairs={{0,2},{1,3},{2,0},{3,1},{4,6},{5,7},{6,4},{7,5},{8,10},{9,11},{10,... | collective-permute-start | bytes 983048 | tf_op jit(solution)/shard_map/ppermute | solution.py:1185
  132.4 20.9 %collective-permute-start.40 = (bf16[320,1280]{1,0:T(8,128)(2,1)S(1)}, bf16[320,1280]{1,0:T(8,128)(2,1)S(1)}, u32[]{:S(2)}, u32[]{:S(2)}) collective-permute-start(bf16[320,1280]{1,0:T(8,128)(2,1)S(1)} %z_send.4.sent), channel_id=1, source_target_pairs={{0,8},{8,0},{16,24},{24,16},{1,9},{9,1},{17,25},{25,17},{2,10},{10... | collective-permute-start | bytes 2457608 | tf_op jit(solution)/shard_map/ppermute | solution.py:1201
  136.1 17.2 %collective-permute-start.41 = (bf16[320,1280]{1,0:T(8,128)(2,1)S(1)}, bf16[320,1280]{1,0:T(8,128)(2,1)S(1)}, u32[]{:S(2)}, u32[]{:S(2)}) collective-permute-start(bf16[320,1280]{1,0:T(8,128)(2,1)S(1)} %add.33.half), channel_id=1, source_target_pairs={{8,16},{16,8},{9,17},{17,9},{10,18},{18,10},{11,19},{19,11},{12,20... | collective-permute-start | bytes 2457608 | tf_op jit(solution)/shard_map/ppermute | solution.py:1201
  153.6 22.5 %collective-permute-start.49 = (bf16[320,1280]{1,0:T(8,128)(2,1)S(1)}, bf16[320,1280]{1,0:T(8,128)(2,1)S(1)}, u32[]{:S(2)}, u32[]{:S(2)}) collective-permute-start(bf16[320,1280]{1,0:T(8,128)(2,1)S(1)} %z_send.5.sent), channel_id=1, source_target_pairs={{0,8},{8,0},{16,24},{24,16},{1,9},{9,1},{17,25},{25,17},{2,10},{10... | collective-permute-start | bytes 2457608 | tf_op jit(solution)/shard_map/ppermute | solution.py:1201
  157.3 18.8 %collective-permute-start.50 = (bf16[320,1280]{1,0:T(8,128)(2,1)S(1)}, bf16[320,1280]{1,0:T(8,128)(2,1)S(1)}, u32[]{:S(2)}, u32[]{:S(2)}) collective-permute-start(bf16[320,1280]{1,0:T(8,128)(2,1)S(1)} %add.34.half), channel_id=1, source_target_pairs={{8,16},{16,8},{9,17},{17,9},{10,18},{18,10},{11,19},{19,11},{12,20... | collective-permute-start | bytes 2457608 | tf_op jit(solution)/shard_map/ppermute | solution.py:1201
  158.2 18.0 %collective-permute-start.46 = (bf16[128,1280]{1,0:T(8,128)(2,1)S(1)}, bf16[128,1280]{1,0:T(8,128)(2,1)S(1)}, u32[]{:S(2)}, u32[]{:S(2)}) collective-permute-start(bf16[128,1280]{1,0:T(8,128)(2,1)S(1)} %get-tuple-element.389), channel_id=1, source_target_pairs={{0,2},{1,3},{2,0},{3,1},{4,6},{5,7},{6,4},{7,5},{8,10},{9,11},{10,... | collective-permute-start | bytes 983048 | tf_op jit(solution)/shard_map/ppermute | solution.py:1185
  159.3 16.9 %collective-permute-start.47 = (bf16[128,1280]{1,0:T(8,128)(2,1)S(1)}, bf16[128,1280]{1,0:T(8,128)(2,1)S(1)}, u32[]{:S(2)}, u32[]{:S(2)}) collective-permute-start(bf16[128,1280]{1,0:T(8,128)(2,1)S(1)} %get-tuple-element.390), channel_id=1, source_target_pairs={{0,4},{1,5},{2,6},{3,7},{4,0},{5,1},{6,2},{7,3},{8,12},{9,13},{10,... | collective-permute-start | bytes 983048 | tf_op jit(solution)/shard_map/ppermute | solution.py:1185
  160.3 15.9 %collective-permute-start.48 = (bf16[128,1280]{1,0:T(8,128)(2,1)S(1)}, bf16[128,1280]{1,0:T(8,128)(2,1)S(1)}, u32[]{:S(2)}, u32[]{:S(2)}) collective-permute-start(bf16[128,1280]{1,0:T(8,128)(2,1)S(1)} %get-tuple-element.391), channel_id=1, source_target_pairs={{0,6},{1,7},{2,4},{3,5},{4,2},{5,3},{6,0},{7,1},{8,14},{9,15},{10,... | collective-permute-start | bytes 983048 | tf_op jit(solution)/shard_map/ppermute | solution.py:1185
  176.5 21.7 %collective-permute-start.54 = (bf16[320,1280]{1,0:T(8,128)(2,1)S(1)}, bf16[320,1280]{1,0:T(8,128)(2,1)S(1)}, u32[]{:S(2)}, u32[]{:S(2)}) collective-permute-start(bf16[320,1280]{1,0:T(8,128)(2,1)S(1)} %z_send.6.sent), channel_id=1, source_target_pairs={{0,8},{8,0},{16,24},{24,16},{1,9},{9,1},{17,25},{25,17},{2,10},{10... | collective-permute-start | bytes 2457608 | tf_op jit(solution)/shard_map/ppermute | solution.py:1201
  180.2 18.0 %collective-permute-start.55 = (bf16[320,1280]{1,0:T(8,128)(2,1)S(1)}, bf16[320,1280]{1,0:T(8,128)(2,1)S(1)}, u32[]{:S(2)}, u32[]{:S(2)}) collective-permute-start(bf16[320,1280]{1,0:T(8,128)(2,1)S(1)} %add.36.half), channel_id=1, source_target_pairs={{8,16},{16,8},{9,17},{17,9},{10,18},{18,10},{11,19},{19,11},{12,20... | collective-permute-start | bytes 2457608 | tf_op jit(solution)/shard_map/ppermute | solution.py:1201
  182.0 15.7 %collective-permute-start.52 = (bf16[128,1280]{1,0:T(8,128)(2,1)S(1)}, bf16[128,1280]{1,0:T(8,128)(2,1)S(1)}, u32[]{:S(2)}, u32[]{:S(2)}) collective-permute-start(bf16[128,1280]{1,0:T(8,128)(2,1)S(1)} %get-tuple-element.403), channel_id=1, source_target_pairs={{0,4},{1,5},{2,6},{3,7},{4,0},{5,1},{6,2},{7,3},{8,12},{9,13},{10,... | collective-permute-start | bytes 983048 | tf_op jit(solution)/shard_map/ppermute | solution.py:1185
  183.0 14.7 %collective-permute-start.53 = (bf16[128,1280]{1,0:T(8,128)(2,1)S(1)}, bf16[128,1280]{1,0:T(8,128)(2,1)S(1)}, u32[]{:S(2)}, u32[]{:S(2)}) collective-permute-start(bf16[128,1280]{1,0:T(8,128)(2,1)S(1)} %get-tuple-element.404), channel_id=1, source_target_pairs={{0,6},{1,7},{2,4},{3,5},{4,2},{5,3},{6,0},{7,1},{8,14},{9,15},{10,... | collective-permute-start | bytes 983048 | tf_op jit(solution)/shard_map/ppermute | solution.py:1185
  198.5 22.6 %collective-permute-start.60 = (bf16[320,1280]{1,0:T(8,128)(2,1)S(1)}, bf16[320,1280]{1,0:T(8,128)(2,1)S(1)}, u32[]{:S(2)}, u32[]{:S(2)}) collective-permute-start(bf16[320,1280]{1,0:T(8,128)(2,1)S(1)} %z_send.7.sent), channel_id=1, source_target_pairs={{0,8},{8,0},{16,24},{24,16},{1,9},{9,1},{17,25},{25,17},{2,10},{10... | collective-permute-start | bytes 2457608 | tf_op jit(solution)/shard_map/ppermute | solution.py:1201
  202.2 18.9 %collective-permute-start.61 = (bf16[320,1280]{1,0:T(8,128)(2,1)S(1)}, bf16[320,1280]{1,0:T(8,128)(2,1)S(1)}, u32[]{:S(2)}, u32[]{:S(2)}) collective-permute-start(bf16[320,1280]{1,0:T(8,128)(2,1)S(1)} %add.37.refs_0_), channel_id=1, source_target_pairs={{8,16},{16,8},{9,17},{17,9},{10,18},{18,10},{11,19},{19,11},{12,20... | collective-permute-start | bytes 2457608 | tf_op jit(solution)/shard_map/ppermute | solution.py:1201
  221.3 21.4 %collective-permute-start.66 = (bf16[320,1280]{1,0:T(8,128)(2,1)S(1)}, bf16[320,1280]{1,0:T(8,128)(2,1)S(1)}, u32[]{:S(2)}, u32[]{:S(2)}) collective-permute-start(bf16[320,1280]{1,0:T(8,128)(2,1)S(1)} %add.40.sent), channel_id=1, source_target_pairs={{0,8},{8,0},{16,24},{24,16},{1,9},{9,1},{17,25},{25,17},{2,10},{10... | collective-permute-start | bytes 2457608 | tf_op jit(solution)/shard_map/ppermute | solution.py:1201
  223.2 19.5 %collective-permute-start.67 = (bf16[320,1280]{1,0:T(8,128)(2,1)S(1)}, bf16[320,1280]{1,0:T(8,128)(2,1)S(1)}, u32[]{:S(2)}, u32[]{:S(2)}) collective-permute-start(bf16[320,1280]{1,0:T(8,128)(2,1)S(1)} %add.39.refs_0_), channel_id=1, source_target_pairs={{8,16},{16,8},{9,17},{17,9},{10,18},{18,10},{11,19},{19,11},{12,20... | collective-permute-start | bytes 2457608 | tf_op jit(solution)/shard_map/ppermute | solution.py:1201
  225.1 17.6 %collective-permute-start.64 = (bf16[160,1280]{1,0:T(8,128)(2,1)S(1)}, bf16[160,1280]{1,0:T(8,128)(2,1)S(1)}, u32[]{:S(2)}, u32[]{:S(2)}) collective-permute-start(bf16[160,1280]{1,0:T(8,128)(2,1)S(1)} %get-tuple-element.441), channel_id=1, source_target_pairs={{0,4},{1,5},{2,6},{3,7},{4,0},{5,1},{6,2},{7,3},{8,12},{9,13},{10,... | collective-permute-start | bytes 1228808 | tf_op jit(solution)/shard_map/ppermute | solution.py:1185
  226.1 16.6 %collective-permute-start.65 = (bf16[160,1280]{1,0:T(8,128)(2,1)S(1)}, bf16[160,1280]{1,0:T(8,128)(2,1)S(1)}, u32[]{:S(2)}, u32[]{:S(2)}) collective-permute-start(bf16[160,1280]{1,0:T(8,128)(2,1)S(1)} %get-tuple-element.442), channel_id=1, source_target_pairs={{0,6},{1,7},{2,4},{3,5},{4,2},{5,3},{6,0},{7,1},{8,14},{9,15},{10,... | collective-permute-start | bytes 1228808 | tf_op jit(solution)/shard_map/ppermute | solution.py:1185
  242.8 20.3 %collective-permute-start.72 = (bf16[320,1280]{1,0:T(8,128)(2,1)S(1)}, bf16[320,1280]{1,0:T(8,128)(2,1)S(1)}, u32[]{:S(2)}, u32[]{:S(2)}) collective-permute-start(bf16[320,1280]{1,0:T(8,128)(2,1)S(1)} %add.42.sent), channel_id=1, source_target_pairs={{8,0},{16,24},{9,1},{17,25},{10,2},{18,26},{11,3},{19,27},{12,4},{... | collective-permute-start | bytes 2457608 | tf_op jit(solution)/shard_map/ppermute | solution.py:1201
  (48 other events, 413.7 us)

commit v8 on v7

--- a/solution.py
+++ b/solution.py
@@ -211,9 +211,13 @@
 
 
 def qkv_blocks_kernel(spot, lengths, padding, weights, *refs):
-    vectors, own, sent, flag = refs[:9], refs[9], refs[10 : 9 + CHIPS], refs[9 + CHIPS]
-    held, marks, whole, vector_sems, sem = refs[10 + CHIPS : 19 + CHIPS], *refs[19 + CHIPS :]
+    vectors, own, sent = refs[:9], refs[9], refs[10 : 9 + CHIPS]
+    flag, role, refs = refs[9 + CHIPS], refs[10 + CHIPS], refs[11 + CHIPS :]
+    held, marks, whole, vector_sems, sem = refs[:9], *refs[9:]
     flag[...] = jnp.full(flag.shape, spot[3].astype(f32), f32).astype(bf16)
+    for i in range(3):
+        role[i : i + 1, :] = jnp.full((1, 128), spot[i].astype(f32), f32)
+    role[3:, :] = jnp.zeros((5, 128), f32)
     copies = [
         pltpu.make_async_copy(vector, here, vector_sems.at[i])
         for i, (vector, here) in enumerate(zip(vectors, held))
@@ -253,7 +257,7 @@
         qkv_blocks_kernel,
         "qkv_blocks",
         "ss" + "h" * 11,
-        [((SHARE + EXTRA, 3 * D_CHIP), bf16)] + [half] * (CHIPS - 1) + [((FLAG_ROWS, D), bf16)],
+        [((SHARE + EXTRA, 3 * D_CHIP), bf16)] + [half] * (CHIPS - 1) + [((FLAG_ROWS, D), bf16), ((8, 128), f32)],
         [pltpu.VMEM(v.shape, v.dtype) for v in vectors]
         + [
             pltpu.VMEM(padding.shape, padding.dtype),
@@ -583,6 +587,10 @@
     )(spot, part, *passed, down_mine, down_other)
 
 
+def number(role, i):
+    return jnp.max(role[i : i + 1, :]).astype(jnp.int32)
+
+
 def hidden_rows(at, second, up, table, grad_act, pre_act, act, grad_pre, bias_sum):
     size = at.stop - at.start
 
@@ -647,7 +655,7 @@
 
 
 def hidden_last_kernel(
-    spot,
+    role,
     s3,
     grad_act,
     table,
@@ -670,7 +678,7 @@
     second[at, :] = s3[...]
     bias_sum[...] = bias_in[...]
     hidden_rows(at, second, up, table, grad_act, pre_act, act, grad_pre, bias_sum)
-    down_product(act, cotangent, 1 - spot[1], 0, down_sent)
+    down_product(act, cotangent, 1 - number(role, 1), 0, down_sent)
 
 
 def down_product(act, cotangent, of_core, half, target):
@@ -694,11 +702,11 @@
         target[i * SHARE : (i + 1) * SHARE, :] = work[pl.ds(start, SHARE), :].astype(target.dtype)
 
 
-def hidden_last(spot, block, grad_act, table, cotangent, up, second, act, grad_pre, bias_sum):
+def hidden_last(role, block, grad_act, table, cotangent, up, second, act, grad_pre, bias_sum):
     total = second.shape[0]
     return pl.pallas_call(
         hidden_last_kernel,
-        in_specs=[SMEM] + [VMEM] * 9,
+        in_specs=[VMEM] * 10,
         out_specs=[VMEM] * 5,
         out_shape=[
             jax.ShapeDtypeStruct(second.shape, bf16),
@@ -712,7 +720,7 @@
         compiler_params=pltpu.CompilerParams(vmem_limit_bytes=16 * 2**20),
         cost_estimate=COST,
         name="hidden_last",
-    )(spot, block, grad_act, table, cotangent, up, second, act, grad_pre, bias_sum)
+    )(role, block, grad_act, table, cotangent, up, second, act, grad_pre, bias_sum)
 
 
 def second_last_kernel(grad_pre, up, partial):
@@ -725,18 +733,18 @@
     return call(second_last_kernel, "second_last", "vv", [((rows, D), bf16)])(grad_pre, up)[0]
 
 
-def up_sent_kernel(spot, grad_pre, second, up_sent, work):
-    up_product(second, grad_pre, 0, 1 - spot[1], up_sent, work)
-
-
-def up_sent_of(spot, grad_pre, second):
+def up_sent_kernel(role, grad_pre, second, up_sent, work):
+    up_product(second, grad_pre, 0, 1 - number(role, 1), up_sent, work)
+
+
+def up_sent_of(role, grad_pre, second):
     return call(
         up_sent_kernel,
         "up_sent",
-        "svv",
+        "vvv",
         [((ROWS_Z, FF_CHIP), bf16)],
         [pltpu.VMEM((256, FF_CHIP), f32)],
-    )(spot, grad_pre, second)[0]
+    )(role, grad_pre, second)[0]
 
 
 def split_rows(core, whole, sent, kept):
@@ -747,14 +755,14 @@
             target[at] = whole[pl.ds(start, SHARE), :].astype(bf16)
 
 
-def down_grad_kernel(spot, act, cotangent, got, total):
-    down_product(act, cotangent, spot[1], 0, total)
+def down_grad_kernel(role, act, cotangent, got, total):
+    down_product(act, cotangent, number(role, 1), 0, total)
     total[...] = (total[...].astype(f32) + got[...].astype(f32)).astype(bf16)
 
 
-def down_grad_of(spot, act, cotangent, got):
-    return call(down_grad_kernel, "down_grad", "svvv", [((ROWS_Z, D), bf16)])(
-        spot, act, cotangent, got
+def down_grad_of(role, act, cotangent, got):
+    return call(down_grad_kernel, "down_grad", "vvvv", [((ROWS_Z, D), bf16)])(
+        role, act, cotangent, got
     )[0]
 
 
@@ -1215,7 +1223,7 @@
 
     w_qkv, w_out, w_up, w_down = (gather_shards(w) for w in (w_qkv, w_out, w_up, w_down))
     given = (ln1_gain, ln1_bias, b_out, ln2_gain, ln2_bias, b_down, b_query, b_value, b_up)
-    *qkv_sent, flag = qkv_blocks(spot, lengths, padding, w_qkv, [gather_shards(v) for v in given])
+    *qkv_sent, flag, role = qkv_blocks(spot, lengths, padding, w_qkv, [gather_shards(v) for v in given])
     qkv_got = from_chips(qkv_sent)
     x1, x2, *qkv_got = fence(swap(tokens, 2), swap(tokens, 4), *qkv_got)
     qkv_near, qkv_half, x1_half, x2_half = qkv_join(qkv_got, x1, x2)
@@ -1270,13 +1278,13 @@
     )
     block, up_bias_sum = fence(second_blocks[3], up_bias_sum)
     second_low, act_low, grad_pre, up_bias_sum, down_sent = hidden_last(
-        spot, block, grad_act, table, whole_cotangent, up, second_low, act_low, grad_pre, up_bias_sum
+        role, block, grad_act, table, whole_cotangent, up, second_low, act_low, grad_pre, up_bias_sum
     )
     down_got = swap(down_sent, 1)
-    up_sent = up_sent_of(spot, grad_pre, second_low)
+    up_sent = up_sent_of(role, grad_pre, second_low)
     up_got = swap(up_sent, 1)
     act_low, up_sent = fence(act_low, up_sent)
-    down_a = down_grad_of(spot, act_low, whole_cotangent, down_got)
+    down_a = down_grad_of(role, act_low, whole_cotangent, down_got)
     side0 = z_swap(down_a)
     up_late, _ = fence(up, down_a)
     partial_second = partial_second + [second_last(grad_pre, up_late)]

time: 265 us -> 264 us (level)
  transfers between devices with their start and end apart: 73 -> 73, of which waited for: 39 -> 39; matrix products, arithmetic and copies ran while one was open for 0% -> 0% of each run, Pallas kernels for 23% -> 22%
where the time goes in v8:
time: 264 us
  waiting for transfers between devices  112 us (42%)
  starting transfers between devices  85.2 us (32%)
  Pallas kernels  64 us (24%)
    ppermute x55, waiting for transfers between devices, swap(): return lax.ppermute(value, 'fsdp', pairs)  83 us
    pallas_call x48, Pallas kernels, run(): return made(*placed)  56.6 us
    ppermute x55, starting transfers between devices, swap(): return lax.ppermute(value, 'fsdp', pairs)  53 us
    ppermute x18, starting transfers between devices, along_z(): return lax.ppermute(value, 'dp', pairs)  32.2 us
    ppermute x18, waiting for transfers between devices, along_z(): return lax.ppermute(value, 'dp', pairs)  29.3 us
  transfers between devices with their start and end apart: 73, of which 39 were waited for; matrix products, arithmetic and copies ran while one was open for 0% of the time, Pallas kernels for 22%

profile of v8, /device:TPU:0, one launch (start us, length us, event | category | flops | bytes accessed | tf_op | source)
XLA Modules:
  0.0 263.7 jit_solution(10295992572656346144)
XLA Ops:
  0.7 3.0 %collective-permute-start.1 = (bf16[128,1280]{1,0:T(8,128)(2,1)}, bf16[128,1280]{1,0:T(8,128)(2,1)S(1)}, u32[]{:S(2)}, u32[]{:S(2)}) collective-permute-start(bf16[128,1280]{1,0:T(8,128)(2,1)} %tokens.3), channel_id=1, source_target_pairs={{0,4},{1,5},{2,6},{3,7},{4,0},{5,1},{6,2},{7,3},{8,12},{9,13},{10,... | collective-permute-start | bytes 983048 | tf_op jit(solution)/shard_map/ppermute | solution.py:1193
  5.9 2.9 %qkv_blocks.1 = (bf16[168,960]{1,0:T(8,128)(2,1)S(1)}, bf16[88,960]{1,0:T(8,128)(2,1)S(1)}, bf16[88,960]{1,0:T(8,128)(2,1)S(1)}, bf16[88,960]{1,0:T(8,128)(2,1)S...) custom-call(s32[4]{0:T(128)S(1)} %pad_add_fusion.spot, s32[1,2]{1,0:T(1,128)S(1)} %copy-done.3, s32[128]{0:T(128)} %padding.1, ...), custom_call_target="tpu_custom_call" | custom-call | flops 1 | bytes 1 | tf_op jit(solution)/shard_map/qkv_blocks/pallas_call | solution.py:143
  9.5 2.9 %collective-permute-start.4 = (bf16[88,960]{1,0:T(8,128)(2,1)S(1)}, bf16[88,960]{1,0:T(8,128)(2,1)S(1)}, u32[]{:S(2)}, u32[]{:S(2)}) collective-permute-start(bf16[88,960]{1,0:T(8,128)(2,1)S(1)} %get-tuple-element.254), channel_id=1, source_target_pairs={{0,6},{1,7},{2,4},{3,5},{4,2},{5,3},{6,0},{7,1},{8,14},{9,15},{10,... | collective-permute-start | bytes 506888 | tf_op jit(solution)/shard_map/ppermute | solution.py:1193
  12.4 6.0 %collective-permute-done.2.q1 = bf16[88,960]{1,0:T(8,128)(2,1)S(1)} collective-permute-done((bf16[88,960]{1,0:T(8,128)(2,1)S(1)}, bf16[88,960]{1,0:T(8,128)(2,1)S(1)}, u32[]{:S(2)}, u32[]{:S(2)}) %collective-permute-start.2) | collective-permute-done | bytes 168992 | tf_op jit(solution)/shard_map/ppermute | solution.py:1193
  31.4 5.7 %collective-permute-done.7.whole.refs_1_ = bf16[240,960]{1,0:T(8,128)(2,1)S(1)} collective-permute-done((bf16[240,960]{1,0:T(8,128)(2,1)S(1)}, bf16[240,960]{1,0:T(8,128)(2,1)S(1)}, u32[]{:S(2)}, u32[]{:S(2)}) %collective-permute-start.7) | collective-permute-done | bytes 460832 | tf_op jit(solution)/shard_map/ppermute | solution.py:1209
  39.0 7.3 %enter.1 = (f32[8,1280]{1,0:T(8,128)S(1)}, bf16[512,128]{1,0:T(8,128)(2,1)S(1)}, bf16[1280,960]{1,0:T(8,128)(2,1)S(1)}, bf16[320,1280]{1,0:T(8,128)(2,1)S(1)}, b...) custom-call(s32[4]{0:T(128)S(1)} %pad_add_fusion.spot, ...), custom_call_target="tpu_custom_call" | custom-call | flops 1 | bytes 1 | tf_op jit(solution)/shard_map/enter/pallas_call | solution.py:143
  52.7 3.1 %collective-permute-done.18.h1 = bf16[64,1280]{1,0:T(8,128)(2,1)S(1)} collective-permute-done((bf16[64,1280]{1,0:T(8,128)(2,1)S(1)}, bf16[64,1280]{1,0:T(8,128)(2,1)S(1)}, u32[]{:S(2)}, u32[]{:S(2)}) %collective-permute-start.18) | collective-permute-done | bytes 163872 | tf_op jit(solution)/shard_map/ppermute | solution.py:1193
  60.1 5.8 %collective-permute-done.20.p1 = bf16[128,1280]{1,0:T(8,128)(2,1)S(1)} collective-permute-done((bf16[128,1280]{1,0:T(8,128)(2,1)S(1)}, bf16[128,1280]{1,0:T(8,128)(2,1)S(1)}, u32[]{:S(2)}, u32[]{:S(2)}) %collective-permute-start.20) | collective-permute-done | bytes 327712 | tf_op jit(solution)/shard_map/ppermute | solution.py:1193
  72.5 4.7 %act_grad.1 = (f32[512,1280]{1,0:T(8,128)S(1)}, bf16[1280,1280]{1,0:T(8,128)(2,1)S(1)}, bf16[512,1280]{1,0:T(8,128)(2,1)S(1)}) custom-call(s32[4]{0:T(128)S(1)} %pad_add_fusion.spot, bf16[384,1280]{1,0:T(8,128)(2,1)S(1)} %get-tuple-element.299.part, bf16[64,1280]{1,0:T(8,128)(2,1)S(1)} %collective-permute-done.16.g1, ...), custom_call_target="tpu_custom_call" | custom-call | flops 1 | bytes 1 | tf_op jit(solution)/shard_map/act_grad/pallas_call | solution.py:143
  79.2 5.9 %hidden_first.1 = (bf16[512,1280]{1,0:T(8,128)(2,1)S(1)}, bf16[512,1280]{1,0:T(8,128)(2,1)S(1)}, bf16[512,1280]{1,0:T(8,128)(2,1)S(1)}, f32[1,1280]{1,0:T(1,128)...) custom-call(s32[4]{0:T(128)S(1)} %pad_add_fusion.spot, ...), custom_call_target="tpu_custom_call" | custom-call | flops 1 | bytes 1 | tf_op jit(solution)/shard_map/hidden_first/pallas_call | solution.py:143
  96.9 3.9 %rest.1 = (bf16[320,1280]{1,0:T(8,128)(2,1)S(1)}, bf16[320,1280]{1,0:T(8,128)(2,1)S(1)}, bf16[320,1280]{1,0:T(8,128)(2,1)S(1)}, bf16[320,1280]{1,0:T(8,128)(2,1)S(1)}, bf16[320,1280]{1,0:T(8,128)(2,1)S(1)}) custom-call(s32[4]{0:T(128)S(1)} %pad_add_fusion.spot, bf16[512,1280]{1,0:T(8,128)(2,1)S(1)} %get-tuple-element.326.second, ...), custom_call_target="tpu_custom_call" | custom-call | flops 1 | bytes 1 | tf_op jit(solution)/shard_map/rest/pallas_call | solution.py:143
  102.5 6.7 %collective-permute-done.28.p2 = bf16[128,1280]{1,0:T(8,128)(2,1)S(1)} collective-permute-done((bf16[128,1280]{1,0:T(8,128)(2,1)S(1)}, bf16[128,1280]{1,0:T(8,128)(2,1)S(1)}, u32[]{:S(2)}, u32[]{:S(2)}) %collective-permute-start.28) | collective-permute-done | bytes 327712 | tf_op jit(solution)/shard_map/ppermute | solution.py:1193
  116.6 2.6 result.1
  119.2 5.4 %collective-permute-done.35.b3 = bf16[128,1280]{1,0:T(8,128)(2,1)S(1)} collective-permute-done((bf16[128,1280]{1,0:T(8,128)(2,1)S(1)}, bf16[128,1280]{1,0:T(8,128)(2,1)S(1)}, u32[]{:S(2)}, u32[]{:S(2)}) %collective-permute-start.35) | collective-permute-done | bytes 327712 | tf_op jit(solution)/shard_map/ppermute | solution.py:1193
  124.7 5.0 %collective-permute-done.34.b2 = bf16[128,1280]{1,0:T(8,128)(2,1)S(1)} collective-permute-done((bf16[128,1280]{1,0:T(8,128)(2,1)S(1)}, bf16[128,1280]{1,0:T(8,128)(2,1)S(1)}, u32[]{:S(2)}, u32[]{:S(2)}) %collective-permute-start.34) | collective-permute-done | bytes 327712 | tf_op jit(solution)/shard_map/ppermute | solution.py:1193
  131.6 3.7 %collective-permute-start.40 = (bf16[320,1280]{1,0:T(8,128)(2,1)S(1)}, bf16[320,1280]{1,0:T(8,128)(2,1)S(1)}, u32[]{:S(2)}, u32[]{:S(2)}) collective-permute-start(bf16[320,1280]{1,0:T(8,128)(2,1)S(1)} %z_send.4.sent), channel_id=1, source_target_pairs={{0,8},{8,0},{16,24},{24,16},{1,9},{9,1},{17,25},{25,17},{2,10},{10... | collective-permute-start | bytes 2457608 | tf_op jit(solution)/shard_map/ppermute | solution.py:1209
  136.0 6.8 %leave.1 = (bf16[512,1280]{1,0:T(8,128)(2,1)S(1)}, bf16[512,960]{1,0:T(8,128)(2,1)S(1)}, f32[1,960]{1,0:T(1,128)S(1)}, bf16[128,1280]{1,0:T(8,128)(2,1)S(1)}, bf...) custom-call(bf16[128,1280]{1,0:T(8,128)(2,1)S(1)} %get-tuple-element.354.b0, ...), custom_call_target="tpu_custom_call" | custom-call | flops 1 | bytes 1 | tf_op jit(solution)/shard_map/leave/pallas_call | solution.py:143
  142.8 3.8 %qkv_grad.1 = (bf16[2,160,960]{2,1,0:T(8,128)(2,1)S(1)}, bf16[2,160,960]{2,1,0:T(8,128)(2,1)S(1)}, bf16[4,160,960]{2,1,0:T(8,128)(2,1)S(1)}, bf16[160,1280]{1,0:T(8,128)(2,1)S(1)}, bf16[160,1280]{1,0:T(8,128)(2,1)S(1)}) custom-call(s32[4]{0:T(128)S(1)} %pad_add_fusion.spot, bf16[512,1280]{1,0:T(8,128)(2,1)S(1)} %get-tuple-element.375.first_low, ...), custom_call_target="tpu_custom_call" | custom-call | flops 1 | bytes 1 | tf_op jit(solution)/shard_map/qkv_grad/pallas_call | solution.py:143
  147.3 3.0 %collective-permute-done.44.out_got = bf16[160,1280]{1,0:T(8,128)(2,1)S(1)} collective-permute-done((bf16[160,1280]{1,0:T(8,128)(2,1)S(1)}, bf16[160,1280]{1,0:T(8,128)(2,1)S(1)}, u32[]{:S(2)}, u32[]{:S(2)}) %collective-permute-start.44) | collective-permute-done | bytes 409632 | tf_op jit(solution)/shard_map/ppermute | solution.py:1193
  152.8 3.7 %collective-permute-start.49 = (bf16[320,1280]{1,0:T(8,128)(2,1)S(1)}, bf16[320,1280]{1,0:T(8,128)(2,1)S(1)}, u32[]{:S(2)}, u32[]{:S(2)}) collective-permute-start(bf16[320,1280]{1,0:T(8,128)(2,1)S(1)} %z_send.5.sent), channel_id=1, source_target_pairs={{0,8},{8,0},{16,24},{24,16},{1,9},{9,1},{17,25},{25,17},{2,10},{10... | collective-permute-start | bytes 2457608 | tf_op jit(solution)/shard_map/ppermute | solution.py:1209
  160.8 14.5 %collective-permute-done.49.refs_1_.got_side = bf16[320,1280]{1,0:T(8,128)(2,1)S(1)} collective-permute-done((bf16[320,1280]{1,0:T(8,128)(2,1)S(1)}, bf16[320,1280]{1,0:T(8,128)(2,1)S(1)}, u32[]{:S(2)}, u32[]{:S(2)}) %collective-permute-start.49) | collective-permute-done | bytes 819232 | tf_op jit(solution)/shard_map/ppermute | solution.py:1209
  175.6 3.7 %collective-permute-start.54 = (bf16[320,1280]{1,0:T(8,128)(2,1)S(1)}, bf16[320,1280]{1,0:T(8,128)(2,1)S(1)}, u32[]{:S(2)}, u32[]{:S(2)}) collective-permute-start(bf16[320,1280]{1,0:T(8,128)(2,1)S(1)} %z_send.6.sent), channel_id=1, source_target_pairs={{0,8},{8,0},{16,24},{24,16},{1,9},{9,1},{17,25},{25,17},{2,10},{10... | collective-permute-start | bytes 2457608 | tf_op jit(solution)/shard_map/ppermute | solution.py:1209
  183.6 7.2 %collective-permute-done.51.r1 = bf16[128,1280]{1,0:T(8,128)(2,1)S(1)} collective-permute-done((bf16[128,1280]{1,0:T(8,128)(2,1)S(1)}, bf16[128,1280]{1,0:T(8,128)(2,1)S(1)}, u32[]{:S(2)}, u32[]{:S(2)}) %collective-permute-start.51) | collective-permute-done | bytes 327712 | tf_op jit(solution)/shard_map/ppermute | solution.py:1193
  190.7 6.2 %collective-permute-done.52.r2 = bf16[128,1280]{1,0:T(8,128)(2,1)S(1)} collective-permute-done((bf16[128,1280]{1,0:T(8,128)(2,1)S(1)}, bf16[128,1280]{1,0:T(8,128)(2,1)S(1)}, u32[]{:S(2)}, u32[]{:S(2)}) %collective-permute-start.52) | collective-permute-done | bytes 327712 | tf_op jit(solution)/shard_map/ppermute | solution.py:1193
  197.6 3.7 %collective-permute-start.60 = (bf16[320,1280]{1,0:T(8,128)(2,1)S(1)}, bf16[320,1280]{1,0:T(8,128)(2,1)S(1)}, u32[]{:S(2)}, u32[]{:S(2)}) collective-permute-start(bf16[320,1280]{1,0:T(8,128)(2,1)S(1)} %z_send.7.sent), channel_id=1, source_target_pairs={{0,8},{8,0},{16,24},{24,16},{1,9},{9,1},{17,25},{25,17},{2,10},{10... | collective-permute-start | bytes 2457608 | tf_op jit(solution)/shard_map/ppermute | solution.py:1209
  202.3 2.6 end.1
  217.5 2.6 %collective-permute-done.62.refs_1_ = f32[16,1280]{1,0:T(8,128)S(1)} collective-permute-done((f32[16,1280]{1,0:T(8,128)S(1)}, f32[16,1280]{1,0:T(8,128)S(1)}, u32[]{:S(2)}, u32[]{:S(2)}) %collective-permute-start.62) | collective-permute-done | bytes 81952 | tf_op jit(solution)/shard_map/ppermute | solution.py:1209
  227.3 8.2 %collective-permute-done.63.b1 = bf16[160,1280]{1,0:T(8,128)(2,1)S(1)} collective-permute-done((bf16[160,1280]{1,0:T(8,128)(2,1)S(1)}, bf16[160,1280]{1,0:T(8,128)(2,1)S(1)}, u32[]{:S(2)}, u32[]{:S(2)}) %collective-permute-start.63) | collective-permute-done | bytes 409632 | tf_op jit(solution)/shard_map/ppermute | solution.py:1193
  235.5 6.3 %collective-permute-done.64.b2 = bf16[160,1280]{1,0:T(8,128)(2,1)S(1)} collective-permute-done((bf16[160,1280]{1,0:T(8,128)(2,1)S(1)}, bf16[160,1280]{1,0:T(8,128)(2,1)S(1)}, u32[]{:S(2)}, u32[]{:S(2)}) %collective-permute-start.64) | collective-permute-done | bytes 409632 | tf_op jit(solution)/shard_map/ppermute | solution.py:1193
  248.4 3.3 %collective-permute-start.71 = (f32[16,1280]{1,0:T(8,128)S(1)}, f32[16,1280]{1,0:T(8,128)S(1)}, u32[]{:S(2)}, u32[]{:S(2)}) collective-permute-start(f32[16,1280]{1,0:T(8,128)S(1)} %add.41.refs_1_), channel_id=1, source_target_pairs={{0,16},{8,24},{16,0},{24,8},{1,17},{9,25},{17,1},{25,9},{2,18},{10... | collective-permute-start | bytes 245768 | tf_op jit(solution)/shard_map/ppermute | solution.py:1209
  253.5 2.5 up_rows.1
  258.8 2.2 qkv_rows.1
  (181 shorter events, 107.4 us)
Async XLA Ops:
  0.7 19.9 %collective-permute-start.1 = (bf16[128,1280]{1,0:T(8,128)(2,1)}, bf16[128,1280]{1,0:T(8,128)(2,1)S(1)}, u32[]{:S(2)}, u32[]{:S(2)}) collective-permute-start(bf16[128,1280]{1,0:T(8,128)(2,1)} %tokens.3), channel_id=1, source_target_pairs={{0,4},{1,5},{2,6},{3,7},{4,0},{5,1},{6,2},{7,3},{8,12},{9,13},{10,... | collective-permute-start | bytes 983048 | tf_op jit(solution)/shard_map/ppermute | solution.py:1193
  3.7 16.9 %collective-permute-start = (bf16[128,1280]{1,0:T(8,128)(2,1)}, bf16[128,1280]{1,0:T(8,128)(2,1)S(1)}, u32[]{:S(2)}, u32[]{:S(2)}) collective-permute-start(bf16[128,1280]{1,0:T(8,128)(2,1)} %tokens.3), channel_id=1, source_target_pairs={{0,2},{1,3},{2,0},{3,1},{4,6},{5,7},{6,4},{7,5},{8,10},{9,11},{10,... | collective-permute-start | bytes 983048 | tf_op jit(solution)/shard_map/ppermute | solution.py:1193
  20.7 16.3 %collective-permute-start.8 = (bf16[432,960]{1,0:T(8,128)(2,1)S(1)}, bf16[432,960]{1,0:T(8,128)(2,1)S(1)}, u32[]{:S(2)}, u32[]{:S(2)}) collective-permute-start(bf16[432,960]{1,0:T(8,128)(2,1)S(1)} %get-tuple-element.264.refs_0_), channel_id=1, source_target_pairs={{0,1},{1,0},{2,3},{3,2},{4,5},{5,4},{6,7},{7,6},{8,9},{9,8},{10,11... | collective-permute-start | bytes 2488328 | tf_op jit(solution)/shard_map/ppermute | solution.py:1193
  27.4 19.3 %collective-permute-start.12 = (bf16[208,1280]{1,0:T(8,128)(2,1)S(1)}, bf16[208,1280]{1,0:T(8,128)(2,1)S(1)}, u32[]{:S(2)}, u32[]{:S(2)}) collective-permute-start(bf16[208,1280]{1,0:T(8,128)(2,1)S(1)} %get-tuple-element.278), channel_id=1, source_target_pairs={{0,2},{1,3},{2,0},{3,1},{4,6},{5,7},{6,4},{7,5},{8,10},{9,11},{10,... | collective-permute-start | bytes 1597448 | tf_op jit(solution)/shard_map/ppermute | solution.py:1193
  29.1 17.8 %collective-permute-start.13 = (bf16[208,1280]{1,0:T(8,128)(2,1)S(1)}, bf16[208,1280]{1,0:T(8,128)(2,1)S(1)}, u32[]{:S(2)}, u32[]{:S(2)}) collective-permute-start(bf16[208,1280]{1,0:T(8,128)(2,1)S(1)} %get-tuple-element.279), channel_id=1, source_target_pairs={{0,4},{1,5},{2,6},{3,7},{4,0},{5,1},{6,2},{7,3},{8,12},{9,13},{10,... | collective-permute-start | bytes 1597448 | tf_op jit(solution)/shard_map/ppermute | solution.py:1193
  47.0 19.6 %collective-permute-start.15 = (bf16[240,1280]{1,0:T(8,128)(2,1)S(1)}, bf16[240,1280]{1,0:T(8,128)(2,1)S(1)}, u32[]{:S(2)}, u32[]{:S(2)}) collective-permute-start(bf16[240,1280]{1,0:T(8,128)(2,1)S(1)} %get-tuple-element.281.refs_0_), channel_id=1, source_target_pairs={{0,8},{8,0},{16,24},{24,16},{1,9},{9,1},{17,25},{25,17},{2,10},{10... | collective-permute-start | bytes 1843208 | tf_op jit(solution)/shard_map/ppermute | solution.py:1209
  70.6 15.5 %collective-permute-start.29 = (bf16[128,1280]{1,0:T(8,128)(2,1)S(1)}, bf16[128,1280]{1,0:T(8,128)(2,1)S(1)}, u32[]{:S(2)}, u32[]{:S(2)}) collective-permute-start(bf16[128,1280]{1,0:T(8,128)(2,1)S(1)} %get-tuple-element.296.s0), channel_id=1, source_target_pairs={{0,6},{1,7},{2,4},{3,5},{4,2},{5,3},{6,0},{7,1},{8,14},{9,15},{10,... | collective-permute-start | bytes 983048 | tf_op jit(solution)/shard_map/ppermute | solution.py:1193
  91.4 20.4 %collective-permute-start.36 = (bf16[320,1280]{1,0:T(8,128)(2,1)S(1)}, bf16[320,1280]{1,0:T(8,128)(2,1)S(1)}, u32[]{:S(2)}, u32[]{:S(2)}) collective-permute-start(bf16[320,1280]{1,0:T(8,128)(2,1)S(1)} %down_grad.1.refs_0_), channel_id=1, source_target_pairs={{0,8},{8,0},{16,24},{24,16},{1,9},{9,1},{17,25},{25,17},{2,10},{10... | collective-permute-start | bytes 2457608 | tf_op jit(solution)/shard_map/ppermute | solution.py:1209
  92.9 16.2 %collective-permute-start.28 = (bf16[128,1280]{1,0:T(8,128)(2,1)S(1)}, bf16[128,1280]{1,0:T(8,128)(2,1)S(1)}, u32[]{:S(2)}, u32[]{:S(2)}) collective-permute-start(bf16[128,1280]{1,0:T(8,128)(2,1)S(1)} %get-tuple-element.310), channel_id=1, source_target_pairs={{0,4},{1,5},{2,6},{3,7},{4,0},{5,1},{6,2},{7,3},{8,12},{9,13},{10,... | collective-permute-start | bytes 983048 | tf_op jit(solution)/shard_map/ppermute | solution.py:1193
  100.8 14.8 %collective-permute-start.39 = (bf16[320,1280]{1,0:T(8,128)(2,1)S(1)}, bf16[320,1280]{1,0:T(8,128)(2,1)S(1)}, u32[]{:S(2)}, u32[]{:S(2)}) collective-permute-start(bf16[320,1280]{1,0:T(8,128)(2,1)S(1)} %get-tuple-element.339), channel_id=1, source_target_pairs={{0,1},{1,0},{2,3},{3,2},{4,5},{5,4},{6,7},{7,6},{8,9},{9,8},{10,11... | collective-permute-start | bytes 2457608 | tf_op jit(solution)/shard_map/ppermute | solution.py:1193
  111.8 19.5 %collective-permute-start.37 = (bf16[320,1280]{1,0:T(8,128)(2,1)S(1)}, bf16[320,1280]{1,0:T(8,128)(2,1)S(1)}, u32[]{:S(2)}, u32[]{:S(2)}) collective-permute-start(bf16[320,1280]{1,0:T(8,128)(2,1)S(1)} %add.30.refs_0_), channel_id=1, source_target_pairs={{0,8},{8,0},{16,24},{24,16},{1,9},{9,1},{17,25},{25,17},{2,10},{10... | collective-permute-start | bytes 2457608 | tf_op jit(solution)/shard_map/ppermute | solution.py:1209
  112.3 19.0 %collective-permute-start.38 = (bf16[320,1280]{1,0:T(8,128)(2,1)S(1)}, bf16[320,1280]{1,0:T(8,128)(2,1)S(1)}, u32[]{:S(2)}, u32[]{:S(2)}) collective-permute-start(bf16[320,1280]{1,0:T(8,128)(2,1)S(1)} %add.31.half), channel_id=1, source_target_pairs={{8,16},{16,8},{9,17},{17,9},{10,18},{18,10},{11,19},{19,11},{12,20... | collective-permute-start | bytes 2457608 | tf_op jit(solution)/shard_map/ppermute | solution.py:1209
  115.0 14.6 %collective-permute-start.34 = (bf16[128,1280]{1,0:T(8,128)(2,1)S(1)}, bf16[128,1280]{1,0:T(8,128)(2,1)S(1)}, u32[]{:S(2)}, u32[]{:S(2)}) collective-permute-start(bf16[128,1280]{1,0:T(8,128)(2,1)S(1)} %get-tuple-element.354.b0), channel_id=1, source_target_pairs={{0,4},{1,5},{2,6},{3,7},{4,0},{5,1},{6,2},{7,3},{8,12},{9,13},{10,... | collective-permute-start | bytes 983048 | tf_op jit(solution)/shard_map/ppermute | solution.py:1193
  115.6 14.0 %collective-permute-start.33 = (bf16[128,1280]{1,0:T(8,128)(2,1)S(1)}, bf16[128,1280]{1,0:T(8,128)(2,1)S(1)}, u32[]{:S(2)}, u32[]{:S(2)}) collective-permute-start(bf16[128,1280]{1,0:T(8,128)(2,1)S(1)} %get-tuple-element.354.b0), channel_id=1, source_target_pairs={{0,2},{1,3},{2,0},{3,1},{4,6},{5,7},{6,4},{7,5},{8,10},{9,11},{10,... | collective-permute-start | bytes 983048 | tf_op jit(solution)/shard_map/ppermute | solution.py:1193
  131.6 20.9 %collective-permute-start.40 = (bf16[320,1280]{1,0:T(8,128)(2,1)S(1)}, bf16[320,1280]{1,0:T(8,128)(2,1)S(1)}, u32[]{:S(2)}, u32[]{:S(2)}) collective-permute-start(bf16[320,1280]{1,0:T(8,128)(2,1)S(1)} %z_send.4.sent), channel_id=1, source_target_pairs={{0,8},{8,0},{16,24},{24,16},{1,9},{9,1},{17,25},{25,17},{2,10},{10... | collective-permute-start | bytes 2457608 | tf_op jit(solution)/shard_map/ppermute | solution.py:1209
  135.2 17.2 %collective-permute-start.41 = (bf16[320,1280]{1,0:T(8,128)(2,1)S(1)}, bf16[320,1280]{1,0:T(8,128)(2,1)S(1)}, u32[]{:S(2)}, u32[]{:S(2)}) collective-permute-start(bf16[320,1280]{1,0:T(8,128)(2,1)S(1)} %add.33.half), channel_id=1, source_target_pairs={{8,16},{16,8},{9,17},{17,9},{10,18},{18,10},{11,19},{19,11},{12,20... | collective-permute-start | bytes 2457608 | tf_op jit(solution)/shard_map/ppermute | solution.py:1209
  152.8 22.5 %collective-permute-start.49 = (bf16[320,1280]{1,0:T(8,128)(2,1)S(1)}, bf16[320,1280]{1,0:T(8,128)(2,1)S(1)}, u32[]{:S(2)}, u32[]{:S(2)}) collective-permute-start(bf16[320,1280]{1,0:T(8,128)(2,1)S(1)} %z_send.5.sent), channel_id=1, source_target_pairs={{0,8},{8,0},{16,24},{24,16},{1,9},{9,1},{17,25},{25,17},{2,10},{10... | collective-permute-start | bytes 2457608 | tf_op jit(solution)/shard_map/ppermute | solution.py:1209
  156.5 18.8 %collective-permute-start.50 = (bf16[320,1280]{1,0:T(8,128)(2,1)S(1)}, bf16[320,1280]{1,0:T(8,128)(2,1)S(1)}, u32[]{:S(2)}, u32[]{:S(2)}) collective-permute-start(bf16[320,1280]{1,0:T(8,128)(2,1)S(1)} %add.34.half), channel_id=1, source_target_pairs={{8,16},{16,8},{9,17},{17,9},{10,18},{18,10},{11,19},{19,11},{12,20... | collective-permute-start | bytes 2457608 | tf_op jit(solution)/shard_map/ppermute | solution.py:1209
  157.3 18.0 %collective-permute-start.46 = (bf16[128,1280]{1,0:T(8,128)(2,1)S(1)}, bf16[128,1280]{1,0:T(8,128)(2,1)S(1)}, u32[]{:S(2)}, u32[]{:S(2)}) collective-permute-start(bf16[128,1280]{1,0:T(8,128)(2,1)S(1)} %get-tuple-element.391), channel_id=1, source_target_pairs={{0,2},{1,3},{2,0},{3,1},{4,6},{5,7},{6,4},{7,5},{8,10},{9,11},{10,... | collective-permute-start | bytes 983048 | tf_op jit(solution)/shard_map/ppermute | solution.py:1193
  158.5 16.9 %collective-permute-start.47 = (bf16[128,1280]{1,0:T(8,128)(2,1)S(1)}, bf16[128,1280]{1,0:T(8,128)(2,1)S(1)}, u32[]{:S(2)}, u32[]{:S(2)}) collective-permute-start(bf16[128,1280]{1,0:T(8,128)(2,1)S(1)} %get-tuple-element.392), channel_id=1, source_target_pairs={{0,4},{1,5},{2,6},{3,7},{4,0},{5,1},{6,2},{7,3},{8,12},{9,13},{10,... | collective-permute-start | bytes 983048 | tf_op jit(solution)/shard_map/ppermute | solution.py:1193
  159.4 15.9 %collective-permute-start.48 = (bf16[128,1280]{1,0:T(8,128)(2,1)S(1)}, bf16[128,1280]{1,0:T(8,128)(2,1)S(1)}, u32[]{:S(2)}, u32[]{:S(2)}) collective-permute-start(bf16[128,1280]{1,0:T(8,128)(2,1)S(1)} %get-tuple-element.393), channel_id=1, source_target_pairs={{0,6},{1,7},{2,4},{3,5},{4,2},{5,3},{6,0},{7,1},{8,14},{9,15},{10,... | collective-permute-start | bytes 983048 | tf_op jit(solution)/shard_map/ppermute | solution.py:1193
  175.6 21.7 %collective-permute-start.54 = (bf16[320,1280]{1,0:T(8,128)(2,1)S(1)}, bf16[320,1280]{1,0:T(8,128)(2,1)S(1)}, u32[]{:S(2)}, u32[]{:S(2)}) collective-permute-start(bf16[320,1280]{1,0:T(8,128)(2,1)S(1)} %z_send.6.sent), channel_id=1, source_target_pairs={{0,8},{8,0},{16,24},{24,16},{1,9},{9,1},{17,25},{25,17},{2,10},{10... | collective-permute-start | bytes 2457608 | tf_op jit(solution)/shard_map/ppermute | solution.py:1209
  179.3 18.0 %collective-permute-start.55 = (bf16[320,1280]{1,0:T(8,128)(2,1)S(1)}, bf16[320,1280]{1,0:T(8,128)(2,1)S(1)}, u32[]{:S(2)}, u32[]{:S(2)}) collective-permute-start(bf16[320,1280]{1,0:T(8,128)(2,1)S(1)} %add.36.half), channel_id=1, source_target_pairs={{8,16},{16,8},{9,17},{17,9},{10,18},{18,10},{11,19},{19,11},{12,20... | collective-permute-start | bytes 2457608 | tf_op jit(solution)/shard_map/ppermute | solution.py:1209
  181.2 15.7 %collective-permute-start.52 = (bf16[128,1280]{1,0:T(8,128)(2,1)S(1)}, bf16[128,1280]{1,0:T(8,128)(2,1)S(1)}, u32[]{:S(2)}, u32[]{:S(2)}) collective-permute-start(bf16[128,1280]{1,0:T(8,128)(2,1)S(1)} %get-tuple-element.405), channel_id=1, source_target_pairs={{0,4},{1,5},{2,6},{3,7},{4,0},{5,1},{6,2},{7,3},{8,12},{9,13},{10,... | collective-permute-start | bytes 983048 | tf_op jit(solution)/shard_map/ppermute | solution.py:1193
  182.2 14.7 %collective-permute-start.53 = (bf16[128,1280]{1,0:T(8,128)(2,1)S(1)}, bf16[128,1280]{1,0:T(8,128)(2,1)S(1)}, u32[]{:S(2)}, u32[]{:S(2)}) collective-permute-start(bf16[128,1280]{1,0:T(8,128)(2,1)S(1)} %get-tuple-element.406), channel_id=1, source_target_pairs={{0,6},{1,7},{2,4},{3,5},{4,2},{5,3},{6,0},{7,1},{8,14},{9,15},{10,... | collective-permute-start | bytes 983048 | tf_op jit(solution)/shard_map/ppermute | solution.py:1193
  197.6 22.6 %collective-permute-start.60 = (bf16[320,1280]{1,0:T(8,128)(2,1)S(1)}, bf16[320,1280]{1,0:T(8,128)(2,1)S(1)}, u32[]{:S(2)}, u32[]{:S(2)}) collective-permute-start(bf16[320,1280]{1,0:T(8,128)(2,1)S(1)} %z_send.7.sent), channel_id=1, source_target_pairs={{0,8},{8,0},{16,24},{24,16},{1,9},{9,1},{17,25},{25,17},{2,10},{10... | collective-permute-start | bytes 2457608 | tf_op jit(solution)/shard_map/ppermute | solution.py:1209
  201.3 18.9 %collective-permute-start.61 = (bf16[320,1280]{1,0:T(8,128)(2,1)S(1)}, bf16[320,1280]{1,0:T(8,128)(2,1)S(1)}, u32[]{:S(2)}, u32[]{:S(2)}) collective-permute-start(bf16[320,1280]{1,0:T(8,128)(2,1)S(1)} %add.37.refs_0_), channel_id=1, source_target_pairs={{8,16},{16,8},{9,17},{17,9},{10,18},{18,10},{11,19},{19,11},{12,20... | collective-permute-start | bytes 2457608 | tf_op jit(solution)/shard_map/ppermute | solution.py:1209
  220.4 21.5 %collective-permute-start.66 = (bf16[320,1280]{1,0:T(8,128)(2,1)S(1)}, bf16[320,1280]{1,0:T(8,128)(2,1)S(1)}, u32[]{:S(2)}, u32[]{:S(2)}) collective-permute-start(bf16[320,1280]{1,0:T(8,128)(2,1)S(1)} %add.40.sent), channel_id=1, source_target_pairs={{0,8},{8,0},{16,24},{24,16},{1,9},{9,1},{17,25},{25,17},{2,10},{10... | collective-permute-start | bytes 2457608 | tf_op jit(solution)/shard_map/ppermute | solution.py:1209
  222.3 19.5 %collective-permute-start.67 = (bf16[320,1280]{1,0:T(8,128)(2,1)S(1)}, bf16[320,1280]{1,0:T(8,128)(2,1)S(1)}, u32[]{:S(2)}, u32[]{:S(2)}) collective-permute-start(bf16[320,1280]{1,0:T(8,128)(2,1)S(1)} %add.39.refs_0_), channel_id=1, source_target_pairs={{8,16},{16,8},{9,17},{17,9},{10,18},{18,10},{11,19},{19,11},{12,20... | collective-permute-start | bytes 2457608 | tf_op jit(solution)/shard_map/ppermute | solution.py:1209
  224.2 17.6 %collective-permute-start.64 = (bf16[160,1280]{1,0:T(8,128)(2,1)S(1)}, bf16[160,1280]{1,0:T(8,128)(2,1)S(1)}, u32[]{:S(2)}, u32[]{:S(2)}) collective-permute-start(bf16[160,1280]{1,0:T(8,128)(2,1)S(1)} %get-tuple-element.443), channel_id=1, source_target_pairs={{0,4},{1,5},{2,6},{3,7},{4,0},{5,1},{6,2},{7,3},{8,12},{9,13},{10,... | collective-permute-start | bytes 1228808 | tf_op jit(solution)/shard_map/ppermute | solution.py:1193
  225.2 16.6 %collective-permute-start.65 = (bf16[160,1280]{1,0:T(8,128)(2,1)S(1)}, bf16[160,1280]{1,0:T(8,128)(2,1)S(1)}, u32[]{:S(2)}, u32[]{:S(2)}) collective-permute-start(bf16[160,1280]{1,0:T(8,128)(2,1)S(1)} %get-tuple-element.444), channel_id=1, source_target_pairs={{0,6},{1,7},{2,4},{3,5},{4,2},{5,3},{6,0},{7,1},{8,14},{9,15},{10,... | collective-permute-start | bytes 1228808 | tf_op jit(solution)/shard_map/ppermute | solution.py:1193
  241.9 20.3 %collective-permute-start.72 = (bf16[320,1280]{1,0:T(8,128)(2,1)S(1)}, bf16[320,1280]{1,0:T(8,128)(2,1)S(1)}, u32[]{:S(2)}, u32[]{:S(2)}) collective-permute-start(bf16[320,1280]{1,0:T(8,128)(2,1)S(1)} %add.42.sent), channel_id=1, source_target_pairs={{8,0},{16,24},{9,1},{17,25},{10,2},{18,26},{11,3},{19,27},{12,4},{... | collective-permute-start | bytes 2457608 | tf_op jit(solution)/shard_map/ppermute | solution.py:1209
  (48 other events, 413.5 us)

commit v9 on v8

--- a/solution.py
+++ b/solution.py
@@ -363,6 +363,14 @@
     )[0]
 
 
+def number(role, i):
+    return jnp.max(role[i : i + 1, :]).astype(jnp.int32)
+
+
+def numbers(role):
+    return [number(role, i) for i in range(3)]
+
+
 def fill_table(spot, extras, table, mask):
     chip, core = spot[0], spot[1]
     rows = mask.shape[1]
@@ -404,7 +412,8 @@
     return call(token_norm_kernel, "token_norm", "v" * len(blocks), [(shape, f32)])(*blocks)[0]
 
 
-def enter_kernel(spot, normed, *refs):
+def enter_kernel(role, normed, *refs):
+    spot = numbers(role)
     mine, other, refs = refs[:2], refs[2:4], refs[4:]
     out_mine, out_other, refs = *refs[:2], refs[2:]
     table, mask, qkv, out, first_low, projected, context = refs[:7]
@@ -445,13 +454,13 @@
     tiled(D, 256, partial)
 
 
-def enter(spot, normed, mine, other, out_mine, out_other):
+def enter(role, normed, mine, other, out_mine, out_other):
     total = normed.shape[0]
     rows = total // CHIPS
     outs = call(
         enter_kernel,
         "enter",
-        "sv" + "v" * 4 + "hv",
+        "vv" + "v" * 4 + "hv",
         [
             ((TABLE_ROWS, D), f32),
             ((total, rows), bf16),
@@ -464,7 +473,7 @@
         + [((rows, D), bf16)] * (CHIPS - 1)
         + [((rows // 2, D), bf16)] * 2,
         [pltpu.VMEM((TEAM, EXTRA, 3 * D_CHIP), f32), sems(2)],
-    )(spot, normed, *mine, *other, out_mine, out_other)
+    )(role, normed, *mine, *other, out_mine, out_other)
     return outs[:7], outs[7:]
 
 
@@ -587,10 +596,6 @@
     )(spot, part, *passed, down_mine, down_other)
 
 
-def number(role, i):
-    return jnp.max(role[i : i + 1, :]).astype(jnp.int32)
-
-
 def hidden_rows(at, second, up, table, grad_act, pre_act, act, grad_pre, bias_sum):
     size = at.stop - at.start
 
@@ -611,7 +616,8 @@
         bias_sum[...] += jnp.sum(grad.astype(f32), axis=0, keepdims=True)
 
 
-def hidden_first_kernel(spot, s0, s1, s2, grad_act, table, *refs):
+def hidden_first_kernel(role, s0, s1, s2, grad_act, table, *refs):
+    spot = numbers(role)
     columns = [(own, rest, rest.at[3 * HALF :]) for own, rest in (refs[:2], refs[2:4])]
     second, act, grad_pre, bias_sum, up = refs[4:9]
     partials, pre_act = refs[9:12], refs[12]
@@ -636,12 +642,12 @@
     tiled(D, 640, columns)
 
 
-def hidden_first(spot, blocks, grad_act, table, mine, other):
+def hidden_first(role, blocks, grad_act, table, mine, other):
     total = grad_act.shape[0]
     return call(
         hidden_first_kernel,
         "hidden_first",
-        "svvvvv" + "v" * 4,
+        "v" * 10,
         [
             ((total, D), bf16),
             ((total, FF_CHIP), bf16),
@@ -651,7 +657,7 @@
         ]
         + [((total // CHIPS, D), bf16)] * 3,
         [pltpu.VMEM((total, FF_CHIP), f32)],
-    )(spot, *blocks, grad_act, table, *mine, *other)
+    )(role, *blocks, grad_act, table, *mine, *other)
 
 
 def hidden_last_kernel(
@@ -1240,7 +1246,7 @@
     qkv_far_other = join([swap(half, 1) for half in halves(qkv_far)])
 
     (table, mask, qkv, out, first_low, projected, context), partial_out = enter(
-        spot,
+        role,
         normed,
         [qkv_near, qkv_far],
         [qkv_near_other, qkv_far_other],
@@ -1269,7 +1275,7 @@
     grad_act, down, whole_cotangent = act_grad(spot, part, passed, w_down, down_other)
 
     second_low, act_low, grad_pre, up_bias_sum, up, *partial_second = hidden_first(
-        spot,
+        role,
         second_blocks[:3],
         grad_act,
         table,

time: 264 us -> 263 us (level)
  no operation moved by 1% of the time
where the time goes in v9:
time: 263 us
  waiting for transfers between devices  113 us (43%)
  starting transfers between devices  85 us (32%)
  Pallas kernels  63.2 us (24%)
    ppermute x55, waiting for transfers between devices, swap(): return lax.ppermute(value, 'fsdp', pairs)  83 us
    pallas_call x48, Pallas kernels, run(): return made(*placed)  55.8 us
    ppermute x55, starting transfers between devices, swap(): return lax.ppermute(value, 'fsdp', pairs)  52.8 us
    ppermute x18, starting transfers between devices, along_z(): return lax.ppermute(value, 'dp', pairs)  32.2 us
    ppermute x18, waiting for transfers between devices, along_z(): return lax.ppermute(value, 'dp', pairs)  29.7 us
  transfers between devices with their start and end apart: 73, of which 39 were waited for; matrix products, arithmetic and copies ran while one was open for 0% of the time, Pallas kernels for 22%

profile of v9, /device:TPU:0, one launch (start us, length us, event | category | flops | bytes accessed | tf_op | source)
XLA Modules:
  0.0 263.1 jit_solution(17619099542447455247)
XLA Ops:
  0.7 3.0 %collective-permute-start.1 = (bf16[128,1280]{1,0:T(8,128)(2,1)}, bf16[128,1280]{1,0:T(8,128)(2,1)S(1)}, u32[]{:S(2)}, u32[]{:S(2)}) collective-permute-start(bf16[128,1280]{1,0:T(8,128)(2,1)} %tokens.3), channel_id=1, source_target_pairs={{0,4},{1,5},{2,6},{3,7},{4,0},{5,1},{6,2},{7,3},{8,12},{9,13},{10,... | collective-permute-start | bytes 983048 | tf_op jit(solution)/shard_map/ppermute | solution.py:1199
  5.9 2.9 %qkv_blocks.1 = (bf16[168,960]{1,0:T(8,128)(2,1)S(1)}, bf16[88,960]{1,0:T(8,128)(2,1)S(1)}, bf16[88,960]{1,0:T(8,128)(2,1)S(1)}, bf16[88,960]{1,0:T(8,128)(2,1)S...) custom-call(s32[4]{0:T(128)S(1)} %pad_add_fusion.spot, s32[1,2]{1,0:T(1,128)S(1)} %copy-done.3, s32[128]{0:T(128)} %padding.1, ...), custom_call_target="tpu_custom_call" | custom-call | flops 1 | bytes 1 | tf_op jit(solution)/shard_map/qkv_blocks/pallas_call | solution.py:143
  9.5 2.9 %collective-permute-start.4 = (bf16[88,960]{1,0:T(8,128)(2,1)S(1)}, bf16[88,960]{1,0:T(8,128)(2,1)S(1)}, u32[]{:S(2)}, u32[]{:S(2)}) collective-permute-start(bf16[88,960]{1,0:T(8,128)(2,1)S(1)} %get-tuple-element.255), channel_id=1, source_target_pairs={{0,6},{1,7},{2,4},{3,5},{4,2},{5,3},{6,0},{7,1},{8,14},{9,15},{10,... | collective-permute-start | bytes 506888 | tf_op jit(solution)/shard_map/ppermute | solution.py:1199
  12.4 6.0 %collective-permute-done.2.q1 = bf16[88,960]{1,0:T(8,128)(2,1)S(1)} collective-permute-done((bf16[88,960]{1,0:T(8,128)(2,1)S(1)}, bf16[88,960]{1,0:T(8,128)(2,1)S(1)}, u32[]{:S(2)}, u32[]{:S(2)}) %collective-permute-start.2) | collective-permute-done | bytes 168992 | tf_op jit(solution)/shard_map/ppermute | solution.py:1199
  31.4 5.7 %collective-permute-done.7.whole.refs_1_ = bf16[240,960]{1,0:T(8,128)(2,1)S(1)} collective-permute-done((bf16[240,960]{1,0:T(8,128)(2,1)S(1)}, bf16[240,960]{1,0:T(8,128)(2,1)S(1)}, u32[]{:S(2)}, u32[]{:S(2)}) %collective-permute-start.7) | collective-permute-done | bytes 460832 | tf_op jit(solution)/shard_map/ppermute | solution.py:1215
  39.0 6.9 %enter.1 = (f32[8,1280]{1,0:T(8,128)S(1)}, bf16[512,128]{1,0:T(8,128)(2,1)S(1)}, bf16[1280,960]{1,0:T(8,128)(2,1)S(1)}, bf16[320,1280]{1,0:T(8,128)(2,1)S(1)}, b...) custom-call(f32[8,128]{1,0:T(8,128)S(1)} %get-tuple-element.251.role, ...), custom_call_target="tpu_custom_call" | custom-call | flops 1 | bytes 1 | tf_op jit(solution)/shard_map/enter/pallas_call | solution.py:143
  52.7 2.8 %collective-permute-done.18.h1 = bf16[64,1280]{1,0:T(8,128)(2,1)S(1)} collective-permute-done((bf16[64,1280]{1,0:T(8,128)(2,1)S(1)}, bf16[64,1280]{1,0:T(8,128)(2,1)S(1)}, u32[]{:S(2)}, u32[]{:S(2)}) %collective-permute-start.18) | collective-permute-done | bytes 163872 | tf_op jit(solution)/shard_map/ppermute | solution.py:1199
  59.9 5.2 %collective-permute-done.20.p1 = bf16[128,1280]{1,0:T(8,128)(2,1)S(1)} collective-permute-done((bf16[128,1280]{1,0:T(8,128)(2,1)S(1)}, bf16[128,1280]{1,0:T(8,128)(2,1)S(1)}, u32[]{:S(2)}, u32[]{:S(2)}) %collective-permute-start.20) | collective-permute-done | bytes 327712 | tf_op jit(solution)/shard_map/ppermute | solution.py:1199
  71.7 4.7 %act_grad.1 = (f32[512,1280]{1,0:T(8,128)S(1)}, bf16[1280,1280]{1,0:T(8,128)(2,1)S(1)}, bf16[512,1280]{1,0:T(8,128)(2,1)S(1)}) custom-call(s32[4]{0:T(128)S(1)} %pad_add_fusion.spot, bf16[384,1280]{1,0:T(8,128)(2,1)S(1)} %get-tuple-element.300.part, bf16[64,1280]{1,0:T(8,128)(2,1)S(1)} %collective-permute-done.16.g1, ...), custom_call_target="tpu_custom_call" | custom-call | flops 1 | bytes 1 | tf_op jit(solution)/shard_map/act_grad/pallas_call | solution.py:143
  78.7 5.5 %hidden_first.1 = (bf16[512,1280]{1,0:T(8,128)(2,1)S(1)}, bf16[512,1280]{1,0:T(8,128)(2,1)S(1)}, bf16[512,1280]{1,0:T(8,128)(2,1)S(1)}, f32[1,1280]{1,0:T(1,128)...) custom-call(f32[8,128]{1,0:T(8,128)S(1)} %get-tuple-element.251.role, ...), custom_call_target="tpu_custom_call" | custom-call | flops 1 | bytes 1 | tf_op jit(solution)/shard_map/hidden_first/pallas_call | solution.py:143
  96.3 3.9 %rest.1 = (bf16[320,1280]{1,0:T(8,128)(2,1)S(1)}, bf16[320,1280]{1,0:T(8,128)(2,1)S(1)}, bf16[320,1280]{1,0:T(8,128)(2,1)S(1)}, bf16[320,1280]{1,0:T(8,128)(2,1)S(1)}, bf16[320,1280]{1,0:T(8,128)(2,1)S(1)}) custom-call(s32[4]{0:T(128)S(1)} %pad_add_fusion.spot, bf16[512,1280]{1,0:T(8,128)(2,1)S(1)} %get-tuple-element.326.second, ...), custom_call_target="tpu_custom_call" | custom-call | flops 1 | bytes 1 | tf_op jit(solution)/shard_map/rest/pallas_call | solution.py:143
  101.8 6.5 %collective-permute-done.28.p2 = bf16[128,1280]{1,0:T(8,128)(2,1)S(1)} collective-permute-done((bf16[128,1280]{1,0:T(8,128)(2,1)S(1)}, bf16[128,1280]{1,0:T(8,128)(2,1)S(1)}, u32[]{:S(2)}, u32[]{:S(2)}) %collective-permute-start.28) | collective-permute-done | bytes 327712 | tf_op jit(solution)/shard_map/ppermute | solution.py:1199
  116.0 2.6 result.1
  118.6 5.4 %collective-permute-done.35.b3 = bf16[128,1280]{1,0:T(8,128)(2,1)S(1)} collective-permute-done((bf16[128,1280]{1,0:T(8,128)(2,1)S(1)}, bf16[128,1280]{1,0:T(8,128)(2,1)S(1)}, u32[]{:S(2)}, u32[]{:S(2)}) %collective-permute-start.35) | collective-permute-done | bytes 327712 | tf_op jit(solution)/shard_map/ppermute | solution.py:1199
  124.0 5.0 %collective-permute-done.34.b2 = bf16[128,1280]{1,0:T(8,128)(2,1)S(1)} collective-permute-done((bf16[128,1280]{1,0:T(8,128)(2,1)S(1)}, bf16[128,1280]{1,0:T(8,128)(2,1)S(1)}, u32[]{:S(2)}, u32[]{:S(2)}) %collective-permute-start.34) | collective-permute-done | bytes 327712 | tf_op jit(solution)/shard_map/ppermute | solution.py:1199
  130.9 3.7 %collective-permute-start.40 = (bf16[320,1280]{1,0:T(8,128)(2,1)S(1)}, bf16[320,1280]{1,0:T(8,128)(2,1)S(1)}, u32[]{:S(2)}, u32[]{:S(2)}) collective-permute-start(bf16[320,1280]{1,0:T(8,128)(2,1)S(1)} %z_send.4.sent), channel_id=1, source_target_pairs={{0,8},{8,0},{16,24},{24,16},{1,9},{9,1},{17,25},{25,17},{2,10},{10... | collective-permute-start | bytes 2457608 | tf_op jit(solution)/shard_map/ppermute | solution.py:1215
  135.3 6.8 %leave.1 = (bf16[512,1280]{1,0:T(8,128)(2,1)S(1)}, bf16[512,960]{1,0:T(8,128)(2,1)S(1)}, f32[1,960]{1,0:T(1,128)S(1)}, bf16[128,1280]{1,0:T(8,128)(2,1)S(1)}, bf...) custom-call(bf16[128,1280]{1,0:T(8,128)(2,1)S(1)} %get-tuple-element.354.b0, ...), custom_call_target="tpu_custom_call" | custom-call | flops 1 | bytes 1 | tf_op jit(solution)/shard_map/leave/pallas_call | solution.py:143
  142.2 3.8 %qkv_grad.1 = (bf16[2,160,960]{2,1,0:T(8,128)(2,1)S(1)}, bf16[2,160,960]{2,1,0:T(8,128)(2,1)S(1)}, bf16[4,160,960]{2,1,0:T(8,128)(2,1)S(1)}, bf16[160,1280]{1,0:T(8,128)(2,1)S(1)}, bf16[160,1280]{1,0:T(8,128)(2,1)S(1)}) custom-call(s32[4]{0:T(128)S(1)} %pad_add_fusion.spot, bf16[512,1280]{1,0:T(8,128)(2,1)S(1)} %get-tuple-element.375.first_low, ...), custom_call_target="tpu_custom_call" | custom-call | flops 1 | bytes 1 | tf_op jit(solution)/shard_map/qkv_grad/pallas_call | solution.py:143
  146.7 3.0 %collective-permute-done.44.out_got = bf16[160,1280]{1,0:T(8,128)(2,1)S(1)} collective-permute-done((bf16[160,1280]{1,0:T(8,128)(2,1)S(1)}, bf16[160,1280]{1,0:T(8,128)(2,1)S(1)}, u32[]{:S(2)}, u32[]{:S(2)}) %collective-permute-start.44) | collective-permute-done | bytes 409632 | tf_op jit(solution)/shard_map/ppermute | solution.py:1199
  152.1 3.7 %collective-permute-start.49 = (bf16[320,1280]{1,0:T(8,128)(2,1)S(1)}, bf16[320,1280]{1,0:T(8,128)(2,1)S(1)}, u32[]{:S(2)}, u32[]{:S(2)}) collective-permute-start(bf16[320,1280]{1,0:T(8,128)(2,1)S(1)} %z_send.5.sent), channel_id=1, source_target_pairs={{0,8},{8,0},{16,24},{24,16},{1,9},{9,1},{17,25},{25,17},{2,10},{10... | collective-permute-start | bytes 2457608 | tf_op jit(solution)/shard_map/ppermute | solution.py:1215
  160.2 14.5 %collective-permute-done.49.refs_1_.got_side = bf16[320,1280]{1,0:T(8,128)(2,1)S(1)} collective-permute-done((bf16[320,1280]{1,0:T(8,128)(2,1)S(1)}, bf16[320,1280]{1,0:T(8,128)(2,1)S(1)}, u32[]{:S(2)}, u32[]{:S(2)}) %collective-permute-start.49) | collective-permute-done | bytes 819232 | tf_op jit(solution)/shard_map/ppermute | solution.py:1215
  174.9 3.7 %collective-permute-start.54 = (bf16[320,1280]{1,0:T(8,128)(2,1)S(1)}, bf16[320,1280]{1,0:T(8,128)(2,1)S(1)}, u32[]{:S(2)}, u32[]{:S(2)}) collective-permute-start(bf16[320,1280]{1,0:T(8,128)(2,1)S(1)} %z_send.6.sent), channel_id=1, source_target_pairs={{0,8},{8,0},{16,24},{24,16},{1,9},{9,1},{17,25},{25,17},{2,10},{10... | collective-permute-start | bytes 2457608 | tf_op jit(solution)/shard_map/ppermute | solution.py:1215
  182.9 7.2 %collective-permute-done.51.r1 = bf16[128,1280]{1,0:T(8,128)(2,1)S(1)} collective-permute-done((bf16[128,1280]{1,0:T(8,128)(2,1)S(1)}, bf16[128,1280]{1,0:T(8,128)(2,1)S(1)}, u32[]{:S(2)}, u32[]{:S(2)}) %collective-permute-start.51) | collective-permute-done | bytes 327712 | tf_op jit(solution)/shard_map/ppermute | solution.py:1199
  190.1 6.0 %collective-permute-done.52.r2 = bf16[128,1280]{1,0:T(8,128)(2,1)S(1)} collective-permute-done((bf16[128,1280]{1,0:T(8,128)(2,1)S(1)}, bf16[128,1280]{1,0:T(8,128)(2,1)S(1)}, u32[]{:S(2)}, u32[]{:S(2)}) %collective-permute-start.52) | collective-permute-done | bytes 327712 | tf_op jit(solution)/shard_map/ppermute | solution.py:1199
  196.9 3.7 %collective-permute-start.60 = (bf16[320,1280]{1,0:T(8,128)(2,1)S(1)}, bf16[320,1280]{1,0:T(8,128)(2,1)S(1)}, u32[]{:S(2)}, u32[]{:S(2)}) collective-permute-start(bf16[320,1280]{1,0:T(8,128)(2,1)S(1)} %z_send.7.sent), channel_id=1, source_target_pairs={{0,8},{8,0},{16,24},{24,16},{1,9},{9,1},{17,25},{25,17},{2,10},{10... | collective-permute-start | bytes 2457608 | tf_op jit(solution)/shard_map/ppermute | solution.py:1215
  201.6 2.6 end.1
  216.9 2.7 %collective-permute-done.62.refs_1_ = f32[16,1280]{1,0:T(8,128)S(1)} collective-permute-done((f32[16,1280]{1,0:T(8,128)S(1)}, f32[16,1280]{1,0:T(8,128)S(1)}, u32[]{:S(2)}, u32[]{:S(2)}) %collective-permute-start.62) | collective-permute-done | bytes 81952 | tf_op jit(solution)/shard_map/ppermute | solution.py:1215
  226.6 8.2 %collective-permute-done.63.b1 = bf16[160,1280]{1,0:T(8,128)(2,1)S(1)} collective-permute-done((bf16[160,1280]{1,0:T(8,128)(2,1)S(1)}, bf16[160,1280]{1,0:T(8,128)(2,1)S(1)}, u32[]{:S(2)}, u32[]{:S(2)}) %collective-permute-start.63) | collective-permute-done | bytes 409632 | tf_op jit(solution)/shard_map/ppermute | solution.py:1199
  234.9 6.1 %collective-permute-done.64.b2 = bf16[160,1280]{1,0:T(8,128)(2,1)S(1)} collective-permute-done((bf16[160,1280]{1,0:T(8,128)(2,1)S(1)}, bf16[160,1280]{1,0:T(8,128)(2,1)S(1)}, u32[]{:S(2)}, u32[]{:S(2)}) %collective-permute-start.64) | collective-permute-done | bytes 409632 | tf_op jit(solution)/shard_map/ppermute | solution.py:1199
  247.5 3.3 %collective-permute-start.71 = (f32[16,1280]{1,0:T(8,128)S(1)}, f32[16,1280]{1,0:T(8,128)S(1)}, u32[]{:S(2)}, u32[]{:S(2)}) collective-permute-start(f32[16,1280]{1,0:T(8,128)S(1)} %add.41.refs_1_), channel_id=1, source_target_pairs={{0,16},{8,24},{16,0},{24,8},{1,17},{9,25},{17,1},{25,9},{2,18},{10... | collective-permute-start | bytes 245768 | tf_op jit(solution)/shard_map/ppermute | solution.py:1215
  252.7 2.5 up_rows.1
  255.8 2.4 collective-permute-done.69.b2
  (181 shorter events, 108.9 us)
Async XLA Ops:
  0.7 19.9 %collective-permute-start.1 = (bf16[128,1280]{1,0:T(8,128)(2,1)}, bf16[128,1280]{1,0:T(8,128)(2,1)S(1)}, u32[]{:S(2)}, u32[]{:S(2)}) collective-permute-start(bf16[128,1280]{1,0:T(8,128)(2,1)} %tokens.3), channel_id=1, source_target_pairs={{0,4},{1,5},{2,6},{3,7},{4,0},{5,1},{6,2},{7,3},{8,12},{9,13},{10,... | collective-permute-start | bytes 983048 | tf_op jit(solution)/shard_map/ppermute | solution.py:1199
  3.7 16.9 %collective-permute-start = (bf16[128,1280]{1,0:T(8,128)(2,1)}, bf16[128,1280]{1,0:T(8,128)(2,1)S(1)}, u32[]{:S(2)}, u32[]{:S(2)}) collective-permute-start(bf16[128,1280]{1,0:T(8,128)(2,1)} %tokens.3), channel_id=1, source_target_pairs={{0,2},{1,3},{2,0},{3,1},{4,6},{5,7},{6,4},{7,5},{8,10},{9,11},{10,... | collective-permute-start | bytes 983048 | tf_op jit(solution)/shard_map/ppermute | solution.py:1199
  20.7 16.3 %collective-permute-start.8 = (bf16[432,960]{1,0:T(8,128)(2,1)S(1)}, bf16[432,960]{1,0:T(8,128)(2,1)S(1)}, u32[]{:S(2)}, u32[]{:S(2)}) collective-permute-start(bf16[432,960]{1,0:T(8,128)(2,1)S(1)} %get-tuple-element.265.refs_0_), channel_id=1, source_target_pairs={{0,1},{1,0},{2,3},{3,2},{4,5},{5,4},{6,7},{7,6},{8,9},{9,8},{10,11... | collective-permute-start | bytes 2488328 | tf_op jit(solution)/shard_map/ppermute | solution.py:1199
  27.4 19.3 %collective-permute-start.12 = (bf16[208,1280]{1,0:T(8,128)(2,1)S(1)}, bf16[208,1280]{1,0:T(8,128)(2,1)S(1)}, u32[]{:S(2)}, u32[]{:S(2)}) collective-permute-start(bf16[208,1280]{1,0:T(8,128)(2,1)S(1)} %get-tuple-element.279), channel_id=1, source_target_pairs={{0,2},{1,3},{2,0},{3,1},{4,6},{5,7},{6,4},{7,5},{8,10},{9,11},{10,... | collective-permute-start | bytes 1597448 | tf_op jit(solution)/shard_map/ppermute | solution.py:1199
  29.1 17.8 %collective-permute-start.13 = (bf16[208,1280]{1,0:T(8,128)(2,1)S(1)}, bf16[208,1280]{1,0:T(8,128)(2,1)S(1)}, u32[]{:S(2)}, u32[]{:S(2)}) collective-permute-start(bf16[208,1280]{1,0:T(8,128)(2,1)S(1)} %get-tuple-element.280), channel_id=1, source_target_pairs={{0,4},{1,5},{2,6},{3,7},{4,0},{5,1},{6,2},{7,3},{8,12},{9,13},{10,... | collective-permute-start | bytes 1597448 | tf_op jit(solution)/shard_map/ppermute | solution.py:1199
  47.0 19.0 %collective-permute-start.15 = (bf16[240,1280]{1,0:T(8,128)(2,1)S(1)}, bf16[240,1280]{1,0:T(8,128)(2,1)S(1)}, u32[]{:S(2)}, u32[]{:S(2)}) collective-permute-start(bf16[240,1280]{1,0:T(8,128)(2,1)S(1)} %get-tuple-element.282.refs_0_), channel_id=1, source_target_pairs={{0,8},{8,0},{16,24},{24,16},{1,9},{9,1},{17,25},{25,17},{2,10},{10... | collective-permute-start | bytes 1843208 | tf_op jit(solution)/shard_map/ppermute | solution.py:1215
  69.9 15.5 %collective-permute-start.29 = (bf16[128,1280]{1,0:T(8,128)(2,1)S(1)}, bf16[128,1280]{1,0:T(8,128)(2,1)S(1)}, u32[]{:S(2)}, u32[]{:S(2)}) collective-permute-start(bf16[128,1280]{1,0:T(8,128)(2,1)S(1)} %get-tuple-element.297.s0), channel_id=1, source_target_pairs={{0,6},{1,7},{2,4},{3,5},{4,2},{5,3},{6,0},{7,1},{8,14},{9,15},{10,... | collective-permute-start | bytes 983048 | tf_op jit(solution)/shard_map/ppermute | solution.py:1199
  90.7 20.4 %collective-permute-start.36 = (bf16[320,1280]{1,0:T(8,128)(2,1)S(1)}, bf16[320,1280]{1,0:T(8,128)(2,1)S(1)}, u32[]{:S(2)}, u32[]{:S(2)}) collective-permute-start(bf16[320,1280]{1,0:T(8,128)(2,1)S(1)} %down_grad.1.refs_0_), channel_id=1, source_target_pairs={{0,8},{8,0},{16,24},{24,16},{1,9},{9,1},{17,25},{25,17},{2,10},{10... | collective-permute-start | bytes 2457608 | tf_op jit(solution)/shard_map/ppermute | solution.py:1215
  92.1 16.2 %collective-permute-start.28 = (bf16[128,1280]{1,0:T(8,128)(2,1)S(1)}, bf16[128,1280]{1,0:T(8,128)(2,1)S(1)}, u32[]{:S(2)}, u32[]{:S(2)}) collective-permute-start(bf16[128,1280]{1,0:T(8,128)(2,1)S(1)} %get-tuple-element.311), channel_id=1, source_target_pairs={{0,4},{1,5},{2,6},{3,7},{4,0},{5,1},{6,2},{7,3},{8,12},{9,13},{10,... | collective-permute-start | bytes 983048 | tf_op jit(solution)/shard_map/ppermute | solution.py:1199
  100.2 14.6 %collective-permute-start.39 = (bf16[320,1280]{1,0:T(8,128)(2,1)S(1)}, bf16[320,1280]{1,0:T(8,128)(2,1)S(1)}, u32[]{:S(2)}, u32[]{:S(2)}) collective-permute-start(bf16[320,1280]{1,0:T(8,128)(2,1)S(1)} %get-tuple-element.339), channel_id=1, source_target_pairs={{0,1},{1,0},{2,3},{3,2},{4,5},{5,4},{6,7},{7,6},{8,9},{9,8},{10,11... | collective-permute-start | bytes 2457608 | tf_op jit(solution)/shard_map/ppermute | solution.py:1199
  111.2 19.5 %collective-permute-start.37 = (bf16[320,1280]{1,0:T(8,128)(2,1)S(1)}, bf16[320,1280]{1,0:T(8,128)(2,1)S(1)}, u32[]{:S(2)}, u32[]{:S(2)}) collective-permute-start(bf16[320,1280]{1,0:T(8,128)(2,1)S(1)} %add.30.refs_0_), channel_id=1, source_target_pairs={{0,8},{8,0},{16,24},{24,16},{1,9},{9,1},{17,25},{25,17},{2,10},{10... | collective-permute-start | bytes 2457608 | tf_op jit(solution)/shard_map/ppermute | solution.py:1215
  111.7 19.0 %collective-permute-start.38 = (bf16[320,1280]{1,0:T(8,128)(2,1)S(1)}, bf16[320,1280]{1,0:T(8,128)(2,1)S(1)}, u32[]{:S(2)}, u32[]{:S(2)}) collective-permute-start(bf16[320,1280]{1,0:T(8,128)(2,1)S(1)} %add.31.half), channel_id=1, source_target_pairs={{8,16},{16,8},{9,17},{17,9},{10,18},{18,10},{11,19},{19,11},{12,20... | collective-permute-start | bytes 2457608 | tf_op jit(solution)/shard_map/ppermute | solution.py:1215
  114.2 14.8 %collective-permute-start.34 = (bf16[128,1280]{1,0:T(8,128)(2,1)S(1)}, bf16[128,1280]{1,0:T(8,128)(2,1)S(1)}, u32[]{:S(2)}, u32[]{:S(2)}) collective-permute-start(bf16[128,1280]{1,0:T(8,128)(2,1)S(1)} %get-tuple-element.354.b0), channel_id=1, source_target_pairs={{0,4},{1,5},{2,6},{3,7},{4,0},{5,1},{6,2},{7,3},{8,12},{9,13},{10,... | collective-permute-start | bytes 983048 | tf_op jit(solution)/shard_map/ppermute | solution.py:1199
  114.8 14.2 %collective-permute-start.33 = (bf16[128,1280]{1,0:T(8,128)(2,1)S(1)}, bf16[128,1280]{1,0:T(8,128)(2,1)S(1)}, u32[]{:S(2)}, u32[]{:S(2)}) collective-permute-start(bf16[128,1280]{1,0:T(8,128)(2,1)S(1)} %get-tuple-element.354.b0), channel_id=1, source_target_pairs={{0,2},{1,3},{2,0},{3,1},{4,6},{5,7},{6,4},{7,5},{8,10},{9,11},{10,... | collective-permute-start | bytes 983048 | tf_op jit(solution)/shard_map/ppermute | solution.py:1199
  130.9 20.9 %collective-permute-start.40 = (bf16[320,1280]{1,0:T(8,128)(2,1)S(1)}, bf16[320,1280]{1,0:T(8,128)(2,1)S(1)}, u32[]{:S(2)}, u32[]{:S(2)}) collective-permute-start(bf16[320,1280]{1,0:T(8,128)(2,1)S(1)} %z_send.4.sent), channel_id=1, source_target_pairs={{0,8},{8,0},{16,24},{24,16},{1,9},{9,1},{17,25},{25,17},{2,10},{10... | collective-permute-start | bytes 2457608 | tf_op jit(solution)/shard_map/ppermute | solution.py:1215
  134.6 17.2 %collective-permute-start.41 = (bf16[320,1280]{1,0:T(8,128)(2,1)S(1)}, bf16[320,1280]{1,0:T(8,128)(2,1)S(1)}, u32[]{:S(2)}, u32[]{:S(2)}) collective-permute-start(bf16[320,1280]{1,0:T(8,128)(2,1)S(1)} %add.33.half), channel_id=1, source_target_pairs={{8,16},{16,8},{9,17},{17,9},{10,18},{18,10},{11,19},{19,11},{12,20... | collective-permute-start | bytes 2457608 | tf_op jit(solution)/shard_map/ppermute | solution.py:1215
  152.1 22.5 %collective-permute-start.49 = (bf16[320,1280]{1,0:T(8,128)(2,1)S(1)}, bf16[320,1280]{1,0:T(8,128)(2,1)S(1)}, u32[]{:S(2)}, u32[]{:S(2)}) collective-permute-start(bf16[320,1280]{1,0:T(8,128)(2,1)S(1)} %z_send.5.sent), channel_id=1, source_target_pairs={{0,8},{8,0},{16,24},{24,16},{1,9},{9,1},{17,25},{25,17},{2,10},{10... | collective-permute-start | bytes 2457608 | tf_op jit(solution)/shard_map/ppermute | solution.py:1215
  155.8 18.8 %collective-permute-start.50 = (bf16[320,1280]{1,0:T(8,128)(2,1)S(1)}, bf16[320,1280]{1,0:T(8,128)(2,1)S(1)}, u32[]{:S(2)}, u32[]{:S(2)}) collective-permute-start(bf16[320,1280]{1,0:T(8,128)(2,1)S(1)} %add.34.half), channel_id=1, source_target_pairs={{8,16},{16,8},{9,17},{17,9},{10,18},{18,10},{11,19},{19,11},{12,20... | collective-permute-start | bytes 2457608 | tf_op jit(solution)/shard_map/ppermute | solution.py:1215
  156.6 18.0 %collective-permute-start.46 = (bf16[128,1280]{1,0:T(8,128)(2,1)S(1)}, bf16[128,1280]{1,0:T(8,128)(2,1)S(1)}, u32[]{:S(2)}, u32[]{:S(2)}) collective-permute-start(bf16[128,1280]{1,0:T(8,128)(2,1)S(1)} %get-tuple-element.391), channel_id=1, source_target_pairs={{0,2},{1,3},{2,0},{3,1},{4,6},{5,7},{6,4},{7,5},{8,10},{9,11},{10,... | collective-permute-start | bytes 983048 | tf_op jit(solution)/shard_map/ppermute | solution.py:1199
  157.6 17.1 %collective-permute-start.47 = (bf16[128,1280]{1,0:T(8,128)(2,1)S(1)}, bf16[128,1280]{1,0:T(8,128)(2,1)S(1)}, u32[]{:S(2)}, u32[]{:S(2)}) collective-permute-start(bf16[128,1280]{1,0:T(8,128)(2,1)S(1)} %get-tuple-element.392), channel_id=1, source_target_pairs={{0,4},{1,5},{2,6},{3,7},{4,0},{5,1},{6,2},{7,3},{8,12},{9,13},{10,... | collective-permute-start | bytes 983048 | tf_op jit(solution)/shard_map/ppermute | solution.py:1199
  158.9 15.7 %collective-permute-start.48 = (bf16[128,1280]{1,0:T(8,128)(2,1)S(1)}, bf16[128,1280]{1,0:T(8,128)(2,1)S(1)}, u32[]{:S(2)}, u32[]{:S(2)}) collective-permute-start(bf16[128,1280]{1,0:T(8,128)(2,1)S(1)} %get-tuple-element.393), channel_id=1, source_target_pairs={{0,6},{1,7},{2,4},{3,5},{4,2},{5,3},{6,0},{7,1},{8,14},{9,15},{10,... | collective-permute-start | bytes 983048 | tf_op jit(solution)/shard_map/ppermute | solution.py:1199
  174.9 21.7 %collective-permute-start.54 = (bf16[320,1280]{1,0:T(8,128)(2,1)S(1)}, bf16[320,1280]{1,0:T(8,128)(2,1)S(1)}, u32[]{:S(2)}, u32[]{:S(2)}) collective-permute-start(bf16[320,1280]{1,0:T(8,128)(2,1)S(1)} %z_send.6.sent), channel_id=1, source_target_pairs={{0,8},{8,0},{16,24},{24,16},{1,9},{9,1},{17,25},{25,17},{2,10},{10... | collective-permute-start | bytes 2457608 | tf_op jit(solution)/shard_map/ppermute | solution.py:1215
  178.6 18.0 %collective-permute-start.55 = (bf16[320,1280]{1,0:T(8,128)(2,1)S(1)}, bf16[320,1280]{1,0:T(8,128)(2,1)S(1)}, u32[]{:S(2)}, u32[]{:S(2)}) collective-permute-start(bf16[320,1280]{1,0:T(8,128)(2,1)S(1)} %add.36.half), channel_id=1, source_target_pairs={{8,16},{16,8},{9,17},{17,9},{10,18},{18,10},{11,19},{19,11},{12,20... | collective-permute-start | bytes 2457608 | tf_op jit(solution)/shard_map/ppermute | solution.py:1215
  180.3 15.7 %collective-permute-start.52 = (bf16[128,1280]{1,0:T(8,128)(2,1)S(1)}, bf16[128,1280]{1,0:T(8,128)(2,1)S(1)}, u32[]{:S(2)}, u32[]{:S(2)}) collective-permute-start(bf16[128,1280]{1,0:T(8,128)(2,1)S(1)} %get-tuple-element.405), channel_id=1, source_target_pairs={{0,4},{1,5},{2,6},{3,7},{4,0},{5,1},{6,2},{7,3},{8,12},{9,13},{10,... | collective-permute-start | bytes 983048 | tf_op jit(solution)/shard_map/ppermute | solution.py:1199
  181.7 14.4 %collective-permute-start.53 = (bf16[128,1280]{1,0:T(8,128)(2,1)S(1)}, bf16[128,1280]{1,0:T(8,128)(2,1)S(1)}, u32[]{:S(2)}, u32[]{:S(2)}) collective-permute-start(bf16[128,1280]{1,0:T(8,128)(2,1)S(1)} %get-tuple-element.406), channel_id=1, source_target_pairs={{0,6},{1,7},{2,4},{3,5},{4,2},{5,3},{6,0},{7,1},{8,14},{9,15},{10,... | collective-permute-start | bytes 983048 | tf_op jit(solution)/shard_map/ppermute | solution.py:1199
  196.9 22.6 %collective-permute-start.60 = (bf16[320,1280]{1,0:T(8,128)(2,1)S(1)}, bf16[320,1280]{1,0:T(8,128)(2,1)S(1)}, u32[]{:S(2)}, u32[]{:S(2)}) collective-permute-start(bf16[320,1280]{1,0:T(8,128)(2,1)S(1)} %z_send.7.sent), channel_id=1, source_target_pairs={{0,8},{8,0},{16,24},{24,16},{1,9},{9,1},{17,25},{25,17},{2,10},{10... | collective-permute-start | bytes 2457608 | tf_op jit(solution)/shard_map/ppermute | solution.py:1215
  200.6 18.9 %collective-permute-start.61 = (bf16[320,1280]{1,0:T(8,128)(2,1)S(1)}, bf16[320,1280]{1,0:T(8,128)(2,1)S(1)}, u32[]{:S(2)}, u32[]{:S(2)}) collective-permute-start(bf16[320,1280]{1,0:T(8,128)(2,1)S(1)} %add.37.refs_0_), channel_id=1, source_target_pairs={{8,16},{16,8},{9,17},{17,9},{10,18},{18,10},{11,19},{19,11},{12,20... | collective-permute-start | bytes 2457608 | tf_op jit(solution)/shard_map/ppermute | solution.py:1215
  219.7 21.2 %collective-permute-start.66 = (bf16[320,1280]{1,0:T(8,128)(2,1)S(1)}, bf16[320,1280]{1,0:T(8,128)(2,1)S(1)}, u32[]{:S(2)}, u32[]{:S(2)}) collective-permute-start(bf16[320,1280]{1,0:T(8,128)(2,1)S(1)} %add.40.sent), channel_id=1, source_target_pairs={{0,8},{8,0},{16,24},{24,16},{1,9},{9,1},{17,25},{25,17},{2,10},{10... | collective-permute-start | bytes 2457608 | tf_op jit(solution)/shard_map/ppermute | solution.py:1215
  221.7 19.3 %collective-permute-start.67 = (bf16[320,1280]{1,0:T(8,128)(2,1)S(1)}, bf16[320,1280]{1,0:T(8,128)(2,1)S(1)}, u32[]{:S(2)}, u32[]{:S(2)}) collective-permute-start(bf16[320,1280]{1,0:T(8,128)(2,1)S(1)} %add.39.refs_0_), channel_id=1, source_target_pairs={{8,16},{16,8},{9,17},{17,9},{10,18},{18,10},{11,19},{19,11},{12,20... | collective-permute-start | bytes 2457608 | tf_op jit(solution)/shard_map/ppermute | solution.py:1215
  223.3 17.6 %collective-permute-start.64 = (bf16[160,1280]{1,0:T(8,128)(2,1)S(1)}, bf16[160,1280]{1,0:T(8,128)(2,1)S(1)}, u32[]{:S(2)}, u32[]{:S(2)}) collective-permute-start(bf16[160,1280]{1,0:T(8,128)(2,1)S(1)} %get-tuple-element.443), channel_id=1, source_target_pairs={{0,4},{1,5},{2,6},{3,7},{4,0},{5,1},{6,2},{7,3},{8,12},{9,13},{10,... | collective-permute-start | bytes 1228808 | tf_op jit(solution)/shard_map/ppermute | solution.py:1199
  224.7 16.2 %collective-permute-start.65 = (bf16[160,1280]{1,0:T(8,128)(2,1)S(1)}, bf16[160,1280]{1,0:T(8,128)(2,1)S(1)}, u32[]{:S(2)}, u32[]{:S(2)}) collective-permute-start(bf16[160,1280]{1,0:T(8,128)(2,1)S(1)} %get-tuple-element.444), channel_id=1, source_target_pairs={{0,6},{1,7},{2,4},{3,5},{4,2},{5,3},{6,0},{7,1},{8,14},{9,15},{10,... | collective-permute-start | bytes 1228808 | tf_op jit(solution)/shard_map/ppermute | solution.py:1199
  241.1 20.6 %collective-permute-start.72 = (bf16[320,1280]{1,0:T(8,128)(2,1)S(1)}, bf16[320,1280]{1,0:T(8,128)(2,1)S(1)}, u32[]{:S(2)}, u32[]{:S(2)}) collective-permute-start(bf16[320,1280]{1,0:T(8,128)(2,1)S(1)} %add.42.sent), channel_id=1, source_target_pairs={{8,0},{16,24},{9,1},{17,25},{10,2},{18,26},{11,3},{19,27},{12,4},{... | collective-permute-start | bytes 2457608 | tf_op jit(solution)/shard_map/ppermute | solution.py:1215
  (48 other events, 411.0 us)
